TPU v7x, 32 devices: a whole 2x2x4 slice. The times are simulated.
32 devices in a mesh: pa: 4 (over x, core), pb: 8 (over z, y).
Axes of the slice: x: 2, y: 2, z: 4, core: 2. Of those that a mesh axis runs over, the one named last changes fastest.
Arguments:
- point_keys: bfloat16 [4096, 768], P(('pa', 'pb')), may hold values from -7 to 7
- point_values: bfloat16 [4096, 768], P(('pa', 'pb')), may hold values from -40 to 40
- out_grad: bfloat16 [4096, 768], P(('pa', 'pb')), may hold values from -512 to 512
- decoder_norm: float32 [12, 4096], P(None, ('pa', 'pb')), as said below
- latent_query: bfloat16 [1024, 768], P(('pa', 'pb')), may hold values from -4 to 4
- latent_out: bfloat16 [1024, 768], P(('pa', 'pb')), may hold values from -5 to 5
- encoder_norm: float32 [12, 1024], replicated, as said below
Outputs:
- keys_grad: bfloat16 [4096, 768], P(('pa', 'pb'))
- values_grad: bfloat16 [4096, 768], P(('pa', 'pb'))
- latent_grad: float32 [1024, 768], P(('pa', 'pb'))
Inputs may be any that keep to these rules, and one draw needn't show every extreme that they name: `decoder_norm`: each entry lies between log(1024) - 0.3 and log(1024) + 1.3. `encoder_norm`: each entry lies between log(4096) - 0.3 and log(4096) + 1.3.
All inputs are finite; a program needn't handle non-finite values.
Results may differ from a plain program's by a relative error of at most 0.004.
The roundings to bfloat16 on the way count: a program that leaves them out, or rounds other values in their place, can miss the bound.
Values may be sent and summed in bfloat16 or wider, within the bound.
No kernel may reach another device: no remote copies, remote signals or barrier semaphores. Data moves between devices by JAX's collectives and lax.ppermute only.
A program may use at most 64 MiB of HBM per device.

v0:
```python
import jax
import jax.numpy as jnp
from jax import lax
from jax.sharding import PartitionSpec as P

HEADS = 12
HEAD_DIM = 64


def column(block, current):
    return lax.dynamic_slice_in_dim(block, current * HEAD_DIM, HEAD_DIM, 1)


def put_head(total, piece, current):
    return lax.dynamic_update_slice_in_dim(total, piece, current * HEAD_DIM, 1)


def add_head(total, piece, current):
    return put_head(total, column(total, current) + piece, current)


def across(left, right):
    return lax.dot_general(
        left, right, (((1,), (1,)), ((), ())), preferred_element_type=jnp.float32
    )


def down_rows(left, right):
    return lax.dot_general(
        left, right, (((0,), (0,)), ((), ())), preferred_element_type=jnp.float32
    )


def shards(
    point_keys, point_values, out_grad, decoder_norm, latent_query, latent_out, encoder_norm
):
    scale_factor = HEAD_DIM ** (-0.5)
    lat_all, out_all = (
        lax.all_gather(latent_query, ("pa", "pb"), axis=0, tiled=True),
        lax.all_gather(latent_out, ("pa", "pb"), axis=0, tiled=True),
    )
    point_rows = point_keys.shape[0]
    latent_rows = lat_all.shape[0]
    width = point_keys.shape[1]

    def encoder_row(current):
        return lax.dynamic_slice_in_dim(encoder_norm, current, 1, 0)

    def pass_one(current, state):
        mix_acc, query_acc, key_acc, weighted_acc = state
        key_head = column(point_keys, current)
        grad_head = column(out_grad, current)
        lat_head = column(lat_all, current)
        scores = across(key_head, lat_head) * scale_factor
        decoder_weights = jnp.exp(scores - lax.dynamic_slice_in_dim(decoder_norm, current, 1, 0).T)
        decoder_gradient = across(grad_head, column(out_all, current))
        row_total = jnp.sum(decoder_weights * decoder_gradient, axis=1, keepdims=True)
        decoder_scores_grad = (decoder_weights * (decoder_gradient - row_total)).astype(
            jnp.bfloat16
        )
        mix_acc = put_head(
            mix_acc, down_rows(decoder_weights.astype(jnp.bfloat16), grad_head), current
        )
        query_acc = put_head(
            query_acc, down_rows(decoder_scores_grad, key_head) * scale_factor, current
        )
        key_acc = put_head(
            key_acc,
            jnp.dot(decoder_scores_grad, lat_head, preferred_element_type=jnp.float32)
            * scale_factor,
            current,
        )
        return (mix_acc, query_acc, key_acc, weighted_acc)

    weighted_blank = jnp.zeros((1, 1), jnp.float32)
    latent_blank = jnp.zeros((latent_rows, width), jnp.float32)
    begin = (
        latent_blank,
        latent_blank,
        jnp.zeros((point_rows, width), jnp.float32),
        weighted_blank,
    )
    mix_acc, query_acc, key_acc, weighted_acc = lax.fori_loop(0, HEADS, pass_one, begin)
    mix_grad = lax.psum(mix_acc, ("pa", "pb"))
    mixing_portion = mix_grad.astype(jnp.bfloat16)

    def pass_two(current, state):
        partial_rows, value_acc = state
        scores = across(column(point_keys, current), column(lat_all, current)) * scale_factor
        encoder_portion = jnp.exp(scores - encoder_row(current)).astype(jnp.bfloat16)
        mix_head = column(mixing_portion, current)
        encoder_gradient = across(column(point_values, current), mix_head)
        sums = jnp.sum(encoder_portion.astype(jnp.float32) * encoder_gradient, axis=0)[None, :]
        partial_rows = lax.dynamic_update_slice_in_dim(partial_rows, sums, current, 0)
        value_acc = put_head(
            value_acc,
            jnp.dot(encoder_portion, mix_head, preferred_element_type=jnp.float32),
            current,
        )
        return (partial_rows, value_acc)

    partial_rows, value_acc = lax.fori_loop(
        0,
        HEADS,
        pass_two,
        (jnp.zeros((HEADS, latent_rows), jnp.float32), jnp.zeros((point_rows, width), jnp.float32)),
    )
    column_total = lax.psum(partial_rows, ("pa", "pb"))

    def pass_three(current, state):
        query_acc, key_acc, value_acc = state
        key_head = column(point_keys, current)
        lat_head = column(lat_all, current)
        mix_head = column(mixing_portion, current)
        scores = across(key_head, lat_head) * scale_factor
        encoder = jnp.exp(scores - encoder_row(current))
        encoder_gradient = across(column(point_values, current), mix_head)
        encoder_scores_grad = (
            encoder * (encoder_gradient - lax.dynamic_slice_in_dim(column_total, current, 1, 0))
        ).astype(jnp.bfloat16)
        query_acc = add_head(
            query_acc, down_rows(encoder_scores_grad, key_head) * scale_factor, current
        )
        key_acc = add_head(
            key_acc,
            jnp.dot(encoder_scores_grad, lat_head, preferred_element_type=jnp.float32)
            * scale_factor,
            current,
        )
        return (query_acc, key_acc, value_acc)

    query_acc, key_acc, value_acc = lax.fori_loop(
        0, HEADS, pass_three, (query_acc, key_acc, value_acc)
    )
    latent_grad = lax.psum_scatter(query_acc, ("pa", "pb"), scatter_dimension=0, tiled=True)
    return (key_acc.astype(jnp.bfloat16), value_acc.astype(jnp.bfloat16), latent_grad)


def solution(mesh):
    in_specs = (
        P(("pa", "pb"), None),
        P(("pa", "pb"), None),
        P(("pa", "pb"), None),
        P(None, ("pa", "pb")),
        P(("pa", "pb"), None),
        P(("pa", "pb"), None),
        P(),
    )
    out_specs = (P(("pa", "pb"), None), P(("pa", "pb"), None), P(("pa", "pb"), None))
    return jax.shard_map(shards, mesh=mesh, in_specs=in_specs, out_specs=out_specs, check_vma=False)
```

profile of v0, /device:TPU:0, one launch (start us, length us, event | category | flops | bytes accessed | tf_op | source)
XLA Modules:
  0.0 576.5 jit_solution(12292148037386380637)
XLA Ops:
  9.4 59.3 %all-gather.3.cloned.1.call-done = bf16[1024,768]{1,0:T(8,128)(2,1)} async-done(((bf16[32,768]{1,0:T(8,128)(2,1)}), bf16[1024,768]{1,0:T(8,128)(2,1)}) %all-gather.3.cloned.1.call-update) | async-done | bytes 1572880 | tf_op jit(solution)/shard_map/all_gather | solution.py:39
  68.7 56.9 %all-gather.5.cloned.1.call-done = bf16[1024,768]{1,0:T(8,128)(2,1)} async-done(((bf16[32,768]{1,0:T(8,128)(2,1)}), bf16[1024,768]{1,0:T(8,128)(2,1)}) %all-gather.5.cloned.1.call-update) | async-done | bytes 1572880 | tf_op jit(solution)/shard_map/all_gather | solution.py:40
  125.5 2.0 broadcast_in_dim.16
  127.6 2.1 broadcast_in_dim.16.clone
  129.7 86.6 %while.47 = (s32[]{:T(128)}, f32[1024,768]{0,1:T(8,128)}, f32[1024,768]{0,1:T(8,128)}, f32[128,768]{0,1:T(8,128)S(1)}, bf16[128,768]{1,0:T(8,128)(2,1)}, /*index...) while((s32[]{:T(128)}, f32[1024,768]{0,1:T(8,128)}, ...), condition=%wide.region_2.0_spmd, body=%wide.region_0.0_spmd.sunk | while | flops 85008256 | bytes 5414575 | solution.py:83
  133.0 1.8 fusion.95
  134.8 1.7 convolution_dynamic-update-slice_fusion.4
  140.2 1.8 fusion.95
  142.0 1.7 convolution_dynamic-update-slice_fusion.4
  147.4 1.8 fusion.95
  149.2 1.7 convolution_dynamic-update-slice_fusion.4
  154.6 1.8 fusion.95
  156.3 1.8 convolution_dynamic-update-slice_fusion.4
  161.8 1.8 fusion.95
  163.6 1.8 convolution_dynamic-update-slice_fusion.4
  169.0 1.8 fusion.95
  170.8 1.8 convolution_dynamic-update-slice_fusion.4
  176.2 1.8 fusion.95
  178.0 1.8 convolution_dynamic-update-slice_fusion.4
  183.4 1.8 fusion.95
  185.2 1.8 convolution_dynamic-update-slice_fusion.4
  190.6 1.8 fusion.95
  192.4 1.8 convolution_dynamic-update-slice_fusion.4
  197.9 1.8 fusion.95
  199.7 1.8 convolution_dynamic-update-slice_fusion.4
  205.1 1.8 fusion.95
  206.9 1.8 convolution_dynamic-update-slice_fusion.4
  212.4 1.8 fusion.95
  214.1 1.8 convolution_dynamic-update-slice_fusion.4
  216.3 3.6 copy.10
  219.9 76.8 %all-reduce.1 = bf16[1024,768]{1,0:T(8,128)(2,1)S(1)} all-reduce(f32[1024,768]{1,0:T(8,128)} %copy.10), channel_id=1, replica_groups=mesh['pa'=4,'pb'=8] {'pa','pb'}, use_global_device_ids=true, to_apply=%region_3.0 | all-reduce | flops 786432 | bytes 4718592 | tf_op jit(solution)/shard_map/psum | solution.py:84
  296.7 64.0 %while.48 = (s32[]{:T(128)}, f32[12,1024]{1,0:T(8,128)}, bf16[128,768]{0,1:T(8,128)(2,1)}, bf16[128,768]{1,0:T(8,128)(2,1)}, bf16[1024,768]{1,0:T(8,128)(2,1)S(1...) while((s32[]{:T(128)}, f32[12,1024]{1,0:T(8,128)}, ...), condition=%wide.region_6.0_spmd, body=%wide.region_4.0_spmd.sunk | while | flops 51117060 | bytes 1698987 | solution.py:102
  360.7 39.1 %psum.15 = f32[12,1024]{1,0:T(8,128)} all-reduce(f32[12,1024]{1,0:T(8,128)} %get-tuple-element.457), channel_id=1, replica_groups=mesh['pa'=4,'pb'=8] {'pa','pb'}, use_global_device_ids=true, to_apply=%region_7.0 | all-reduce | flops 12288 | bytes 98304 | tf_op jit(solution)/shard_map/psum | solution.py:108
  399.8 64.4 %while.49 = (s32[]{:T(128)}, f32[1024,768]{0,1:T(8,128)}, f32[128,768]{0,1:T(8,128)S(1)}, bf16[128,768]{1,0:T(8,128)(2,1)}, bf16[1024,768]{1,0:T(8,128)(2,1)S(1)...) while((s32[]{:T(128)}, f32[1024,768]{0,1:T(8,128)}, ...), condition=%wide.region_9.0_spmd, body=%wide.region_8.0_spmd.sunk | while | flops 67911680 | bytes 3338415 | solution.py:132
  402.8 2.0 fusion.114
  408.1 2.0 fusion.114
  413.5 2.0 fusion.114
  418.8 2.0 fusion.114
  424.2 2.0 fusion.114
  429.5 2.0 fusion.114
  434.9 2.0 fusion.114
  440.3 2.0 fusion.114
  445.6 2.0 fusion.114
  451.0 2.0 fusion.114
  456.4 2.0 fusion.114
  461.8 2.0 fusion.114
  464.1 3.5 copy.13
  469.4 100.6 %reduce-scatter.2.cloned.1.call-done = f32[32,768]{1,0:T(8,128)} async-done(((f32[1024,768]{1,0:T(8,128)}), f32[32,768]{1,0:T(8,128)}) %reduce-scatter.2.cloned.1.call-update) | async-done | bytes 98320 | tf_op jit(solution)/shard_map/reduce_scatter | solution.py:135
  (183 shorter events, 151.5 us)
Async XLA Ops:
  7.2 61.5 %all-gather.3.cloned.1.call-start = ((), (), s32[]{:S(2)}) async-start(), calls=%async_computation.1 | async-start | bytes 1622016 | tf_op jit(solution)/shard_map/all_gather | solution.py:39
  7.9 117.6 %all-gather.5.cloned.1.call-start = ((), (), s32[]{:S(2)}) async-start(), calls=%async_computation.2 | async-start | bytes 1622016 | tf_op jit(solution)/shard_map/all_gather | solution.py:40
  8.6 561.4 %reduce-scatter.2.cloned.1.call-start = ((), (), s32[]{:S(2)}) async-start(), calls=%async_computation.3 | async-start | bytes 3244032 | tf_op jit(solution)/shard_map/reduce_scatter | solution.py:135
  68.7 61.0 %copy-start = (bf16[1024,768]{1,0:T(8,128)(2,1)S(1)}, bf16[1024,768]{1,0:T(8,128)(2,1)}, u32[]{:S(2)}) copy-start(bf16[1024,768]{1,0:T(8,128)(2,1)} %all-gather.3.cloned.1.call-done) | copy-start | bytes 4718596
  467.7 0.9 copy-start.1
Sparse Core Ops, SparseCore 0:
  10.9 57.7 all-gather.2
  71.6 53.9 all-gather.4
  467.8 102.1 reduce-scatter.1
where the time goes:
time: 586 us; the launch traced here: 577 us
  waiting for transfers between devices  218 us (37%)
  matrix products  168 us (29%)
  blocking collectives  116 us (20%)
  local copies, waits for them, and re-layouts  56.8 us (10%)
  between operations  13.8 us (2%)
    reduce_scatter x1, waiting for transfers between devices, shards(): lax.psum_scatter(query_acc, ('pa', 'pb'), scatter_dimension=0, tiled=True)  101 us
    dot_general x72, matrix products, across(): lax.dot_general(left, right, (((1,), (1,)), ((), ())), preferred_element_...  81.6 us
    psum x1, blocking collectives, shards(): mix_grad = lax.psum(mix_acc, ('pa', 'pb'))  76.8 us
    dot_general x36, matrix products, down_rows(): lax.dot_general(left, right, (((0,), (0,)), ((), ())), preferred_element_...  66.1 us
    all_gather x1, waiting for transfers between devices, shards(): lax.all_gather(latent_query, ('pa', 'pb'), axis=0, tiled=True)  59.3 us
    all_gather x1, waiting for transfers between devices, shards(): lax.all_gather(latent_out, ('pa', 'pb'), axis=0, tiled=True)  56.9 us
    psum x1, blocking collectives, shards(): column_total = lax.psum(partial_rows, ('pa', 'pb'))  39.1 us
    dynamic_slice x24, local copies, waits for them, and re-layouts, encoder_row(): return lax.dynamic_slice_in_dim(encoder_norm, current, 1, 0)  18.6 us
  transfers between devices with their start and end apart: 3, of which 3 were waited for; matrix products, arithmetic and copies ran while one was open for 0% of the time, Pallas kernels for 0%

commit v1 on v0

--- a/solution.py
+++ b/solution.py
@@ -1,10 +1,452 @@
+import math
+
 import jax
 import jax.numpy as jnp
 from jax import lax
+from jax.experimental import pallas as pl
+from jax.experimental.pallas import tpu as pltpu
 from jax.sharding import PartitionSpec as P
+
 
 HEADS = 12
 HEAD_DIM = 64
+LANES = 128
+AXES = ("pa", "pb")
+MOST_IN_PLANE = 16
+GROUPS = 4
+VMEM_BYTES = 20 * 2**20
+LOG2E = math.log2(math.e)
+
+
+class Plan:
+    def __init__(self, npa, npb, rows, lat_rows, width):
+        self.npa, self.npb = npa, npb
+        self.fast = npb // GROUPS
+        self.plane = npa * self.fast
+        self.rows, self.lat_rows, self.width = rows, lat_rows, width
+        self.heads = HEADS // GROUPS
+        self.cols = self.heads * HEAD_DIM
+        self.points = rows * GROUPS
+        self.block = lat_rows * GROUPS
+        self.latents = self.block * self.plane
+        self.pts_cols = 3 * self.cols + HEAD_DIM
+        self.ct_rows = self.cols + 16
+
+    @staticmethod
+    def fits(npa, npb, rows, lat_rows, width):
+        def power(v):
+            return v > 0 and v & (v - 1) == 0
+
+        return (
+            power(npa)
+            and power(npb)
+            and npb % GROUPS == 0
+            and npa * npb // GROUPS <= MOST_IN_PLANE
+            and lat_rows * GROUPS == LANES
+            and rows % LANES == 0
+            and width == HEADS * HEAD_DIM
+        )
+
+    def exchange(self, value, over_group, step):
+        pairs = []
+        for a in range(self.npa):
+            for b in range(self.npb):
+                z, f = divmod(b, self.fast)
+                if over_group:
+                    a2, z2, f2 = a, z ^ step, f
+                else:
+                    a2, z2, f2 = a ^ (step // self.fast), z, f ^ (step % self.fast)
+                pairs.append((a * self.npb + b, a2 * self.npb + z2 * self.fast + f2))
+        return lax.ppermute(value, AXES, pairs)
+
+
+def vmem():
+    return pl.BlockSpec(memory_space=pltpu.VMEM)
+
+
+def call(kernel, outs, args, scratch=(), flops=0):
+    nbytes = sum(a.size * a.dtype.itemsize for a in args)
+    nbytes += sum(math.prod(o.shape) * o.dtype.itemsize for o in outs)
+    return pl.pallas_call(
+        kernel,
+        out_shape=tuple(outs),
+        in_specs=[vmem()] * len(args),
+        out_specs=tuple(vmem() for _ in outs),
+        scratch_shapes=list(scratch),
+        cost_estimate=pl.CostEstimate(flops=flops, bytes_accessed=nbytes, transcendentals=flops // 256),
+        compiler_params=pltpu.CompilerParams(vmem_limit_bytes=VMEM_BYTES),
+    )(*args)
+
+
+def shaped(shape, dtype):
+    return jax.ShapeDtypeStruct(shape, dtype)
+
+
+def by_group(pieces, z):
+    out = list(pieces)
+    bit = 1
+    while bit < len(out):
+        on = (z & bit) != 0
+        out = [jnp.where(on, out[g ^ bit], out[g]) for g in range(len(out))]
+        bit *= 2
+    return out
+
+
+def group_index(plan):
+    return lax.axis_index("pb") // plan.fast
+
+
+def split3(value):
+    hi = value.astype(jnp.bfloat16).astype(jnp.float32)
+    rest = value - hi
+    mid = rest.astype(jnp.bfloat16).astype(jnp.float32)
+    return hi, mid, rest - mid
+
+
+def nn(a, b):
+    return lax.dot_general(a, b, (((1,), (0,)), ((), ())), preferred_element_type=jnp.float32)
+
+
+def nt(a, b):
+    return lax.dot_general(a, b, (((1,), (1,)), ((), ())), preferred_element_type=jnp.float32)
+
+
+def turned(block):
+    return block.astype(jnp.float32).T.astype(block.dtype)
+
+
+def pack_latents(plan, query, out):
+    def kernel(q_ref, o_ref, *outs):
+        z = group_index(plan)
+        q, o = q_ref[...].astype(jnp.float32), o_ref[...].astype(jnp.float32)
+        c = plan.cols
+        pieces = by_group(
+            [
+                jnp.concatenate([q[:, g * c : (g + 1) * c], o[:, g * c : (g + 1) * c]], axis=1)
+                for g in range(GROUPS)
+            ],
+            z,
+        )
+        for ref, piece in zip(outs, pieces, strict=True):
+            ref[...] = piece.astype(jnp.bfloat16)
+
+    outs = [shaped((plan.lat_rows, 2 * plan.cols), jnp.bfloat16)] * GROUPS
+    return call(kernel, outs, (query, out))
+
+
+def pack_points(plan, keys, grads, values, norm):
+    def kernel(k_ref, g_ref, v_ref, n_ref, *outs):
+        z = group_index(plan)
+        c, hs = plan.cols, plan.heads
+        for first, ref in ((0, k_ref), (1, g_ref), (2, v_ref)):
+            whole = ref[...].astype(jnp.float32)
+            pieces = by_group([whole[:, g * c : (g + 1) * c] for g in range(GROUPS)], z)
+            for out, piece in zip(outs, pieces, strict=True):
+                out[:, first * c : (first + 1) * c] = piece.astype(jnp.bfloat16)
+        norms = by_group([n_ref[g * hs : (g + 1) * hs, :] for g in range(GROUPS)], z)
+        for out, norm_rows in zip(outs, norms, strict=True):
+            fill = jnp.zeros((HEAD_DIM - 3 * hs, plan.rows), jnp.float32)
+            stack = jnp.concatenate([*split3(norm_rows), fill], axis=0)
+            out[:, 3 * c :] = stack.T.astype(jnp.bfloat16)
+
+    outs = [shaped((plan.rows, plan.pts_cols), jnp.bfloat16)] * GROUPS
+    return call(kernel, outs, (keys, grads, values, norm))
+
+
+def order_norm(plan, norm):
+    def kernel(n_ref, out_ref):
+        z = group_index(plan)
+        member = lax.axis_index("pa") * plan.npb + lax.axis_index("pb")
+        hs, m = plan.heads, plan.latents
+        rows = by_group([n_ref[g * hs : (g + 1) * hs, :] for g in range(GROUPS)], z)[0]
+        fill = jnp.zeros((16 - 3 * hs, m), jnp.float32)
+        stack = jnp.concatenate([*split3(rows), fill], axis=0).astype(jnp.bfloat16)
+        lane = lax.broadcasted_iota(jnp.int32, (1, m), 1)
+        inner, j, k = lane % plan.lat_rows, (lane // plan.lat_rows) % GROUPS, lane // plan.block
+        owner = (k // plan.fast) * plan.npb + j * plan.fast + k % plan.fast
+        source = (owner ^ member) * plan.lat_rows + inner
+        total = jnp.zeros((16, m), jnp.float32)
+        step = 256
+        for start in range(0, m, step):
+            row = lax.broadcasted_iota(jnp.int32, (step, m), 0) + start
+            chosen = jnp.where(row == source, 1.0, 0.0).astype(jnp.bfloat16)
+            total = total + nn(stack[:, start : start + step], chosen)
+        out_ref[0:hs, :] = (total[:hs] + total[hs : 2 * hs]) + total[2 * hs : 3 * hs]
+
+    return call(kernel, [shaped((plan.heads, plan.latents), jnp.float32)], (norm,))[0]
+
+
+def turn_latents(plan, slots):
+    def kernel(*refs):
+        *ins, out = refs
+        out[...] = turned(jnp.concatenate([r[...] for r in ins], axis=0))
+
+    outs = [shaped((2 * plan.cols, plan.block), jnp.bfloat16)]
+    return call(kernel, outs, slots)[0]
+
+
+def norm_column(plan, pts, head):
+    base, hs = 3 * plan.cols, plan.heads
+    parts = [
+        pts[:, base + i * hs + head : base + i * hs + head + 1].astype(jnp.float32) for i in range(3)
+    ]
+    return (parts[0] + parts[1]) + parts[2]
+
+
+def first_pass(plan, lats, pts, norm):
+    n_lat, n_pts = len(lats), len(pts)
+    c, m = plan.cols, plan.latents
+
+    def kernel(*refs):
+        lat_refs, pts_refs, norm_ref = refs[:n_lat], refs[n_lat : n_lat + n_pts], refs[n_lat + n_pts]
+        outs = refs[n_lat + n_pts + 1 : -4]
+        query, sides, dec, enc = refs[-4:]
+        for k, ref in enumerate(lat_refs):
+            query[:, k * plan.block : (k + 1) * plan.block] = ref[:c, :]
+        for j, ref in enumerate(pts_refs):
+            sides[:, j * plan.rows : (j + 1) * plan.rows] = turned(ref[:, c : 3 * c])
+        for h in range(plan.heads):
+            mine = slice(h * HEAD_DIM, (h + 1) * HEAD_DIM)
+            enc_norm = norm_ref[h : h + 1, :] * LOG2E
+            for j, ref in enumerate(pts_refs):
+                scores = nn(ref[:, mine], query[mine, :]) * (HEAD_DIM**-0.5 * LOG2E)
+                rows = slice(j * plan.rows, (j + 1) * plan.rows)
+                dec_norm = norm_column(plan, ref, h) * LOG2E
+                dec[rows, :] = jnp.exp2(scores - dec_norm).astype(jnp.bfloat16)
+                enc[rows, :] = jnp.exp2(scores - enc_norm).astype(jnp.bfloat16)
+            below = slice(c + h * HEAD_DIM, c + (h + 1) * HEAD_DIM)
+            mix = nn(sides[mine, :], dec[...])
+            weighted = nn(sides[below, :], enc[...])
+            for k, out in enumerate(outs):
+                lanes = slice(k * plan.block, (k + 1) * plan.block)
+                out[mine, :] = mix[:, lanes]
+                out[below, :] = weighted[:, lanes]
+
+    outs = [shaped((2 * c, plan.block), jnp.float32)] * plan.plane
+    scratch = [
+        pltpu.VMEM((c, m), jnp.bfloat16),
+        pltpu.VMEM((2 * c, plan.points), jnp.bfloat16),
+        pltpu.VMEM((plan.points, m), jnp.bfloat16),
+        pltpu.VMEM((plan.points, m), jnp.bfloat16),
+    ]
+    flops = 6 * plan.points * m * c
+    return call(kernel, outs, (*lats, *pts, norm), scratch, flops)
+
+
+def decoder_pass(plan, lats, pts, heads):
+    n_lat = len(lats)
+    c, m = plan.cols, plan.latents
+
+    def kernel(*refs):
+        lat_refs, pts_refs = refs[:n_lat], refs[n_lat:-5]
+        key_ref, lat_ref = refs[-5:-3]
+        both, keys_t, ds = refs[-3:]
+        for k, ref in enumerate(lat_refs):
+            both[:, k * plan.block : (k + 1) * plan.block] = ref[...]
+        for j, ref in enumerate(pts_refs):
+            keys_t[:, j * plan.rows : (j + 1) * plan.rows] = turned(ref[:, :c])
+        for at, h in enumerate(heads):
+            mine = slice(h * HEAD_DIM, (h + 1) * HEAD_DIM)
+            put = slice(at * HEAD_DIM, (at + 1) * HEAD_DIM)
+            other = slice(c + h * HEAD_DIM, c + (h + 1) * HEAD_DIM)
+            for j, ref in enumerate(pts_refs):
+                rows = slice(j * plan.rows, (j + 1) * plan.rows)
+                scores = nn(ref[:, mine], both[mine, :]) * (HEAD_DIM**-0.5 * LOG2E)
+                dec = jnp.exp2(scores - norm_column(plan, ref, h) * LOG2E)
+                grad = nn(ref[:, other], both[other, :])
+                total = jnp.sum(dec * grad, axis=1, keepdims=True)
+                tile = (dec * (grad - total)).astype(jnp.bfloat16)
+                ds[rows, :] = tile
+                key_ref[rows, put] = nt(tile, both[mine, :])
+            lat_ref[put, :] = nn(keys_t[mine, :], ds[...])
+
+    width = len(heads) * HEAD_DIM
+    outs = [shaped((plan.points, width), jnp.float32), shaped((width, m), jnp.float32)]
+    scratch = [
+        pltpu.VMEM((2 * c, m), jnp.bfloat16),
+        pltpu.VMEM((c, plan.points), jnp.bfloat16),
+        pltpu.VMEM((plan.points, m), jnp.bfloat16),
+    ]
+    flops = 8 * plan.points * m * width
+    return call(kernel, outs, (*lats, *pts), scratch, flops)
+
+
+def reduce_mix(plan, parts):
+    c, hs = plan.cols, plan.heads
+
+    def kernel(*refs):
+        *ins, out = refs
+        total = ins[0][...]
+        for ref in ins[1:]:
+            total = total + ref[...]
+        half = total[:c].astype(jnp.bfloat16)
+        out[:c, :] = half
+        product = half.astype(jnp.float32) * total[c:]
+        sums = [
+            jnp.sum(product[h * HEAD_DIM : (h + 1) * HEAD_DIM], axis=0, keepdims=True) for h in range(hs)
+        ]
+        fill = jnp.zeros((16 - 3 * hs, plan.block), jnp.float32)
+        stack = jnp.concatenate([*split3(jnp.concatenate(sums, axis=0)), fill], axis=0)
+        out[c:, :] = stack.astype(jnp.bfloat16)
+
+    outs = [shaped((plan.ct_rows, plan.block), jnp.bfloat16)]
+    return call(kernel, outs, parts)[0]
+
+
+def encoder_pass(plan, lats, pts, norm, mixes, before):
+    places = [(part, at) for part, (heads, _) in enumerate(before) for at in range(len(heads))]
+    n_lat, n_pts, n_mix = len(lats), len(pts), len(mixes)
+    c, m, hs = plan.cols, plan.latents, plan.heads
+
+    def kernel(*refs):
+        refs = list(refs)
+
+        def take(n):
+            got = refs[:n]
+            del refs[:n]
+            return got
+
+        lat_refs, pts_refs = take(n_lat), take(n_pts)
+        (norm_ref,) = take(1)
+        mix_refs = take(n_mix)
+        parts_in = [take(2) for _ in before]
+        pts_outs, lat_outs = take(n_pts), take(n_lat)
+        query, mix, keys_t, ds = refs
+        for k, ref in enumerate(lat_refs):
+            query[:, k * plan.block : (k + 1) * plan.block] = ref[:c, :]
+        for k, ref in enumerate(mix_refs):
+            mix[:, k * plan.block : (k + 1) * plan.block] = ref[...]
+        for j, ref in enumerate(pts_refs):
+            keys_t[:, j * plan.rows : (j + 1) * plan.rows] = turned(ref[:, :c])
+        tail = mix[c:, :].astype(jnp.float32)
+        columns = (tail[:hs] + tail[hs : 2 * hs]) + tail[2 * hs : 3 * hs]
+        for h in range(plan.heads):
+            mine = slice(h * HEAD_DIM, (h + 1) * HEAD_DIM)
+            third = slice(2 * c + h * HEAD_DIM, 2 * c + (h + 1) * HEAD_DIM)
+            enc_norm = norm_ref[h : h + 1, :] * LOG2E
+            column = columns[h : h + 1, :]
+            part, at = places[h]
+            key_in, lat_in = parts_in[part]
+            put = slice(at * HEAD_DIM, (at + 1) * HEAD_DIM)
+            for j, ref in enumerate(pts_refs):
+                rows = slice(j * plan.rows, (j + 1) * plan.rows)
+                scores = nn(ref[:, mine], query[mine, :]) * (HEAD_DIM**-0.5 * LOG2E)
+                enc = jnp.exp2(scores - enc_norm)
+                grad = nn(ref[:, third], mix[mine, :])
+                tile = (enc * (grad - column)).astype(jnp.bfloat16)
+                ds[rows, :] = tile
+                key = (key_in[rows, put] + nt(tile, query[mine, :])) * HEAD_DIM**-0.5
+                pts_outs[j][:, mine] = key.astype(jnp.bfloat16)
+                value = nt(enc.astype(jnp.bfloat16), mix[mine, :])
+                pts_outs[j][:, c + h * HEAD_DIM : c + (h + 1) * HEAD_DIM] = value.astype(jnp.bfloat16)
+            lat = (lat_in[put, :] + nn(keys_t[mine, :], ds[...])) * HEAD_DIM**-0.5
+            for k, out in enumerate(lat_outs):
+                out[mine, :] = lat[:, k * plan.block : (k + 1) * plan.block]
+
+    outs = [shaped((plan.rows, 2 * c), jnp.bfloat16)] * n_pts
+    outs += [shaped((c, plan.block), jnp.float32)] * n_lat
+    scratch = [
+        pltpu.VMEM((c, m), jnp.bfloat16),
+        pltpu.VMEM((plan.ct_rows, m), jnp.bfloat16),
+        pltpu.VMEM((c, plan.points), jnp.bfloat16),
+        pltpu.VMEM((plan.points, m), jnp.bfloat16),
+    ]
+    flops = 10 * plan.points * m * c
+    args = (*lats, *pts, norm, *mixes, *(a for _, part in before for a in part))
+    got = call(kernel, outs, args, scratch, flops)
+    return got[:n_pts], got[n_pts:]
+
+
+def add_pairs(mine, theirs):
+    def kernel(*refs):
+        n = len(mine)
+        for a, b, out in zip(refs[:n], refs[n : 2 * n], refs[2 * n :], strict=True):
+            out[...] = a[...] + b[...]
+
+    outs = [shaped(a.shape, a.dtype) for a in mine]
+    return call(kernel, outs, (*mine, *theirs))
+
+
+def reduce_latents(plan, parts):
+    def kernel(*refs):
+        ins, outs = refs[: len(parts)], refs[len(parts) :]
+        total = ins[0][...]
+        for ref in ins[1:]:
+            total = total + ref[...]
+        total = total.T
+        for j, out in enumerate(outs):
+            out[...] = total[j * plan.lat_rows : (j + 1) * plan.lat_rows]
+
+    outs = [shaped((plan.lat_rows, plan.cols), jnp.float32)] * GROUPS
+    return call(kernel, outs, parts)
+
+
+def place_points(plan, slots):
+    def kernel(*refs):
+        ins, (key_out, value_out) = refs[:GROUPS], refs[GROUPS:]
+        z = group_index(plan)
+        c = plan.cols
+        pieces = by_group([r[...].astype(jnp.float32) for r in ins], z)
+        for g, piece in enumerate(pieces):
+            key_out[:, g * c : (g + 1) * c] = piece[:, :c].astype(jnp.bfloat16)
+            value_out[:, g * c : (g + 1) * c] = piece[:, c:].astype(jnp.bfloat16)
+
+    outs = [shaped((plan.rows, plan.width), jnp.bfloat16)] * 2
+    return call(kernel, outs, slots)
+
+
+def place_latents(plan, slots):
+    def kernel(*refs):
+        *ins, out = refs
+        pieces = by_group([r[...] for r in ins], group_index(plan))
+        for g, piece in enumerate(pieces):
+            out[:, g * plan.cols : (g + 1) * plan.cols] = piece
+
+    outs = [shaped((plan.lat_rows, plan.width), jnp.float32)]
+    return call(kernel, outs, slots)[0]
+
+
+def grouped(
+    plan, point_keys, point_values, out_grad, decoder_norm, latent_query, latent_out, encoder_norm
+):
+    def over_group(slots):
+        return (slots[0], *(plan.exchange(s, True, j) for j, s in enumerate(slots) if j))
+
+    def sum_cores(blocks):
+        near = [k for k in range(plan.plane) if not k & plan.fast]
+        theirs = [plan.exchange(blocks[k | plan.fast], False, plan.fast) for k in near]
+        return near, add_pairs([blocks[k] for k in near], theirs)
+
+    def from_chips(near, blocks):
+        return [b if k == 0 else plan.exchange(b, False, k) for k, b in zip(near, blocks, strict=True)]
+
+    def to_plane(block):
+        got = {0: block}
+        for k in range(1, plan.plane):
+            if not k & plan.fast:
+                got[k] = plan.exchange(block, False, k)
+        for k in range(plan.plane):
+            if k & plan.fast:
+                got[k] = plan.exchange(got[k ^ plan.fast], False, plan.fast)
+        return tuple(got[k] for k in range(plan.plane))
+
+    lat_slots = over_group(pack_latents(plan, latent_query, latent_out))
+    pts = pack_points(plan, point_keys, out_grad, point_values, decoder_norm)
+    pts = over_group(pts)
+    norm = order_norm(plan, encoder_norm)
+    lats = to_plane(turn_latents(plan, lat_slots))
+    cores = sum_cores(first_pass(plan, lats, pts, norm))
+    early, late = tuple(range(plan.heads))[:-1], tuple(range(plan.heads))[-1:]
+    before = [(early, decoder_pass(plan, lats, pts, early))]
+    sums = from_chips(*cores)
+    before.append((late, decoder_pass(plan, lats, pts, late)))
+    mixes = to_plane(reduce_mix(plan, sums))
+    pts_out, lat_out = encoder_pass(plan, lats, pts, norm, mixes, before)
+    lat_out = from_chips(*sum_cores(lat_out))
+    pts_out = over_group(pts_out)
+    lat_rows = over_group(reduce_latents(plan, lat_out))
+    keys_grad, values_grad = place_points(plan, pts_out)
+    return keys_grad, values_grad, place_latents(plan, lat_rows)
 
 
 def column(block, current):
@@ -31,7 +473,7 @@
     )
 
 
-def shards(
+def gathered(
     point_keys, point_values, out_grad, decoder_norm, latent_query, latent_out, encoder_norm
 ):
     scale_factor = HEAD_DIM ** (-0.5)
@@ -80,7 +522,7 @@
         jnp.zeros((point_rows, width), jnp.float32),
         weighted_blank,
     )
-    mix_acc, query_acc, key_acc, weighted_acc = lax.fori_loop(0, HEADS, pass_one, begin)
+    mix_acc, query_acc, key_acc, _ = lax.fori_loop(0, HEADS, pass_one, begin)
     mix_grad = lax.psum(mix_acc, ("pa", "pb"))
     mixing_portion = mix_grad.astype(jnp.bfloat16)
 
@@ -147,4 +589,12 @@
         P(),
     )
     out_specs = (P(("pa", "pb"), None), P(("pa", "pb"), None), P(("pa", "pb"), None))
+    npa, npb = mesh.shape["pa"], mesh.shape["pb"]
+
+    def shards(*args):
+        plan_of = (npa, npb, args[0].shape[0], args[4].shape[0], args[0].shape[1])
+        if Plan.fits(*plan_of):
+            return grouped(Plan(*plan_of), *args)
+        return gathered(*args)
+
     return jax.shard_map(shards, mesh=mesh, in_specs=in_specs, out_specs=out_specs, check_vma=False)

time: 586 us -> 95.2 us (0.16); the launches traced: 577 us -> 95 us
  waiting for transfers between devices: 218 us -> 36.7 us
  matrix products: 168 us -> 0 us
  blocking collectives: 116 us -> 0 us
  local copies, waits for them, and re-layouts: 56.8 us -> 3.49 us
  starting transfers between devices: 0.11 us -> 37 us
  Pallas kernels: 0 us -> 17 us
  between operations: 13.8 us -> 0.81 us
    dot_general x144 -> x0, matrix products: 168 us -> none  [the longest x72 81.6 us: across(): lax.dot_general(left, right, (((1,), (1,)), ((), ())), preferred_element_...]
    all_gather x2 -> x0, waiting for transfers between devices: 116 us -> none  [the longest x1 59.3 us: shards(): lax.all_gather(latent_query, ('pa', 'pb'), axis=0, tiled=True)]
    psum x2 -> x0, blocking collectives: 116 us -> none  [the longest x1 76.8 us: shards(): mix_grad = lax.psum(mix_acc, ('pa', 'pb'))]
    reduce_scatter x1 -> x0, waiting for transfers between devices: 101 us -> none  [shards(): lax.psum_scatter(query_acc, ('pa', 'pb'), scatter_dimension=0, tiled=True)]
    ppermute x0 -> x40, starting transfers between devices: none -> 37 us  [exchange(): return lax.ppermute(value, AXES, pairs)]
    ppermute x0 -> x40, waiting for transfers between devices: none -> 36.7 us  [exchange(): return lax.ppermute(value, AXES, pairs)]
    dynamic_slice x24 -> x0, local copies, waits for them, and re-layouts: 18.6 us -> none  [encoder_row(): return lax.dynamic_slice_in_dim(encoder_norm, current, 1, 0)]
    pallas_call x0 -> x14, Pallas kernels: none -> 17 us  [call(): pl.pallas_call(kernel, out_shape=tuple(outs), in_specs=[vmem()] * len(arg...]
  transfers between devices with their start and end apart: 3 -> 40, of which waited for: 3 -> 21; matrix products, arithmetic and copies ran while one was open for 0% -> 0% of each run, Pallas kernels for 0% -> 8%
where the time goes in v1:
time: 95.2 us; the launch traced here: 95 us
  starting transfers between devices  37 us (39%)
  waiting for transfers between devices  36.7 us (39%)
  Pallas kernels  17 us (18%)
  local copies, waits for them, and re-layouts  3.49 us (4%)
    ppermute x40, starting transfers between devices, exchange(): return lax.ppermute(value, AXES, pairs)  37 us
    ppermute x40, waiting for transfers between devices, exchange(): return lax.ppermute(value, AXES, pairs)  36.7 us
    pallas_call x14, Pallas kernels, call(): pl.pallas_call(kernel, out_shape=tuple(outs), in_specs=[vmem()] * len(arg...  17 us
    unnamed x14, local copies, waits for them, and re-layouts  3.49 us
  transfers between devices with their start and end apart: 40, of which 21 were waited for; matrix products, arithmetic and copies ran while one was open for 0% of the time, Pallas kernels for 8%

profile of v1, /device:TPU:0, one launch (start us, length us, event | category | flops | bytes accessed | tf_op | source)
XLA Modules:
  0.0 95.0 jit_solution(17657566532299170329)
XLA Ops:
  0.7 0.8 copy-done.4
  1.5 0.8 copy-done.5
  2.4 3.1 %collective-permute-start = (bf16[32,384]{1,0:T(8,128)(2,1)S(1)}, bf16[32,384]{1,0:T(8,128)(2,1)S(1)}, u32[]{:S(2)}, u32[]{:S(2)}) collective-permute-start(bf16[32,384]{1,0:T(8,128)(2,1)S(1)} %get-tuple-element.50), channel_id=1, source_target_pairs={{0,2},{1,3},{2,0},{3,1},{4,6},{5,7},{6,4},{7,5},{8,10},{9,11},{10,... | collective-permute-start | bytes 73736 | tf_op jit(solution)/shard_map/ppermute | solution.py:60
  5.5 2.6 %collective-permute-start.1 = (bf16[32,384]{1,0:T(8,128)(2,1)S(1)}, bf16[32,384]{1,0:T(8,128)(2,1)S(1)}, u32[]{:S(2)}, u32[]{:S(2)}) collective-permute-start(bf16[32,384]{1,0:T(8,128)(2,1)S(1)} %get-tuple-element.51), channel_id=1, source_target_pairs={{0,4},{1,5},{2,6},{3,7},{4,0},{5,1},{6,2},{7,3},{8,12},{9,13},{10,... | collective-permute-start | bytes 73736 | tf_op jit(solution)/shard_map/ppermute | solution.py:60
  8.1 2.5 %collective-permute-done.1.refs_2_ = bf16[32,384]{1,0:T(8,128)(2,1)S(1)} collective-permute-done((bf16[32,384]{1,0:T(8,128)(2,1)S(1)}, bf16[32,384]{1,0:T(8,128)(2,1)S(1)}, u32[]{:S(2)}, u32[]{:S(2)}) %collective-permute-start.1) | collective-permute-done | bytes 24608 | tf_op jit(solution)/shard_map/ppermute | solution.py:60
  10.6 3.1 %collective-permute-done.2.refs_3_ = bf16[32,384]{1,0:T(8,128)(2,1)S(1)} collective-permute-done((bf16[32,384]{1,0:T(8,128)(2,1)S(1)}, bf16[32,384]{1,0:T(8,128)(2,1)S(1)}, u32[]{:S(2)}, u32[]{:S(2)}) %collective-permute-start.2) | collective-permute-done | bytes 24608 | tf_op jit(solution)/shard_map/ppermute | solution.py:60
  13.8 1.6 %collective-permute-start.3 = (bf16[384,128]{1,0:T(8,128)(2,1)S(1)}, bf16[384,128]{1,0:T(8,128)(2,1)S(1)}, u32[]{:S(2)}, u32[]{:S(2)}) collective-permute-start(bf16[384,128]{1,0:T(8,128)(2,1)S(1)} %shard_map.95.refs_0_), channel_id=1, source_target_pairs={{0,1},{1,0},{2,3},{3,2},{4,5},{5,4},{6,7},{7,6},{8,9},{9,8},{10,11... | collective-permute-start | bytes 294920 | tf_op jit(solution)/shard_map/ppermute | solution.py:60
  15.4 0.9 copy-done.1
  16.4 0.9 copy-done.2
  17.3 0.7 shard_map.96
  18.0 1.6 %collective-permute-start.6 = (bf16[384,128]{1,0:T(8,128)(2,1)S(1)}, bf16[384,128]{1,0:T(8,128)(2,1)S(1)}, u32[]{:S(2)}, u32[]{:S(2)}) collective-permute-start(bf16[384,128]{1,0:T(8,128)(2,1)S(1)} %shard_map.95.refs_0_), channel_id=1, source_target_pairs={{0,16},{1,17},{2,18},{3,19},{4,20},{5,21},{6,22},{7,23},{8,24},{9,... | collective-permute-start | bytes 294920 | tf_op jit(solution)/shard_map/ppermute | solution.py:60
  19.6 0.5 collective-permute-start.7
  20.1 0.7 collective-permute-start.11
  20.8 3.6 %collective-permute-start.12 = (bf16[128,640]{1,0:T(8,128)(2,1)S(1)}, bf16[128,640]{1,0:T(8,128)(2,1)S(1)}, u32[]{:S(2)}, u32[]{:S(2)}) collective-permute-start(bf16[128,640]{1,0:T(8,128)(2,1)S(1)} %get-tuple-element.56), channel_id=1, source_target_pairs={{0,6},{1,7},{2,4},{3,5},{4,2},{5,3},{6,0},{7,1},{8,14},{9,15},{10,... | collective-permute-start | bytes 491528 | tf_op jit(solution)/shard_map/ppermute | solution.py:60
  24.4 1.0 %collective-permute-done.7.refs_5_ = bf16[384,128]{1,0:T(8,128)(2,1)S(1)} collective-permute-done((bf16[384,128]{1,0:T(8,128)(2,1)S(1)}, bf16[384,128]{1,0:T(8,128)(2,1)S(1)}, u32[]{:S(2)}, u32[]{:S(2)}) %collective-permute-start.7) | collective-permute-done | bytes 98336 | tf_op jit(solution)/shard_map/ppermute | solution.py:60
  25.9 0.4 shard_map.97.refs_12_
  26.4 8.7 %collective-permute-done.11.refs_10_ = bf16[128,640]{1,0:T(8,128)(2,1)S(1)} collective-permute-done((bf16[128,640]{1,0:T(8,128)(2,1)S(1)}, bf16[128,640]{1,0:T(8,128)(2,1)S(1)}, u32[]{:S(2)}, u32[]{:S(2)}) %collective-permute-start.11) | collective-permute-done | bytes 163872 | tf_op jit(solution)/shard_map/ppermute | solution.py:60
  35.1 3.2 %shard_map.98 = (f32[384,128]{1,0:T(8,128)S(1)}, f32[384,128]{1,0:T(8,128)S(1)}, f32[384,128]{1,0:T(8,128)S(1)}, f32[384,128]{1,0:T(8,128)S(1)}, f32[384,128]{1,...) custom-call(bf16[384,128]{1,0:T(8,128)(2,1)S(1)} %shard_map.95.refs_0_, ...), custom_call_target="tpu_custom_call" | custom-call | flops 603979776 | bytes 3026944 | tf_op jit(solution)/shard_map/pallas_call | solution.py:70
  38.4 0.5 collective-permute-start.14
  38.9 0.4 collective-permute-start.16
  40.7 1.6 %collective-permute-start.17 = (f32[384,128]{1,0:T(8,128)S(1)}, f32[384,128]{1,0:T(8,128)S(1)}, u32[]{:S(2)}, u32[]{:S(2)}) collective-permute-start(f32[384,128]{1,0:T(8,128)S(1)} %get-tuple-element.66), channel_id=1, source_target_pairs={{0,1},{1,0},{2,3},{3,2},{4,5},{5,4},{6,7},{7,6},{8,9},{9,8},{10,11... | collective-permute-start | bytes 589832 | tf_op jit(solution)/shard_map/ppermute | solution.py:60
  42.3 1.5 %collective-permute-start.18 = (f32[384,128]{1,0:T(8,128)S(1)}, f32[384,128]{1,0:T(8,128)S(1)}, u32[]{:S(2)}, u32[]{:S(2)}) collective-permute-start(f32[384,128]{1,0:T(8,128)S(1)} %get-tuple-element.67), channel_id=1, source_target_pairs={{0,16},{1,17},{2,18},{3,19},{4,20},{5,21},{6,22},{7,23},{8,24},{9,... | collective-permute-start | bytes 589832 | tf_op jit(solution)/shard_map/ppermute | solution.py:60
  43.8 0.5 collective-permute-start.19
  44.3 3.5 %collective-permute-done.17.refs_1_ = f32[384,128]{1,0:T(8,128)S(1)} collective-permute-done((f32[384,128]{1,0:T(8,128)S(1)}, f32[384,128]{1,0:T(8,128)S(1)}, u32[]{:S(2)}, u32[]{:S(2)}) %collective-permute-start.17) | collective-permute-done | bytes 196640 | tf_op jit(solution)/shard_map/ppermute | solution.py:60
  47.8 2.3 %collective-permute-done.18.refs_2_ = f32[384,128]{1,0:T(8,128)S(1)} collective-permute-done((f32[384,128]{1,0:T(8,128)S(1)}, f32[384,128]{1,0:T(8,128)S(1)}, u32[]{:S(2)}, u32[]{:S(2)}) %collective-permute-start.18) | collective-permute-done | bytes 196640 | tf_op jit(solution)/shard_map/ppermute | solution.py:60
  50.1 3.1 %collective-permute-done.19.refs_3_ = f32[384,128]{1,0:T(8,128)S(1)} collective-permute-done((f32[384,128]{1,0:T(8,128)S(1)}, f32[384,128]{1,0:T(8,128)S(1)}, u32[]{:S(2)}, u32[]{:S(2)}) %collective-permute-start.19) | collective-permute-done | bytes 196640 | tf_op jit(solution)/shard_map/ppermute | solution.py:60
  53.3 1.6 %collective-permute-start.20 = (bf16[208,128]{1,0:T(8,128)(2,1)S(1)}, bf16[208,128]{1,0:T(8,128)(2,1)S(1)}, u32[]{:S(2)}, u32[]{:S(2)}) collective-permute-start(bf16[208,128]{1,0:T(8,128)(2,1)S(1)} %shard_map.100.refs_13_), channel_id=1, source_target_pairs={{0,1},{1,0},{2,3},{3,2},{4,5},{5,4},{6,7},{7,6},{8,9},{9,8},{10,11... | collective-permute-start | bytes 159752 | tf_op jit(solution)/shard_map/ppermute | solution.py:60
  54.9 1.5 %collective-permute-start.23 = (bf16[208,128]{1,0:T(8,128)(2,1)S(1)}, bf16[208,128]{1,0:T(8,128)(2,1)S(1)}, u32[]{:S(2)}, u32[]{:S(2)}) collective-permute-start(bf16[208,128]{1,0:T(8,128)(2,1)S(1)} %shard_map.100.refs_13_), channel_id=1, source_target_pairs={{0,16},{1,17},{2,18},{3,19},{4,20},{5,21},{6,22},{7,23},{8,24},{9,... | collective-permute-start | bytes 159752 | tf_op jit(solution)/shard_map/ppermute | solution.py:60
  56.4 0.5 collective-permute-start.24
  56.8 0.6 collective-permute-done.20.refs_14_
  57.5 1.5 %collective-permute-done.23.refs_17_ = bf16[208,128]{1,0:T(8,128)(2,1)S(1)} collective-permute-done((bf16[208,128]{1,0:T(8,128)(2,1)S(1)}, bf16[208,128]{1,0:T(8,128)(2,1)S(1)}, u32[]{:S(2)}, u32[]{:S(2)}) %collective-permute-start.23) | collective-permute-done | bytes 53280 | tf_op jit(solution)/shard_map/ppermute | solution.py:60
  59.0 2.4 %collective-permute-done.24.refs_18_ = bf16[208,128]{1,0:T(8,128)(2,1)S(1)} collective-permute-done((bf16[208,128]{1,0:T(8,128)(2,1)S(1)}, bf16[208,128]{1,0:T(8,128)(2,1)S(1)}, u32[]{:S(2)}, u32[]{:S(2)}) %collective-permute-start.24) | collective-permute-done | bytes 53280 | tf_op jit(solution)/shard_map/ppermute | solution.py:60
  61.4 1.9 %shard_map.102 = (f32[512,64]{1,0:T(8,128)S(1)}, f32[64,1024]{1,0:T(8,128)S(1)}) custom-call(bf16[384,128]{1,0:T(8,128)(2,1)S(1)} %shard_map.95.refs_0_, bf16[384,128]{1,0:T(8,128)(2,1)S(1)} %collective-permute-done.3.refs_1_, bf16[384,128]{1,0:T(8,128)(2,1)S(1)} %collective-permute-done.4.refs_2_, bf16[384,128]{1,0:T(8,128)(2,1)S(1)} %collective-permute-done.5.refs_3_, ...), custom_call_target="tpu_custom_call" | custom-call | flops 268435456 | bytes 1835008 | tf_op jit(solution)/shard_map/pallas_call | solution.py:70
  63.3 3.7 %shard_map.101 = (f32[512,128]{1,0:T(8,128)S(1)}, f32[128,1024]{1,0:T(8,128)S(1)}) custom-call(bf16[384,128]{1,0:T(8,128)(2,1)S(1)} %shard_map.95.refs_0_, bf16[384,128]{1,0:T(8,128)(2,1)S(1)} %collective-permute-done.3.refs_1_, bf16[384,128]{1,0:T(8,128)(2,1)S(1)} %collective-permute-done.4.refs_2_, bf16[384,128]{1,0:T(8,128)(2,1)S(1)} %collective-permute-done.5.refs_3_, ...), custom_call_target="tpu_custom_call" | custom-call | flops 536870912 | bytes 2228224 | tf_op jit(solution)/shard_map/pallas_call | solution.py:70
  67.1 4.9 %shard_map.103 = (bf16[128,384]{1,0:T(8,128)(2,1)S(1)}, bf16[128,384]{1,0:T(8,128)(2,1)S(1)}, bf16[128,384]{1,0:T(8,128)(2,1)S(1)}, bf16[128,384]{1,0:T(8,128)(2...) custom-call(bf16[384,128]{1,0:T(8,128)(2,1)S(1)} %shard_map.95.refs_, ...), custom_call_target="tpu_custom_call" | custom-call | flops 1006632960 | bytes 4239360 | tf_op jit(solution)/shard_map/pallas_call | solution.py:70
  72.0 0.6 collective-permute-start.30
  72.7 0.4 collective-permute-start.32
  74.5 0.6 collective-permute-start.34
  75.0 0.6 collective-permute-start.35
  75.7 2.4 %collective-permute-start.36 = (f32[192,128]{1,0:T(8,128)S(1)}, f32[192,128]{1,0:T(8,128)S(1)}, u32[]{:S(2)}, u32[]{:S(2)}) collective-permute-start(f32[192,128]{1,0:T(8,128)S(1)} %get-tuple-element.90), channel_id=1, source_target_pairs={{0,17},{1,16},{2,19},{3,18},{4,21},{5,20},{6,23},{7,22},{8,25},{9,... | collective-permute-start | bytes 294920 | tf_op jit(solution)/shard_map/ppermute | solution.py:60
  78.0 3.1 %collective-permute-start.27 = (bf16[128,384]{1,0:T(8,128)(2,1)S(1)}, bf16[128,384]{1,0:T(8,128)(2,1)S(1)}, u32[]{:S(2)}, u32[]{:S(2)}) collective-permute-start(bf16[128,384]{1,0:T(8,128)(2,1)S(1)} %get-tuple-element.74), channel_id=1, source_target_pairs={{0,2},{1,3},{2,0},{3,1},{4,6},{5,7},{6,4},{7,5},{8,10},{9,11},{10,... | collective-permute-start | bytes 294920 | tf_op jit(solution)/shard_map/ppermute | solution.py:60
  81.1 2.4 %collective-permute-start.29 = (bf16[128,384]{1,0:T(8,128)(2,1)S(1)}, bf16[128,384]{1,0:T(8,128)(2,1)S(1)}, u32[]{:S(2)}, u32[]{:S(2)}) collective-permute-start(bf16[128,384]{1,0:T(8,128)(2,1)S(1)} %get-tuple-element.76), channel_id=1, source_target_pairs={{0,6},{1,7},{2,4},{3,5},{4,2},{5,3},{6,0},{7,1},{8,14},{9,15},{10,... | collective-permute-start | bytes 294920 | tf_op jit(solution)/shard_map/ppermute | solution.py:60
  83.6 2.3 %collective-permute-start.37 = (f32[32,192]{1,0:T(8,128)S(1)}, f32[32,192]{1,0:T(8,128)S(1)}, u32[]{:S(2)}, u32[]{:S(2)}) collective-permute-start(f32[32,192]{1,0:T(8,128)S(1)} %get-tuple-element.92), channel_id=1, source_target_pairs={{0,2},{1,3},{2,0},{3,1},{4,6},{5,7},{6,4},{7,5},{8,10},{9,11},{10,... | collective-permute-start | bytes 73736 | tf_op jit(solution)/shard_map/ppermute | solution.py:60
  85.9 2.4 %collective-permute-start.39 = (f32[32,192]{1,0:T(8,128)S(1)}, f32[32,192]{1,0:T(8,128)S(1)}, u32[]{:S(2)}, u32[]{:S(2)}) collective-permute-start(f32[32,192]{1,0:T(8,128)S(1)} %get-tuple-element.94), channel_id=1, source_target_pairs={{0,6},{1,7},{2,4},{3,5},{4,2},{5,3},{6,0},{7,1},{8,14},{9,15},{10,... | collective-permute-start | bytes 73736 | tf_op jit(solution)/shard_map/ppermute | solution.py:60
  88.4 3.5 %collective-permute-done.28.refs_2_ = bf16[128,384]{1,0:T(8,128)(2,1)S(1)} collective-permute-done((bf16[128,384]{1,0:T(8,128)(2,1)S(1)}, bf16[128,384]{1,0:T(8,128)(2,1)S(1)}, u32[]{:S(2)}, u32[]{:S(2)}) %collective-permute-start.28) | collective-permute-done | bytes 98336 | tf_op jit(solution)/shard_map/ppermute | solution.py:60
  91.9 0.9 shard_map.104
  92.8 1.4 %collective-permute-done.38.refs_2_ = f32[32,192]{1,0:T(8,128)S(1)} collective-permute-done((f32[32,192]{1,0:T(8,128)S(1)}, f32[32,192]{1,0:T(8,128)S(1)}, u32[]{:S(2)}, u32[]{:S(2)}) %collective-permute-start.38) | collective-permute-done | bytes 24608 | tf_op jit(solution)/shard_map/ppermute | solution.py:60
  94.3 0.7 shard_map.107
  (60 shorter events, 4.0 us)
Async XLA Ops:
  0.6 14.8 %copy-start = (bf16[128,768]{1,0:T(8,128)(2,1)S(1)}, bf16[128,768]{1,0:T(8,128)(2,1)}, u32[]{:S(2)}) copy-start(bf16[128,768]{1,0:T(8,128)(2,1)} %k_ref.1) | copy-start | bytes 589828
  0.6 0.8 copy-start.4
  1.5 0.8 copy-start.5
  2.4 5.7 %collective-permute-start = (bf16[32,384]{1,0:T(8,128)(2,1)S(1)}, bf16[32,384]{1,0:T(8,128)(2,1)S(1)}, u32[]{:S(2)}, u32[]{:S(2)}) collective-permute-start(bf16[32,384]{1,0:T(8,128)(2,1)S(1)} %get-tuple-element.50), channel_id=1, source_target_pairs={{0,2},{1,3},{2,0},{3,1},{4,6},{5,7},{6,4},{7,5},{8,10},{9,11},{10,... | collective-permute-start | bytes 73736 | tf_op jit(solution)/shard_map/ppermute | solution.py:60
  5.5 5.1 %collective-permute-start.1 = (bf16[32,384]{1,0:T(8,128)(2,1)S(1)}, bf16[32,384]{1,0:T(8,128)(2,1)S(1)}, u32[]{:S(2)}, u32[]{:S(2)}) collective-permute-start(bf16[32,384]{1,0:T(8,128)(2,1)S(1)} %get-tuple-element.51), channel_id=1, source_target_pairs={{0,4},{1,5},{2,6},{3,7},{4,0},{5,1},{6,2},{7,3},{8,12},{9,13},{10,... | collective-permute-start | bytes 73736 | tf_op jit(solution)/shard_map/ppermute | solution.py:60
  8.1 5.6 %collective-permute-start.2 = (bf16[32,384]{1,0:T(8,128)(2,1)S(1)}, bf16[32,384]{1,0:T(8,128)(2,1)S(1)}, u32[]{:S(2)}, u32[]{:S(2)}) collective-permute-start(bf16[32,384]{1,0:T(8,128)(2,1)S(1)} %get-tuple-element.52), channel_id=1, source_target_pairs={{0,6},{1,7},{2,4},{3,5},{4,2},{5,3},{6,0},{7,1},{8,14},{9,15},{10,... | collective-permute-start | bytes 73736 | tf_op jit(solution)/shard_map/ppermute | solution.py:60
  13.7 1.7 %copy-start.6 = (f32[12,128]{1,0:T(8,128)S(1)}, f32[12,128]{1,0:T(8,128)}, u32[]{:S(2)}) copy-start(f32[12,128]{1,0:T(8,128)} %n_ref.2) | copy-start | bytes 18436
  13.7 12.2 %copy-start.3 = (f32[12,1024]{1,0:T(8,128)S(1)}, f32[12,1024]{1,0:T(8,128)}, u32[]{:S(2)}) copy-start(f32[12,1024]{1,0:T(8,128)} %n_ref.3) | copy-start | bytes 147460
  13.8 6.2 %collective-permute-start.3 = (bf16[384,128]{1,0:T(8,128)(2,1)S(1)}, bf16[384,128]{1,0:T(8,128)(2,1)S(1)}, u32[]{:S(2)}, u32[]{:S(2)}) collective-permute-start(bf16[384,128]{1,0:T(8,128)(2,1)S(1)} %shard_map.95.refs_0_), channel_id=1, source_target_pairs={{0,1},{1,0},{2,3},{3,2},{4,5},{5,4},{6,7},{7,6},{8,9},{9,8},{10,11... | collective-permute-start | bytes 294920 | tf_op jit(solution)/shard_map/ppermute | solution.py:60
  15.4 5.4 %collective-permute-start.4 = (bf16[384,128]{1,0:T(8,128)(2,1)S(1)}, bf16[384,128]{1,0:T(8,128)(2,1)S(1)}, u32[]{:S(2)}, u32[]{:S(2)}) collective-permute-start(bf16[384,128]{1,0:T(8,128)(2,1)S(1)} %shard_map.95.refs_0_), channel_id=1, source_target_pairs={{0,8},{1,9},{2,10},{3,11},{4,12},{5,13},{6,14},{7,15},{8,0},{9,1},... | collective-permute-start | bytes 294920 | tf_op jit(solution)/shard_map/ppermute | solution.py:60
  15.4 0.9 copy-start.1
  16.4 0.9 copy-start.2
  18.0 7.8 %collective-permute-start.10 = (bf16[128,640]{1,0:T(8,128)(2,1)S(1)}, bf16[128,640]{1,0:T(8,128)(2,1)S(1)}, u32[]{:S(2)}, u32[]{:S(2)}) collective-permute-start(bf16[128,640]{1,0:T(8,128)(2,1)S(1)} %get-tuple-element.54), channel_id=1, source_target_pairs={{0,2},{1,3},{2,0},{3,1},{4,6},{5,7},{6,4},{7,5},{8,10},{9,11},{10,... | collective-permute-start | bytes 491528 | tf_op jit(solution)/shard_map/ppermute | solution.py:60
  18.0 6.4 %collective-permute-start.6 = (bf16[384,128]{1,0:T(8,128)(2,1)S(1)}, bf16[384,128]{1,0:T(8,128)(2,1)S(1)}, u32[]{:S(2)}, u32[]{:S(2)}) collective-permute-start(bf16[384,128]{1,0:T(8,128)(2,1)S(1)} %shard_map.95.refs_0_), channel_id=1, source_target_pairs={{0,16},{1,17},{2,18},{3,19},{4,20},{5,21},{6,22},{7,23},{8,24},{9,... | collective-permute-start | bytes 294920 | tf_op jit(solution)/shard_map/ppermute | solution.py:60
  19.6 5.8 %collective-permute-start.7 = (bf16[384,128]{1,0:T(8,128)(2,1)S(1)}, bf16[384,128]{1,0:T(8,128)(2,1)S(1)}, u32[]{:S(2)}, u32[]{:S(2)}) collective-permute-start(bf16[384,128]{1,0:T(8,128)(2,1)S(1)} %shard_map.95.refs_0_), channel_id=1, source_target_pairs={{0,17},{1,16},{2,19},{3,18},{4,21},{5,20},{6,23},{7,22},{8,25},{9,... | collective-permute-start | bytes 294920 | tf_op jit(solution)/shard_map/ppermute | solution.py:60
  20.1 15.0 %collective-permute-start.11 = (bf16[128,640]{1,0:T(8,128)(2,1)S(1)}, bf16[128,640]{1,0:T(8,128)(2,1)S(1)}, u32[]{:S(2)}, u32[]{:S(2)}) collective-permute-start(bf16[128,640]{1,0:T(8,128)(2,1)S(1)} %get-tuple-element.55), channel_id=1, source_target_pairs={{0,4},{1,5},{2,6},{3,7},{4,0},{5,1},{6,2},{7,3},{8,12},{9,13},{10,... | collective-permute-start | bytes 491528 | tf_op jit(solution)/shard_map/ppermute | solution.py:60
  20.8 14.2 %collective-permute-start.12 = (bf16[128,640]{1,0:T(8,128)(2,1)S(1)}, bf16[128,640]{1,0:T(8,128)(2,1)S(1)}, u32[]{:S(2)}, u32[]{:S(2)}) collective-permute-start(bf16[128,640]{1,0:T(8,128)(2,1)S(1)} %get-tuple-element.56), channel_id=1, source_target_pairs={{0,6},{1,7},{2,4},{3,5},{4,2},{5,3},{6,0},{7,1},{8,14},{9,15},{10,... | collective-permute-start | bytes 491528 | tf_op jit(solution)/shard_map/ppermute | solution.py:60
  24.4 10.7 %collective-permute-start.5 = (bf16[384,128]{1,0:T(8,128)(2,1)S(1)}, bf16[384,128]{1,0:T(8,128)(2,1)S(1)}, u32[]{:S(2)}, u32[]{:S(2)}) collective-permute-start(bf16[384,128]{1,0:T(8,128)(2,1)S(1)} %collective-permute-done.3.refs_1_), channel_id=1, source_target_pairs={{0,8},{1,9},{2,10},{3,11},{4,12},{5,13},{6,14},{7,15},{8,0},{9,1},... | collective-permute-start | bytes 294920 | tf_op jit(solution)/shard_map/ppermute | solution.py:60
  25.4 9.7 %collective-permute-start.8 = (bf16[384,128]{1,0:T(8,128)(2,1)S(1)}, bf16[384,128]{1,0:T(8,128)(2,1)S(1)}, u32[]{:S(2)}, u32[]{:S(2)}) collective-permute-start(bf16[384,128]{1,0:T(8,128)(2,1)S(1)} %collective-permute-done.6.refs_4_), channel_id=1, source_target_pairs={{0,8},{1,9},{2,10},{3,11},{4,12},{5,13},{6,14},{7,15},{8,0},{9,1},... | collective-permute-start | bytes 294920 | tf_op jit(solution)/shard_map/ppermute | solution.py:60
  25.8 9.3 %collective-permute-start.9 = (bf16[384,128]{1,0:T(8,128)(2,1)S(1)}, bf16[384,128]{1,0:T(8,128)(2,1)S(1)}, u32[]{:S(2)}, u32[]{:S(2)}) collective-permute-start(bf16[384,128]{1,0:T(8,128)(2,1)S(1)} %collective-permute-done.7.refs_5_), channel_id=1, source_target_pairs={{0,8},{1,9},{2,10},{3,11},{4,12},{5,13},{6,14},{7,15},{8,0},{9,1},... | collective-permute-start | bytes 294920 | tf_op jit(solution)/shard_map/ppermute | solution.py:60
  38.3 1.5 %collective-permute-start.13 = (f32[384,128]{1,0:T(8,128)S(1)}, f32[384,128]{1,0:T(8,128)S(1)}, u32[]{:S(2)}, u32[]{:S(2)}) collective-permute-start(f32[384,128]{1,0:T(8,128)S(1)} %get-tuple-element.61), channel_id=1, source_target_pairs={{0,8},{1,9},{2,10},{3,11},{4,12},{5,13},{6,14},{7,15},{8,0},{9,1},... | collective-permute-start | bytes 589832 | tf_op jit(solution)/shard_map/ppermute | solution.py:60
  38.4 1.7 %collective-permute-start.14 = (f32[384,128]{1,0:T(8,128)S(1)}, f32[384,128]{1,0:T(8,128)S(1)}, u32[]{:S(2)}, u32[]{:S(2)}) collective-permute-start(f32[384,128]{1,0:T(8,128)S(1)} %get-tuple-element.62), channel_id=1, source_target_pairs={{0,8},{1,9},{2,10},{3,11},{4,12},{5,13},{6,14},{7,15},{8,0},{9,1},... | collective-permute-start | bytes 589832 | tf_op jit(solution)/shard_map/ppermute | solution.py:60
  38.9 1.5 %collective-permute-start.15 = (f32[384,128]{1,0:T(8,128)S(1)}, f32[384,128]{1,0:T(8,128)S(1)}, u32[]{:S(2)}, u32[]{:S(2)}) collective-permute-start(f32[384,128]{1,0:T(8,128)S(1)} %get-tuple-element.63), channel_id=1, source_target_pairs={{0,8},{1,9},{2,10},{3,11},{4,12},{5,13},{6,14},{7,15},{8,0},{9,1},... | collective-permute-start | bytes 589832 | tf_op jit(solution)/shard_map/ppermute | solution.py:60
  38.9 1.7 %collective-permute-start.16 = (f32[384,128]{1,0:T(8,128)S(1)}, f32[384,128]{1,0:T(8,128)S(1)}, u32[]{:S(2)}, u32[]{:S(2)}) collective-permute-start(f32[384,128]{1,0:T(8,128)S(1)} %get-tuple-element.64), channel_id=1, source_target_pairs={{0,8},{1,9},{2,10},{3,11},{4,12},{5,13},{6,14},{7,15},{8,0},{9,1},... | collective-permute-start | bytes 589832 | tf_op jit(solution)/shard_map/ppermute | solution.py:60
  40.7 7.1 %collective-permute-start.17 = (f32[384,128]{1,0:T(8,128)S(1)}, f32[384,128]{1,0:T(8,128)S(1)}, u32[]{:S(2)}, u32[]{:S(2)}) collective-permute-start(f32[384,128]{1,0:T(8,128)S(1)} %get-tuple-element.66), channel_id=1, source_target_pairs={{0,1},{1,0},{2,3},{3,2},{4,5},{5,4},{6,7},{7,6},{8,9},{9,8},{10,11... | collective-permute-start | bytes 589832 | tf_op jit(solution)/shard_map/ppermute | solution.py:60
  42.3 7.8 %collective-permute-start.18 = (f32[384,128]{1,0:T(8,128)S(1)}, f32[384,128]{1,0:T(8,128)S(1)}, u32[]{:S(2)}, u32[]{:S(2)}) collective-permute-start(f32[384,128]{1,0:T(8,128)S(1)} %get-tuple-element.67), channel_id=1, source_target_pairs={{0,16},{1,17},{2,18},{3,19},{4,20},{5,21},{6,22},{7,23},{8,24},{9,... | collective-permute-start | bytes 589832 | tf_op jit(solution)/shard_map/ppermute | solution.py:60
  43.8 9.4 %collective-permute-start.19 = (f32[384,128]{1,0:T(8,128)S(1)}, f32[384,128]{1,0:T(8,128)S(1)}, u32[]{:S(2)}, u32[]{:S(2)}) collective-permute-start(f32[384,128]{1,0:T(8,128)S(1)} %get-tuple-element.68), channel_id=1, source_target_pairs={{0,17},{1,16},{2,19},{3,18},{4,21},{5,20},{6,23},{7,22},{8,25},{9,... | collective-permute-start | bytes 589832 | tf_op jit(solution)/shard_map/ppermute | solution.py:60
  53.3 4.2 %collective-permute-start.20 = (bf16[208,128]{1,0:T(8,128)(2,1)S(1)}, bf16[208,128]{1,0:T(8,128)(2,1)S(1)}, u32[]{:S(2)}, u32[]{:S(2)}) collective-permute-start(bf16[208,128]{1,0:T(8,128)(2,1)S(1)} %shard_map.100.refs_13_), channel_id=1, source_target_pairs={{0,1},{1,0},{2,3},{3,2},{4,5},{5,4},{6,7},{7,6},{8,9},{9,8},{10,11... | collective-permute-start | bytes 159752 | tf_op jit(solution)/shard_map/ppermute | solution.py:60
  54.9 4.1 %collective-permute-start.23 = (bf16[208,128]{1,0:T(8,128)(2,1)S(1)}, bf16[208,128]{1,0:T(8,128)(2,1)S(1)}, u32[]{:S(2)}, u32[]{:S(2)}) collective-permute-start(bf16[208,128]{1,0:T(8,128)(2,1)S(1)} %shard_map.100.refs_13_), channel_id=1, source_target_pairs={{0,16},{1,17},{2,18},{3,19},{4,20},{5,21},{6,22},{7,23},{8,24},{9,... | collective-permute-start | bytes 159752 | tf_op jit(solution)/shard_map/ppermute | solution.py:60
  56.4 5.0 %collective-permute-start.24 = (bf16[208,128]{1,0:T(8,128)(2,1)S(1)}, bf16[208,128]{1,0:T(8,128)(2,1)S(1)}, u32[]{:S(2)}, u32[]{:S(2)}) collective-permute-start(bf16[208,128]{1,0:T(8,128)(2,1)S(1)} %shard_map.100.refs_13_), channel_id=1, source_target_pairs={{0,17},{1,16},{2,19},{3,18},{4,21},{5,20},{6,23},{7,22},{8,25},{9,... | collective-permute-start | bytes 159752 | tf_op jit(solution)/shard_map/ppermute | solution.py:60
  56.8 10.2 %collective-permute-start.21 = (bf16[208,128]{1,0:T(8,128)(2,1)S(1)}, bf16[208,128]{1,0:T(8,128)(2,1)S(1)}, u32[]{:S(2)}, u32[]{:S(2)}) collective-permute-start(bf16[208,128]{1,0:T(8,128)(2,1)S(1)} %shard_map.100.refs_13_), channel_id=1, source_target_pairs={{0,8},{1,9},{2,10},{3,11},{4,12},{5,13},{6,14},{7,15},{8,0},{9,1},... | collective-permute-start | bytes 159752 | tf_op jit(solution)/shard_map/ppermute | solution.py:60
  57.5 9.6 %collective-permute-start.22 = (bf16[208,128]{1,0:T(8,128)(2,1)S(1)}, bf16[208,128]{1,0:T(8,128)(2,1)S(1)}, u32[]{:S(2)}, u32[]{:S(2)}) collective-permute-start(bf16[208,128]{1,0:T(8,128)(2,1)S(1)} %collective-permute-done.20.refs_14_), channel_id=1, source_target_pairs={{0,8},{1,9},{2,10},{3,11},{4,12},{5,13},{6,14},{7,15},{8,0},{9,1},... | collective-permute-start | bytes 159752 | tf_op jit(solution)/shard_map/ppermute | solution.py:60
  59.0 8.1 %collective-permute-start.25 = (bf16[208,128]{1,0:T(8,128)(2,1)S(1)}, bf16[208,128]{1,0:T(8,128)(2,1)S(1)}, u32[]{:S(2)}, u32[]{:S(2)}) collective-permute-start(bf16[208,128]{1,0:T(8,128)(2,1)S(1)} %collective-permute-done.23.refs_17_), channel_id=1, source_target_pairs={{0,8},{1,9},{2,10},{3,11},{4,12},{5,13},{6,14},{7,15},{8,0},{9,1},... | collective-permute-start | bytes 159752 | tf_op jit(solution)/shard_map/ppermute | solution.py:60
  61.4 5.7 %collective-permute-start.26 = (bf16[208,128]{1,0:T(8,128)(2,1)S(1)}, bf16[208,128]{1,0:T(8,128)(2,1)S(1)}, u32[]{:S(2)}, u32[]{:S(2)}) collective-permute-start(bf16[208,128]{1,0:T(8,128)(2,1)S(1)} %collective-permute-done.24.refs_18_), channel_id=1, source_target_pairs={{0,8},{1,9},{2,10},{3,11},{4,12},{5,13},{6,14},{7,15},{8,0},{9,1},... | collective-permute-start | bytes 159752 | tf_op jit(solution)/shard_map/ppermute | solution.py:60
  72.0 1.5 %collective-permute-start.30 = (f32[192,128]{1,0:T(8,128)S(1)}, f32[192,128]{1,0:T(8,128)S(1)}, u32[]{:S(2)}, u32[]{:S(2)}) collective-permute-start(f32[192,128]{1,0:T(8,128)S(1)} %get-tuple-element.83), channel_id=1, source_target_pairs={{0,8},{1,9},{2,10},{3,11},{4,12},{5,13},{6,14},{7,15},{8,0},{9,1},... | collective-permute-start | bytes 294920 | tf_op jit(solution)/shard_map/ppermute | solution.py:60
  72.6 1.3 %collective-permute-start.31 = (f32[192,128]{1,0:T(8,128)S(1)}, f32[192,128]{1,0:T(8,128)S(1)}, u32[]{:S(2)}, u32[]{:S(2)}) collective-permute-start(f32[192,128]{1,0:T(8,128)S(1)} %get-tuple-element.84), channel_id=1, source_target_pairs={{0,8},{1,9},{2,10},{3,11},{4,12},{5,13},{6,14},{7,15},{8,0},{9,1},... | collective-permute-start | bytes 294920 | tf_op jit(solution)/shard_map/ppermute | solution.py:60
  72.7 1.4 %collective-permute-start.32 = (f32[192,128]{1,0:T(8,128)S(1)}, f32[192,128]{1,0:T(8,128)S(1)}, u32[]{:S(2)}, u32[]{:S(2)}) collective-permute-start(f32[192,128]{1,0:T(8,128)S(1)} %get-tuple-element.85), channel_id=1, source_target_pairs={{0,8},{1,9},{2,10},{3,11},{4,12},{5,13},{6,14},{7,15},{8,0},{9,1},... | collective-permute-start | bytes 294920 | tf_op jit(solution)/shard_map/ppermute | solution.py:60
  73.1 1.3 %collective-permute-start.33 = (f32[192,128]{1,0:T(8,128)S(1)}, f32[192,128]{1,0:T(8,128)S(1)}, u32[]{:S(2)}, u32[]{:S(2)}) collective-permute-start(f32[192,128]{1,0:T(8,128)S(1)} %get-tuple-element.86), channel_id=1, source_target_pairs={{0,8},{1,9},{2,10},{3,11},{4,12},{5,13},{6,14},{7,15},{8,0},{9,1},... | collective-permute-start | bytes 294920 | tf_op jit(solution)/shard_map/ppermute | solution.py:60
  74.5 6.6 %collective-permute-start.34 = (f32[192,128]{1,0:T(8,128)S(1)}, f32[192,128]{1,0:T(8,128)S(1)}, u32[]{:S(2)}, u32[]{:S(2)}) collective-permute-start(f32[192,128]{1,0:T(8,128)S(1)} %get-tuple-element.88), channel_id=1, source_target_pairs={{0,1},{1,0},{2,3},{3,2},{4,5},{5,4},{6,7},{7,6},{8,9},{9,8},{10,11... | collective-permute-start | bytes 294920 | tf_op jit(solution)/shard_map/ppermute | solution.py:60
  75.0 8.4 %collective-permute-start.35 = (f32[192,128]{1,0:T(8,128)S(1)}, f32[192,128]{1,0:T(8,128)S(1)}, u32[]{:S(2)}, u32[]{:S(2)}) collective-permute-start(f32[192,128]{1,0:T(8,128)S(1)} %get-tuple-element.89), channel_id=1, source_target_pairs={{0,16},{1,17},{2,18},{3,19},{4,20},{5,21},{6,22},{7,23},{8,24},{9,... | collective-permute-start | bytes 294920 | tf_op jit(solution)/shard_map/ppermute | solution.py:60
  75.7 7.8 %collective-permute-start.36 = (f32[192,128]{1,0:T(8,128)S(1)}, f32[192,128]{1,0:T(8,128)S(1)}, u32[]{:S(2)}, u32[]{:S(2)}) collective-permute-start(f32[192,128]{1,0:T(8,128)S(1)} %get-tuple-element.90), channel_id=1, source_target_pairs={{0,17},{1,16},{2,19},{3,18},{4,21},{5,20},{6,23},{7,22},{8,25},{9,... | collective-permute-start | bytes 294920 | tf_op jit(solution)/shard_map/ppermute | solution.py:60
  78.0 7.9 %collective-permute-start.27 = (bf16[128,384]{1,0:T(8,128)(2,1)S(1)}, bf16[128,384]{1,0:T(8,128)(2,1)S(1)}, u32[]{:S(2)}, u32[]{:S(2)}) collective-permute-start(bf16[128,384]{1,0:T(8,128)(2,1)S(1)} %get-tuple-element.74), channel_id=1, source_target_pairs={{0,2},{1,3},{2,0},{3,1},{4,6},{5,7},{6,4},{7,5},{8,10},{9,11},{10,... | collective-permute-start | bytes 294920 | tf_op jit(solution)/shard_map/ppermute | solution.py:60
  81.1 10.8 %collective-permute-start.28 = (bf16[128,384]{1,0:T(8,128)(2,1)S(1)}, bf16[128,384]{1,0:T(8,128)(2,1)S(1)}, u32[]{:S(2)}, u32[]{:S(2)}) collective-permute-start(bf16[128,384]{1,0:T(8,128)(2,1)S(1)} %get-tuple-element.75), channel_id=1, source_target_pairs={{0,4},{1,5},{2,6},{3,7},{4,0},{5,1},{6,2},{7,3},{8,12},{9,13},{10,... | collective-permute-start | bytes 294920 | tf_op jit(solution)/shard_map/ppermute | solution.py:60
  81.1 10.8 %collective-permute-start.29 = (bf16[128,384]{1,0:T(8,128)(2,1)S(1)}, bf16[128,384]{1,0:T(8,128)(2,1)S(1)}, u32[]{:S(2)}, u32[]{:S(2)}) collective-permute-start(bf16[128,384]{1,0:T(8,128)(2,1)S(1)} %get-tuple-element.76), channel_id=1, source_target_pairs={{0,6},{1,7},{2,4},{3,5},{4,2},{5,3},{6,0},{7,1},{8,14},{9,15},{10,... | collective-permute-start | bytes 294920 | tf_op jit(solution)/shard_map/ppermute | solution.py:60
  83.6 9.3 %collective-permute-start.37 = (f32[32,192]{1,0:T(8,128)S(1)}, f32[32,192]{1,0:T(8,128)S(1)}, u32[]{:S(2)}, u32[]{:S(2)}) collective-permute-start(f32[32,192]{1,0:T(8,128)S(1)} %get-tuple-element.92), channel_id=1, source_target_pairs={{0,2},{1,3},{2,0},{3,1},{4,6},{5,7},{6,4},{7,5},{8,10},{9,11},{10,... | collective-permute-start | bytes 73736 | tf_op jit(solution)/shard_map/ppermute | solution.py:60
  85.9 8.3 %collective-permute-start.38 = (f32[32,192]{1,0:T(8,128)S(1)}, f32[32,192]{1,0:T(8,128)S(1)}, u32[]{:S(2)}, u32[]{:S(2)}) collective-permute-start(f32[32,192]{1,0:T(8,128)S(1)} %get-tuple-element.93), channel_id=1, source_target_pairs={{0,4},{1,5},{2,6},{3,7},{4,0},{5,1},{6,2},{7,3},{8,12},{9,13},{10,... | collective-permute-start | bytes 73736 | tf_op jit(solution)/shard_map/ppermute | solution.py:60
  85.9 8.3 %collective-permute-start.39 = (f32[32,192]{1,0:T(8,128)S(1)}, f32[32,192]{1,0:T(8,128)S(1)}, u32[]{:S(2)}, u32[]{:S(2)}) collective-permute-start(f32[32,192]{1,0:T(8,128)S(1)} %get-tuple-element.94), channel_id=1, source_target_pairs={{0,6},{1,7},{2,4},{3,5},{4,2},{5,3},{6,0},{7,1},{8,14},{9,15},{10,... | collective-permute-start | bytes 73736 | tf_op jit(solution)/shard_map/ppermute | solution.py:60

commit v2 on v1

--- a/solution.py
+++ b/solution.py
@@ -15,6 +15,7 @@
 MOST_IN_PLANE = 16
 GROUPS = 4
 VMEM_BYTES = 20 * 2**20
+WHOLE_VMEM_BYTES = 60 * 2**20
 LOG2E = math.log2(math.e)
 
 
@@ -29,7 +30,7 @@
         self.points = rows * GROUPS
         self.block = lat_rows * GROUPS
         self.latents = self.block * self.plane
-        self.pts_cols = 3 * self.cols + HEAD_DIM
+        self.slot = lat_rows + 16
         self.ct_rows = self.cols + 16
 
     @staticmethod
@@ -43,8 +44,11 @@
             and npb % GROUPS == 0
             and npa * npb // GROUPS <= MOST_IN_PLANE
             and lat_rows * GROUPS == LANES
-            and rows % LANES == 0
+            and rows == LANES
+            and HEADS % GROUPS == 0
+            and HEADS // GROUPS * rows == 2 * HEADS // GROUPS * HEAD_DIM
             and width == HEADS * HEAD_DIM
+            and 2 * width // GROUPS == 3 * LANES
         )
 
     def exchange(self, value, over_group, step):
@@ -64,18 +68,38 @@
     return pl.BlockSpec(memory_space=pltpu.VMEM)
 
 
-def call(kernel, outs, args, scratch=(), flops=0):
+def call(kernel, outs, args, scratch=(), flops=0, from_hbm=False):
+    limit = WHOLE_VMEM_BYTES if from_hbm else VMEM_BYTES
     nbytes = sum(a.size * a.dtype.itemsize for a in args)
     nbytes += sum(math.prod(o.shape) * o.dtype.itemsize for o in outs)
     return pl.pallas_call(
         kernel,
         out_shape=tuple(outs),
-        in_specs=[vmem()] * len(args),
+        in_specs=[pl.BlockSpec(memory_space=pltpu.HBM) if from_hbm else vmem()] * len(args),
         out_specs=tuple(vmem() for _ in outs),
         scratch_shapes=list(scratch),
         cost_estimate=pl.CostEstimate(flops=flops, bytes_accessed=nbytes, transcendentals=flops // 256),
-        compiler_params=pltpu.CompilerParams(vmem_limit_bytes=VMEM_BYTES),
+        compiler_params=pltpu.CompilerParams(vmem_limit_bytes=limit),
     )(*args)
+
+
+def fetched(kernel, args):
+    n = len(args)
+
+    def body(*refs):
+        held, sems = refs[-n - 1 : -1], refs[-1]
+        copies = [
+            pltpu.make_async_copy(src, dst, sems.at[i])
+            for i, (src, dst) in enumerate(zip(refs[:n], held, strict=True))
+        ]
+        for copy in copies:
+            copy.start()
+        for copy in copies:
+            copy.wait()
+        kernel(*held, *refs[n : -n - 1])
+
+    scratch = [pltpu.VMEM(a.shape, a.dtype) for a in args] + [pltpu.SemaphoreType.DMA((n,))]
+    return body, scratch
 
 
 def shaped(shape, dtype):
@@ -115,42 +139,49 @@
     return block.astype(jnp.float32).T.astype(block.dtype)
 
 
-def pack_latents(plan, query, out):
-    def kernel(q_ref, o_ref, *outs):
-        z = group_index(plan)
-        q, o = q_ref[...].astype(jnp.float32), o_ref[...].astype(jnp.float32)
-        c = plan.cols
-        pieces = by_group(
-            [
-                jnp.concatenate([q[:, g * c : (g + 1) * c], o[:, g * c : (g + 1) * c]], axis=1)
-                for g in range(GROUPS)
-            ],
-            z,
-        )
-        for ref, piece in zip(outs, pieces, strict=True):
-            ref[...] = piece.astype(jnp.bfloat16)
-
-    outs = [shaped((plan.lat_rows, 2 * plan.cols), jnp.bfloat16)] * GROUPS
-    return call(kernel, outs, (query, out))
-
-
-def pack_points(plan, keys, grads, values, norm):
-    def kernel(k_ref, g_ref, v_ref, n_ref, *outs):
+def pack_latents(plan, query, out, norm):
+    def kernel(q_ref, o_ref, n_ref, *outs):
         z = group_index(plan)
         c, hs = plan.cols, plan.heads
-        for first, ref in ((0, k_ref), (1, g_ref), (2, v_ref)):
+        q, o = q_ref[...].astype(jnp.float32), o_ref[...].astype(jnp.float32)
+        parts = split3(n_ref[...])
+        fill = jnp.zeros((plan.slot - plan.lat_rows - 3, hs * plan.rows), jnp.float32)
+        pieces = []
+        for g in range(GROUPS):
+            top = jnp.concatenate([q[:, g * c : (g + 1) * c], o[:, g * c : (g + 1) * c]], axis=1)
+            lines = [
+                jnp.concatenate([p[h : h + 1, :] for h in range(g * hs, (g + 1) * hs)], axis=1) for p in parts
+            ]
+            pieces.append(jnp.concatenate([top, *lines, fill], axis=0))
+        for ref, piece in zip(outs, by_group(pieces, z), strict=True):
+            ref[...] = piece.astype(jnp.bfloat16)
+
+    outs = [shaped((plan.slot, 2 * plan.cols), jnp.bfloat16)] * GROUPS
+    args = (query, out, norm)
+    body, scratch = fetched(kernel, args)
+    return call(body, outs, args, scratch, from_hbm=True)
+
+
+def pack_points(plan, keys, grads, values):
+    def kernel(k_ref, g_ref, v_ref, *outs):
+        z = group_index(plan)
+        c = plan.cols
+        for first, ref in ((0, k_ref), (1, g_ref)):
             whole = ref[...].astype(jnp.float32)
             pieces = by_group([whole[:, g * c : (g + 1) * c] for g in range(GROUPS)], z)
             for out, piece in zip(outs, pieces, strict=True):
-                out[:, first * c : (first + 1) * c] = piece.astype(jnp.bfloat16)
-        norms = by_group([n_ref[g * hs : (g + 1) * hs, :] for g in range(GROUPS)], z)
-        for out, norm_rows in zip(outs, norms, strict=True):
-            fill = jnp.zeros((HEAD_DIM - 3 * hs, plan.rows), jnp.float32)
-            stack = jnp.concatenate([*split3(norm_rows), fill], axis=0)
-            out[:, 3 * c :] = stack.T.astype(jnp.bfloat16)
-
-    outs = [shaped((plan.rows, plan.pts_cols), jnp.bfloat16)] * GROUPS
-    return call(kernel, outs, (keys, grads, values, norm))
+                out[: plan.rows, first * c : (first + 1) * c] = piece.astype(jnp.bfloat16)
+        across = v_ref[...].astype(jnp.float32).T.astype(jnp.bfloat16)
+        pieces = by_group([across[g * c : (g + 1) * c] for g in range(GROUPS)], z)
+        for out, piece in zip(outs, pieces, strict=True):
+            for h in range(plan.heads):
+                lanes = slice(h * plan.rows, (h + 1) * plan.rows)
+                out[plan.rows :, lanes] = piece[h * HEAD_DIM : (h + 1) * HEAD_DIM]
+
+    outs = [shaped((plan.rows + HEAD_DIM, 2 * plan.cols), jnp.bfloat16)] * GROUPS
+    args = (keys, grads, values)
+    body, scratch = fetched(kernel, args)
+    return call(body, outs, args, scratch, from_hbm=True)
 
 
 def order_norm(plan, norm):
@@ -178,82 +209,94 @@
 
 def turn_latents(plan, slots):
     def kernel(*refs):
-        *ins, out = refs
-        out[...] = turned(jnp.concatenate([r[...] for r in ins], axis=0))
-
-    outs = [shaped((2 * plan.cols, plan.block), jnp.bfloat16)]
-    return call(kernel, outs, slots)[0]
-
-
-def norm_column(plan, pts, head):
-    base, hs = 3 * plan.cols, plan.heads
-    parts = [
-        pts[:, base + i * hs + head : base + i * hs + head + 1].astype(jnp.float32) for i in range(3)
+        *slots, out, norm_out = refs
+        n, rows = plan.lat_rows, plan.rows
+        slots = [s[...] for s in slots]
+        out[...] = turned(jnp.concatenate([s[:n] for s in slots], axis=0))
+        for j, slot in enumerate(slots):
+            parts = slot[n : n + 3].astype(jnp.float32)
+            line = (parts[0:1] + parts[1:2]) + parts[2:3]
+            lines = [line[:, h * rows : (h + 1) * rows] for h in range(plan.heads)]
+            fill = jnp.zeros((LANES - plan.heads, rows), jnp.float32)
+            norm_out[j * rows : (j + 1) * rows, :] = jnp.concatenate([*lines, fill], axis=0).T
+
+    outs = [
+        shaped((2 * plan.cols, plan.block), jnp.bfloat16),
+        shaped((plan.points, LANES), jnp.float32),
     ]
-    return (parts[0] + parts[1]) + parts[2]
-
-
-def first_pass(plan, lats, pts, norm):
-    n_lat, n_pts = len(lats), len(pts)
+    return call(kernel, outs, slots)
+
+
+def lane_tiles(plan):
+    width = min(2 * plan.block, plan.latents)
+    return [slice(at, at + width) for at in range(0, plan.latents, width)]
+
+
+def store_blocks(plan, outs, rows, lanes, value):
+    for at in range(lanes.start, lanes.stop, plan.block):
+        outs[at // plan.block][rows, :] = value[:, at - lanes.start : at - lanes.start + plan.block]
+
+
+def first_pass(plan, lats, pts, dec_norm, enc_norm):
+    n_lat = len(lats)
     c, m = plan.cols, plan.latents
 
     def kernel(*refs):
-        lat_refs, pts_refs, norm_ref = refs[:n_lat], refs[n_lat : n_lat + n_pts], refs[n_lat + n_pts]
-        outs = refs[n_lat + n_pts + 1 : -4]
-        query, sides, dec, enc = refs[-4:]
+        lat_refs, pts_refs, (dec_ref, enc_ref) = refs[:n_lat], refs[n_lat:-5 - n_lat], refs[-5 - n_lat : -3 - n_lat]
+        outs = refs[-3 - n_lat : -3]
+        query, sides, keys = refs[-3:]
         for k, ref in enumerate(lat_refs):
             query[:, k * plan.block : (k + 1) * plan.block] = ref[:c, :]
         for j, ref in enumerate(pts_refs):
-            sides[:, j * plan.rows : (j + 1) * plan.rows] = turned(ref[:, c : 3 * c])
+            rows = slice(j * plan.rows, (j + 1) * plan.rows)
+            keys[rows, :] = ref[: plan.rows, :c]
+            sides[:c, rows] = turned(ref[: plan.rows, c:])
+            for h in range(plan.heads):
+                below = slice(c + h * HEAD_DIM, c + (h + 1) * HEAD_DIM)
+                sides[below, rows] = ref[plan.rows :, h * plan.rows : (h + 1) * plan.rows]
         for h in range(plan.heads):
             mine = slice(h * HEAD_DIM, (h + 1) * HEAD_DIM)
-            enc_norm = norm_ref[h : h + 1, :] * LOG2E
-            for j, ref in enumerate(pts_refs):
-                scores = nn(ref[:, mine], query[mine, :]) * (HEAD_DIM**-0.5 * LOG2E)
-                rows = slice(j * plan.rows, (j + 1) * plan.rows)
-                dec_norm = norm_column(plan, ref, h) * LOG2E
-                dec[rows, :] = jnp.exp2(scores - dec_norm).astype(jnp.bfloat16)
-                enc[rows, :] = jnp.exp2(scores - enc_norm).astype(jnp.bfloat16)
             below = slice(c + h * HEAD_DIM, c + (h + 1) * HEAD_DIM)
-            mix = nn(sides[mine, :], dec[...])
-            weighted = nn(sides[below, :], enc[...])
-            for k, out in enumerate(outs):
-                lanes = slice(k * plan.block, (k + 1) * plan.block)
-                out[mine, :] = mix[:, lanes]
-                out[below, :] = weighted[:, lanes]
+            key = keys[:, mine]
+            row_norm = dec_ref[:, h : h + 1] * LOG2E
+            for lanes in lane_tiles(plan):
+                scores = nn(key, query[mine, lanes]) * (HEAD_DIM**-0.5 * LOG2E)
+                dec = jnp.exp2(scores - row_norm).astype(jnp.bfloat16)
+                enc = jnp.exp2(scores - enc_ref[h : h + 1, lanes] * LOG2E).astype(jnp.bfloat16)
+                store_blocks(plan, outs, mine, lanes, nn(sides[mine, :], dec))
+                store_blocks(plan, outs, below, lanes, nn(sides[below, :], enc))
 
     outs = [shaped((2 * c, plan.block), jnp.float32)] * plan.plane
     scratch = [
         pltpu.VMEM((c, m), jnp.bfloat16),
         pltpu.VMEM((2 * c, plan.points), jnp.bfloat16),
-        pltpu.VMEM((plan.points, m), jnp.bfloat16),
-        pltpu.VMEM((plan.points, m), jnp.bfloat16),
+        pltpu.VMEM((plan.points, c), jnp.bfloat16),
     ]
     flops = 6 * plan.points * m * c
-    return call(kernel, outs, (*lats, *pts, norm), scratch, flops)
-
-
-def decoder_pass(plan, lats, pts, heads):
+    return call(kernel, outs, (*lats, *pts, dec_norm, enc_norm), scratch, flops)
+
+
+def decoder_pass(plan, lats, pts, dec_norm, heads):
     n_lat = len(lats)
     c, m = plan.cols, plan.latents
 
     def kernel(*refs):
-        lat_refs, pts_refs = refs[:n_lat], refs[n_lat:-5]
+        lat_refs, pts_refs, dec_ref = refs[:n_lat], refs[n_lat:-6], refs[-6]
         key_ref, lat_ref = refs[-5:-3]
         both, keys_t, ds = refs[-3:]
         for k, ref in enumerate(lat_refs):
             both[:, k * plan.block : (k + 1) * plan.block] = ref[...]
         for j, ref in enumerate(pts_refs):
-            keys_t[:, j * plan.rows : (j + 1) * plan.rows] = turned(ref[:, :c])
+            keys_t[:, j * plan.rows : (j + 1) * plan.rows] = turned(ref[: plan.rows, :c])
         for at, h in enumerate(heads):
             mine = slice(h * HEAD_DIM, (h + 1) * HEAD_DIM)
             put = slice(at * HEAD_DIM, (at + 1) * HEAD_DIM)
             other = slice(c + h * HEAD_DIM, c + (h + 1) * HEAD_DIM)
             for j, ref in enumerate(pts_refs):
                 rows = slice(j * plan.rows, (j + 1) * plan.rows)
-                scores = nn(ref[:, mine], both[mine, :]) * (HEAD_DIM**-0.5 * LOG2E)
-                dec = jnp.exp2(scores - norm_column(plan, ref, h) * LOG2E)
-                grad = nn(ref[:, other], both[other, :])
+                scores = nn(ref[: plan.rows, mine], both[mine, :]) * (HEAD_DIM**-0.5 * LOG2E)
+                dec = jnp.exp2(scores - dec_ref[rows, h : h + 1] * LOG2E)
+                grad = nn(ref[: plan.rows, other], both[other, :])
                 total = jnp.sum(dec * grad, axis=1, keepdims=True)
                 tile = (dec * (grad - total)).astype(jnp.bfloat16)
                 ds[rows, :] = tile
@@ -268,7 +311,7 @@
         pltpu.VMEM((plan.points, m), jnp.bfloat16),
     ]
     flops = 8 * plan.points * m * width
-    return call(kernel, outs, (*lats, *pts), scratch, flops)
+    return call(kernel, outs, (*lats, *pts, dec_norm), scratch, flops)
 
 
 def reduce_mix(plan, parts):
@@ -311,45 +354,52 @@
         mix_refs = take(n_mix)
         parts_in = [take(2) for _ in before]
         pts_outs, lat_outs = take(n_pts), take(n_lat)
-        query, mix, keys_t, ds = refs
+        query, mix, keys, keys_t, values = refs
         for k, ref in enumerate(lat_refs):
             query[:, k * plan.block : (k + 1) * plan.block] = ref[:c, :]
         for k, ref in enumerate(mix_refs):
             mix[:, k * plan.block : (k + 1) * plan.block] = ref[...]
         for j, ref in enumerate(pts_refs):
-            keys_t[:, j * plan.rows : (j + 1) * plan.rows] = turned(ref[:, :c])
+            rows = slice(j * plan.rows, (j + 1) * plan.rows)
+            keys[rows, :] = ref[: plan.rows, :c]
+            keys_t[:, rows] = turned(ref[: plan.rows, :c])
+            across = [ref[plan.rows :, h * plan.rows : (h + 1) * plan.rows] for h in range(hs)]
+            values[rows, :] = turned(jnp.concatenate(across, axis=0))
         tail = mix[c:, :].astype(jnp.float32)
         columns = (tail[:hs] + tail[hs : 2 * hs]) + tail[2 * hs : 3 * hs]
-        for h in range(plan.heads):
+        for h in range(hs):
             mine = slice(h * HEAD_DIM, (h + 1) * HEAD_DIM)
-            third = slice(2 * c + h * HEAD_DIM, 2 * c + (h + 1) * HEAD_DIM)
-            enc_norm = norm_ref[h : h + 1, :] * LOG2E
-            column = columns[h : h + 1, :]
             part, at = places[h]
             key_in, lat_in = parts_in[part]
             put = slice(at * HEAD_DIM, (at + 1) * HEAD_DIM)
-            for j, ref in enumerate(pts_refs):
+            key, value = keys[:, mine], values[:, mine]
+            key_sum = key_in[:, put]
+            value_sum = None
+            for lanes in lane_tiles(plan):
+                scores = nn(key, query[mine, lanes]) * (HEAD_DIM**-0.5 * LOG2E)
+                enc = jnp.exp2(scores - norm_ref[h : h + 1, lanes] * LOG2E)
+                grad = nn(value, mix[mine, lanes])
+                ds = (enc * (grad - columns[h : h + 1, lanes])).astype(jnp.bfloat16)
+                key_sum = key_sum + nt(ds, query[mine, lanes])
+                more = nt(enc.astype(jnp.bfloat16), mix[mine, lanes])
+                value_sum = more if value_sum is None else value_sum + more
+                lat = (lat_in[put, lanes] + nn(keys_t[mine, :], ds)) * HEAD_DIM**-0.5
+                store_blocks(plan, lat_outs, mine, lanes, lat)
+            key_sum = (key_sum * HEAD_DIM**-0.5).astype(jnp.bfloat16)
+            value_sum = value_sum.astype(jnp.bfloat16)
+            for j, out in enumerate(pts_outs):
                 rows = slice(j * plan.rows, (j + 1) * plan.rows)
-                scores = nn(ref[:, mine], query[mine, :]) * (HEAD_DIM**-0.5 * LOG2E)
-                enc = jnp.exp2(scores - enc_norm)
-                grad = nn(ref[:, third], mix[mine, :])
-                tile = (enc * (grad - column)).astype(jnp.bfloat16)
-                ds[rows, :] = tile
-                key = (key_in[rows, put] + nt(tile, query[mine, :])) * HEAD_DIM**-0.5
-                pts_outs[j][:, mine] = key.astype(jnp.bfloat16)
-                value = nt(enc.astype(jnp.bfloat16), mix[mine, :])
-                pts_outs[j][:, c + h * HEAD_DIM : c + (h + 1) * HEAD_DIM] = value.astype(jnp.bfloat16)
-            lat = (lat_in[put, :] + nn(keys_t[mine, :], ds[...])) * HEAD_DIM**-0.5
-            for k, out in enumerate(lat_outs):
-                out[mine, :] = lat[:, k * plan.block : (k + 1) * plan.block]
+                out[:, mine] = key_sum[rows]
+                out[:, c + h * HEAD_DIM : c + (h + 1) * HEAD_DIM] = value_sum[rows]
 
     outs = [shaped((plan.rows, 2 * c), jnp.bfloat16)] * n_pts
     outs += [shaped((c, plan.block), jnp.float32)] * n_lat
     scratch = [
         pltpu.VMEM((c, m), jnp.bfloat16),
         pltpu.VMEM((plan.ct_rows, m), jnp.bfloat16),
+        pltpu.VMEM((plan.points, c), jnp.bfloat16),
         pltpu.VMEM((c, plan.points), jnp.bfloat16),
-        pltpu.VMEM((plan.points, m), jnp.bfloat16),
+        pltpu.VMEM((plan.points, c), jnp.bfloat16),
     ]
     flops = 10 * plan.points * m * c
     args = (*lats, *pts, norm, *mixes, *(a for _, part in before for a in part))
@@ -375,9 +425,12 @@
             total = total + ref[...]
         total = total.T
         for j, out in enumerate(outs):
-            out[...] = total[j * plan.lat_rows : (j + 1) * plan.lat_rows]
-
-    outs = [shaped((plan.lat_rows, plan.cols), jnp.float32)] * GROUPS
+            rows = total[j * plan.lat_rows : (j + 1) * plan.lat_rows]
+            n, half = plan.lat_rows, plan.lat_rows // 2
+            out[:n, :] = rows[:, :LANES]
+            out[n:, :] = jnp.concatenate([rows[:half, LANES:], rows[half:, LANES:]], axis=1)
+
+    outs = [shaped((3 * plan.lat_rows // 2, LANES), jnp.float32)] * GROUPS
     return call(kernel, outs, parts)
 
 
@@ -398,9 +451,10 @@
 def place_latents(plan, slots):
     def kernel(*refs):
         *ins, out = refs
-        pieces = by_group([r[...] for r in ins], group_index(plan))
-        for g, piece in enumerate(pieces):
-            out[:, g * plan.cols : (g + 1) * plan.cols] = piece
+        n, at = plan.lat_rows, plan.cols - LANES
+        for g, piece in enumerate(by_group([r[...] for r in ins], group_index(plan))):
+            rest = jnp.concatenate([piece[n:, :at], piece[n:, at:]], axis=0)
+            out[:, g * plan.cols : (g + 1) * plan.cols] = jnp.concatenate([piece[:n], rest], axis=1)
 
     outs = [shaped((plan.lat_rows, plan.width), jnp.float32)]
     return call(kernel, outs, slots)[0]
@@ -410,39 +464,45 @@
     plan, point_keys, point_values, out_grad, decoder_norm, latent_query, latent_out, encoder_norm
 ):
     def over_group(slots):
-        return (slots[0], *(plan.exchange(s, True, j) for j, s in enumerate(slots) if j))
+        got = [slots[0]]
+        for j in range(1, GROUPS):
+            got.append(plan.exchange(slots[j], True, j))
+        return got
+
+    def chip_steps():
+        return [k for k in range(plan.plane) if not k & plan.fast]
+
+    def from_chips(blocks):
+        got = []
+        for k, block in zip(chip_steps(), blocks, strict=True):
+            got.append(plan.exchange(block, False, k) if k else block)
+        return got
 
     def sum_cores(blocks):
-        near = [k for k in range(plan.plane) if not k & plan.fast]
+        near = chip_steps()
         theirs = [plan.exchange(blocks[k | plan.fast], False, plan.fast) for k in near]
-        return near, add_pairs([blocks[k] for k in near], theirs)
-
-    def from_chips(near, blocks):
-        return [b if k == 0 else plan.exchange(b, False, k) for k, b in zip(near, blocks, strict=True)]
+        return add_pairs([blocks[k] for k in near], theirs)
 
     def to_plane(block):
-        got = {0: block}
-        for k in range(1, plan.plane):
-            if not k & plan.fast:
-                got[k] = plan.exchange(block, False, k)
-        for k in range(plan.plane):
-            if k & plan.fast:
-                got[k] = plan.exchange(got[k ^ plan.fast], False, plan.fast)
+        got = dict(zip(chip_steps(), from_chips([block] * len(chip_steps())), strict=True))
+        for k in chip_steps():
+            got[k | plan.fast] = plan.exchange(got[k], False, plan.fast)
         return tuple(got[k] for k in range(plan.plane))
 
-    lat_slots = over_group(pack_latents(plan, latent_query, latent_out))
-    pts = pack_points(plan, point_keys, out_grad, point_values, decoder_norm)
+    lat_slots = over_group(pack_latents(plan, latent_query, latent_out, decoder_norm))
+    pts = pack_points(plan, point_keys, out_grad, point_values)
     pts = over_group(pts)
     norm = order_norm(plan, encoder_norm)
-    lats = to_plane(turn_latents(plan, lat_slots))
-    cores = sum_cores(first_pass(plan, lats, pts, norm))
-    early, late = tuple(range(plan.heads))[:-1], tuple(range(plan.heads))[-1:]
-    before = [(early, decoder_pass(plan, lats, pts, early))]
-    sums = from_chips(*cores)
-    before.append((late, decoder_pass(plan, lats, pts, late)))
+    block, dec_norm = turn_latents(plan, lat_slots)
+    lats = to_plane(block)
+    cores = sum_cores(first_pass(plan, lats, pts, dec_norm, norm))
+    early, late = tuple(range(plan.heads))[:1], tuple(range(plan.heads))[1:]
+    before = [(early, decoder_pass(plan, lats, pts, dec_norm, early))]
+    sums = from_chips(cores)
+    before.append((late, decoder_pass(plan, lats, pts, dec_norm, late)))
     mixes = to_plane(reduce_mix(plan, sums))
     pts_out, lat_out = encoder_pass(plan, lats, pts, norm, mixes, before)
-    lat_out = from_chips(*sum_cores(lat_out))
+    lat_out = from_chips(sum_cores(lat_out))
     pts_out = over_group(pts_out)
     lat_rows = over_group(reduce_latents(plan, lat_out))
     keys_grad, values_grad = place_points(plan, pts_out)

time: 95.2 us -> 94.3 us (level)
  Pallas kernels: 17 us -> 19.4 us
  local copies, waits for them, and re-layouts: 3.49 us -> 1.68 us
  waiting for transfers between devices: 36.7 us -> 35.4 us
    pallas_call x14, Pallas kernels: 17 us -> 19.4 us  [call(): pl.pallas_call(kernel, out_shape=tuple(outs), in_specs=[pl.BlockSpec(memo...]
    unnamed x14 -> x8, local copies, waits for them, and re-layouts: 3.49 us -> 1.68 us
    ppermute x40, waiting for transfers between devices: 36.7 us -> 35.4 us  [exchange(): return lax.ppermute(value, AXES, pairs)]
  transfers between devices with their start and end apart: 40 -> 40, of which waited for: 21 -> 21; matrix products, arithmetic and copies ran while one was open for 0% -> 0% of each run, Pallas kernels for 8% -> 10%
where the time goes in v2:
time: 94.3 us; the launch traced here: 94 us
  starting transfers between devices  36.7 us (39%)
  waiting for transfers between devices  35.4 us (38%)
  Pallas kernels  19.4 us (21%)
  local copies, waits for them, and re-layouts  1.68 us (2%)
    ppermute x40, starting transfers between devices, exchange(): return lax.ppermute(value, AXES, pairs)  36.7 us
    ppermute x40, waiting for transfers between devices, exchange(): return lax.ppermute(value, AXES, pairs)  35.4 us
    pallas_call x14, Pallas kernels, call(): pl.pallas_call(kernel, out_shape=tuple(outs), in_specs=[pl.BlockSpec(memo...  19.4 us
  transfers between devices with their start and end apart: 40, of which 21 were waited for; matrix products, arithmetic and copies ran while one was open for 0% of the time, Pallas kernels for 10%

profile of v2, /device:TPU:0, one launch (start us, length us, event | category | flops | bytes accessed | tf_op | source)
XLA Modules:
  0.0 94.0 jit_solution(1128708993275731694)
XLA Ops:
  0.6 1.6 %shard_map.94 = (bf16[48,384]{1,0:T(8,128)(2,1)}, bf16[48,384]{1,0:T(8,128)(2,1)}, bf16[48,384]{1,0:T(8,128)(2,1)}, bf16[48,384]{1,0:T(8,128)(2,1)}) custom-call(bf16[32,768]{1,0:T(8,128)(2,1)} %refs_0_.2, bf16[32,768]{1,0:T(8,128)(2,1)} %refs_1_.2, f32[12,128]{1,0:T(8,128)} %refs_2_.2), custom_call_target="tpu_custom_call" | custom-call | bytes 251904 | tf_op jit(solution)/shard_map/pallas_call | solution.py:75
  2.2 3.1 %collective-permute-start = (bf16[48,384]{1,0:T(8,128)(2,1)}, bf16[48,384]{1,0:T(8,128)(2,1)S(1)}, u32[]{:S(2)}, u32[]{:S(2)}) collective-permute-start(bf16[48,384]{1,0:T(8,128)(2,1)} %get-tuple-element.52), channel_id=1, source_target_pairs={{0,2},{1,3},{2,0},{3,1},{4,6},{5,7},{6,4},{7,5},{8,10},{9,11},{10,... | collective-permute-start | bytes 110600 | tf_op jit(solution)/shard_map/ppermute | solution.py:64
  5.4 2.6 %collective-permute-start.1 = (bf16[48,384]{1,0:T(8,128)(2,1)}, bf16[48,384]{1,0:T(8,128)(2,1)S(1)}, u32[]{:S(2)}, u32[]{:S(2)}) collective-permute-start(bf16[48,384]{1,0:T(8,128)(2,1)} %get-tuple-element.53), channel_id=1, source_target_pairs={{0,4},{1,5},{2,6},{3,7},{4,0},{5,1},{6,2},{7,3},{8,12},{9,13},{10,... | collective-permute-start | bytes 110600 | tf_op jit(solution)/shard_map/ppermute | solution.py:64
  7.9 3.1 %collective-permute-done.1.refs_2_ = bf16[48,384]{1,0:T(8,128)(2,1)S(1)} collective-permute-done((bf16[48,384]{1,0:T(8,128)(2,1)}, bf16[48,384]{1,0:T(8,128)(2,1)S(1)}, u32[]{:S(2)}, u32[]{:S(2)}) %collective-permute-start.1) | collective-permute-done | bytes 36896 | tf_op jit(solution)/shard_map/ppermute | solution.py:64
  11.1 2.8 %collective-permute-done.2.refs_3_ = bf16[48,384]{1,0:T(8,128)(2,1)S(1)} collective-permute-done((bf16[48,384]{1,0:T(8,128)(2,1)}, bf16[48,384]{1,0:T(8,128)(2,1)S(1)}, u32[]{:S(2)}, u32[]{:S(2)}) %collective-permute-start.2) | collective-permute-done | bytes 36896 | tf_op jit(solution)/shard_map/ppermute | solution.py:64
  13.9 0.8 copy-done.1
  14.9 1.6 %collective-permute-start.3 = (bf16[384,128]{1,0:T(8,128)(2,1)S(1)}, bf16[384,128]{1,0:T(8,128)(2,1)S(1)}, u32[]{:S(2)}, u32[]{:S(2)}) collective-permute-start(bf16[384,128]{1,0:T(8,128)(2,1)S(1)} %get-tuple-element.55.refs_0_), channel_id=1, source_target_pairs={{0,1},{1,0},{2,3},{3,2},{4,5},{5,4},{6,7},{7,6},{8,9},{9,8},{10,11... | collective-permute-start | bytes 294920 | tf_op jit(solution)/shard_map/ppermute | solution.py:64
  16.5 2.4 %shard_map.96 = (bf16[192,384]{1,0:T(8,128)(2,1)}, bf16[192,384]{1,0:T(8,128)(2,1)}, bf16[192,384]{1,0:T(8,128)(2,1)}, bf16[192,384]{1,0:T(8,128)(2,1)}) custom-call(bf16[128,768]{1,0:T(8,128)(2,1)} %refs_0_.3, bf16[128,768]{1,0:T(8,128)(2,1)} %refs_1_.3, bf16[128,768]{1,0:T(8,128)(2,1)} %refs_2_.3), custom_call_target="tpu_custom_call" | custom-call | bytes 1179648 | tf_op jit(solution)/shard_map/pallas_call | solution.py:75
  19.0 1.6 %collective-permute-start.6 = (bf16[384,128]{1,0:T(8,128)(2,1)S(1)}, bf16[384,128]{1,0:T(8,128)(2,1)S(1)}, u32[]{:S(2)}, u32[]{:S(2)}) collective-permute-start(bf16[384,128]{1,0:T(8,128)(2,1)S(1)} %get-tuple-element.55.refs_0_), channel_id=1, source_target_pairs={{0,16},{1,17},{2,18},{3,19},{4,20},{5,21},{6,22},{7,23},{8,24},{9,... | collective-permute-start | bytes 294920 | tf_op jit(solution)/shard_map/ppermute | solution.py:64
  20.5 0.5 collective-permute-start.7
  21.0 1.0 %collective-permute-start.11 = (bf16[192,384]{1,0:T(8,128)(2,1)}, bf16[192,384]{1,0:T(8,128)(2,1)S(1)}, u32[]{:S(2)}, u32[]{:S(2)}) collective-permute-start(bf16[192,384]{1,0:T(8,128)(2,1)} %get-tuple-element.58), channel_id=1, source_target_pairs={{0,4},{1,5},{2,6},{3,7},{4,0},{5,1},{6,2},{7,3},{8,12},{9,13},{10,... | collective-permute-start | bytes 442376 | tf_op jit(solution)/shard_map/ppermute | solution.py:64
  22.0 3.3 %collective-permute-start.12 = (bf16[192,384]{1,0:T(8,128)(2,1)}, bf16[192,384]{1,0:T(8,128)(2,1)S(1)}, u32[]{:S(2)}, u32[]{:S(2)}) collective-permute-start(bf16[192,384]{1,0:T(8,128)(2,1)} %get-tuple-element.59), channel_id=1, source_target_pairs={{0,6},{1,7},{2,4},{3,5},{4,2},{5,3},{6,0},{7,1},{8,14},{9,15},{10,... | collective-permute-start | bytes 442376 | tf_op jit(solution)/shard_map/ppermute | solution.py:64
  25.3 1.0 %collective-permute-done.7.refs_5_ = bf16[384,128]{1,0:T(8,128)(2,1)S(1)} collective-permute-done((bf16[384,128]{1,0:T(8,128)(2,1)S(1)}, bf16[384,128]{1,0:T(8,128)(2,1)S(1)}, u32[]{:S(2)}, u32[]{:S(2)}) %collective-permute-start.7) | collective-permute-done | bytes 98336 | tf_op jit(solution)/shard_map/ppermute | solution.py:64
  26.9 0.4 shard_map.97.refs_13_.refs_12_
  27.3 7.9 %collective-permute-done.11.refs_10_ = bf16[192,384]{1,0:T(8,128)(2,1)S(1)} collective-permute-done((bf16[192,384]{1,0:T(8,128)(2,1)}, bf16[192,384]{1,0:T(8,128)(2,1)S(1)}, u32[]{:S(2)}, u32[]{:S(2)}) %collective-permute-start.11) | collective-permute-done | bytes 147488 | tf_op jit(solution)/shard_map/ppermute | solution.py:64
  35.2 0.9 copy-done.2
  36.1 2.4 %shard_map.98 = (f32[384,128]{1,0:T(8,128)S(1)}, f32[384,128]{1,0:T(8,128)S(1)}, f32[384,128]{1,0:T(8,128)S(1)}, f32[384,128]{1,0:T(8,128)S(1)}, f32[384,128]{1,...) custom-call(bf16[384,128]{1,0:T(8,128)(2,1)S(1)} %get-tuple-element.55.refs_0_, ...), custom_call_target="tpu_custom_call" | custom-call | flops 603979776 | bytes 3223552 | tf_op jit(solution)/shard_map/pallas_call | solution.py:75
  38.5 0.5 collective-permute-start.14
  39.1 0.4 collective-permute-start.16
  39.5 0.4 collective-permute-done.13.refs_4_
  40.9 1.6 %collective-permute-start.17 = (f32[384,128]{1,0:T(8,128)S(1)}, f32[384,128]{1,0:T(8,128)S(1)}, u32[]{:S(2)}, u32[]{:S(2)}) collective-permute-start(f32[384,128]{1,0:T(8,128)S(1)} %get-tuple-element.70), channel_id=1, source_target_pairs={{0,1},{1,0},{2,3},{3,2},{4,5},{5,4},{6,7},{7,6},{8,9},{9,8},{10,11... | collective-permute-start | bytes 589832 | tf_op jit(solution)/shard_map/ppermute | solution.py:64
  42.5 1.5 %collective-permute-start.18 = (f32[384,128]{1,0:T(8,128)S(1)}, f32[384,128]{1,0:T(8,128)S(1)}, u32[]{:S(2)}, u32[]{:S(2)}) collective-permute-start(f32[384,128]{1,0:T(8,128)S(1)} %get-tuple-element.71), channel_id=1, source_target_pairs={{0,16},{1,17},{2,18},{3,19},{4,20},{5,21},{6,22},{7,23},{8,24},{9,... | collective-permute-start | bytes 589832 | tf_op jit(solution)/shard_map/ppermute | solution.py:64
  44.0 0.5 collective-permute-start.19
  44.4 3.5 %collective-permute-done.17.refs_1_ = f32[384,128]{1,0:T(8,128)S(1)} collective-permute-done((f32[384,128]{1,0:T(8,128)S(1)}, f32[384,128]{1,0:T(8,128)S(1)}, u32[]{:S(2)}, u32[]{:S(2)}) %collective-permute-start.17) | collective-permute-done | bytes 196640 | tf_op jit(solution)/shard_map/ppermute | solution.py:64
  48.0 2.3 %collective-permute-done.18.refs_2_ = f32[384,128]{1,0:T(8,128)S(1)} collective-permute-done((f32[384,128]{1,0:T(8,128)S(1)}, f32[384,128]{1,0:T(8,128)S(1)}, u32[]{:S(2)}, u32[]{:S(2)}) %collective-permute-start.18) | collective-permute-done | bytes 196640 | tf_op jit(solution)/shard_map/ppermute | solution.py:64
  50.3 3.1 %collective-permute-done.19.refs_3_ = f32[384,128]{1,0:T(8,128)S(1)} collective-permute-done((f32[384,128]{1,0:T(8,128)S(1)}, f32[384,128]{1,0:T(8,128)S(1)}, u32[]{:S(2)}, u32[]{:S(2)}) %collective-permute-start.19) | collective-permute-done | bytes 196640 | tf_op jit(solution)/shard_map/ppermute | solution.py:64
  53.5 1.6 %collective-permute-start.20 = (bf16[208,128]{1,0:T(8,128)(2,1)S(1)}, bf16[208,128]{1,0:T(8,128)(2,1)S(1)}, u32[]{:S(2)}, u32[]{:S(2)}) collective-permute-start(bf16[208,128]{1,0:T(8,128)(2,1)S(1)} %shard_map.100.refs_13_), channel_id=1, source_target_pairs={{0,1},{1,0},{2,3},{3,2},{4,5},{5,4},{6,7},{7,6},{8,9},{9,8},{10,11... | collective-permute-start | bytes 159752 | tf_op jit(solution)/shard_map/ppermute | solution.py:64
  55.0 1.5 %collective-permute-start.23 = (bf16[208,128]{1,0:T(8,128)(2,1)S(1)}, bf16[208,128]{1,0:T(8,128)(2,1)S(1)}, u32[]{:S(2)}, u32[]{:S(2)}) collective-permute-start(bf16[208,128]{1,0:T(8,128)(2,1)S(1)} %shard_map.100.refs_13_), channel_id=1, source_target_pairs={{0,16},{1,17},{2,18},{3,19},{4,20},{5,21},{6,22},{7,23},{8,24},{9,... | collective-permute-start | bytes 159752 | tf_op jit(solution)/shard_map/ppermute | solution.py:64
  56.5 0.5 collective-permute-start.24
  57.0 0.6 collective-permute-done.20.refs_14_
  57.7 1.5 %collective-permute-done.23.refs_17_ = bf16[208,128]{1,0:T(8,128)(2,1)S(1)} collective-permute-done((bf16[208,128]{1,0:T(8,128)(2,1)S(1)}, bf16[208,128]{1,0:T(8,128)(2,1)S(1)}, u32[]{:S(2)}, u32[]{:S(2)}) %collective-permute-start.23) | collective-permute-done | bytes 53280 | tf_op jit(solution)/shard_map/ppermute | solution.py:64
  59.2 2.4 %collective-permute-done.24.refs_18_ = bf16[208,128]{1,0:T(8,128)(2,1)S(1)} collective-permute-done((bf16[208,128]{1,0:T(8,128)(2,1)S(1)}, bf16[208,128]{1,0:T(8,128)(2,1)S(1)}, u32[]{:S(2)}, u32[]{:S(2)}) %collective-permute-start.24) | collective-permute-done | bytes 53280 | tf_op jit(solution)/shard_map/ppermute | solution.py:64
  61.6 1.9 %shard_map.101 = (f32[512,64]{1,0:T(8,128)S(1)}, f32[64,1024]{1,0:T(8,128)S(1)}) custom-call(bf16[384,128]{1,0:T(8,128)(2,1)S(1)} %get-tuple-element.55.refs_0_, bf16[384,128]{1,0:T(8,128)(2,1)S(1)} %collective-permute-done.3.refs_1_, bf16[384,128]{1,0:T(8,128)(2,1)S(1)} %collective-permute-done.4.refs_2_, ...), custom_call_target="tpu_custom_call" | custom-call | flops 268435456 | bytes 2031616 | tf_op jit(solution)/shard_map/pallas_call | solution.py:75
  63.5 3.7 %shard_map.102 = (f32[512,128]{1,0:T(8,128)S(1)}, f32[128,1024]{1,0:T(8,128)S(1)}) custom-call(bf16[384,128]{1,0:T(8,128)(2,1)S(1)} %get-tuple-element.55.refs_0_, bf16[384,128]{1,0:T(8,128)(2,1)S(1)} %collective-permute-done.3.refs_1_, bf16[384,128]{1,0:T(8,128)(2,1)S(1)} %collective-permute-done.4.refs_2_, ...), custom_call_target="tpu_custom_call" | custom-call | flops 536870912 | bytes 2424832 | tf_op jit(solution)/shard_map/pallas_call | solution.py:75
  67.2 4.7 %shard_map.103 = (bf16[128,384]{1,0:T(8,128)(2,1)S(1)}, bf16[128,384]{1,0:T(8,128)(2,1)S(1)}, bf16[128,384]{1,0:T(8,128)(2,1)S(1)}, bf16[128,384]{1,0:T(8,128)(2...) custom-call(bf16[384,128]{1,0:T(8,128)(2,1)S(1)} %get-tuple-element., ...), custom_call_target="tpu_custom_call" | custom-call | flops 1006632960 | bytes 4173824 | tf_op jit(solution)/shard_map/pallas_call | solution.py:75
  71.9 0.6 collective-permute-start.30
  72.6 0.4 collective-permute-start.32
  74.3 0.6 collective-permute-start.34
  74.9 0.6 collective-permute-start.35
  75.5 2.4 %collective-permute-start.36 = (f32[192,128]{1,0:T(8,128)S(1)}, f32[192,128]{1,0:T(8,128)S(1)}, u32[]{:S(2)}, u32[]{:S(2)}) collective-permute-start(f32[192,128]{1,0:T(8,128)S(1)} %get-tuple-element.94), channel_id=1, source_target_pairs={{0,17},{1,16},{2,19},{3,18},{4,21},{5,20},{6,23},{7,22},{8,25},{9,... | collective-permute-start | bytes 294920 | tf_op jit(solution)/shard_map/ppermute | solution.py:64
  77.9 2.7 %collective-permute-start.27 = (bf16[128,384]{1,0:T(8,128)(2,1)S(1)}, bf16[128,384]{1,0:T(8,128)(2,1)S(1)}, u32[]{:S(2)}, u32[]{:S(2)}) collective-permute-start(bf16[128,384]{1,0:T(8,128)(2,1)S(1)} %get-tuple-element.78), channel_id=1, source_target_pairs={{0,2},{1,3},{2,0},{3,1},{4,6},{5,7},{6,4},{7,5},{8,10},{9,11},{10,... | collective-permute-start | bytes 294920 | tf_op jit(solution)/shard_map/ppermute | solution.py:64
  80.6 2.4 %collective-permute-start.29 = (bf16[128,384]{1,0:T(8,128)(2,1)S(1)}, bf16[128,384]{1,0:T(8,128)(2,1)S(1)}, u32[]{:S(2)}, u32[]{:S(2)}) collective-permute-start(bf16[128,384]{1,0:T(8,128)(2,1)S(1)} %get-tuple-element.80), channel_id=1, source_target_pairs={{0,6},{1,7},{2,4},{3,5},{4,2},{5,3},{6,0},{7,1},{8,14},{9,15},{10,... | collective-permute-start | bytes 294920 | tf_op jit(solution)/shard_map/ppermute | solution.py:64
  83.1 2.3 %collective-permute-start.37 = (f32[48,128]{1,0:T(8,128)S(1)}, f32[48,128]{1,0:T(8,128)S(1)}, u32[]{:S(2)}, u32[]{:S(2)}) collective-permute-start(f32[48,128]{1,0:T(8,128)S(1)} %get-tuple-element.96), channel_id=1, source_target_pairs={{0,2},{1,3},{2,0},{3,1},{4,6},{5,7},{6,4},{7,5},{8,10},{9,11},{10,... | collective-permute-start | bytes 73736 | tf_op jit(solution)/shard_map/ppermute | solution.py:64
  85.5 2.4 %collective-permute-start.39 = (f32[48,128]{1,0:T(8,128)S(1)}, f32[48,128]{1,0:T(8,128)S(1)}, u32[]{:S(2)}, u32[]{:S(2)}) collective-permute-start(f32[48,128]{1,0:T(8,128)S(1)} %get-tuple-element.98), channel_id=1, source_target_pairs={{0,6},{1,7},{2,4},{3,5},{4,2},{5,3},{6,0},{7,1},{8,14},{9,15},{10,... | collective-permute-start | bytes 73736 | tf_op jit(solution)/shard_map/ppermute | solution.py:64
  87.9 2.9 %collective-permute-done.28.refs_2_ = bf16[128,384]{1,0:T(8,128)(2,1)S(1)} collective-permute-done((bf16[128,384]{1,0:T(8,128)(2,1)S(1)}, bf16[128,384]{1,0:T(8,128)(2,1)S(1)}, u32[]{:S(2)}, u32[]{:S(2)}) %collective-permute-start.28) | collective-permute-done | bytes 98336 | tf_op jit(solution)/shard_map/ppermute | solution.py:64
  90.8 0.9 %shard_map.104 = (bf16[128,768]{1,0:T(8,128)(2,1)}, bf16[128,768]{1,0:T(8,128)(2,1)}) custom-call(bf16[128,384]{1,0:T(8,128)(2,1)S(1)} %get-tuple-element.77.refs_0_, bf16[128,384]{1,0:T(8,128)(2,1)S(1)} %collective-permute-done.27.refs_1_, bf16[128,384]{1,0:T(8,128)(2,1)S(1)} %collective-permute-done.28.refs_2_, ...), custom_call_target="tpu_custom_call" | custom-call | bytes 786432 | tf_op jit(solution)/shard_map/pallas_call | solution.py:75
  91.7 1.4 %collective-permute-done.38.refs_2_ = f32[48,128]{1,0:T(8,128)S(1)} collective-permute-done((f32[48,128]{1,0:T(8,128)S(1)}, f32[48,128]{1,0:T(8,128)S(1)}, u32[]{:S(2)}, u32[]{:S(2)}) %collective-permute-start.38) | collective-permute-done | bytes 24608 | tf_op jit(solution)/shard_map/ppermute | solution.py:64
  93.2 0.8 shard_map.107
  (54 shorter events, 3.6 us)
Async XLA Ops:
  2.2 5.7 %collective-permute-start = (bf16[48,384]{1,0:T(8,128)(2,1)}, bf16[48,384]{1,0:T(8,128)(2,1)S(1)}, u32[]{:S(2)}, u32[]{:S(2)}) collective-permute-start(bf16[48,384]{1,0:T(8,128)(2,1)} %get-tuple-element.52), channel_id=1, source_target_pairs={{0,2},{1,3},{2,0},{3,1},{4,6},{5,7},{6,4},{7,5},{8,10},{9,11},{10,... | collective-permute-start | bytes 110600 | tf_op jit(solution)/shard_map/ppermute | solution.py:64
  5.4 5.7 %collective-permute-start.1 = (bf16[48,384]{1,0:T(8,128)(2,1)}, bf16[48,384]{1,0:T(8,128)(2,1)S(1)}, u32[]{:S(2)}, u32[]{:S(2)}) collective-permute-start(bf16[48,384]{1,0:T(8,128)(2,1)} %get-tuple-element.53), channel_id=1, source_target_pairs={{0,4},{1,5},{2,6},{3,7},{4,0},{5,1},{6,2},{7,3},{8,12},{9,13},{10,... | collective-permute-start | bytes 110600 | tf_op jit(solution)/shard_map/ppermute | solution.py:64
  7.9 6.0 %collective-permute-start.2 = (bf16[48,384]{1,0:T(8,128)(2,1)}, bf16[48,384]{1,0:T(8,128)(2,1)S(1)}, u32[]{:S(2)}, u32[]{:S(2)}) collective-permute-start(bf16[48,384]{1,0:T(8,128)(2,1)} %get-tuple-element.54), channel_id=1, source_target_pairs={{0,6},{1,7},{2,4},{3,5},{4,2},{5,3},{6,0},{7,1},{8,14},{9,15},{10,... | collective-permute-start | bytes 110600 | tf_op jit(solution)/shard_map/ppermute | solution.py:64
  13.9 0.8 copy-start.1
  14.9 12.0 %copy-start = (f32[12,1024]{1,0:T(8,128)S(1)}, f32[12,1024]{1,0:T(8,128)}, u32[]{:S(2)}) copy-start(f32[12,1024]{1,0:T(8,128)} %n_ref.1) | copy-start | bytes 147460
  14.9 6.1 %collective-permute-start.3 = (bf16[384,128]{1,0:T(8,128)(2,1)S(1)}, bf16[384,128]{1,0:T(8,128)(2,1)S(1)}, u32[]{:S(2)}, u32[]{:S(2)}) collective-permute-start(bf16[384,128]{1,0:T(8,128)(2,1)S(1)} %get-tuple-element.55.refs_0_), channel_id=1, source_target_pairs={{0,1},{1,0},{2,3},{3,2},{4,5},{5,4},{6,7},{7,6},{8,9},{9,8},{10,11... | collective-permute-start | bytes 294920 | tf_op jit(solution)/shard_map/ppermute | solution.py:64
  16.5 5.5 %collective-permute-start.4 = (bf16[384,128]{1,0:T(8,128)(2,1)S(1)}, bf16[384,128]{1,0:T(8,128)(2,1)S(1)}, u32[]{:S(2)}, u32[]{:S(2)}) collective-permute-start(bf16[384,128]{1,0:T(8,128)(2,1)S(1)} %get-tuple-element.55.refs_0_), channel_id=1, source_target_pairs={{0,8},{1,9},{2,10},{3,11},{4,12},{5,13},{6,14},{7,15},{8,0},{9,1},... | collective-permute-start | bytes 294920 | tf_op jit(solution)/shard_map/ppermute | solution.py:64
  18.9 7.7 %collective-permute-start.10 = (bf16[192,384]{1,0:T(8,128)(2,1)}, bf16[192,384]{1,0:T(8,128)(2,1)S(1)}, u32[]{:S(2)}, u32[]{:S(2)}) collective-permute-start(bf16[192,384]{1,0:T(8,128)(2,1)} %get-tuple-element.57), channel_id=1, source_target_pairs={{0,2},{1,3},{2,0},{3,1},{4,6},{5,7},{6,4},{7,5},{8,10},{9,11},{10,... | collective-permute-start | bytes 442376 | tf_op jit(solution)/shard_map/ppermute | solution.py:64
  19.0 6.4 %collective-permute-start.6 = (bf16[384,128]{1,0:T(8,128)(2,1)S(1)}, bf16[384,128]{1,0:T(8,128)(2,1)S(1)}, u32[]{:S(2)}, u32[]{:S(2)}) collective-permute-start(bf16[384,128]{1,0:T(8,128)(2,1)S(1)} %get-tuple-element.55.refs_0_), channel_id=1, source_target_pairs={{0,16},{1,17},{2,18},{3,19},{4,20},{5,21},{6,22},{7,23},{8,24},{9,... | collective-permute-start | bytes 294920 | tf_op jit(solution)/shard_map/ppermute | solution.py:64
  20.5 5.8 %collective-permute-start.7 = (bf16[384,128]{1,0:T(8,128)(2,1)S(1)}, bf16[384,128]{1,0:T(8,128)(2,1)S(1)}, u32[]{:S(2)}, u32[]{:S(2)}) collective-permute-start(bf16[384,128]{1,0:T(8,128)(2,1)S(1)} %get-tuple-element.55.refs_0_), channel_id=1, source_target_pairs={{0,17},{1,16},{2,19},{3,18},{4,21},{5,20},{6,23},{7,22},{8,25},{9,... | collective-permute-start | bytes 294920 | tf_op jit(solution)/shard_map/ppermute | solution.py:64
  21.0 14.2 %collective-permute-start.11 = (bf16[192,384]{1,0:T(8,128)(2,1)}, bf16[192,384]{1,0:T(8,128)(2,1)S(1)}, u32[]{:S(2)}, u32[]{:S(2)}) collective-permute-start(bf16[192,384]{1,0:T(8,128)(2,1)} %get-tuple-element.58), channel_id=1, source_target_pairs={{0,4},{1,5},{2,6},{3,7},{4,0},{5,1},{6,2},{7,3},{8,12},{9,13},{10,... | collective-permute-start | bytes 442376 | tf_op jit(solution)/shard_map/ppermute | solution.py:64
  22.0 13.2 %collective-permute-start.12 = (bf16[192,384]{1,0:T(8,128)(2,1)}, bf16[192,384]{1,0:T(8,128)(2,1)S(1)}, u32[]{:S(2)}, u32[]{:S(2)}) collective-permute-start(bf16[192,384]{1,0:T(8,128)(2,1)} %get-tuple-element.59), channel_id=1, source_target_pairs={{0,6},{1,7},{2,4},{3,5},{4,2},{5,3},{6,0},{7,1},{8,14},{9,15},{10,... | collective-permute-start | bytes 442376 | tf_op jit(solution)/shard_map/ppermute | solution.py:64
  25.3 9.8 %collective-permute-start.5 = (bf16[384,128]{1,0:T(8,128)(2,1)S(1)}, bf16[384,128]{1,0:T(8,128)(2,1)S(1)}, u32[]{:S(2)}, u32[]{:S(2)}) collective-permute-start(bf16[384,128]{1,0:T(8,128)(2,1)S(1)} %collective-permute-done.3.refs_1_), channel_id=1, source_target_pairs={{0,8},{1,9},{2,10},{3,11},{4,12},{5,13},{6,14},{7,15},{8,0},{9,1},... | collective-permute-start | bytes 294920 | tf_op jit(solution)/shard_map/ppermute | solution.py:64
  26.4 8.8 %collective-permute-start.8 = (bf16[384,128]{1,0:T(8,128)(2,1)S(1)}, bf16[384,128]{1,0:T(8,128)(2,1)S(1)}, u32[]{:S(2)}, u32[]{:S(2)}) collective-permute-start(bf16[384,128]{1,0:T(8,128)(2,1)S(1)} %collective-permute-done.6.refs_4_), channel_id=1, source_target_pairs={{0,8},{1,9},{2,10},{3,11},{4,12},{5,13},{6,14},{7,15},{8,0},{9,1},... | collective-permute-start | bytes 294920 | tf_op jit(solution)/shard_map/ppermute | solution.py:64
  26.6 8.6 %collective-permute-start.9 = (bf16[384,128]{1,0:T(8,128)(2,1)S(1)}, bf16[384,128]{1,0:T(8,128)(2,1)S(1)}, u32[]{:S(2)}, u32[]{:S(2)}) collective-permute-start(bf16[384,128]{1,0:T(8,128)(2,1)S(1)} %collective-permute-done.7.refs_5_), channel_id=1, source_target_pairs={{0,8},{1,9},{2,10},{3,11},{4,12},{5,13},{6,14},{7,15},{8,0},{9,1},... | collective-permute-start | bytes 294920 | tf_op jit(solution)/shard_map/ppermute | solution.py:64
  35.2 0.9 copy-start.2
  38.5 1.5 %collective-permute-start.13 = (f32[384,128]{1,0:T(8,128)S(1)}, f32[384,128]{1,0:T(8,128)S(1)}, u32[]{:S(2)}, u32[]{:S(2)}) collective-permute-start(f32[384,128]{1,0:T(8,128)S(1)} %get-tuple-element.65), channel_id=1, source_target_pairs={{0,8},{1,9},{2,10},{3,11},{4,12},{5,13},{6,14},{7,15},{8,0},{9,1},... | collective-permute-start | bytes 589832 | tf_op jit(solution)/shard_map/ppermute | solution.py:64
  38.5 1.7 %collective-permute-start.14 = (f32[384,128]{1,0:T(8,128)S(1)}, f32[384,128]{1,0:T(8,128)S(1)}, u32[]{:S(2)}, u32[]{:S(2)}) collective-permute-start(f32[384,128]{1,0:T(8,128)S(1)} %get-tuple-element.66), channel_id=1, source_target_pairs={{0,8},{1,9},{2,10},{3,11},{4,12},{5,13},{6,14},{7,15},{8,0},{9,1},... | collective-permute-start | bytes 589832 | tf_op jit(solution)/shard_map/ppermute | solution.py:64
  39.0 1.5 %collective-permute-start.15 = (f32[384,128]{1,0:T(8,128)S(1)}, f32[384,128]{1,0:T(8,128)S(1)}, u32[]{:S(2)}, u32[]{:S(2)}) collective-permute-start(f32[384,128]{1,0:T(8,128)S(1)} %get-tuple-element.67), channel_id=1, source_target_pairs={{0,8},{1,9},{2,10},{3,11},{4,12},{5,13},{6,14},{7,15},{8,0},{9,1},... | collective-permute-start | bytes 589832 | tf_op jit(solution)/shard_map/ppermute | solution.py:64
  39.1 1.7 %collective-permute-start.16 = (f32[384,128]{1,0:T(8,128)S(1)}, f32[384,128]{1,0:T(8,128)S(1)}, u32[]{:S(2)}, u32[]{:S(2)}) collective-permute-start(f32[384,128]{1,0:T(8,128)S(1)} %get-tuple-element.68), channel_id=1, source_target_pairs={{0,8},{1,9},{2,10},{3,11},{4,12},{5,13},{6,14},{7,15},{8,0},{9,1},... | collective-permute-start | bytes 589832 | tf_op jit(solution)/shard_map/ppermute | solution.py:64
  40.9 7.1 %collective-permute-start.17 = (f32[384,128]{1,0:T(8,128)S(1)}, f32[384,128]{1,0:T(8,128)S(1)}, u32[]{:S(2)}, u32[]{:S(2)}) collective-permute-start(f32[384,128]{1,0:T(8,128)S(1)} %get-tuple-element.70), channel_id=1, source_target_pairs={{0,1},{1,0},{2,3},{3,2},{4,5},{5,4},{6,7},{7,6},{8,9},{9,8},{10,11... | collective-permute-start | bytes 589832 | tf_op jit(solution)/shard_map/ppermute | solution.py:64
  42.5 7.8 %collective-permute-start.18 = (f32[384,128]{1,0:T(8,128)S(1)}, f32[384,128]{1,0:T(8,128)S(1)}, u32[]{:S(2)}, u32[]{:S(2)}) collective-permute-start(f32[384,128]{1,0:T(8,128)S(1)} %get-tuple-element.71), channel_id=1, source_target_pairs={{0,16},{1,17},{2,18},{3,19},{4,20},{5,21},{6,22},{7,23},{8,24},{9,... | collective-permute-start | bytes 589832 | tf_op jit(solution)/shard_map/ppermute | solution.py:64
  44.0 9.4 %collective-permute-start.19 = (f32[384,128]{1,0:T(8,128)S(1)}, f32[384,128]{1,0:T(8,128)S(1)}, u32[]{:S(2)}, u32[]{:S(2)}) collective-permute-start(f32[384,128]{1,0:T(8,128)S(1)} %get-tuple-element.72), channel_id=1, source_target_pairs={{0,17},{1,16},{2,19},{3,18},{4,21},{5,20},{6,23},{7,22},{8,25},{9,... | collective-permute-start | bytes 589832 | tf_op jit(solution)/shard_map/ppermute | solution.py:64
  53.4 8.2 %copy-start.3 = (bf16[192,384]{1,0:T(8,128)(2,1)S(1)}, bf16[192,384]{1,0:T(8,128)(2,1)}, u32[]{:S(2)}) copy-start(bf16[192,384]{1,0:T(8,128)(2,1)} %get-tuple-element.56.refs_8_) | copy-start | bytes 442372
  53.5 4.2 %collective-permute-start.20 = (bf16[208,128]{1,0:T(8,128)(2,1)S(1)}, bf16[208,128]{1,0:T(8,128)(2,1)S(1)}, u32[]{:S(2)}, u32[]{:S(2)}) collective-permute-start(bf16[208,128]{1,0:T(8,128)(2,1)S(1)} %shard_map.100.refs_13_), channel_id=1, source_target_pairs={{0,1},{1,0},{2,3},{3,2},{4,5},{5,4},{6,7},{7,6},{8,9},{9,8},{10,11... | collective-permute-start | bytes 159752 | tf_op jit(solution)/shard_map/ppermute | solution.py:64
  55.0 4.1 %collective-permute-start.23 = (bf16[208,128]{1,0:T(8,128)(2,1)S(1)}, bf16[208,128]{1,0:T(8,128)(2,1)S(1)}, u32[]{:S(2)}, u32[]{:S(2)}) collective-permute-start(bf16[208,128]{1,0:T(8,128)(2,1)S(1)} %shard_map.100.refs_13_), channel_id=1, source_target_pairs={{0,16},{1,17},{2,18},{3,19},{4,20},{5,21},{6,22},{7,23},{8,24},{9,... | collective-permute-start | bytes 159752 | tf_op jit(solution)/shard_map/ppermute | solution.py:64
  56.5 5.0 %collective-permute-start.24 = (bf16[208,128]{1,0:T(8,128)(2,1)S(1)}, bf16[208,128]{1,0:T(8,128)(2,1)S(1)}, u32[]{:S(2)}, u32[]{:S(2)}) collective-permute-start(bf16[208,128]{1,0:T(8,128)(2,1)S(1)} %shard_map.100.refs_13_), channel_id=1, source_target_pairs={{0,17},{1,16},{2,19},{3,18},{4,21},{5,20},{6,23},{7,22},{8,25},{9,... | collective-permute-start | bytes 159752 | tf_op jit(solution)/shard_map/ppermute | solution.py:64
  57.0 10.2 %collective-permute-start.21 = (bf16[208,128]{1,0:T(8,128)(2,1)S(1)}, bf16[208,128]{1,0:T(8,128)(2,1)S(1)}, u32[]{:S(2)}, u32[]{:S(2)}) collective-permute-start(bf16[208,128]{1,0:T(8,128)(2,1)S(1)} %shard_map.100.refs_13_), channel_id=1, source_target_pairs={{0,8},{1,9},{2,10},{3,11},{4,12},{5,13},{6,14},{7,15},{8,0},{9,1},... | collective-permute-start | bytes 159752 | tf_op jit(solution)/shard_map/ppermute | solution.py:64
  57.7 9.5 %collective-permute-start.22 = (bf16[208,128]{1,0:T(8,128)(2,1)S(1)}, bf16[208,128]{1,0:T(8,128)(2,1)S(1)}, u32[]{:S(2)}, u32[]{:S(2)}) collective-permute-start(bf16[208,128]{1,0:T(8,128)(2,1)S(1)} %collective-permute-done.20.refs_14_), channel_id=1, source_target_pairs={{0,8},{1,9},{2,10},{3,11},{4,12},{5,13},{6,14},{7,15},{8,0},{9,1},... | collective-permute-start | bytes 159752 | tf_op jit(solution)/shard_map/ppermute | solution.py:64
  59.2 8.0 %collective-permute-start.25 = (bf16[208,128]{1,0:T(8,128)(2,1)S(1)}, bf16[208,128]{1,0:T(8,128)(2,1)S(1)}, u32[]{:S(2)}, u32[]{:S(2)}) collective-permute-start(bf16[208,128]{1,0:T(8,128)(2,1)S(1)} %collective-permute-done.23.refs_17_), channel_id=1, source_target_pairs={{0,8},{1,9},{2,10},{3,11},{4,12},{5,13},{6,14},{7,15},{8,0},{9,1},... | collective-permute-start | bytes 159752 | tf_op jit(solution)/shard_map/ppermute | solution.py:64
  61.6 5.6 %collective-permute-start.26 = (bf16[208,128]{1,0:T(8,128)(2,1)S(1)}, bf16[208,128]{1,0:T(8,128)(2,1)S(1)}, u32[]{:S(2)}, u32[]{:S(2)}) collective-permute-start(bf16[208,128]{1,0:T(8,128)(2,1)S(1)} %collective-permute-done.24.refs_18_), channel_id=1, source_target_pairs={{0,8},{1,9},{2,10},{3,11},{4,12},{5,13},{6,14},{7,15},{8,0},{9,1},... | collective-permute-start | bytes 159752 | tf_op jit(solution)/shard_map/ppermute | solution.py:64
  71.9 1.5 %collective-permute-start.30 = (f32[192,128]{1,0:T(8,128)S(1)}, f32[192,128]{1,0:T(8,128)S(1)}, u32[]{:S(2)}, u32[]{:S(2)}) collective-permute-start(f32[192,128]{1,0:T(8,128)S(1)} %get-tuple-element.87), channel_id=1, source_target_pairs={{0,8},{1,9},{2,10},{3,11},{4,12},{5,13},{6,14},{7,15},{8,0},{9,1},... | collective-permute-start | bytes 294920 | tf_op jit(solution)/shard_map/ppermute | solution.py:64
  72.5 1.3 %collective-permute-start.31 = (f32[192,128]{1,0:T(8,128)S(1)}, f32[192,128]{1,0:T(8,128)S(1)}, u32[]{:S(2)}, u32[]{:S(2)}) collective-permute-start(f32[192,128]{1,0:T(8,128)S(1)} %get-tuple-element.88), channel_id=1, source_target_pairs={{0,8},{1,9},{2,10},{3,11},{4,12},{5,13},{6,14},{7,15},{8,0},{9,1},... | collective-permute-start | bytes 294920 | tf_op jit(solution)/shard_map/ppermute | solution.py:64
  72.6 1.4 %collective-permute-start.32 = (f32[192,128]{1,0:T(8,128)S(1)}, f32[192,128]{1,0:T(8,128)S(1)}, u32[]{:S(2)}, u32[]{:S(2)}) collective-permute-start(f32[192,128]{1,0:T(8,128)S(1)} %get-tuple-element.89), channel_id=1, source_target_pairs={{0,8},{1,9},{2,10},{3,11},{4,12},{5,13},{6,14},{7,15},{8,0},{9,1},... | collective-permute-start | bytes 294920 | tf_op jit(solution)/shard_map/ppermute | solution.py:64
  73.0 1.3 %collective-permute-start.33 = (f32[192,128]{1,0:T(8,128)S(1)}, f32[192,128]{1,0:T(8,128)S(1)}, u32[]{:S(2)}, u32[]{:S(2)}) collective-permute-start(f32[192,128]{1,0:T(8,128)S(1)} %get-tuple-element.90), channel_id=1, source_target_pairs={{0,8},{1,9},{2,10},{3,11},{4,12},{5,13},{6,14},{7,15},{8,0},{9,1},... | collective-permute-start | bytes 294920 | tf_op jit(solution)/shard_map/ppermute | solution.py:64
  74.3 6.3 %collective-permute-start.34 = (f32[192,128]{1,0:T(8,128)S(1)}, f32[192,128]{1,0:T(8,128)S(1)}, u32[]{:S(2)}, u32[]{:S(2)}) collective-permute-start(f32[192,128]{1,0:T(8,128)S(1)} %get-tuple-element.92), channel_id=1, source_target_pairs={{0,1},{1,0},{2,3},{3,2},{4,5},{5,4},{6,7},{7,6},{8,9},{9,8},{10,11... | collective-permute-start | bytes 294920 | tf_op jit(solution)/shard_map/ppermute | solution.py:64
  74.9 8.1 %collective-permute-start.35 = (f32[192,128]{1,0:T(8,128)S(1)}, f32[192,128]{1,0:T(8,128)S(1)}, u32[]{:S(2)}, u32[]{:S(2)}) collective-permute-start(f32[192,128]{1,0:T(8,128)S(1)} %get-tuple-element.93), channel_id=1, source_target_pairs={{0,16},{1,17},{2,18},{3,19},{4,20},{5,21},{6,22},{7,23},{8,24},{9,... | collective-permute-start | bytes 294920 | tf_op jit(solution)/shard_map/ppermute | solution.py:64
  75.5 7.4 %collective-permute-start.36 = (f32[192,128]{1,0:T(8,128)S(1)}, f32[192,128]{1,0:T(8,128)S(1)}, u32[]{:S(2)}, u32[]{:S(2)}) collective-permute-start(f32[192,128]{1,0:T(8,128)S(1)} %get-tuple-element.94), channel_id=1, source_target_pairs={{0,17},{1,16},{2,19},{3,18},{4,21},{5,20},{6,23},{7,22},{8,25},{9,... | collective-permute-start | bytes 294920 | tf_op jit(solution)/shard_map/ppermute | solution.py:64
  77.9 7.6 %collective-permute-start.27 = (bf16[128,384]{1,0:T(8,128)(2,1)S(1)}, bf16[128,384]{1,0:T(8,128)(2,1)S(1)}, u32[]{:S(2)}, u32[]{:S(2)}) collective-permute-start(bf16[128,384]{1,0:T(8,128)(2,1)S(1)} %get-tuple-element.78), channel_id=1, source_target_pairs={{0,2},{1,3},{2,0},{3,1},{4,6},{5,7},{6,4},{7,5},{8,10},{9,11},{10,... | collective-permute-start | bytes 294920 | tf_op jit(solution)/shard_map/ppermute | solution.py:64
  80.6 10.2 %collective-permute-start.28 = (bf16[128,384]{1,0:T(8,128)(2,1)S(1)}, bf16[128,384]{1,0:T(8,128)(2,1)S(1)}, u32[]{:S(2)}, u32[]{:S(2)}) collective-permute-start(bf16[128,384]{1,0:T(8,128)(2,1)S(1)} %get-tuple-element.79), channel_id=1, source_target_pairs={{0,4},{1,5},{2,6},{3,7},{4,0},{5,1},{6,2},{7,3},{8,12},{9,13},{10,... | collective-permute-start | bytes 294920 | tf_op jit(solution)/shard_map/ppermute | solution.py:64
  80.6 10.2 %collective-permute-start.29 = (bf16[128,384]{1,0:T(8,128)(2,1)S(1)}, bf16[128,384]{1,0:T(8,128)(2,1)S(1)}, u32[]{:S(2)}, u32[]{:S(2)}) collective-permute-start(bf16[128,384]{1,0:T(8,128)(2,1)S(1)} %get-tuple-element.80), channel_id=1, source_target_pairs={{0,6},{1,7},{2,4},{3,5},{4,2},{5,3},{6,0},{7,1},{8,14},{9,15},{10,... | collective-permute-start | bytes 294920 | tf_op jit(solution)/shard_map/ppermute | solution.py:64
  83.1 8.6 %collective-permute-start.37 = (f32[48,128]{1,0:T(8,128)S(1)}, f32[48,128]{1,0:T(8,128)S(1)}, u32[]{:S(2)}, u32[]{:S(2)}) collective-permute-start(f32[48,128]{1,0:T(8,128)S(1)} %get-tuple-element.96), channel_id=1, source_target_pairs={{0,2},{1,3},{2,0},{3,1},{4,6},{5,7},{6,4},{7,5},{8,10},{9,11},{10,... | collective-permute-start | bytes 73736 | tf_op jit(solution)/shard_map/ppermute | solution.py:64
  85.5 7.7 %collective-permute-start.38 = (f32[48,128]{1,0:T(8,128)S(1)}, f32[48,128]{1,0:T(8,128)S(1)}, u32[]{:S(2)}, u32[]{:S(2)}) collective-permute-start(f32[48,128]{1,0:T(8,128)S(1)} %get-tuple-element.97), channel_id=1, source_target_pairs={{0,4},{1,5},{2,6},{3,7},{4,0},{5,1},{6,2},{7,3},{8,12},{9,13},{10,... | collective-permute-start | bytes 73736 | tf_op jit(solution)/shard_map/ppermute | solution.py:64
  85.5 7.7 %collective-permute-start.39 = (f32[48,128]{1,0:T(8,128)S(1)}, f32[48,128]{1,0:T(8,128)S(1)}, u32[]{:S(2)}, u32[]{:S(2)}) collective-permute-start(f32[48,128]{1,0:T(8,128)S(1)} %get-tuple-element.98), channel_id=1, source_target_pairs={{0,6},{1,7},{2,4},{3,5},{4,2},{5,3},{6,0},{7,1},{8,14},{9,15},{10,... | collective-permute-start | bytes 73736 | tf_op jit(solution)/shard_map/ppermute | solution.py:64

commit v3 on v2

--- a/solution.py
+++ b/solution.py
@@ -13,6 +13,7 @@
 LANES = 128
 AXES = ("pa", "pb")
 MOST_IN_PLANE = 16
+LAG, SLOTS = 1, 3
 GROUPS = 4
 VMEM_BYTES = 20 * 2**20
 WHOLE_VMEM_BYTES = 60 * 2**20
@@ -139,8 +140,8 @@
     return block.astype(jnp.float32).T.astype(block.dtype)
 
 
-def pack_latents(plan, query, out, norm):
-    def kernel(q_ref, o_ref, n_ref, *outs):
+def pack(plan, query, out, norm, keys, grads, values):
+    def kernel(q_ref, o_ref, n_ref, k_ref, g_ref, v_ref, *outs):
         z = group_index(plan)
         c, hs = plan.cols, plan.heads
         q, o = q_ref[...].astype(jnp.float32), o_ref[...].astype(jnp.float32)
@@ -152,36 +153,27 @@
             lines = [
                 jnp.concatenate([p[h : h + 1, :] for h in range(g * hs, (g + 1) * hs)], axis=1) for p in parts
             ]
-            pieces.append(jnp.concatenate([top, *lines, fill], axis=0))
-        for ref, piece in zip(outs, by_group(pieces, z), strict=True):
-            ref[...] = piece.astype(jnp.bfloat16)
-
-    outs = [shaped((plan.slot, 2 * plan.cols), jnp.bfloat16)] * GROUPS
-    args = (query, out, norm)
-    body, scratch = fetched(kernel, args)
-    return call(body, outs, args, scratch, from_hbm=True)
-
-
-def pack_points(plan, keys, grads, values):
-    def kernel(k_ref, g_ref, v_ref, *outs):
-        z = group_index(plan)
-        c = plan.cols
+            pieces.append(jnp.concatenate([top, *lines, fill], axis=0).astype(jnp.bfloat16))
+        for ref, piece in zip(outs[:GROUPS], by_group(pieces, z), strict=True):
+            ref[...] = piece
+        outs = outs[GROUPS:]
         for first, ref in ((0, k_ref), (1, g_ref)):
-            whole = ref[...].astype(jnp.float32)
-            pieces = by_group([whole[:, g * c : (g + 1) * c] for g in range(GROUPS)], z)
+            pieces = by_group([ref[:, g * c : (g + 1) * c] for g in range(GROUPS)], z)
             for out, piece in zip(outs, pieces, strict=True):
-                out[: plan.rows, first * c : (first + 1) * c] = piece.astype(jnp.bfloat16)
-        across = v_ref[...].astype(jnp.float32).T.astype(jnp.bfloat16)
+                out[: plan.rows, first * c : (first + 1) * c] = piece
+        across = v_ref[...].T
         pieces = by_group([across[g * c : (g + 1) * c] for g in range(GROUPS)], z)
         for out, piece in zip(outs, pieces, strict=True):
-            for h in range(plan.heads):
+            for h in range(hs):
                 lanes = slice(h * plan.rows, (h + 1) * plan.rows)
                 out[plan.rows :, lanes] = piece[h * HEAD_DIM : (h + 1) * HEAD_DIM]
 
-    outs = [shaped((plan.rows + HEAD_DIM, 2 * plan.cols), jnp.bfloat16)] * GROUPS
-    args = (keys, grads, values)
+    outs = [shaped((plan.slot, 2 * plan.cols), jnp.bfloat16)] * GROUPS
+    outs += [shaped((plan.rows + HEAD_DIM, 2 * plan.cols), jnp.bfloat16)] * GROUPS
+    args = (query, out, norm, keys, grads, values)
     body, scratch = fetched(kernel, args)
-    return call(body, outs, args, scratch, from_hbm=True)
+    got = call(body, outs, args, scratch, from_hbm=True)
+    return got[:GROUPS], got[GROUPS:]
 
 
 def order_norm(plan, norm):
@@ -300,11 +292,11 @@
                 total = jnp.sum(dec * grad, axis=1, keepdims=True)
                 tile = (dec * (grad - total)).astype(jnp.bfloat16)
                 ds[rows, :] = tile
-                key_ref[rows, put] = nt(tile, both[mine, :])
+            key_ref[put, :] = nt(both[mine, :], ds[...])
             lat_ref[put, :] = nn(keys_t[mine, :], ds[...])
 
     width = len(heads) * HEAD_DIM
-    outs = [shaped((plan.points, width), jnp.float32), shaped((width, m), jnp.float32)]
+    outs = [shaped((width, plan.points), jnp.float32), shaped((width, m), jnp.float32)]
     scratch = [
         pltpu.VMEM((2 * c, m), jnp.bfloat16),
         pltpu.VMEM((c, plan.points), jnp.bfloat16),
@@ -354,7 +346,7 @@
         mix_refs = take(n_mix)
         parts_in = [take(2) for _ in before]
         pts_outs, lat_outs = take(n_pts), take(n_lat)
-        query, mix, keys, keys_t, values = refs
+        query, mix, keys, keys_t, values, ds, encs = refs
         for k, ref in enumerate(lat_refs):
             query[:, k * plan.block : (k + 1) * plan.block] = ref[:c, :]
         for k, ref in enumerate(mix_refs):
@@ -367,30 +359,44 @@
             values[rows, :] = turned(jnp.concatenate(across, axis=0))
         tail = mix[c:, :].astype(jnp.float32)
         columns = (tail[:hs] + tail[hs : 2 * hs]) + tail[2 * hs : 3 * hs]
-        for h in range(hs):
-            mine = slice(h * HEAD_DIM, (h + 1) * HEAD_DIM)
+        tiles = lane_tiles(plan)
+        sums = {}
+
+        def weigh(h, t, slot):
+            mine, lanes = slice(h * HEAD_DIM, (h + 1) * HEAD_DIM), tiles[t]
+            scores = nn(keys[:, mine], query[mine, lanes]) * (HEAD_DIM**-0.5 * LOG2E)
+            enc = jnp.exp2(scores - norm_ref[h : h + 1, lanes] * LOG2E)
+            grad = nn(values[:, mine], mix[mine, lanes])
+            encs[slot] = enc.astype(jnp.bfloat16)
+            ds[slot] = (enc * (grad - columns[h : h + 1, lanes])).astype(jnp.bfloat16)
+
+        def gather(h, t, slot):
+            mine, lanes = slice(h * HEAD_DIM, (h + 1) * HEAD_DIM), tiles[t]
             part, at = places[h]
             key_in, lat_in = parts_in[part]
             put = slice(at * HEAD_DIM, (at + 1) * HEAD_DIM)
-            key, value = keys[:, mine], values[:, mine]
-            key_sum = key_in[:, put]
-            value_sum = None
-            for lanes in lane_tiles(plan):
-                scores = nn(key, query[mine, lanes]) * (HEAD_DIM**-0.5 * LOG2E)
-                enc = jnp.exp2(scores - norm_ref[h : h + 1, lanes] * LOG2E)
-                grad = nn(value, mix[mine, lanes])
-                ds = (enc * (grad - columns[h : h + 1, lanes])).astype(jnp.bfloat16)
-                key_sum = key_sum + nt(ds, query[mine, lanes])
-                more = nt(enc.astype(jnp.bfloat16), mix[mine, lanes])
-                value_sum = more if value_sum is None else value_sum + more
-                lat = (lat_in[put, lanes] + nn(keys_t[mine, :], ds)) * HEAD_DIM**-0.5
-                store_blocks(plan, lat_outs, mine, lanes, lat)
-            key_sum = (key_sum * HEAD_DIM**-0.5).astype(jnp.bfloat16)
-            value_sum = value_sum.astype(jnp.bfloat16)
+            lat = (lat_in[put, lanes] + nn(keys_t[mine, :], ds[slot])) * HEAD_DIM**-0.5
+            store_blocks(plan, lat_outs, mine, lanes, lat)
+            key, value = nt(query[mine, lanes], ds[slot]), nt(mix[mine, lanes], encs[slot])
+            key = key + (sums[h][0] if t else key_in[put, :])
+            sums[h] = (key, value + sums[h][1] if t else value)
+            if t < len(tiles) - 1:
+                return
+            key, value = sums.pop(h)
+            key = (key * HEAD_DIM**-0.5).T.astype(jnp.bfloat16)
+            value = value.T.astype(jnp.bfloat16)
             for j, out in enumerate(pts_outs):
                 rows = slice(j * plan.rows, (j + 1) * plan.rows)
-                out[:, mine] = key_sum[rows]
-                out[:, c + h * HEAD_DIM : c + (h + 1) * HEAD_DIM] = value_sum[rows]
+                out[:, mine] = key[rows]
+                out[:, c + h * HEAD_DIM : c + (h + 1) * HEAD_DIM] = value[rows]
+
+        work = [(h, t) for h in range(hs) for t in range(len(tiles))]
+        for n, place in enumerate(work):
+            weigh(*place, n % SLOTS)
+            if n >= LAG:
+                gather(*work[n - LAG], (n - LAG) % SLOTS)
+        for n in range(len(work) - LAG, len(work)):
+            gather(*work[n], n % SLOTS)
 
     outs = [shaped((plan.rows, 2 * c), jnp.bfloat16)] * n_pts
     outs += [shaped((c, plan.block), jnp.float32)] * n_lat
@@ -400,6 +406,8 @@
         pltpu.VMEM((plan.points, c), jnp.bfloat16),
         pltpu.VMEM((c, plan.points), jnp.bfloat16),
         pltpu.VMEM((plan.points, c), jnp.bfloat16),
+        pltpu.VMEM((SLOTS, plan.points, 2 * plan.block), jnp.bfloat16),
+        pltpu.VMEM((SLOTS, plan.points, 2 * plan.block), jnp.bfloat16),
     ]
     flops = 10 * plan.points * m * c
     args = (*lats, *pts, norm, *mixes, *(a for _, part in before for a in part))
@@ -489,8 +497,10 @@
             got[k | plan.fast] = plan.exchange(got[k], False, plan.fast)
         return tuple(got[k] for k in range(plan.plane))
 
-    lat_slots = over_group(pack_latents(plan, latent_query, latent_out, decoder_norm))
-    pts = pack_points(plan, point_keys, out_grad, point_values)
+    lat_slots, pts = pack(
+        plan, latent_query, latent_out, decoder_norm, point_keys, out_grad, point_values
+    )
+    lat_slots = over_group(lat_slots)
     pts = over_group(pts)
     norm = order_norm(plan, encoder_norm)
     block, dec_norm = turn_latents(plan, lat_slots)

time: 94.3 us -> 89.6 us (0.950)
  Pallas kernels: 19.4 us -> 15.8 us
  starting transfers between devices: 36.7 us -> 35.1 us
  waiting for transfers between devices: 35.4 us -> 36.9 us
    pallas_call x14 -> x13, Pallas kernels: 19.4 us -> 15.8 us  [call(): pl.pallas_call(kernel, out_shape=tuple(outs), in_specs=[pl.BlockSpec(memo...]
    ppermute x40, starting transfers between devices: 36.7 us -> 35.1 us  [exchange(): return lax.ppermute(value, AXES, pairs)]
    ppermute x40, waiting for transfers between devices: 35.4 us -> 36.9 us  [exchange(): return lax.ppermute(value, AXES, pairs)]
  transfers between devices with their start and end apart: 40 -> 40, of which waited for: 21 -> 22; matrix products, arithmetic and copies ran while one was open for 0% -> 0% of each run, Pallas kernels for 10% -> 6%
where the time goes in v3:
time: 89.6 us; the launch traced here: 89.4 us
  waiting for transfers between devices  36.9 us (41%)
  starting transfers between devices  35.1 us (39%)
  Pallas kernels  15.8 us (18%)
    ppermute x40, waiting for transfers between devices, exchange(): return lax.ppermute(value, AXES, pairs)  36.9 us
    ppermute x40, starting transfers between devices, exchange(): return lax.ppermute(value, AXES, pairs)  35.1 us
    pallas_call x13, Pallas kernels, call(): pl.pallas_call(kernel, out_shape=tuple(outs), in_specs=[pl.BlockSpec(memo...  15.8 us
  transfers between devices with their start and end apart: 40, of which 22 were waited for; matrix products, arithmetic and copies ran while one was open for 0% of the time, Pallas kernels for 6%

profile of v3, /device:TPU:0, one launch (start us, length us, event | category | flops | bytes accessed | tf_op | source)
XLA Modules:
  0.0 89.4 jit_solution(6875578052482488317)
XLA Ops:
  0.6 2.5 %shard_map.94 = (bf16[48,384]{1,0:T(8,128)(2,1)}, bf16[48,384]{1,0:T(8,128)(2,1)}, bf16[48,384]{1,0:T(8,128)(2,1)}, bf16[48,384]{1,0:T(8,128)(2,1)}, bf16[192,38...) custom-call(bf16[32,768]{1,0:T(8,128)(2,1)} %refs_0_.1, ...), custom_call_target="tpu_custom_call" | custom-call | bytes 1431552 | tf_op jit(solution)/shard_map/pallas_call | solution.py:76
  3.1 3.1 %collective-permute-start = (bf16[48,384]{1,0:T(8,128)(2,1)}, bf16[48,384]{1,0:T(8,128)(2,1)S(1)}, u32[]{:S(2)}, u32[]{:S(2)}) collective-permute-start(bf16[48,384]{1,0:T(8,128)(2,1)} %get-tuple-element.52), channel_id=1, source_target_pairs={{0,2},{1,3},{2,0},{3,1},{4,6},{5,7},{6,4},{7,5},{8,10},{9,11},{10,... | collective-permute-start | bytes 110600 | tf_op jit(solution)/shard_map/ppermute | solution.py:65
  6.2 2.6 %collective-permute-start.1 = (bf16[48,384]{1,0:T(8,128)(2,1)}, bf16[48,384]{1,0:T(8,128)(2,1)S(1)}, u32[]{:S(2)}, u32[]{:S(2)}) collective-permute-start(bf16[48,384]{1,0:T(8,128)(2,1)} %get-tuple-element.53), channel_id=1, source_target_pairs={{0,4},{1,5},{2,6},{3,7},{4,0},{5,1},{6,2},{7,3},{8,12},{9,13},{10,... | collective-permute-start | bytes 110600 | tf_op jit(solution)/shard_map/ppermute | solution.py:65
  8.8 3.1 %collective-permute-done.1.refs_2_ = bf16[48,384]{1,0:T(8,128)(2,1)S(1)} collective-permute-done((bf16[48,384]{1,0:T(8,128)(2,1)}, bf16[48,384]{1,0:T(8,128)(2,1)S(1)}, u32[]{:S(2)}, u32[]{:S(2)}) %collective-permute-start.1) | collective-permute-done | bytes 36896 | tf_op jit(solution)/shard_map/ppermute | solution.py:65
  12.0 2.8 %collective-permute-done.2.refs_3_ = bf16[48,384]{1,0:T(8,128)(2,1)S(1)} collective-permute-done((bf16[48,384]{1,0:T(8,128)(2,1)}, bf16[48,384]{1,0:T(8,128)(2,1)S(1)}, u32[]{:S(2)}, u32[]{:S(2)}) %collective-permute-start.2) | collective-permute-done | bytes 36896 | tf_op jit(solution)/shard_map/ppermute | solution.py:65
  14.8 0.8 copy-done.1
  15.8 1.6 %collective-permute-start.3 = (bf16[384,128]{1,0:T(8,128)(2,1)S(1)}, bf16[384,128]{1,0:T(8,128)(2,1)S(1)}, u32[]{:S(2)}, u32[]{:S(2)}) collective-permute-start(bf16[384,128]{1,0:T(8,128)(2,1)S(1)} %get-tuple-element.55.refs_0_), channel_id=1, source_target_pairs={{0,1},{1,0},{2,3},{3,2},{4,5},{5,4},{6,7},{7,6},{8,9},{9,8},{10,11... | collective-permute-start | bytes 294920 | tf_op jit(solution)/shard_map/ppermute | solution.py:65
  17.4 1.5 %collective-permute-start.6 = (bf16[384,128]{1,0:T(8,128)(2,1)S(1)}, bf16[384,128]{1,0:T(8,128)(2,1)S(1)}, u32[]{:S(2)}, u32[]{:S(2)}) collective-permute-start(bf16[384,128]{1,0:T(8,128)(2,1)S(1)} %get-tuple-element.55.refs_0_), channel_id=1, source_target_pairs={{0,16},{1,17},{2,18},{3,19},{4,20},{5,21},{6,22},{7,23},{8,24},{9,... | collective-permute-start | bytes 294920 | tf_op jit(solution)/shard_map/ppermute | solution.py:65
  18.8 0.5 collective-permute-start.7
  19.3 1.1 %collective-permute-done.3.refs_1_ = bf16[384,128]{1,0:T(8,128)(2,1)S(1)} collective-permute-done((bf16[384,128]{1,0:T(8,128)(2,1)S(1)}, bf16[384,128]{1,0:T(8,128)(2,1)S(1)}, u32[]{:S(2)}, u32[]{:S(2)}) %collective-permute-start.3) | collective-permute-done | bytes 98336 | tf_op jit(solution)/shard_map/ppermute | solution.py:65
  20.4 3.3 %collective-permute-start.12 = (bf16[192,384]{1,0:T(8,128)(2,1)}, bf16[192,384]{1,0:T(8,128)(2,1)S(1)}, u32[]{:S(2)}, u32[]{:S(2)}) collective-permute-start(bf16[192,384]{1,0:T(8,128)(2,1)} %get-tuple-element.59), channel_id=1, source_target_pairs={{0,6},{1,7},{2,4},{3,5},{4,2},{5,3},{6,0},{7,1},{8,14},{9,15},{10,... | collective-permute-start | bytes 442376 | tf_op jit(solution)/shard_map/ppermute | solution.py:65
  23.7 0.9 %collective-permute-done.7.refs_5_ = bf16[384,128]{1,0:T(8,128)(2,1)S(1)} collective-permute-done((bf16[384,128]{1,0:T(8,128)(2,1)S(1)}, bf16[384,128]{1,0:T(8,128)(2,1)S(1)}, u32[]{:S(2)}, u32[]{:S(2)}) %collective-permute-start.7) | collective-permute-done | bytes 98336 | tf_op jit(solution)/shard_map/ppermute | solution.py:65
  24.7 0.4 collective-permute-done.10.refs_9_
  25.2 0.4 shard_map.96.refs_13_.refs_12_
  25.6 8.1 %collective-permute-done.11.refs_10_ = bf16[192,384]{1,0:T(8,128)(2,1)S(1)} collective-permute-done((bf16[192,384]{1,0:T(8,128)(2,1)}, bf16[192,384]{1,0:T(8,128)(2,1)S(1)}, u32[]{:S(2)}, u32[]{:S(2)}) %collective-permute-start.11) | collective-permute-done | bytes 147488 | tf_op jit(solution)/shard_map/ppermute | solution.py:65
  33.8 2.4 %shard_map.97 = (f32[384,128]{1,0:T(8,128)S(1)}, f32[384,128]{1,0:T(8,128)S(1)}, f32[384,128]{1,0:T(8,128)S(1)}, f32[384,128]{1,0:T(8,128)S(1)}, f32[384,128]{1,...) custom-call(bf16[384,128]{1,0:T(8,128)(2,1)S(1)} %get-tuple-element.55.refs_0_, ...), custom_call_target="tpu_custom_call" | custom-call | flops 603979776 | bytes 3223552 | tf_op jit(solution)/shard_map/pallas_call | solution.py:76
  36.2 0.5 collective-permute-start.14
  36.8 0.4 collective-permute-start.16
  37.2 0.4 collective-permute-done.13.refs_4_
  38.6 1.6 %collective-permute-start.17 = (f32[384,128]{1,0:T(8,128)S(1)}, f32[384,128]{1,0:T(8,128)S(1)}, u32[]{:S(2)}, u32[]{:S(2)}) collective-permute-start(f32[384,128]{1,0:T(8,128)S(1)} %get-tuple-element.70), channel_id=1, source_target_pairs={{0,1},{1,0},{2,3},{3,2},{4,5},{5,4},{6,7},{7,6},{8,9},{9,8},{10,11... | collective-permute-start | bytes 589832 | tf_op jit(solution)/shard_map/ppermute | solution.py:65
  40.2 1.5 %collective-permute-start.18 = (f32[384,128]{1,0:T(8,128)S(1)}, f32[384,128]{1,0:T(8,128)S(1)}, u32[]{:S(2)}, u32[]{:S(2)}) collective-permute-start(f32[384,128]{1,0:T(8,128)S(1)} %get-tuple-element.71), channel_id=1, source_target_pairs={{0,16},{1,17},{2,18},{3,19},{4,20},{5,21},{6,22},{7,23},{8,24},{9,... | collective-permute-start | bytes 589832 | tf_op jit(solution)/shard_map/ppermute | solution.py:65
  41.7 0.5 collective-permute-start.19
  42.1 3.5 %collective-permute-done.17.refs_1_ = f32[384,128]{1,0:T(8,128)S(1)} collective-permute-done((f32[384,128]{1,0:T(8,128)S(1)}, f32[384,128]{1,0:T(8,128)S(1)}, u32[]{:S(2)}, u32[]{:S(2)}) %collective-permute-start.17) | collective-permute-done | bytes 196640 | tf_op jit(solution)/shard_map/ppermute | solution.py:65
  45.7 2.3 %collective-permute-done.18.refs_2_ = f32[384,128]{1,0:T(8,128)S(1)} collective-permute-done((f32[384,128]{1,0:T(8,128)S(1)}, f32[384,128]{1,0:T(8,128)S(1)}, u32[]{:S(2)}, u32[]{:S(2)}) %collective-permute-start.18) | collective-permute-done | bytes 196640 | tf_op jit(solution)/shard_map/ppermute | solution.py:65
  47.9 3.1 %collective-permute-done.19.refs_3_ = f32[384,128]{1,0:T(8,128)S(1)} collective-permute-done((f32[384,128]{1,0:T(8,128)S(1)}, f32[384,128]{1,0:T(8,128)S(1)}, u32[]{:S(2)}, u32[]{:S(2)}) %collective-permute-start.19) | collective-permute-done | bytes 196640 | tf_op jit(solution)/shard_map/ppermute | solution.py:65
  51.1 1.6 %collective-permute-start.20 = (bf16[208,128]{1,0:T(8,128)(2,1)S(1)}, bf16[208,128]{1,0:T(8,128)(2,1)S(1)}, u32[]{:S(2)}, u32[]{:S(2)}) collective-permute-start(bf16[208,128]{1,0:T(8,128)(2,1)S(1)} %shard_map.99.refs_13_), channel_id=1, source_target_pairs={{0,1},{1,0},{2,3},{3,2},{4,5},{5,4},{6,7},{7,6},{8,9},{9,8},{10,11... | collective-permute-start | bytes 159752 | tf_op jit(solution)/shard_map/ppermute | solution.py:65
  52.7 1.5 %collective-permute-start.23 = (bf16[208,128]{1,0:T(8,128)(2,1)S(1)}, bf16[208,128]{1,0:T(8,128)(2,1)S(1)}, u32[]{:S(2)}, u32[]{:S(2)}) collective-permute-start(bf16[208,128]{1,0:T(8,128)(2,1)S(1)} %shard_map.99.refs_13_), channel_id=1, source_target_pairs={{0,16},{1,17},{2,18},{3,19},{4,20},{5,21},{6,22},{7,23},{8,24},{9,... | collective-permute-start | bytes 159752 | tf_op jit(solution)/shard_map/ppermute | solution.py:65
  54.2 0.5 collective-permute-start.24
  54.7 0.6 collective-permute-done.20.refs_14_
  55.3 1.5 %collective-permute-done.23.refs_17_ = bf16[208,128]{1,0:T(8,128)(2,1)S(1)} collective-permute-done((bf16[208,128]{1,0:T(8,128)(2,1)S(1)}, bf16[208,128]{1,0:T(8,128)(2,1)S(1)}, u32[]{:S(2)}, u32[]{:S(2)}) %collective-permute-start.23) | collective-permute-done | bytes 53280 | tf_op jit(solution)/shard_map/ppermute | solution.py:65
  56.9 2.4 %collective-permute-done.24.refs_18_ = bf16[208,128]{1,0:T(8,128)(2,1)S(1)} collective-permute-done((bf16[208,128]{1,0:T(8,128)(2,1)S(1)}, bf16[208,128]{1,0:T(8,128)(2,1)S(1)}, u32[]{:S(2)}, u32[]{:S(2)}) %collective-permute-start.24) | collective-permute-done | bytes 53280 | tf_op jit(solution)/shard_map/ppermute | solution.py:65
  59.3 1.4 %shard_map.100 = (f32[64,512]{1,0:T(8,128)S(1)}, f32[64,1024]{1,0:T(8,128)S(1)}) custom-call(bf16[384,128]{1,0:T(8,128)(2,1)S(1)} %get-tuple-element.55.refs_0_, bf16[384,128]{1,0:T(8,128)(2,1)S(1)} %collective-permute-done.3.refs_1_, bf16[384,128]{1,0:T(8,128)(2,1)S(1)} %collective-permute-done.4.refs_2_, ...), custom_call_target="tpu_custom_call" | custom-call | flops 268435456 | bytes 2031616 | tf_op jit(solution)/shard_map/pallas_call | solution.py:76
  60.7 2.7 %shard_map.101 = (f32[128,512]{1,0:T(8,128)S(1)}, f32[128,1024]{1,0:T(8,128)S(1)}) custom-call(bf16[384,128]{1,0:T(8,128)(2,1)S(1)} %get-tuple-element.55.refs_0_, bf16[384,128]{1,0:T(8,128)(2,1)S(1)} %collective-permute-done.3.refs_1_, bf16[384,128]{1,0:T(8,128)(2,1)S(1)} %collective-permute-done.4.refs_2_, ...), custom_call_target="tpu_custom_call" | custom-call | flops 536870912 | bytes 2424832 | tf_op jit(solution)/shard_map/pallas_call | solution.py:76
  63.4 4.1 %shard_map.102 = (bf16[128,384]{1,0:T(8,128)(2,1)S(1)}, bf16[128,384]{1,0:T(8,128)(2,1)S(1)}, bf16[128,384]{1,0:T(8,128)(2,1)S(1)}, bf16[128,384]{1,0:T(8,128)(2...) custom-call(bf16[384,128]{1,0:T(8,128)(2,1)S(1)} %get-tuple-element., ...), custom_call_target="tpu_custom_call" | custom-call | flops 1006632960 | bytes 4173824 | tf_op jit(solution)/shard_map/pallas_call | solution.py:76
  67.5 0.6 collective-permute-start.30
  68.2 0.4 collective-permute-start.32
  69.1 0.4 collective-permute-done.31.refs_5_
  70.0 0.6 collective-permute-start.34
  70.5 0.6 collective-permute-start.35
  71.2 2.4 %collective-permute-start.36 = (f32[192,128]{1,0:T(8,128)S(1)}, f32[192,128]{1,0:T(8,128)S(1)}, u32[]{:S(2)}, u32[]{:S(2)}) collective-permute-start(f32[192,128]{1,0:T(8,128)S(1)} %get-tuple-element.94), channel_id=1, source_target_pairs={{0,17},{1,16},{2,19},{3,18},{4,21},{5,20},{6,23},{7,22},{8,25},{9,... | collective-permute-start | bytes 294920 | tf_op jit(solution)/shard_map/ppermute | solution.py:65
  73.5 2.4 %collective-permute-start.27 = (bf16[128,384]{1,0:T(8,128)(2,1)S(1)}, bf16[128,384]{1,0:T(8,128)(2,1)S(1)}, u32[]{:S(2)}, u32[]{:S(2)}) collective-permute-start(bf16[128,384]{1,0:T(8,128)(2,1)S(1)} %get-tuple-element.78), channel_id=1, source_target_pairs={{0,2},{1,3},{2,0},{3,1},{4,6},{5,7},{6,4},{7,5},{8,10},{9,11},{10,... | collective-permute-start | bytes 294920 | tf_op jit(solution)/shard_map/ppermute | solution.py:65
  76.0 2.4 %collective-permute-start.29 = (bf16[128,384]{1,0:T(8,128)(2,1)S(1)}, bf16[128,384]{1,0:T(8,128)(2,1)S(1)}, u32[]{:S(2)}, u32[]{:S(2)}) collective-permute-start(bf16[128,384]{1,0:T(8,128)(2,1)S(1)} %get-tuple-element.80), channel_id=1, source_target_pairs={{0,6},{1,7},{2,4},{3,5},{4,2},{5,3},{6,0},{7,1},{8,14},{9,15},{10,... | collective-permute-start | bytes 294920 | tf_op jit(solution)/shard_map/ppermute | solution.py:65
  78.5 2.3 %collective-permute-start.37 = (f32[48,128]{1,0:T(8,128)S(1)}, f32[48,128]{1,0:T(8,128)S(1)}, u32[]{:S(2)}, u32[]{:S(2)}) collective-permute-start(f32[48,128]{1,0:T(8,128)S(1)} %get-tuple-element.96), channel_id=1, source_target_pairs={{0,2},{1,3},{2,0},{3,1},{4,6},{5,7},{6,4},{7,5},{8,10},{9,11},{10,... | collective-permute-start | bytes 73736 | tf_op jit(solution)/shard_map/ppermute | solution.py:65
  80.9 2.4 %collective-permute-start.39 = (f32[48,128]{1,0:T(8,128)S(1)}, f32[48,128]{1,0:T(8,128)S(1)}, u32[]{:S(2)}, u32[]{:S(2)}) collective-permute-start(f32[48,128]{1,0:T(8,128)S(1)} %get-tuple-element.98), channel_id=1, source_target_pairs={{0,6},{1,7},{2,4},{3,5},{4,2},{5,3},{6,0},{7,1},{8,14},{9,15},{10,... | collective-permute-start | bytes 73736 | tf_op jit(solution)/shard_map/ppermute | solution.py:65
  83.3 2.9 %collective-permute-done.28.refs_2_ = bf16[128,384]{1,0:T(8,128)(2,1)S(1)} collective-permute-done((bf16[128,384]{1,0:T(8,128)(2,1)S(1)}, bf16[128,384]{1,0:T(8,128)(2,1)S(1)}, u32[]{:S(2)}, u32[]{:S(2)}) %collective-permute-start.28) | collective-permute-done | bytes 98336 | tf_op jit(solution)/shard_map/ppermute | solution.py:65
  86.2 0.9 %shard_map.103 = (bf16[128,768]{1,0:T(8,128)(2,1)}, bf16[128,768]{1,0:T(8,128)(2,1)}) custom-call(bf16[128,384]{1,0:T(8,128)(2,1)S(1)} %get-tuple-element.77.refs_0_, bf16[128,384]{1,0:T(8,128)(2,1)S(1)} %collective-permute-done.27.refs_1_, bf16[128,384]{1,0:T(8,128)(2,1)S(1)} %collective-permute-done.28.refs_2_, ...), custom_call_target="tpu_custom_call" | custom-call | bytes 786432 | tf_op jit(solution)/shard_map/pallas_call | solution.py:76
  87.1 1.5 %collective-permute-done.38.refs_2_ = f32[48,128]{1,0:T(8,128)S(1)} collective-permute-done((f32[48,128]{1,0:T(8,128)S(1)}, f32[48,128]{1,0:T(8,128)S(1)}, u32[]{:S(2)}, u32[]{:S(2)}) %collective-permute-start.38) | collective-permute-done | bytes 24608 | tf_op jit(solution)/shard_map/ppermute | solution.py:65
  88.6 0.8 shard_map.106
  (51 shorter events, 2.8 us)
Async XLA Ops:
  3.1 5.7 %collective-permute-start = (bf16[48,384]{1,0:T(8,128)(2,1)}, bf16[48,384]{1,0:T(8,128)(2,1)S(1)}, u32[]{:S(2)}, u32[]{:S(2)}) collective-permute-start(bf16[48,384]{1,0:T(8,128)(2,1)} %get-tuple-element.52), channel_id=1, source_target_pairs={{0,2},{1,3},{2,0},{3,1},{4,6},{5,7},{6,4},{7,5},{8,10},{9,11},{10,... | collective-permute-start | bytes 110600 | tf_op jit(solution)/shard_map/ppermute | solution.py:65
  6.2 5.7 %collective-permute-start.1 = (bf16[48,384]{1,0:T(8,128)(2,1)}, bf16[48,384]{1,0:T(8,128)(2,1)S(1)}, u32[]{:S(2)}, u32[]{:S(2)}) collective-permute-start(bf16[48,384]{1,0:T(8,128)(2,1)} %get-tuple-element.53), channel_id=1, source_target_pairs={{0,4},{1,5},{2,6},{3,7},{4,0},{5,1},{6,2},{7,3},{8,12},{9,13},{10,... | collective-permute-start | bytes 110600 | tf_op jit(solution)/shard_map/ppermute | solution.py:65
  8.8 6.0 %collective-permute-start.2 = (bf16[48,384]{1,0:T(8,128)(2,1)}, bf16[48,384]{1,0:T(8,128)(2,1)S(1)}, u32[]{:S(2)}, u32[]{:S(2)}) collective-permute-start(bf16[48,384]{1,0:T(8,128)(2,1)} %get-tuple-element.54), channel_id=1, source_target_pairs={{0,6},{1,7},{2,4},{3,5},{4,2},{5,3},{6,0},{7,1},{8,14},{9,15},{10,... | collective-permute-start | bytes 110600 | tf_op jit(solution)/shard_map/ppermute | solution.py:65
  14.8 0.8 copy-start.1
  15.6 9.6 %copy-start = (f32[12,1024]{1,0:T(8,128)S(1)}, f32[12,1024]{1,0:T(8,128)}, u32[]{:S(2)}) copy-start(f32[12,1024]{1,0:T(8,128)} %n_ref.1) | copy-start | bytes 147460
  15.6 18.2 %copy-start.2 = (bf16[192,384]{1,0:T(8,128)(2,1)S(1)}, bf16[192,384]{1,0:T(8,128)(2,1)}, u32[]{:S(2)}) copy-start(bf16[192,384]{1,0:T(8,128)(2,1)} %get-tuple-element.56.refs_8_) | copy-start | bytes 442372
  15.8 4.7 %collective-permute-start.3 = (bf16[384,128]{1,0:T(8,128)(2,1)S(1)}, bf16[384,128]{1,0:T(8,128)(2,1)S(1)}, u32[]{:S(2)}, u32[]{:S(2)}) collective-permute-start(bf16[384,128]{1,0:T(8,128)(2,1)S(1)} %get-tuple-element.55.refs_0_), channel_id=1, source_target_pairs={{0,1},{1,0},{2,3},{3,2},{4,5},{5,4},{6,7},{7,6},{8,9},{9,8},{10,11... | collective-permute-start | bytes 294920 | tf_op jit(solution)/shard_map/ppermute | solution.py:65
  17.3 3.1 %collective-permute-start.4 = (bf16[384,128]{1,0:T(8,128)(2,1)S(1)}, bf16[384,128]{1,0:T(8,128)(2,1)S(1)}, u32[]{:S(2)}, u32[]{:S(2)}) collective-permute-start(bf16[384,128]{1,0:T(8,128)(2,1)S(1)} %get-tuple-element.55.refs_0_), channel_id=1, source_target_pairs={{0,8},{1,9},{2,10},{3,11},{4,12},{5,13},{6,14},{7,15},{8,0},{9,1},... | collective-permute-start | bytes 294920 | tf_op jit(solution)/shard_map/ppermute | solution.py:65
  17.3 7.7 %collective-permute-start.10 = (bf16[192,384]{1,0:T(8,128)(2,1)}, bf16[192,384]{1,0:T(8,128)(2,1)S(1)}, u32[]{:S(2)}, u32[]{:S(2)}) collective-permute-start(bf16[192,384]{1,0:T(8,128)(2,1)} %get-tuple-element.57), channel_id=1, source_target_pairs={{0,2},{1,3},{2,0},{3,1},{4,6},{5,7},{6,4},{7,5},{8,10},{9,11},{10,... | collective-permute-start | bytes 442376 | tf_op jit(solution)/shard_map/ppermute | solution.py:65
  17.4 6.4 %collective-permute-start.6 = (bf16[384,128]{1,0:T(8,128)(2,1)S(1)}, bf16[384,128]{1,0:T(8,128)(2,1)S(1)}, u32[]{:S(2)}, u32[]{:S(2)}) collective-permute-start(bf16[384,128]{1,0:T(8,128)(2,1)S(1)} %get-tuple-element.55.refs_0_), channel_id=1, source_target_pairs={{0,16},{1,17},{2,18},{3,19},{4,20},{5,21},{6,22},{7,23},{8,24},{9,... | collective-permute-start | bytes 294920 | tf_op jit(solution)/shard_map/ppermute | solution.py:65
  18.8 5.8 %collective-permute-start.7 = (bf16[384,128]{1,0:T(8,128)(2,1)S(1)}, bf16[384,128]{1,0:T(8,128)(2,1)S(1)}, u32[]{:S(2)}, u32[]{:S(2)}) collective-permute-start(bf16[384,128]{1,0:T(8,128)(2,1)S(1)} %get-tuple-element.55.refs_0_), channel_id=1, source_target_pairs={{0,17},{1,16},{2,19},{3,18},{4,21},{5,20},{6,23},{7,22},{8,25},{9,... | collective-permute-start | bytes 294920 | tf_op jit(solution)/shard_map/ppermute | solution.py:65
  20.4 13.3 %collective-permute-start.11 = (bf16[192,384]{1,0:T(8,128)(2,1)}, bf16[192,384]{1,0:T(8,128)(2,1)S(1)}, u32[]{:S(2)}, u32[]{:S(2)}) collective-permute-start(bf16[192,384]{1,0:T(8,128)(2,1)} %get-tuple-element.58), channel_id=1, source_target_pairs={{0,4},{1,5},{2,6},{3,7},{4,0},{5,1},{6,2},{7,3},{8,12},{9,13},{10,... | collective-permute-start | bytes 442376 | tf_op jit(solution)/shard_map/ppermute | solution.py:65
  20.4 13.3 %collective-permute-start.12 = (bf16[192,384]{1,0:T(8,128)(2,1)}, bf16[192,384]{1,0:T(8,128)(2,1)S(1)}, u32[]{:S(2)}, u32[]{:S(2)}) collective-permute-start(bf16[192,384]{1,0:T(8,128)(2,1)} %get-tuple-element.59), channel_id=1, source_target_pairs={{0,6},{1,7},{2,4},{3,5},{4,2},{5,3},{6,0},{7,1},{8,14},{9,15},{10,... | collective-permute-start | bytes 442376 | tf_op jit(solution)/shard_map/ppermute | solution.py:65
  23.7 10.0 %collective-permute-start.5 = (bf16[384,128]{1,0:T(8,128)(2,1)S(1)}, bf16[384,128]{1,0:T(8,128)(2,1)S(1)}, u32[]{:S(2)}, u32[]{:S(2)}) collective-permute-start(bf16[384,128]{1,0:T(8,128)(2,1)S(1)} %collective-permute-done.3.refs_1_), channel_id=1, source_target_pairs={{0,8},{1,9},{2,10},{3,11},{4,12},{5,13},{6,14},{7,15},{8,0},{9,1},... | collective-permute-start | bytes 294920 | tf_op jit(solution)/shard_map/ppermute | solution.py:65
  24.7 9.1 %collective-permute-start.8 = (bf16[384,128]{1,0:T(8,128)(2,1)S(1)}, bf16[384,128]{1,0:T(8,128)(2,1)S(1)}, u32[]{:S(2)}, u32[]{:S(2)}) collective-permute-start(bf16[384,128]{1,0:T(8,128)(2,1)S(1)} %collective-permute-done.6.refs_4_), channel_id=1, source_target_pairs={{0,8},{1,9},{2,10},{3,11},{4,12},{5,13},{6,14},{7,15},{8,0},{9,1},... | collective-permute-start | bytes 294920 | tf_op jit(solution)/shard_map/ppermute | solution.py:65
  25.1 8.7 %collective-permute-start.9 = (bf16[384,128]{1,0:T(8,128)(2,1)S(1)}, bf16[384,128]{1,0:T(8,128)(2,1)S(1)}, u32[]{:S(2)}, u32[]{:S(2)}) collective-permute-start(bf16[384,128]{1,0:T(8,128)(2,1)S(1)} %collective-permute-done.7.refs_5_), channel_id=1, source_target_pairs={{0,8},{1,9},{2,10},{3,11},{4,12},{5,13},{6,14},{7,15},{8,0},{9,1},... | collective-permute-start | bytes 294920 | tf_op jit(solution)/shard_map/ppermute | solution.py:65
  36.2 1.5 %collective-permute-start.13 = (f32[384,128]{1,0:T(8,128)S(1)}, f32[384,128]{1,0:T(8,128)S(1)}, u32[]{:S(2)}, u32[]{:S(2)}) collective-permute-start(f32[384,128]{1,0:T(8,128)S(1)} %get-tuple-element.65), channel_id=1, source_target_pairs={{0,8},{1,9},{2,10},{3,11},{4,12},{5,13},{6,14},{7,15},{8,0},{9,1},... | collective-permute-start | bytes 589832 | tf_op jit(solution)/shard_map/ppermute | solution.py:65
  36.2 1.7 %collective-permute-start.14 = (f32[384,128]{1,0:T(8,128)S(1)}, f32[384,128]{1,0:T(8,128)S(1)}, u32[]{:S(2)}, u32[]{:S(2)}) collective-permute-start(f32[384,128]{1,0:T(8,128)S(1)} %get-tuple-element.66), channel_id=1, source_target_pairs={{0,8},{1,9},{2,10},{3,11},{4,12},{5,13},{6,14},{7,15},{8,0},{9,1},... | collective-permute-start | bytes 589832 | tf_op jit(solution)/shard_map/ppermute | solution.py:65
  36.7 1.5 %collective-permute-start.15 = (f32[384,128]{1,0:T(8,128)S(1)}, f32[384,128]{1,0:T(8,128)S(1)}, u32[]{:S(2)}, u32[]{:S(2)}) collective-permute-start(f32[384,128]{1,0:T(8,128)S(1)} %get-tuple-element.67), channel_id=1, source_target_pairs={{0,8},{1,9},{2,10},{3,11},{4,12},{5,13},{6,14},{7,15},{8,0},{9,1},... | collective-permute-start | bytes 589832 | tf_op jit(solution)/shard_map/ppermute | solution.py:65
  36.8 1.7 %collective-permute-start.16 = (f32[384,128]{1,0:T(8,128)S(1)}, f32[384,128]{1,0:T(8,128)S(1)}, u32[]{:S(2)}, u32[]{:S(2)}) collective-permute-start(f32[384,128]{1,0:T(8,128)S(1)} %get-tuple-element.68), channel_id=1, source_target_pairs={{0,8},{1,9},{2,10},{3,11},{4,12},{5,13},{6,14},{7,15},{8,0},{9,1},... | collective-permute-start | bytes 589832 | tf_op jit(solution)/shard_map/ppermute | solution.py:65
  38.6 7.1 %collective-permute-start.17 = (f32[384,128]{1,0:T(8,128)S(1)}, f32[384,128]{1,0:T(8,128)S(1)}, u32[]{:S(2)}, u32[]{:S(2)}) collective-permute-start(f32[384,128]{1,0:T(8,128)S(1)} %get-tuple-element.70), channel_id=1, source_target_pairs={{0,1},{1,0},{2,3},{3,2},{4,5},{5,4},{6,7},{7,6},{8,9},{9,8},{10,11... | collective-permute-start | bytes 589832 | tf_op jit(solution)/shard_map/ppermute | solution.py:65
  40.2 7.8 %collective-permute-start.18 = (f32[384,128]{1,0:T(8,128)S(1)}, f32[384,128]{1,0:T(8,128)S(1)}, u32[]{:S(2)}, u32[]{:S(2)}) collective-permute-start(f32[384,128]{1,0:T(8,128)S(1)} %get-tuple-element.71), channel_id=1, source_target_pairs={{0,16},{1,17},{2,18},{3,19},{4,20},{5,21},{6,22},{7,23},{8,24},{9,... | collective-permute-start | bytes 589832 | tf_op jit(solution)/shard_map/ppermute | solution.py:65
  41.7 9.4 %collective-permute-start.19 = (f32[384,128]{1,0:T(8,128)S(1)}, f32[384,128]{1,0:T(8,128)S(1)}, u32[]{:S(2)}, u32[]{:S(2)}) collective-permute-start(f32[384,128]{1,0:T(8,128)S(1)} %get-tuple-element.72), channel_id=1, source_target_pairs={{0,17},{1,16},{2,19},{3,18},{4,21},{5,20},{6,23},{7,22},{8,25},{9,... | collective-permute-start | bytes 589832 | tf_op jit(solution)/shard_map/ppermute | solution.py:65
  51.1 4.2 %collective-permute-start.20 = (bf16[208,128]{1,0:T(8,128)(2,1)S(1)}, bf16[208,128]{1,0:T(8,128)(2,1)S(1)}, u32[]{:S(2)}, u32[]{:S(2)}) collective-permute-start(bf16[208,128]{1,0:T(8,128)(2,1)S(1)} %shard_map.99.refs_13_), channel_id=1, source_target_pairs={{0,1},{1,0},{2,3},{3,2},{4,5},{5,4},{6,7},{7,6},{8,9},{9,8},{10,11... | collective-permute-start | bytes 159752 | tf_op jit(solution)/shard_map/ppermute | solution.py:65
  52.7 4.1 %collective-permute-start.23 = (bf16[208,128]{1,0:T(8,128)(2,1)S(1)}, bf16[208,128]{1,0:T(8,128)(2,1)S(1)}, u32[]{:S(2)}, u32[]{:S(2)}) collective-permute-start(bf16[208,128]{1,0:T(8,128)(2,1)S(1)} %shard_map.99.refs_13_), channel_id=1, source_target_pairs={{0,16},{1,17},{2,18},{3,19},{4,20},{5,21},{6,22},{7,23},{8,24},{9,... | collective-permute-start | bytes 159752 | tf_op jit(solution)/shard_map/ppermute | solution.py:65
  54.2 5.0 %collective-permute-start.24 = (bf16[208,128]{1,0:T(8,128)(2,1)S(1)}, bf16[208,128]{1,0:T(8,128)(2,1)S(1)}, u32[]{:S(2)}, u32[]{:S(2)}) collective-permute-start(bf16[208,128]{1,0:T(8,128)(2,1)S(1)} %shard_map.99.refs_13_), channel_id=1, source_target_pairs={{0,17},{1,16},{2,19},{3,18},{4,21},{5,20},{6,23},{7,22},{8,25},{9,... | collective-permute-start | bytes 159752 | tf_op jit(solution)/shard_map/ppermute | solution.py:65
  54.7 8.7 %collective-permute-start.21 = (bf16[208,128]{1,0:T(8,128)(2,1)S(1)}, bf16[208,128]{1,0:T(8,128)(2,1)S(1)}, u32[]{:S(2)}, u32[]{:S(2)}) collective-permute-start(bf16[208,128]{1,0:T(8,128)(2,1)S(1)} %shard_map.99.refs_13_), channel_id=1, source_target_pairs={{0,8},{1,9},{2,10},{3,11},{4,12},{5,13},{6,14},{7,15},{8,0},{9,1},... | collective-permute-start | bytes 159752 | tf_op jit(solution)/shard_map/ppermute | solution.py:65
  55.3 8.0 %collective-permute-start.22 = (bf16[208,128]{1,0:T(8,128)(2,1)S(1)}, bf16[208,128]{1,0:T(8,128)(2,1)S(1)}, u32[]{:S(2)}, u32[]{:S(2)}) collective-permute-start(bf16[208,128]{1,0:T(8,128)(2,1)S(1)} %collective-permute-done.20.refs_14_), channel_id=1, source_target_pairs={{0,8},{1,9},{2,10},{3,11},{4,12},{5,13},{6,14},{7,15},{8,0},{9,1},... | collective-permute-start | bytes 159752 | tf_op jit(solution)/shard_map/ppermute | solution.py:65
  56.9 6.5 %collective-permute-start.25 = (bf16[208,128]{1,0:T(8,128)(2,1)S(1)}, bf16[208,128]{1,0:T(8,128)(2,1)S(1)}, u32[]{:S(2)}, u32[]{:S(2)}) collective-permute-start(bf16[208,128]{1,0:T(8,128)(2,1)S(1)} %collective-permute-done.23.refs_17_), channel_id=1, source_target_pairs={{0,8},{1,9},{2,10},{3,11},{4,12},{5,13},{6,14},{7,15},{8,0},{9,1},... | collective-permute-start | bytes 159752 | tf_op jit(solution)/shard_map/ppermute | solution.py:65
  59.2 4.2 %collective-permute-start.26 = (bf16[208,128]{1,0:T(8,128)(2,1)S(1)}, bf16[208,128]{1,0:T(8,128)(2,1)S(1)}, u32[]{:S(2)}, u32[]{:S(2)}) collective-permute-start(bf16[208,128]{1,0:T(8,128)(2,1)S(1)} %collective-permute-done.24.refs_18_), channel_id=1, source_target_pairs={{0,8},{1,9},{2,10},{3,11},{4,12},{5,13},{6,14},{7,15},{8,0},{9,1},... | collective-permute-start | bytes 159752 | tf_op jit(solution)/shard_map/ppermute | solution.py:65
  67.5 1.5 %collective-permute-start.30 = (f32[192,128]{1,0:T(8,128)S(1)}, f32[192,128]{1,0:T(8,128)S(1)}, u32[]{:S(2)}, u32[]{:S(2)}) collective-permute-start(f32[192,128]{1,0:T(8,128)S(1)} %get-tuple-element.87), channel_id=1, source_target_pairs={{0,8},{1,9},{2,10},{3,11},{4,12},{5,13},{6,14},{7,15},{8,0},{9,1},... | collective-permute-start | bytes 294920 | tf_op jit(solution)/shard_map/ppermute | solution.py:65
  68.1 1.3 %collective-permute-start.31 = (f32[192,128]{1,0:T(8,128)S(1)}, f32[192,128]{1,0:T(8,128)S(1)}, u32[]{:S(2)}, u32[]{:S(2)}) collective-permute-start(f32[192,128]{1,0:T(8,128)S(1)} %get-tuple-element.88), channel_id=1, source_target_pairs={{0,8},{1,9},{2,10},{3,11},{4,12},{5,13},{6,14},{7,15},{8,0},{9,1},... | collective-permute-start | bytes 294920 | tf_op jit(solution)/shard_map/ppermute | solution.py:65
  68.2 1.4 %collective-permute-start.32 = (f32[192,128]{1,0:T(8,128)S(1)}, f32[192,128]{1,0:T(8,128)S(1)}, u32[]{:S(2)}, u32[]{:S(2)}) collective-permute-start(f32[192,128]{1,0:T(8,128)S(1)} %get-tuple-element.89), channel_id=1, source_target_pairs={{0,8},{1,9},{2,10},{3,11},{4,12},{5,13},{6,14},{7,15},{8,0},{9,1},... | collective-permute-start | bytes 294920 | tf_op jit(solution)/shard_map/ppermute | solution.py:65
  68.6 1.3 %collective-permute-start.33 = (f32[192,128]{1,0:T(8,128)S(1)}, f32[192,128]{1,0:T(8,128)S(1)}, u32[]{:S(2)}, u32[]{:S(2)}) collective-permute-start(f32[192,128]{1,0:T(8,128)S(1)} %get-tuple-element.90), channel_id=1, source_target_pairs={{0,8},{1,9},{2,10},{3,11},{4,12},{5,13},{6,14},{7,15},{8,0},{9,1},... | collective-permute-start | bytes 294920 | tf_op jit(solution)/shard_map/ppermute | solution.py:65
  70.0 6.0 %collective-permute-start.34 = (f32[192,128]{1,0:T(8,128)S(1)}, f32[192,128]{1,0:T(8,128)S(1)}, u32[]{:S(2)}, u32[]{:S(2)}) collective-permute-start(f32[192,128]{1,0:T(8,128)S(1)} %get-tuple-element.92), channel_id=1, source_target_pairs={{0,1},{1,0},{2,3},{3,2},{4,5},{5,4},{6,7},{7,6},{8,9},{9,8},{10,11... | collective-permute-start | bytes 294920 | tf_op jit(solution)/shard_map/ppermute | solution.py:65
  70.5 7.8 %collective-permute-start.35 = (f32[192,128]{1,0:T(8,128)S(1)}, f32[192,128]{1,0:T(8,128)S(1)}, u32[]{:S(2)}, u32[]{:S(2)}) collective-permute-start(f32[192,128]{1,0:T(8,128)S(1)} %get-tuple-element.93), channel_id=1, source_target_pairs={{0,16},{1,17},{2,18},{3,19},{4,20},{5,21},{6,22},{7,23},{8,24},{9,... | collective-permute-start | bytes 294920 | tf_op jit(solution)/shard_map/ppermute | solution.py:65
  71.2 7.2 %collective-permute-start.36 = (f32[192,128]{1,0:T(8,128)S(1)}, f32[192,128]{1,0:T(8,128)S(1)}, u32[]{:S(2)}, u32[]{:S(2)}) collective-permute-start(f32[192,128]{1,0:T(8,128)S(1)} %get-tuple-element.94), channel_id=1, source_target_pairs={{0,17},{1,16},{2,19},{3,18},{4,21},{5,20},{6,23},{7,22},{8,25},{9,... | collective-permute-start | bytes 294920 | tf_op jit(solution)/shard_map/ppermute | solution.py:65
  73.5 7.4 %collective-permute-start.27 = (bf16[128,384]{1,0:T(8,128)(2,1)S(1)}, bf16[128,384]{1,0:T(8,128)(2,1)S(1)}, u32[]{:S(2)}, u32[]{:S(2)}) collective-permute-start(bf16[128,384]{1,0:T(8,128)(2,1)S(1)} %get-tuple-element.78), channel_id=1, source_target_pairs={{0,2},{1,3},{2,0},{3,1},{4,6},{5,7},{6,4},{7,5},{8,10},{9,11},{10,... | collective-permute-start | bytes 294920 | tf_op jit(solution)/shard_map/ppermute | solution.py:65
  76.0 10.2 %collective-permute-start.28 = (bf16[128,384]{1,0:T(8,128)(2,1)S(1)}, bf16[128,384]{1,0:T(8,128)(2,1)S(1)}, u32[]{:S(2)}, u32[]{:S(2)}) collective-permute-start(bf16[128,384]{1,0:T(8,128)(2,1)S(1)} %get-tuple-element.79), channel_id=1, source_target_pairs={{0,4},{1,5},{2,6},{3,7},{4,0},{5,1},{6,2},{7,3},{8,12},{9,13},{10,... | collective-permute-start | bytes 294920 | tf_op jit(solution)/shard_map/ppermute | solution.py:65
  76.0 10.2 %collective-permute-start.29 = (bf16[128,384]{1,0:T(8,128)(2,1)S(1)}, bf16[128,384]{1,0:T(8,128)(2,1)S(1)}, u32[]{:S(2)}, u32[]{:S(2)}) collective-permute-start(bf16[128,384]{1,0:T(8,128)(2,1)S(1)} %get-tuple-element.80), channel_id=1, source_target_pairs={{0,6},{1,7},{2,4},{3,5},{4,2},{5,3},{6,0},{7,1},{8,14},{9,15},{10,... | collective-permute-start | bytes 294920 | tf_op jit(solution)/shard_map/ppermute | solution.py:65
  78.5 8.6 %collective-permute-start.37 = (f32[48,128]{1,0:T(8,128)S(1)}, f32[48,128]{1,0:T(8,128)S(1)}, u32[]{:S(2)}, u32[]{:S(2)}) collective-permute-start(f32[48,128]{1,0:T(8,128)S(1)} %get-tuple-element.96), channel_id=1, source_target_pairs={{0,2},{1,3},{2,0},{3,1},{4,6},{5,7},{6,4},{7,5},{8,10},{9,11},{10,... | collective-permute-start | bytes 73736 | tf_op jit(solution)/shard_map/ppermute | solution.py:65
  80.8 7.8 %collective-permute-start.38 = (f32[48,128]{1,0:T(8,128)S(1)}, f32[48,128]{1,0:T(8,128)S(1)}, u32[]{:S(2)}, u32[]{:S(2)}) collective-permute-start(f32[48,128]{1,0:T(8,128)S(1)} %get-tuple-element.97), channel_id=1, source_target_pairs={{0,4},{1,5},{2,6},{3,7},{4,0},{5,1},{6,2},{7,3},{8,12},{9,13},{10,... | collective-permute-start | bytes 73736 | tf_op jit(solution)/shard_map/ppermute | solution.py:65
  80.9 7.7 %collective-permute-start.39 = (f32[48,128]{1,0:T(8,128)S(1)}, f32[48,128]{1,0:T(8,128)S(1)}, u32[]{:S(2)}, u32[]{:S(2)}) collective-permute-start(f32[48,128]{1,0:T(8,128)S(1)} %get-tuple-element.98), channel_id=1, source_target_pairs={{0,6},{1,7},{2,4},{3,5},{4,2},{5,3},{6,0},{7,1},{8,14},{9,15},{10,... | collective-permute-start | bytes 73736 | tf_op jit(solution)/shard_map/ppermute | solution.py:65

commit v4 on v3

--- a/solution.py
+++ b/solution.py
@@ -13,6 +13,7 @@
 LANES = 128
 AXES = ("pa", "pb")
 MOST_IN_PLANE = 16
+HALF_SIZE, SMALLEST = 14.0, 2.0**-100
 LAG, SLOTS = 1, 3
 GROUPS = 4
 VMEM_BYTES = 20 * 2**20
@@ -306,14 +307,48 @@
     return call(kernel, outs, (*lats, *pts, dec_norm), scratch, flops)
 
 
+def add_and_scale(plan, mine, theirs):
+    tall = mine[0].shape[0]
+
+    def kernel(*refs):
+        n = len(mine)
+        for k, (a, b, out) in enumerate(zip(refs[:n], refs[n : 2 * n], refs[2 * n :], strict=True)):
+            total = a[...] + b[...]
+            if k == 0:
+                out[...] = total
+                continue
+            sizes = []
+            for at in range(0, tall, HEAD_DIM):
+                part = total[at : at + HEAD_DIM]
+                most = jnp.max(jnp.abs(part), axis=0, keepdims=True)
+                size = jnp.ceil(jnp.log2(jnp.maximum(most, SMALLEST)))
+                out[at : at + HEAD_DIM, :] = part * jnp.exp2(HALF_SIZE - size)
+                sizes.append(size)
+            fill = jnp.zeros((16 - len(sizes), plan.block), jnp.float32)
+            out[tall:, :] = jnp.concatenate([*sizes, fill], axis=0)
+
+    outs = [shaped((tall + 16 * (k > 0), plan.block), jnp.float32) for k in range(len(mine))]
+    return call(kernel, outs, (*mine, *theirs))
+
+
+def scaled_sum(own, *scaled):
+    tall = own.shape[0]
+    pieces = []
+    for n, at in enumerate(range(0, tall, HEAD_DIM)):
+        piece = own[at : at + HEAD_DIM, :]
+        for ref in scaled:
+            size = ref[tall + n : tall + n + 1, :]
+            piece = piece + ref[at : at + HEAD_DIM, :] * jnp.exp2(size - HALF_SIZE)
+        pieces.append(piece)
+    return jnp.concatenate(pieces, axis=0)
+
+
 def reduce_mix(plan, parts):
     c, hs = plan.cols, plan.heads
 
     def kernel(*refs):
         *ins, out = refs
-        total = ins[0][...]
-        for ref in ins[1:]:
-            total = total + ref[...]
+        total = scaled_sum(*ins)
         half = total[:c].astype(jnp.bfloat16)
         out[:c, :] = half
         product = half.astype(jnp.float32) * total[c:]
@@ -415,23 +450,10 @@
     return got[:n_pts], got[n_pts:]
 
 
-def add_pairs(mine, theirs):
-    def kernel(*refs):
-        n = len(mine)
-        for a, b, out in zip(refs[:n], refs[n : 2 * n], refs[2 * n :], strict=True):
-            out[...] = a[...] + b[...]
-
-    outs = [shaped(a.shape, a.dtype) for a in mine]
-    return call(kernel, outs, (*mine, *theirs))
-
-
 def reduce_latents(plan, parts):
     def kernel(*refs):
         ins, outs = refs[: len(parts)], refs[len(parts) :]
-        total = ins[0][...]
-        for ref in ins[1:]:
-            total = total + ref[...]
-        total = total.T
+        total = scaled_sum(*ins).T
         for j, out in enumerate(outs):
             rows = total[j * plan.lat_rows : (j + 1) * plan.lat_rows]
             n, half = plan.lat_rows, plan.lat_rows // 2
@@ -489,7 +511,11 @@
     def sum_cores(blocks):
         near = chip_steps()
         theirs = [plan.exchange(blocks[k | plan.fast], False, plan.fast) for k in near]
-        return add_pairs([blocks[k] for k in near], theirs)
+        return add_and_scale(plan, [blocks[k] for k in near], theirs)
+
+    def sum_chips(blocks):
+        halves = [blocks[0], *(block.astype(jnp.float16) for block in blocks[1:])]
+        return [block.astype(jnp.float32) for block in from_chips(halves)]
 
     def to_plane(block):
         got = dict(zip(chip_steps(), from_chips([block] * len(chip_steps())), strict=True))
@@ -508,11 +534,11 @@
     cores = sum_cores(first_pass(plan, lats, pts, dec_norm, norm))
     early, late = tuple(range(plan.heads))[:1], tuple(range(plan.heads))[1:]
     before = [(early, decoder_pass(plan, lats, pts, dec_norm, early))]
-    sums = from_chips(cores)
+    sums = sum_chips(cores)
     before.append((late, decoder_pass(plan, lats, pts, dec_norm, late)))
     mixes = to_plane(reduce_mix(plan, sums))
     pts_out, lat_out = encoder_pass(plan, lats, pts, norm, mixes, before)
-    lat_out = from_chips(sum_cores(lat_out))
+    lat_out = sum_chips(sum_cores(lat_out))
     pts_out = over_group(pts_out)
     lat_rows = over_group(reduce_latents(plan, lat_out))
     keys_grad, values_grad = place_points(plan, pts_out)

time: 89.6 us -> 86.5 us (0.965)
  waiting for transfers between devices: 36.9 us -> 33.5 us
    ppermute x40, waiting for transfers between devices: 36.9 us -> 33.5 us  [exchange(): return lax.ppermute(value, AXES, pairs)]
  transfers between devices with their start and end apart: 40 -> 40, of which waited for: 22 -> 24; matrix products, arithmetic and copies ran while one was open for 0% -> 0% of each run, Pallas kernels for 6% -> 7%
where the time goes in v4:
time: 86.5 us; the launch traced here: 86.3 us
  starting transfers between devices  35.1 us (41%)
  waiting for transfers between devices  33.5 us (39%)
  Pallas kernels  15.9 us (18%)
    ppermute x40, starting transfers between devices, exchange(): return lax.ppermute(value, AXES, pairs)  35.1 us
    ppermute x40, waiting for transfers between devices, exchange(): return lax.ppermute(value, AXES, pairs)  33.5 us
    pallas_call x13, Pallas kernels, call(): pl.pallas_call(kernel, out_shape=tuple(outs), in_specs=[pl.BlockSpec(memo...  15.9 us
  transfers between devices with their start and end apart: 40, of which 24 were waited for; matrix products, arithmetic and copies ran while one was open for 0% of the time, Pallas kernels for 7%

profile of v4, /device:TPU:0, one launch (start us, length us, event | category | flops | bytes accessed | tf_op | source)
XLA Modules:
  0.0 86.3 jit_solution(4053332398447951652)
XLA Ops:
  0.6 2.5 %shard_map.94 = (bf16[48,384]{1,0:T(8,128)(2,1)}, bf16[48,384]{1,0:T(8,128)(2,1)}, bf16[48,384]{1,0:T(8,128)(2,1)}, bf16[48,384]{1,0:T(8,128)(2,1)}, bf16[192,38...) custom-call(bf16[32,768]{1,0:T(8,128)(2,1)} %refs_0_.1, ...), custom_call_target="tpu_custom_call" | custom-call | bytes 1431552 | tf_op jit(solution)/shard_map/pallas_call | solution.py:77
  3.1 3.1 %collective-permute-start = (bf16[48,384]{1,0:T(8,128)(2,1)}, bf16[48,384]{1,0:T(8,128)(2,1)S(1)}, u32[]{:S(2)}, u32[]{:S(2)}) collective-permute-start(bf16[48,384]{1,0:T(8,128)(2,1)} %get-tuple-element.52), channel_id=1, source_target_pairs={{0,2},{1,3},{2,0},{3,1},{4,6},{5,7},{6,4},{7,5},{8,10},{9,11},{10,... | collective-permute-start | bytes 110600 | tf_op jit(solution)/shard_map/ppermute | solution.py:66
  6.2 2.6 %collective-permute-start.1 = (bf16[48,384]{1,0:T(8,128)(2,1)}, bf16[48,384]{1,0:T(8,128)(2,1)S(1)}, u32[]{:S(2)}, u32[]{:S(2)}) collective-permute-start(bf16[48,384]{1,0:T(8,128)(2,1)} %get-tuple-element.53), channel_id=1, source_target_pairs={{0,4},{1,5},{2,6},{3,7},{4,0},{5,1},{6,2},{7,3},{8,12},{9,13},{10,... | collective-permute-start | bytes 110600 | tf_op jit(solution)/shard_map/ppermute | solution.py:66
  8.8 3.1 %collective-permute-done.1.refs_2_ = bf16[48,384]{1,0:T(8,128)(2,1)S(1)} collective-permute-done((bf16[48,384]{1,0:T(8,128)(2,1)}, bf16[48,384]{1,0:T(8,128)(2,1)S(1)}, u32[]{:S(2)}, u32[]{:S(2)}) %collective-permute-start.1) | collective-permute-done | bytes 36896 | tf_op jit(solution)/shard_map/ppermute | solution.py:66
  12.0 2.8 %collective-permute-done.2.refs_3_ = bf16[48,384]{1,0:T(8,128)(2,1)S(1)} collective-permute-done((bf16[48,384]{1,0:T(8,128)(2,1)}, bf16[48,384]{1,0:T(8,128)(2,1)S(1)}, u32[]{:S(2)}, u32[]{:S(2)}) %collective-permute-start.2) | collective-permute-done | bytes 36896 | tf_op jit(solution)/shard_map/ppermute | solution.py:66
  14.8 0.8 copy-done.1
  15.8 1.6 %collective-permute-start.3 = (bf16[384,128]{1,0:T(8,128)(2,1)S(1)}, bf16[384,128]{1,0:T(8,128)(2,1)S(1)}, u32[]{:S(2)}, u32[]{:S(2)}) collective-permute-start(bf16[384,128]{1,0:T(8,128)(2,1)S(1)} %get-tuple-element.55.refs_0_), channel_id=1, source_target_pairs={{0,1},{1,0},{2,3},{3,2},{4,5},{5,4},{6,7},{7,6},{8,9},{9,8},{10,11... | collective-permute-start | bytes 294920 | tf_op jit(solution)/shard_map/ppermute | solution.py:66
  17.4 1.5 %collective-permute-start.6 = (bf16[384,128]{1,0:T(8,128)(2,1)S(1)}, bf16[384,128]{1,0:T(8,128)(2,1)S(1)}, u32[]{:S(2)}, u32[]{:S(2)}) collective-permute-start(bf16[384,128]{1,0:T(8,128)(2,1)S(1)} %get-tuple-element.55.refs_0_), channel_id=1, source_target_pairs={{0,16},{1,17},{2,18},{3,19},{4,20},{5,21},{6,22},{7,23},{8,24},{9,... | collective-permute-start | bytes 294920 | tf_op jit(solution)/shard_map/ppermute | solution.py:66
  18.8 0.5 collective-permute-start.7
  19.3 1.1 %collective-permute-done.3.refs_1_ = bf16[384,128]{1,0:T(8,128)(2,1)S(1)} collective-permute-done((bf16[384,128]{1,0:T(8,128)(2,1)S(1)}, bf16[384,128]{1,0:T(8,128)(2,1)S(1)}, u32[]{:S(2)}, u32[]{:S(2)}) %collective-permute-start.3) | collective-permute-done | bytes 98336 | tf_op jit(solution)/shard_map/ppermute | solution.py:66
  20.4 3.3 %collective-permute-start.12 = (bf16[192,384]{1,0:T(8,128)(2,1)}, bf16[192,384]{1,0:T(8,128)(2,1)S(1)}, u32[]{:S(2)}, u32[]{:S(2)}) collective-permute-start(bf16[192,384]{1,0:T(8,128)(2,1)} %get-tuple-element.59), channel_id=1, source_target_pairs={{0,6},{1,7},{2,4},{3,5},{4,2},{5,3},{6,0},{7,1},{8,14},{9,15},{10,... | collective-permute-start | bytes 442376 | tf_op jit(solution)/shard_map/ppermute | solution.py:66
  23.7 0.9 %collective-permute-done.7.refs_5_ = bf16[384,128]{1,0:T(8,128)(2,1)S(1)} collective-permute-done((bf16[384,128]{1,0:T(8,128)(2,1)S(1)}, bf16[384,128]{1,0:T(8,128)(2,1)S(1)}, u32[]{:S(2)}, u32[]{:S(2)}) %collective-permute-start.7) | collective-permute-done | bytes 98336 | tf_op jit(solution)/shard_map/ppermute | solution.py:66
  25.2 0.4 shard_map.96.refs_13_.refs_12_
  25.6 8.1 %collective-permute-done.11.refs_10_ = bf16[192,384]{1,0:T(8,128)(2,1)S(1)} collective-permute-done((bf16[192,384]{1,0:T(8,128)(2,1)}, bf16[192,384]{1,0:T(8,128)(2,1)S(1)}, u32[]{:S(2)}, u32[]{:S(2)}) %collective-permute-start.11) | collective-permute-done | bytes 147488 | tf_op jit(solution)/shard_map/ppermute | solution.py:66
  33.8 2.4 %shard_map.97 = (f32[384,128]{1,0:T(8,128)S(1)}, f32[384,128]{1,0:T(8,128)S(1)}, f32[384,128]{1,0:T(8,128)S(1)}, f32[384,128]{1,0:T(8,128)S(1)}, f32[384,128]{1,...) custom-call(bf16[384,128]{1,0:T(8,128)(2,1)S(1)} %get-tuple-element.55.refs_0_, ...), custom_call_target="tpu_custom_call" | custom-call | flops 603979776 | bytes 3223552 | tf_op jit(solution)/shard_map/pallas_call | solution.py:77
  36.2 0.5 collective-permute-start.14
  36.8 0.4 collective-permute-start.16
  38.7 1.6 %collective-permute-start.17 = (f16[400,128]{1,0:T(8,128)(2,1)S(1)}, f16[400,128]{1,0:T(8,128)(2,1)S(1)}, u32[]{:S(2)}, u32[]{:S(2)}) collective-permute-start(f16[400,128]{1,0:T(8,128)(2,1)S(1)} %convert_element_type.36), channel_id=1, source_target_pairs={{0,1},{1,0},{2,3},{3,2},{4,5},{5,4},{6,7},{7,6},{8,9},{9,8},{10,11... | collective-permute-start | bytes 307208 | tf_op jit(solution)/shard_map/ppermute | solution.py:66
  40.3 1.6 %collective-permute-start.18 = (f16[400,128]{1,0:T(8,128)(2,1)S(1)}, f16[400,128]{1,0:T(8,128)(2,1)S(1)}, u32[]{:S(2)}, u32[]{:S(2)}) collective-permute-start(f16[400,128]{1,0:T(8,128)(2,1)S(1)} %convert_element_type.38), channel_id=1, source_target_pairs={{0,16},{1,17},{2,18},{3,19},{4,20},{5,21},{6,22},{7,23},{8,24},{9,... | collective-permute-start | bytes 307208 | tf_op jit(solution)/shard_map/ppermute | solution.py:66
  41.8 0.5 collective-permute-start.19
  42.4 1.4 %collective-permute-done.17 = f16[400,128]{1,0:T(8,128)(2,1)S(1)} collective-permute-done((f16[400,128]{1,0:T(8,128)(2,1)S(1)}, f16[400,128]{1,0:T(8,128)(2,1)S(1)}, u32[]{:S(2)}, u32[]{:S(2)}) %collective-permute-start.17) | collective-permute-done | bytes 102432 | tf_op jit(solution)/shard_map/ppermute | solution.py:66
  43.8 2.2 %collective-permute-done.18 = f16[400,128]{1,0:T(8,128)(2,1)S(1)} collective-permute-done((f16[400,128]{1,0:T(8,128)(2,1)S(1)}, f16[400,128]{1,0:T(8,128)(2,1)S(1)}, u32[]{:S(2)}, u32[]{:S(2)}) %collective-permute-start.18) | collective-permute-done | bytes 102432 | tf_op jit(solution)/shard_map/ppermute | solution.py:66
  46.0 1.4 %collective-permute-done.19 = f16[400,128]{1,0:T(8,128)(2,1)S(1)} collective-permute-done((f16[400,128]{1,0:T(8,128)(2,1)S(1)}, f16[400,128]{1,0:T(8,128)(2,1)S(1)}, u32[]{:S(2)}, u32[]{:S(2)}) %collective-permute-start.19) | collective-permute-done | bytes 102432 | tf_op jit(solution)/shard_map/ppermute | solution.py:66
  47.6 1.3 %collective-permute-start.20 = (bf16[208,128]{1,0:T(8,128)(2,1)S(1)}, bf16[208,128]{1,0:T(8,128)(2,1)S(1)}, u32[]{:S(2)}, u32[]{:S(2)}) collective-permute-start(bf16[208,128]{1,0:T(8,128)(2,1)S(1)} %shard_map.99.refs_13_), channel_id=1, source_target_pairs={{0,1},{1,0},{2,3},{3,2},{4,5},{5,4},{6,7},{7,6},{8,9},{9,8},{10,11... | collective-permute-start | bytes 159752 | tf_op jit(solution)/shard_map/ppermute | solution.py:66
  48.9 1.5 %collective-permute-start.23 = (bf16[208,128]{1,0:T(8,128)(2,1)S(1)}, bf16[208,128]{1,0:T(8,128)(2,1)S(1)}, u32[]{:S(2)}, u32[]{:S(2)}) collective-permute-start(bf16[208,128]{1,0:T(8,128)(2,1)S(1)} %shard_map.99.refs_13_), channel_id=1, source_target_pairs={{0,16},{1,17},{2,18},{3,19},{4,20},{5,21},{6,22},{7,23},{8,24},{9,... | collective-permute-start | bytes 159752 | tf_op jit(solution)/shard_map/ppermute | solution.py:66
  50.4 0.7 collective-permute-start.24
  51.1 0.6 collective-permute-done.20.refs_14_
  51.8 1.2 %collective-permute-done.23.refs_17_ = bf16[208,128]{1,0:T(8,128)(2,1)S(1)} collective-permute-done((bf16[208,128]{1,0:T(8,128)(2,1)S(1)}, bf16[208,128]{1,0:T(8,128)(2,1)S(1)}, u32[]{:S(2)}, u32[]{:S(2)}) %collective-permute-start.23) | collective-permute-done | bytes 53280 | tf_op jit(solution)/shard_map/ppermute | solution.py:66
  53.0 2.4 %collective-permute-done.24.refs_18_ = bf16[208,128]{1,0:T(8,128)(2,1)S(1)} collective-permute-done((bf16[208,128]{1,0:T(8,128)(2,1)S(1)}, bf16[208,128]{1,0:T(8,128)(2,1)S(1)}, u32[]{:S(2)}, u32[]{:S(2)}) %collective-permute-start.24) | collective-permute-done | bytes 53280 | tf_op jit(solution)/shard_map/ppermute | solution.py:66
  55.4 1.4 %shard_map.100 = (f32[64,512]{1,0:T(8,128)S(1)}, f32[64,1024]{1,0:T(8,128)S(1)}) custom-call(bf16[384,128]{1,0:T(8,128)(2,1)S(1)} %get-tuple-element.55.refs_0_, bf16[384,128]{1,0:T(8,128)(2,1)S(1)} %collective-permute-done.3.refs_1_, bf16[384,128]{1,0:T(8,128)(2,1)S(1)} %collective-permute-done.4.refs_2_, ...), custom_call_target="tpu_custom_call" | custom-call | flops 268435456 | bytes 2031616 | tf_op jit(solution)/shard_map/pallas_call | solution.py:77
  56.8 2.7 %shard_map.101 = (f32[128,512]{1,0:T(8,128)S(1)}, f32[128,1024]{1,0:T(8,128)S(1)}) custom-call(bf16[384,128]{1,0:T(8,128)(2,1)S(1)} %get-tuple-element.55.refs_0_, bf16[384,128]{1,0:T(8,128)(2,1)S(1)} %collective-permute-done.3.refs_1_, bf16[384,128]{1,0:T(8,128)(2,1)S(1)} %collective-permute-done.4.refs_2_, ...), custom_call_target="tpu_custom_call" | custom-call | flops 536870912 | bytes 2424832 | tf_op jit(solution)/shard_map/pallas_call | solution.py:77
  59.6 4.1 %shard_map.102 = (bf16[128,384]{1,0:T(8,128)(2,1)S(1)}, bf16[128,384]{1,0:T(8,128)(2,1)S(1)}, bf16[128,384]{1,0:T(8,128)(2,1)S(1)}, bf16[128,384]{1,0:T(8,128)(2...) custom-call(bf16[384,128]{1,0:T(8,128)(2,1)S(1)} %get-tuple-element., ...), custom_call_target="tpu_custom_call" | custom-call | flops 1006632960 | bytes 4173824 | tf_op jit(solution)/shard_map/pallas_call | solution.py:77
  63.7 0.6 collective-permute-start.30
  64.4 0.4 collective-permute-start.32
  66.2 0.6 collective-permute-start.34
  66.8 2.5 %collective-permute-start.27 = (bf16[128,384]{1,0:T(8,128)(2,1)S(1)}, bf16[128,384]{1,0:T(8,128)(2,1)S(1)}, u32[]{:S(2)}, u32[]{:S(2)}) collective-permute-start(bf16[128,384]{1,0:T(8,128)(2,1)S(1)} %get-tuple-element.78), channel_id=1, source_target_pairs={{0,2},{1,3},{2,0},{3,1},{4,6},{5,7},{6,4},{7,5},{8,10},{9,11},{10,... | collective-permute-start | bytes 294920 | tf_op jit(solution)/shard_map/ppermute | solution.py:66
  69.3 2.4 %collective-permute-start.29 = (bf16[128,384]{1,0:T(8,128)(2,1)S(1)}, bf16[128,384]{1,0:T(8,128)(2,1)S(1)}, u32[]{:S(2)}, u32[]{:S(2)}) collective-permute-start(bf16[128,384]{1,0:T(8,128)(2,1)S(1)} %get-tuple-element.80), channel_id=1, source_target_pairs={{0,6},{1,7},{2,4},{3,5},{4,2},{5,3},{6,0},{7,1},{8,14},{9,15},{10,... | collective-permute-start | bytes 294920 | tf_op jit(solution)/shard_map/ppermute | solution.py:66
  71.6 0.8 collective-permute-start.35
  72.5 2.3 %collective-permute-start.36 = (f16[208,128]{1,0:T(8,128)(2,1)S(1)}, f16[208,128]{1,0:T(8,128)(2,1)S(1)}, u32[]{:S(2)}, u32[]{:S(2)}) collective-permute-start(f16[208,128]{1,0:T(8,128)(2,1)S(1)} %convert_element_type.46), channel_id=1, source_target_pairs={{0,17},{1,16},{2,19},{3,18},{4,21},{5,20},{6,23},{7,22},{8,25},{9,... | collective-permute-start | bytes 159752 | tf_op jit(solution)/shard_map/ppermute | solution.py:66
  74.7 1.3 %collective-permute-done.35 = f16[208,128]{1,0:T(8,128)(2,1)S(1)} collective-permute-done((f16[208,128]{1,0:T(8,128)(2,1)S(1)}, f16[208,128]{1,0:T(8,128)(2,1)S(1)}, u32[]{:S(2)}, u32[]{:S(2)}) %collective-permute-start.35) | collective-permute-done | bytes 53280 | tf_op jit(solution)/shard_map/ppermute | solution.py:66
  76.0 1.6 %collective-permute-done.36 = f16[208,128]{1,0:T(8,128)(2,1)S(1)} collective-permute-done((f16[208,128]{1,0:T(8,128)(2,1)S(1)}, f16[208,128]{1,0:T(8,128)(2,1)S(1)}, u32[]{:S(2)}, u32[]{:S(2)}) %collective-permute-start.36) | collective-permute-done | bytes 53280 | tf_op jit(solution)/shard_map/ppermute | solution.py:66
  77.8 1.2 %collective-permute-start.37 = (f32[48,128]{1,0:T(8,128)S(1)}, f32[48,128]{1,0:T(8,128)S(1)}, u32[]{:S(2)}, u32[]{:S(2)}) collective-permute-start(f32[48,128]{1,0:T(8,128)S(1)} %get-tuple-element.96), channel_id=1, source_target_pairs={{0,2},{1,3},{2,0},{3,1},{4,6},{5,7},{6,4},{7,5},{8,10},{9,11},{10,... | collective-permute-start | bytes 73736 | tf_op jit(solution)/shard_map/ppermute | solution.py:66
  78.9 0.9 %collective-permute-start.38 = (f32[48,128]{1,0:T(8,128)S(1)}, f32[48,128]{1,0:T(8,128)S(1)}, u32[]{:S(2)}, u32[]{:S(2)}) collective-permute-start(f32[48,128]{1,0:T(8,128)S(1)} %get-tuple-element.97), channel_id=1, source_target_pairs={{0,4},{1,5},{2,6},{3,7},{4,0},{5,1},{6,2},{7,3},{8,12},{9,13},{10,... | collective-permute-start | bytes 73736 | tf_op jit(solution)/shard_map/ppermute | solution.py:66
  79.8 2.4 %collective-permute-start.39 = (f32[48,128]{1,0:T(8,128)S(1)}, f32[48,128]{1,0:T(8,128)S(1)}, u32[]{:S(2)}, u32[]{:S(2)}) collective-permute-start(f32[48,128]{1,0:T(8,128)S(1)} %get-tuple-element.98), channel_id=1, source_target_pairs={{0,6},{1,7},{2,4},{3,5},{4,2},{5,3},{6,0},{7,1},{8,14},{9,15},{10,... | collective-permute-start | bytes 73736 | tf_op jit(solution)/shard_map/ppermute | solution.py:66
  82.2 1.0 %shard_map.103 = (bf16[128,768]{1,0:T(8,128)(2,1)}, bf16[128,768]{1,0:T(8,128)(2,1)}) custom-call(bf16[128,384]{1,0:T(8,128)(2,1)S(1)} %get-tuple-element.77.refs_0_, bf16[128,384]{1,0:T(8,128)(2,1)S(1)} %collective-permute-done.27.refs_1_, bf16[128,384]{1,0:T(8,128)(2,1)S(1)} %collective-permute-done.28.refs_2_, ...), custom_call_target="tpu_custom_call" | custom-call | bytes 786432 | tf_op jit(solution)/shard_map/pallas_call | solution.py:77
  83.2 0.5 collective-permute-done.38.refs_2_
  83.7 1.8 %collective-permute-done.39.refs_3_ = f32[48,128]{1,0:T(8,128)S(1)} collective-permute-done((f32[48,128]{1,0:T(8,128)S(1)}, f32[48,128]{1,0:T(8,128)S(1)}, u32[]{:S(2)}, u32[]{:S(2)}) %collective-permute-start.39) | collective-permute-done | bytes 24608 | tf_op jit(solution)/shard_map/ppermute | solution.py:66
  85.5 0.8 shard_map.106
  (63 shorter events, 4.2 us)
Async XLA Ops:
  3.1 5.7 %collective-permute-start = (bf16[48,384]{1,0:T(8,128)(2,1)}, bf16[48,384]{1,0:T(8,128)(2,1)S(1)}, u32[]{:S(2)}, u32[]{:S(2)}) collective-permute-start(bf16[48,384]{1,0:T(8,128)(2,1)} %get-tuple-element.52), channel_id=1, source_target_pairs={{0,2},{1,3},{2,0},{3,1},{4,6},{5,7},{6,4},{7,5},{8,10},{9,11},{10,... | collective-permute-start | bytes 110600 | tf_op jit(solution)/shard_map/ppermute | solution.py:66
  6.2 5.7 %collective-permute-start.1 = (bf16[48,384]{1,0:T(8,128)(2,1)}, bf16[48,384]{1,0:T(8,128)(2,1)S(1)}, u32[]{:S(2)}, u32[]{:S(2)}) collective-permute-start(bf16[48,384]{1,0:T(8,128)(2,1)} %get-tuple-element.53), channel_id=1, source_target_pairs={{0,4},{1,5},{2,6},{3,7},{4,0},{5,1},{6,2},{7,3},{8,12},{9,13},{10,... | collective-permute-start | bytes 110600 | tf_op jit(solution)/shard_map/ppermute | solution.py:66
  8.8 6.0 %collective-permute-start.2 = (bf16[48,384]{1,0:T(8,128)(2,1)}, bf16[48,384]{1,0:T(8,128)(2,1)S(1)}, u32[]{:S(2)}, u32[]{:S(2)}) collective-permute-start(bf16[48,384]{1,0:T(8,128)(2,1)} %get-tuple-element.54), channel_id=1, source_target_pairs={{0,6},{1,7},{2,4},{3,5},{4,2},{5,3},{6,0},{7,1},{8,14},{9,15},{10,... | collective-permute-start | bytes 110600 | tf_op jit(solution)/shard_map/ppermute | solution.py:66
  14.8 0.8 copy-start.1
  15.6 9.6 %copy-start = (f32[12,1024]{1,0:T(8,128)S(1)}, f32[12,1024]{1,0:T(8,128)}, u32[]{:S(2)}) copy-start(f32[12,1024]{1,0:T(8,128)} %n_ref.1) | copy-start | bytes 147460
  15.6 18.2 %copy-start.2 = (bf16[192,384]{1,0:T(8,128)(2,1)S(1)}, bf16[192,384]{1,0:T(8,128)(2,1)}, u32[]{:S(2)}) copy-start(bf16[192,384]{1,0:T(8,128)(2,1)} %get-tuple-element.56.refs_8_) | copy-start | bytes 442372
  15.8 4.7 %collective-permute-start.3 = (bf16[384,128]{1,0:T(8,128)(2,1)S(1)}, bf16[384,128]{1,0:T(8,128)(2,1)S(1)}, u32[]{:S(2)}, u32[]{:S(2)}) collective-permute-start(bf16[384,128]{1,0:T(8,128)(2,1)S(1)} %get-tuple-element.55.refs_0_), channel_id=1, source_target_pairs={{0,1},{1,0},{2,3},{3,2},{4,5},{5,4},{6,7},{7,6},{8,9},{9,8},{10,11... | collective-permute-start | bytes 294920 | tf_op jit(solution)/shard_map/ppermute | solution.py:66
  17.3 3.1 %collective-permute-start.4 = (bf16[384,128]{1,0:T(8,128)(2,1)S(1)}, bf16[384,128]{1,0:T(8,128)(2,1)S(1)}, u32[]{:S(2)}, u32[]{:S(2)}) collective-permute-start(bf16[384,128]{1,0:T(8,128)(2,1)S(1)} %get-tuple-element.55.refs_0_), channel_id=1, source_target_pairs={{0,8},{1,9},{2,10},{3,11},{4,12},{5,13},{6,14},{7,15},{8,0},{9,1},... | collective-permute-start | bytes 294920 | tf_op jit(solution)/shard_map/ppermute | solution.py:66
  17.3 7.7 %collective-permute-start.10 = (bf16[192,384]{1,0:T(8,128)(2,1)}, bf16[192,384]{1,0:T(8,128)(2,1)S(1)}, u32[]{:S(2)}, u32[]{:S(2)}) collective-permute-start(bf16[192,384]{1,0:T(8,128)(2,1)} %get-tuple-element.57), channel_id=1, source_target_pairs={{0,2},{1,3},{2,0},{3,1},{4,6},{5,7},{6,4},{7,5},{8,10},{9,11},{10,... | collective-permute-start | bytes 442376 | tf_op jit(solution)/shard_map/ppermute | solution.py:66
  17.4 6.4 %collective-permute-start.6 = (bf16[384,128]{1,0:T(8,128)(2,1)S(1)}, bf16[384,128]{1,0:T(8,128)(2,1)S(1)}, u32[]{:S(2)}, u32[]{:S(2)}) collective-permute-start(bf16[384,128]{1,0:T(8,128)(2,1)S(1)} %get-tuple-element.55.refs_0_), channel_id=1, source_target_pairs={{0,16},{1,17},{2,18},{3,19},{4,20},{5,21},{6,22},{7,23},{8,24},{9,... | collective-permute-start | bytes 294920 | tf_op jit(solution)/shard_map/ppermute | solution.py:66
  18.8 5.8 %collective-permute-start.7 = (bf16[384,128]{1,0:T(8,128)(2,1)S(1)}, bf16[384,128]{1,0:T(8,128)(2,1)S(1)}, u32[]{:S(2)}, u32[]{:S(2)}) collective-permute-start(bf16[384,128]{1,0:T(8,128)(2,1)S(1)} %get-tuple-element.55.refs_0_), channel_id=1, source_target_pairs={{0,17},{1,16},{2,19},{3,18},{4,21},{5,20},{6,23},{7,22},{8,25},{9,... | collective-permute-start | bytes 294920 | tf_op jit(solution)/shard_map/ppermute | solution.py:66
  20.4 13.3 %collective-permute-start.11 = (bf16[192,384]{1,0:T(8,128)(2,1)}, bf16[192,384]{1,0:T(8,128)(2,1)S(1)}, u32[]{:S(2)}, u32[]{:S(2)}) collective-permute-start(bf16[192,384]{1,0:T(8,128)(2,1)} %get-tuple-element.58), channel_id=1, source_target_pairs={{0,4},{1,5},{2,6},{3,7},{4,0},{5,1},{6,2},{7,3},{8,12},{9,13},{10,... | collective-permute-start | bytes 442376 | tf_op jit(solution)/shard_map/ppermute | solution.py:66
  20.4 13.3 %collective-permute-start.12 = (bf16[192,384]{1,0:T(8,128)(2,1)}, bf16[192,384]{1,0:T(8,128)(2,1)S(1)}, u32[]{:S(2)}, u32[]{:S(2)}) collective-permute-start(bf16[192,384]{1,0:T(8,128)(2,1)} %get-tuple-element.59), channel_id=1, source_target_pairs={{0,6},{1,7},{2,4},{3,5},{4,2},{5,3},{6,0},{7,1},{8,14},{9,15},{10,... | collective-permute-start | bytes 442376 | tf_op jit(solution)/shard_map/ppermute | solution.py:66
  23.7 10.0 %collective-permute-start.5 = (bf16[384,128]{1,0:T(8,128)(2,1)S(1)}, bf16[384,128]{1,0:T(8,128)(2,1)S(1)}, u32[]{:S(2)}, u32[]{:S(2)}) collective-permute-start(bf16[384,128]{1,0:T(8,128)(2,1)S(1)} %collective-permute-done.3.refs_1_), channel_id=1, source_target_pairs={{0,8},{1,9},{2,10},{3,11},{4,12},{5,13},{6,14},{7,15},{8,0},{9,1},... | collective-permute-start | bytes 294920 | tf_op jit(solution)/shard_map/ppermute | solution.py:66
  24.7 9.1 %collective-permute-start.8 = (bf16[384,128]{1,0:T(8,128)(2,1)S(1)}, bf16[384,128]{1,0:T(8,128)(2,1)S(1)}, u32[]{:S(2)}, u32[]{:S(2)}) collective-permute-start(bf16[384,128]{1,0:T(8,128)(2,1)S(1)} %collective-permute-done.6.refs_4_), channel_id=1, source_target_pairs={{0,8},{1,9},{2,10},{3,11},{4,12},{5,13},{6,14},{7,15},{8,0},{9,1},... | collective-permute-start | bytes 294920 | tf_op jit(solution)/shard_map/ppermute | solution.py:66
  25.1 8.7 %collective-permute-start.9 = (bf16[384,128]{1,0:T(8,128)(2,1)S(1)}, bf16[384,128]{1,0:T(8,128)(2,1)S(1)}, u32[]{:S(2)}, u32[]{:S(2)}) collective-permute-start(bf16[384,128]{1,0:T(8,128)(2,1)S(1)} %collective-permute-done.7.refs_5_), channel_id=1, source_target_pairs={{0,8},{1,9},{2,10},{3,11},{4,12},{5,13},{6,14},{7,15},{8,0},{9,1},... | collective-permute-start | bytes 294920 | tf_op jit(solution)/shard_map/ppermute | solution.py:66
  36.2 1.5 %collective-permute-start.13 = (f32[384,128]{1,0:T(8,128)S(1)}, f32[384,128]{1,0:T(8,128)S(1)}, u32[]{:S(2)}, u32[]{:S(2)}) collective-permute-start(f32[384,128]{1,0:T(8,128)S(1)} %get-tuple-element.65), channel_id=1, source_target_pairs={{0,8},{1,9},{2,10},{3,11},{4,12},{5,13},{6,14},{7,15},{8,0},{9,1},... | collective-permute-start | bytes 589832 | tf_op jit(solution)/shard_map/ppermute | solution.py:66
  36.2 1.7 %collective-permute-start.14 = (f32[384,128]{1,0:T(8,128)S(1)}, f32[384,128]{1,0:T(8,128)S(1)}, u32[]{:S(2)}, u32[]{:S(2)}) collective-permute-start(f32[384,128]{1,0:T(8,128)S(1)} %get-tuple-element.66), channel_id=1, source_target_pairs={{0,8},{1,9},{2,10},{3,11},{4,12},{5,13},{6,14},{7,15},{8,0},{9,1},... | collective-permute-start | bytes 589832 | tf_op jit(solution)/shard_map/ppermute | solution.py:66
  36.7 1.5 %collective-permute-start.15 = (f32[384,128]{1,0:T(8,128)S(1)}, f32[384,128]{1,0:T(8,128)S(1)}, u32[]{:S(2)}, u32[]{:S(2)}) collective-permute-start(f32[384,128]{1,0:T(8,128)S(1)} %get-tuple-element.67), channel_id=1, source_target_pairs={{0,8},{1,9},{2,10},{3,11},{4,12},{5,13},{6,14},{7,15},{8,0},{9,1},... | collective-permute-start | bytes 589832 | tf_op jit(solution)/shard_map/ppermute | solution.py:66
  36.8 1.7 %collective-permute-start.16 = (f32[384,128]{1,0:T(8,128)S(1)}, f32[384,128]{1,0:T(8,128)S(1)}, u32[]{:S(2)}, u32[]{:S(2)}) collective-permute-start(f32[384,128]{1,0:T(8,128)S(1)} %get-tuple-element.68), channel_id=1, source_target_pairs={{0,8},{1,9},{2,10},{3,11},{4,12},{5,13},{6,14},{7,15},{8,0},{9,1},... | collective-permute-start | bytes 589832 | tf_op jit(solution)/shard_map/ppermute | solution.py:66
  38.7 5.1 %collective-permute-start.17 = (f16[400,128]{1,0:T(8,128)(2,1)S(1)}, f16[400,128]{1,0:T(8,128)(2,1)S(1)}, u32[]{:S(2)}, u32[]{:S(2)}) collective-permute-start(f16[400,128]{1,0:T(8,128)(2,1)S(1)} %convert_element_type.36), channel_id=1, source_target_pairs={{0,1},{1,0},{2,3},{3,2},{4,5},{5,4},{6,7},{7,6},{8,9},{9,8},{10,11... | collective-permute-start | bytes 307208 | tf_op jit(solution)/shard_map/ppermute | solution.py:66
  40.3 5.7 %collective-permute-start.18 = (f16[400,128]{1,0:T(8,128)(2,1)S(1)}, f16[400,128]{1,0:T(8,128)(2,1)S(1)}, u32[]{:S(2)}, u32[]{:S(2)}) collective-permute-start(f16[400,128]{1,0:T(8,128)(2,1)S(1)} %convert_element_type.38), channel_id=1, source_target_pairs={{0,16},{1,17},{2,18},{3,19},{4,20},{5,21},{6,22},{7,23},{8,24},{9,... | collective-permute-start | bytes 307208 | tf_op jit(solution)/shard_map/ppermute | solution.py:66
  41.8 5.6 %collective-permute-start.19 = (f16[400,128]{1,0:T(8,128)(2,1)S(1)}, f16[400,128]{1,0:T(8,128)(2,1)S(1)}, u32[]{:S(2)}, u32[]{:S(2)}) collective-permute-start(f16[400,128]{1,0:T(8,128)(2,1)S(1)} %convert_element_type.40), channel_id=1, source_target_pairs={{0,17},{1,16},{2,19},{3,18},{4,21},{5,20},{6,23},{7,22},{8,25},{9,... | collective-permute-start | bytes 307208 | tf_op jit(solution)/shard_map/ppermute | solution.py:66
  47.6 4.2 %collective-permute-start.20 = (bf16[208,128]{1,0:T(8,128)(2,1)S(1)}, bf16[208,128]{1,0:T(8,128)(2,1)S(1)}, u32[]{:S(2)}, u32[]{:S(2)}) collective-permute-start(bf16[208,128]{1,0:T(8,128)(2,1)S(1)} %shard_map.99.refs_13_), channel_id=1, source_target_pairs={{0,1},{1,0},{2,3},{3,2},{4,5},{5,4},{6,7},{7,6},{8,9},{9,8},{10,11... | collective-permute-start | bytes 159752 | tf_op jit(solution)/shard_map/ppermute | solution.py:66
  48.9 4.1 %collective-permute-start.23 = (bf16[208,128]{1,0:T(8,128)(2,1)S(1)}, bf16[208,128]{1,0:T(8,128)(2,1)S(1)}, u32[]{:S(2)}, u32[]{:S(2)}) collective-permute-start(bf16[208,128]{1,0:T(8,128)(2,1)S(1)} %shard_map.99.refs_13_), channel_id=1, source_target_pairs={{0,16},{1,17},{2,18},{3,19},{4,20},{5,21},{6,22},{7,23},{8,24},{9,... | collective-permute-start | bytes 159752 | tf_op jit(solution)/shard_map/ppermute | solution.py:66
  50.4 5.0 %collective-permute-start.24 = (bf16[208,128]{1,0:T(8,128)(2,1)S(1)}, bf16[208,128]{1,0:T(8,128)(2,1)S(1)}, u32[]{:S(2)}, u32[]{:S(2)}) collective-permute-start(bf16[208,128]{1,0:T(8,128)(2,1)S(1)} %shard_map.99.refs_13_), channel_id=1, source_target_pairs={{0,17},{1,16},{2,19},{3,18},{4,21},{5,20},{6,23},{7,22},{8,25},{9,... | collective-permute-start | bytes 159752 | tf_op jit(solution)/shard_map/ppermute | solution.py:66
  51.1 8.4 %collective-permute-start.21 = (bf16[208,128]{1,0:T(8,128)(2,1)S(1)}, bf16[208,128]{1,0:T(8,128)(2,1)S(1)}, u32[]{:S(2)}, u32[]{:S(2)}) collective-permute-start(bf16[208,128]{1,0:T(8,128)(2,1)S(1)} %shard_map.99.refs_13_), channel_id=1, source_target_pairs={{0,8},{1,9},{2,10},{3,11},{4,12},{5,13},{6,14},{7,15},{8,0},{9,1},... | collective-permute-start | bytes 159752 | tf_op jit(solution)/shard_map/ppermute | solution.py:66
  51.8 7.8 %collective-permute-start.22 = (bf16[208,128]{1,0:T(8,128)(2,1)S(1)}, bf16[208,128]{1,0:T(8,128)(2,1)S(1)}, u32[]{:S(2)}, u32[]{:S(2)}) collective-permute-start(bf16[208,128]{1,0:T(8,128)(2,1)S(1)} %collective-permute-done.20.refs_14_), channel_id=1, source_target_pairs={{0,8},{1,9},{2,10},{3,11},{4,12},{5,13},{6,14},{7,15},{8,0},{9,1},... | collective-permute-start | bytes 159752 | tf_op jit(solution)/shard_map/ppermute | solution.py:66
  53.0 6.5 %collective-permute-start.25 = (bf16[208,128]{1,0:T(8,128)(2,1)S(1)}, bf16[208,128]{1,0:T(8,128)(2,1)S(1)}, u32[]{:S(2)}, u32[]{:S(2)}) collective-permute-start(bf16[208,128]{1,0:T(8,128)(2,1)S(1)} %collective-permute-done.23.refs_17_), channel_id=1, source_target_pairs={{0,8},{1,9},{2,10},{3,11},{4,12},{5,13},{6,14},{7,15},{8,0},{9,1},... | collective-permute-start | bytes 159752 | tf_op jit(solution)/shard_map/ppermute | solution.py:66
  55.4 4.2 %collective-permute-start.26 = (bf16[208,128]{1,0:T(8,128)(2,1)S(1)}, bf16[208,128]{1,0:T(8,128)(2,1)S(1)}, u32[]{:S(2)}, u32[]{:S(2)}) collective-permute-start(bf16[208,128]{1,0:T(8,128)(2,1)S(1)} %collective-permute-done.24.refs_18_), channel_id=1, source_target_pairs={{0,8},{1,9},{2,10},{3,11},{4,12},{5,13},{6,14},{7,15},{8,0},{9,1},... | collective-permute-start | bytes 159752 | tf_op jit(solution)/shard_map/ppermute | solution.py:66
  63.7 1.5 %collective-permute-start.30 = (f32[192,128]{1,0:T(8,128)S(1)}, f32[192,128]{1,0:T(8,128)S(1)}, u32[]{:S(2)}, u32[]{:S(2)}) collective-permute-start(f32[192,128]{1,0:T(8,128)S(1)} %get-tuple-element.87), channel_id=1, source_target_pairs={{0,8},{1,9},{2,10},{3,11},{4,12},{5,13},{6,14},{7,15},{8,0},{9,1},... | collective-permute-start | bytes 294920 | tf_op jit(solution)/shard_map/ppermute | solution.py:66
  64.3 1.3 %collective-permute-start.31 = (f32[192,128]{1,0:T(8,128)S(1)}, f32[192,128]{1,0:T(8,128)S(1)}, u32[]{:S(2)}, u32[]{:S(2)}) collective-permute-start(f32[192,128]{1,0:T(8,128)S(1)} %get-tuple-element.88), channel_id=1, source_target_pairs={{0,8},{1,9},{2,10},{3,11},{4,12},{5,13},{6,14},{7,15},{8,0},{9,1},... | collective-permute-start | bytes 294920 | tf_op jit(solution)/shard_map/ppermute | solution.py:66
  64.4 1.4 %collective-permute-start.32 = (f32[192,128]{1,0:T(8,128)S(1)}, f32[192,128]{1,0:T(8,128)S(1)}, u32[]{:S(2)}, u32[]{:S(2)}) collective-permute-start(f32[192,128]{1,0:T(8,128)S(1)} %get-tuple-element.89), channel_id=1, source_target_pairs={{0,8},{1,9},{2,10},{3,11},{4,12},{5,13},{6,14},{7,15},{8,0},{9,1},... | collective-permute-start | bytes 294920 | tf_op jit(solution)/shard_map/ppermute | solution.py:66
  64.8 1.3 %collective-permute-start.33 = (f32[192,128]{1,0:T(8,128)S(1)}, f32[192,128]{1,0:T(8,128)S(1)}, u32[]{:S(2)}, u32[]{:S(2)}) collective-permute-start(f32[192,128]{1,0:T(8,128)S(1)} %get-tuple-element.90), channel_id=1, source_target_pairs={{0,8},{1,9},{2,10},{3,11},{4,12},{5,13},{6,14},{7,15},{8,0},{9,1},... | collective-permute-start | bytes 294920 | tf_op jit(solution)/shard_map/ppermute | solution.py:66
  66.2 6.3 %collective-permute-start.34 = (f16[208,128]{1,0:T(8,128)(2,1)S(1)}, f16[208,128]{1,0:T(8,128)(2,1)S(1)}, u32[]{:S(2)}, u32[]{:S(2)}) collective-permute-start(f16[208,128]{1,0:T(8,128)(2,1)S(1)} %convert_element_type.42), channel_id=1, source_target_pairs={{0,1},{1,0},{2,3},{3,2},{4,5},{5,4},{6,7},{7,6},{8,9},{9,8},{10,11... | collective-permute-start | bytes 159752 | tf_op jit(solution)/shard_map/ppermute | solution.py:66
  66.8 13.1 %collective-permute-start.27 = (bf16[128,384]{1,0:T(8,128)(2,1)S(1)}, bf16[128,384]{1,0:T(8,128)(2,1)S(1)}, u32[]{:S(2)}, u32[]{:S(2)}) collective-permute-start(bf16[128,384]{1,0:T(8,128)(2,1)S(1)} %get-tuple-element.78), channel_id=1, source_target_pairs={{0,2},{1,3},{2,0},{3,1},{4,6},{5,7},{6,4},{7,5},{8,10},{9,11},{10,... | collective-permute-start | bytes 294920 | tf_op jit(solution)/shard_map/ppermute | solution.py:66
  69.3 13.0 %collective-permute-start.28 = (bf16[128,384]{1,0:T(8,128)(2,1)S(1)}, bf16[128,384]{1,0:T(8,128)(2,1)S(1)}, u32[]{:S(2)}, u32[]{:S(2)}) collective-permute-start(bf16[128,384]{1,0:T(8,128)(2,1)S(1)} %get-tuple-element.79), channel_id=1, source_target_pairs={{0,4},{1,5},{2,6},{3,7},{4,0},{5,1},{6,2},{7,3},{8,12},{9,13},{10,... | collective-permute-start | bytes 294920 | tf_op jit(solution)/shard_map/ppermute | solution.py:66
  69.3 13.0 %collective-permute-start.29 = (bf16[128,384]{1,0:T(8,128)(2,1)S(1)}, bf16[128,384]{1,0:T(8,128)(2,1)S(1)}, u32[]{:S(2)}, u32[]{:S(2)}) collective-permute-start(bf16[128,384]{1,0:T(8,128)(2,1)S(1)} %get-tuple-element.80), channel_id=1, source_target_pairs={{0,6},{1,7},{2,4},{3,5},{4,2},{5,3},{6,0},{7,1},{8,14},{9,15},{10,... | collective-permute-start | bytes 294920 | tf_op jit(solution)/shard_map/ppermute | solution.py:66
  71.6 4.4 %collective-permute-start.35 = (f16[208,128]{1,0:T(8,128)(2,1)S(1)}, f16[208,128]{1,0:T(8,128)(2,1)S(1)}, u32[]{:S(2)}, u32[]{:S(2)}) collective-permute-start(f16[208,128]{1,0:T(8,128)(2,1)S(1)} %convert_element_type.44), channel_id=1, source_target_pairs={{0,16},{1,17},{2,18},{3,19},{4,20},{5,21},{6,22},{7,23},{8,24},{9,... | collective-permute-start | bytes 159752 | tf_op jit(solution)/shard_map/ppermute | solution.py:66
  72.5 5.1 %collective-permute-start.36 = (f16[208,128]{1,0:T(8,128)(2,1)S(1)}, f16[208,128]{1,0:T(8,128)(2,1)S(1)}, u32[]{:S(2)}, u32[]{:S(2)}) collective-permute-start(f16[208,128]{1,0:T(8,128)(2,1)S(1)} %convert_element_type.46), channel_id=1, source_target_pairs={{0,17},{1,16},{2,19},{3,18},{4,21},{5,20},{6,23},{7,22},{8,25},{9,... | collective-permute-start | bytes 159752 | tf_op jit(solution)/shard_map/ppermute | solution.py:66
  77.8 5.4 %collective-permute-start.37 = (f32[48,128]{1,0:T(8,128)S(1)}, f32[48,128]{1,0:T(8,128)S(1)}, u32[]{:S(2)}, u32[]{:S(2)}) collective-permute-start(f32[48,128]{1,0:T(8,128)S(1)} %get-tuple-element.96), channel_id=1, source_target_pairs={{0,2},{1,3},{2,0},{3,1},{4,6},{5,7},{6,4},{7,5},{8,10},{9,11},{10,... | collective-permute-start | bytes 73736 | tf_op jit(solution)/shard_map/ppermute | solution.py:66
  78.9 4.7 %collective-permute-start.38 = (f32[48,128]{1,0:T(8,128)S(1)}, f32[48,128]{1,0:T(8,128)S(1)}, u32[]{:S(2)}, u32[]{:S(2)}) collective-permute-start(f32[48,128]{1,0:T(8,128)S(1)} %get-tuple-element.97), channel_id=1, source_target_pairs={{0,4},{1,5},{2,6},{3,7},{4,0},{5,1},{6,2},{7,3},{8,12},{9,13},{10,... | collective-permute-start | bytes 73736 | tf_op jit(solution)/shard_map/ppermute | solution.py:66
  79.8 5.6 %collective-permute-start.39 = (f32[48,128]{1,0:T(8,128)S(1)}, f32[48,128]{1,0:T(8,128)S(1)}, u32[]{:S(2)}, u32[]{:S(2)}) collective-permute-start(f32[48,128]{1,0:T(8,128)S(1)} %get-tuple-element.98), channel_id=1, source_target_pairs={{0,6},{1,7},{2,4},{3,5},{4,2},{5,3},{6,0},{7,1},{8,14},{9,15},{10,... | collective-permute-start | bytes 73736 | tf_op jit(solution)/shard_map/ppermute | solution.py:66

commit v5 on v4

--- a/solution.py
+++ b/solution.py
@@ -17,7 +17,6 @@
 LAG, SLOTS = 1, 3
 GROUPS = 4
 VMEM_BYTES = 20 * 2**20
-WHOLE_VMEM_BYTES = 60 * 2**20
 LOG2E = math.log2(math.e)
 
 
@@ -66,26 +65,21 @@
         return lax.ppermute(value, AXES, pairs)
 
 
-def vmem():
-    return pl.BlockSpec(memory_space=pltpu.VMEM)
-
-
-def call(kernel, outs, args, scratch=(), flops=0, from_hbm=False):
-    limit = WHOLE_VMEM_BYTES if from_hbm else VMEM_BYTES
+def call(kernel, outs, args, scratch=(), flops=0, space=pltpu.VMEM):
     nbytes = sum(a.size * a.dtype.itemsize for a in args)
     nbytes += sum(math.prod(o.shape) * o.dtype.itemsize for o in outs)
     return pl.pallas_call(
         kernel,
         out_shape=tuple(outs),
-        in_specs=[pl.BlockSpec(memory_space=pltpu.HBM) if from_hbm else vmem()] * len(args),
-        out_specs=tuple(vmem() for _ in outs),
+        in_specs=[pl.BlockSpec(memory_space=space)] * len(args),
+        out_specs=tuple(pl.BlockSpec(memory_space=pltpu.VMEM) for _ in outs),
         scratch_shapes=list(scratch),
         cost_estimate=pl.CostEstimate(flops=flops, bytes_accessed=nbytes, transcendentals=flops // 256),
-        compiler_params=pltpu.CompilerParams(vmem_limit_bytes=limit),
+        compiler_params=pltpu.CompilerParams(vmem_limit_bytes=VMEM_BYTES),
     )(*args)
 
 
-def fetched(kernel, args):
+def call_from_hbm(kernel, outs, args):
     n = len(args)
 
     def body(*refs):
@@ -101,7 +95,8 @@
         kernel(*held, *refs[n : -n - 1])
 
     scratch = [pltpu.VMEM(a.shape, a.dtype) for a in args] + [pltpu.SemaphoreType.DMA((n,))]
-    return body, scratch
+    args = [pltpu.with_memory_space_constraint(a, pltpu.HBM) for a in args]
+    return call(body, outs, args, scratch, space=pltpu.HBM)
 
 
 def shaped(shape, dtype):
@@ -171,9 +166,7 @@
 
     outs = [shaped((plan.slot, 2 * plan.cols), jnp.bfloat16)] * GROUPS
     outs += [shaped((plan.rows + HEAD_DIM, 2 * plan.cols), jnp.bfloat16)] * GROUPS
-    args = (query, out, norm, keys, grads, values)
-    body, scratch = fetched(kernel, args)
-    got = call(body, outs, args, scratch, from_hbm=True)
+    got = call_from_hbm(kernel, outs, (query, out, norm, keys, grads, values))
     return got[:GROUPS], got[GROUPS:]
 
 
@@ -197,7 +190,8 @@
             total = total + nn(stack[:, start : start + step], chosen)
         out_ref[0:hs, :] = (total[:hs] + total[hs : 2 * hs]) + total[2 * hs : 3 * hs]
 
-    return call(kernel, [shaped((plan.heads, plan.latents), jnp.float32)], (norm,))[0]
+    outs = [shaped((plan.heads, plan.latents), jnp.float32)]
+    return call_from_hbm(kernel, outs, (norm,))[0]
 
 
 def turn_latents(plan, slots):
@@ -235,8 +229,8 @@
     c, m = plan.cols, plan.latents
 
     def kernel(*refs):
-        lat_refs, pts_refs, (dec_ref, enc_ref) = refs[:n_lat], refs[n_lat:-5 - n_lat], refs[-5 - n_lat : -3 - n_lat]
-        outs = refs[-3 - n_lat : -3]
+        lat_refs, pts_refs, (dec_ref, enc_ref) = refs[:n_lat], refs[n_lat:-6 - n_lat], refs[-6 - n_lat : -4 - n_lat]
+        outs, kept = refs[-4 - n_lat : -4], refs[-4]
         query, sides, keys = refs[-3:]
         for k, ref in enumerate(lat_refs):
             query[:, k * plan.block : (k + 1) * plan.block] = ref[:c, :]
@@ -255,18 +249,21 @@
             for lanes in lane_tiles(plan):
                 scores = nn(key, query[mine, lanes]) * (HEAD_DIM**-0.5 * LOG2E)
                 dec = jnp.exp2(scores - row_norm).astype(jnp.bfloat16)
-                enc = jnp.exp2(scores - enc_ref[h : h + 1, lanes] * LOG2E).astype(jnp.bfloat16)
+                enc = jnp.exp2(scores - enc_ref[h : h + 1, lanes] * LOG2E)
+                kept[h, :, lanes] = enc
                 store_blocks(plan, outs, mine, lanes, nn(sides[mine, :], dec))
-                store_blocks(plan, outs, below, lanes, nn(sides[below, :], enc))
+                store_blocks(plan, outs, below, lanes, nn(sides[below, :], enc.astype(jnp.bfloat16)))
 
     outs = [shaped((2 * c, plan.block), jnp.float32)] * plan.plane
+    outs += [shaped((plan.heads, plan.points, m), jnp.float32)]
     scratch = [
         pltpu.VMEM((c, m), jnp.bfloat16),
         pltpu.VMEM((2 * c, plan.points), jnp.bfloat16),
         pltpu.VMEM((plan.points, c), jnp.bfloat16),
     ]
     flops = 6 * plan.points * m * c
-    return call(kernel, outs, (*lats, *pts, dec_norm, enc_norm), scratch, flops)
+    *sums, kept = call(kernel, outs, (*lats, *pts, dec_norm, enc_norm), scratch, flops)
+    return sums, kept
 
 
 def decoder_pass(plan, lats, pts, dec_norm, heads):
@@ -363,7 +360,7 @@
     return call(kernel, outs, parts)[0]
 
 
-def encoder_pass(plan, lats, pts, norm, mixes, before):
+def encoder_pass(plan, lats, pts, kept, mixes, before):
     places = [(part, at) for part, (heads, _) in enumerate(before) for at in range(len(heads))]
     n_lat, n_pts, n_mix = len(lats), len(pts), len(mixes)
     c, m, hs = plan.cols, plan.latents, plan.heads
@@ -377,18 +374,17 @@
             return got
 
         lat_refs, pts_refs = take(n_lat), take(n_pts)
-        (norm_ref,) = take(1)
+        (kept_ref,) = take(1)
         mix_refs = take(n_mix)
         parts_in = [take(2) for _ in before]
         pts_outs, lat_outs = take(n_pts), take(n_lat)
-        query, mix, keys, keys_t, values, ds, encs = refs
+        query, mix, keys_t, values, ds, encs = refs
         for k, ref in enumerate(lat_refs):
             query[:, k * plan.block : (k + 1) * plan.block] = ref[:c, :]
         for k, ref in enumerate(mix_refs):
             mix[:, k * plan.block : (k + 1) * plan.block] = ref[...]
         for j, ref in enumerate(pts_refs):
             rows = slice(j * plan.rows, (j + 1) * plan.rows)
-            keys[rows, :] = ref[: plan.rows, :c]
             keys_t[:, rows] = turned(ref[: plan.rows, :c])
             across = [ref[plan.rows :, h * plan.rows : (h + 1) * plan.rows] for h in range(hs)]
             values[rows, :] = turned(jnp.concatenate(across, axis=0))
@@ -399,8 +395,7 @@
 
         def weigh(h, t, slot):
             mine, lanes = slice(h * HEAD_DIM, (h + 1) * HEAD_DIM), tiles[t]
-            scores = nn(keys[:, mine], query[mine, lanes]) * (HEAD_DIM**-0.5 * LOG2E)
-            enc = jnp.exp2(scores - norm_ref[h : h + 1, lanes] * LOG2E)
+            enc = kept_ref[h, :, lanes]
             grad = nn(values[:, mine], mix[mine, lanes])
             encs[slot] = enc.astype(jnp.bfloat16)
             ds[slot] = (enc * (grad - columns[h : h + 1, lanes])).astype(jnp.bfloat16)
@@ -438,14 +433,13 @@
     scratch = [
         pltpu.VMEM((c, m), jnp.bfloat16),
         pltpu.VMEM((plan.ct_rows, m), jnp.bfloat16),
-        pltpu.VMEM((plan.points, c), jnp.bfloat16),
         pltpu.VMEM((c, plan.points), jnp.bfloat16),
         pltpu.VMEM((plan.points, c), jnp.bfloat16),
         pltpu.VMEM((SLOTS, plan.points, 2 * plan.block), jnp.bfloat16),
         pltpu.VMEM((SLOTS, plan.points, 2 * plan.block), jnp.bfloat16),
     ]
     flops = 10 * plan.points * m * c
-    args = (*lats, *pts, norm, *mixes, *(a for _, part in before for a in part))
+    args = (*lats, *pts, kept, *mixes, *(a for _, part in before for a in part))
     got = call(kernel, outs, args, scratch, flops)
     return got[:n_pts], got[n_pts:]
 
@@ -531,13 +525,14 @@
     norm = order_norm(plan, encoder_norm)
     block, dec_norm = turn_latents(plan, lat_slots)
     lats = to_plane(block)
-    cores = sum_cores(first_pass(plan, lats, pts, dec_norm, norm))
+    sums, kept = first_pass(plan, lats, pts, dec_norm, norm)
+    cores = sum_cores(sums)
     early, late = tuple(range(plan.heads))[:1], tuple(range(plan.heads))[1:]
     before = [(early, decoder_pass(plan, lats, pts, dec_norm, early))]
     sums = sum_chips(cores)
     before.append((late, decoder_pass(plan, lats, pts, dec_norm, late)))
     mixes = to_plane(reduce_mix(plan, sums))
-    pts_out, lat_out = encoder_pass(plan, lats, pts, norm, mixes, before)
+    pts_out, lat_out = encoder_pass(plan, lats, pts, kept, mixes, before)
     lat_out = sum_chips(sum_cores(lat_out))
     pts_out = over_group(pts_out)
     lat_rows = over_group(reduce_latents(plan, lat_out))

time: 86.5 us -> 83.8 us (0.969)
  waiting for transfers between devices: 33.5 us -> 32 us
    ppermute x40, waiting for transfers between devices: 33.5 us -> 32 us  [exchange(): return lax.ppermute(value, AXES, pairs)]
  transfers between devices with their start and end apart: 40 -> 40, of which waited for: 24 -> 24; matrix products, arithmetic and copies ran while one was open for 0% -> 0% of each run, Pallas kernels for 7% -> 8%
where the time goes in v5:
time: 83.8 us; the launch traced here: 83.6 us
  starting transfers between devices  35.3 us (42%)
  waiting for transfers between devices  32 us (38%)
  Pallas kernels  15.3 us (18%)
    ppermute x40, starting transfers between devices, exchange(): return lax.ppermute(value, AXES, pairs)  35.3 us
    ppermute x40, waiting for transfers between devices, exchange(): return lax.ppermute(value, AXES, pairs)  32 us
    pallas_call x13, Pallas kernels, call(): pl.pallas_call(kernel, out_shape=tuple(outs), in_specs=[pl.BlockSpec(memo...  15.3 us
  transfers between devices with their start and end apart: 40, of which 24 were waited for; matrix products, arithmetic and copies ran while one was open for 0% of the time, Pallas kernels for 8%

profile of v5, /device:TPU:0, one launch (start us, length us, event | category | flops | bytes accessed | tf_op | source)
XLA Modules:
  0.0 83.6 jit_solution(11879207150085331418)
XLA Ops:
  0.6 1.7 %shard_map.94 = (bf16[48,384]{1,0:T(8,128)(2,1)S(1)}, bf16[48,384]{1,0:T(8,128)(2,1)S(1)}, bf16[48,384]{1,0:T(8,128)(2,1)S(1)}, bf16[48,384]{1,0:T(8,128)(2,1)S(...) custom-call(bf16[32,768]{1,0:T(8,128)(2,1)} %refs_0_.2, ...), custom_call_target="tpu_custom_call" | custom-call | bytes 1431552 | tf_op jit(solution)/shard_map/pallas_call | solution.py:71
  2.3 3.1 %collective-permute-start = (bf16[48,384]{1,0:T(8,128)(2,1)S(1)}, bf16[48,384]{1,0:T(8,128)(2,1)S(1)}, u32[]{:S(2)}, u32[]{:S(2)}) collective-permute-start(bf16[48,384]{1,0:T(8,128)(2,1)S(1)} %get-tuple-element.53), channel_id=1, source_target_pairs={{0,2},{1,3},{2,0},{3,1},{4,6},{5,7},{6,4},{7,5},{8,10},{9,11},{10,... | collective-permute-start | bytes 110600 | tf_op jit(solution)/shard_map/ppermute | solution.py:65
  5.5 2.6 %collective-permute-start.1 = (bf16[48,384]{1,0:T(8,128)(2,1)S(1)}, bf16[48,384]{1,0:T(8,128)(2,1)S(1)}, u32[]{:S(2)}, u32[]{:S(2)}) collective-permute-start(bf16[48,384]{1,0:T(8,128)(2,1)S(1)} %get-tuple-element.54), channel_id=1, source_target_pairs={{0,4},{1,5},{2,6},{3,7},{4,0},{5,1},{6,2},{7,3},{8,12},{9,13},{10,... | collective-permute-start | bytes 110600 | tf_op jit(solution)/shard_map/ppermute | solution.py:65
  8.1 2.9 %collective-permute-done.1.refs_2_ = bf16[48,384]{1,0:T(8,128)(2,1)S(1)} collective-permute-done((bf16[48,384]{1,0:T(8,128)(2,1)S(1)}, bf16[48,384]{1,0:T(8,128)(2,1)S(1)}, u32[]{:S(2)}, u32[]{:S(2)}) %collective-permute-start.1) | collective-permute-done | bytes 36896 | tf_op jit(solution)/shard_map/ppermute | solution.py:65
  11.0 2.8 %collective-permute-done.2.refs_3_ = bf16[48,384]{1,0:T(8,128)(2,1)S(1)} collective-permute-done((bf16[48,384]{1,0:T(8,128)(2,1)S(1)}, bf16[48,384]{1,0:T(8,128)(2,1)S(1)}, u32[]{:S(2)}, u32[]{:S(2)}) %collective-permute-start.2) | collective-permute-done | bytes 36896 | tf_op jit(solution)/shard_map/ppermute | solution.py:65
  14.0 1.6 %collective-permute-start.3 = (bf16[384,128]{1,0:T(8,128)(2,1)S(1)}, bf16[384,128]{1,0:T(8,128)(2,1)S(1)}, u32[]{:S(2)}, u32[]{:S(2)}) collective-permute-start(bf16[384,128]{1,0:T(8,128)(2,1)S(1)} %get-tuple-element.56.refs_0_), channel_id=1, source_target_pairs={{0,1},{1,0},{2,3},{3,2},{4,5},{5,4},{6,7},{7,6},{8,9},{9,8},{10,11... | collective-permute-start | bytes 294920 | tf_op jit(solution)/shard_map/ppermute | solution.py:65
  15.6 1.5 %collective-permute-start.6 = (bf16[384,128]{1,0:T(8,128)(2,1)S(1)}, bf16[384,128]{1,0:T(8,128)(2,1)S(1)}, u32[]{:S(2)}, u32[]{:S(2)}) collective-permute-start(bf16[384,128]{1,0:T(8,128)(2,1)S(1)} %get-tuple-element.56.refs_0_), channel_id=1, source_target_pairs={{0,16},{1,17},{2,18},{3,19},{4,20},{5,21},{6,22},{7,23},{8,24},{9,... | collective-permute-start | bytes 294920 | tf_op jit(solution)/shard_map/ppermute | solution.py:65
  17.1 0.5 collective-permute-start.7
  17.6 1.1 %collective-permute-done.3.refs_1_ = bf16[384,128]{1,0:T(8,128)(2,1)S(1)} collective-permute-done((bf16[384,128]{1,0:T(8,128)(2,1)S(1)}, bf16[384,128]{1,0:T(8,128)(2,1)S(1)}, u32[]{:S(2)}, u32[]{:S(2)}) %collective-permute-start.3) | collective-permute-done | bytes 98336 | tf_op jit(solution)/shard_map/ppermute | solution.py:65
  18.7 3.3 %collective-permute-start.12 = (bf16[192,384]{1,0:T(8,128)(2,1)S(1)}, bf16[192,384]{1,0:T(8,128)(2,1)S(1)}, u32[]{:S(2)}, u32[]{:S(2)}) collective-permute-start(bf16[192,384]{1,0:T(8,128)(2,1)S(1)} %get-tuple-element.60), channel_id=1, source_target_pairs={{0,6},{1,7},{2,4},{3,5},{4,2},{5,3},{6,0},{7,1},{8,14},{9,15},{10,... | collective-permute-start | bytes 442376 | tf_op jit(solution)/shard_map/ppermute | solution.py:65
  22.0 0.9 %collective-permute-done.7.refs_5_ = bf16[384,128]{1,0:T(8,128)(2,1)S(1)} collective-permute-done((bf16[384,128]{1,0:T(8,128)(2,1)S(1)}, bf16[384,128]{1,0:T(8,128)(2,1)S(1)}, u32[]{:S(2)}, u32[]{:S(2)}) %collective-permute-start.7) | collective-permute-done | bytes 98336 | tf_op jit(solution)/shard_map/ppermute | solution.py:65
  23.4 1.3 %shard_map.96.refs_13_ = f32[3,1024]{1,0:T(4,128)S(1)} custom-call(f32[12,1024]{1,0:T(8,128)} %refs_0_.3), custom_call_target="tpu_custom_call" | custom-call | bytes 61440 | tf_op jit(solution)/shard_map/pallas_call | solution.py:71
  24.7 7.0 %collective-permute-done.11.refs_10_ = bf16[192,384]{1,0:T(8,128)(2,1)S(1)} collective-permute-done((bf16[192,384]{1,0:T(8,128)(2,1)S(1)}, bf16[192,384]{1,0:T(8,128)(2,1)S(1)}, u32[]{:S(2)}, u32[]{:S(2)}) %collective-permute-start.11) | collective-permute-done | bytes 147488 | tf_op jit(solution)/shard_map/ppermute | solution.py:65
  31.8 2.4 %shard_map.97 = (f32[384,128]{1,0:T(8,128)S(1)}, f32[384,128]{1,0:T(8,128)S(1)}, f32[384,128]{1,0:T(8,128)S(1)}, f32[384,128]{1,0:T(8,128)S(1)}, f32[384,128]{1,...) custom-call(bf16[384,128]{1,0:T(8,128)(2,1)S(1)} %get-tuple-element., ...), custom_call_target="tpu_custom_call" | custom-call | flops 603979776 | bytes 9515008 | tf_op jit(solution)/shard_map/pallas_call | solution.py:71
  34.2 0.5 collective-permute-start.14
  34.8 0.4 collective-permute-start.16
  35.2 0.4 collective-permute-done.13.refs_4_
  36.7 1.6 %collective-permute-start.17 = (f16[400,128]{1,0:T(8,128)(2,1)S(1)}, f16[400,128]{1,0:T(8,128)(2,1)S(1)}, u32[]{:S(2)}, u32[]{:S(2)}) collective-permute-start(f16[400,128]{1,0:T(8,128)(2,1)S(1)} %convert_element_type.36), channel_id=1, source_target_pairs={{0,1},{1,0},{2,3},{3,2},{4,5},{5,4},{6,7},{7,6},{8,9},{9,8},{10,11... | collective-permute-start | bytes 307208 | tf_op jit(solution)/shard_map/ppermute | solution.py:65
  38.3 1.6 %collective-permute-start.18 = (f16[400,128]{1,0:T(8,128)(2,1)S(1)}, f16[400,128]{1,0:T(8,128)(2,1)S(1)}, u32[]{:S(2)}, u32[]{:S(2)}) collective-permute-start(f16[400,128]{1,0:T(8,128)(2,1)S(1)} %convert_element_type.38), channel_id=1, source_target_pairs={{0,16},{1,17},{2,18},{3,19},{4,20},{5,21},{6,22},{7,23},{8,24},{9,... | collective-permute-start | bytes 307208 | tf_op jit(solution)/shard_map/ppermute | solution.py:65
  39.8 0.5 collective-permute-start.19
  40.4 1.4 %collective-permute-done.17 = f16[400,128]{1,0:T(8,128)(2,1)S(1)} collective-permute-done((f16[400,128]{1,0:T(8,128)(2,1)S(1)}, f16[400,128]{1,0:T(8,128)(2,1)S(1)}, u32[]{:S(2)}, u32[]{:S(2)}) %collective-permute-start.17) | collective-permute-done | bytes 102432 | tf_op jit(solution)/shard_map/ppermute | solution.py:65
  41.8 2.3 %collective-permute-done.18 = f16[400,128]{1,0:T(8,128)(2,1)S(1)} collective-permute-done((f16[400,128]{1,0:T(8,128)(2,1)S(1)}, f16[400,128]{1,0:T(8,128)(2,1)S(1)}, u32[]{:S(2)}, u32[]{:S(2)}) %collective-permute-start.18) | collective-permute-done | bytes 102432 | tf_op jit(solution)/shard_map/ppermute | solution.py:65
  44.0 1.4 %collective-permute-done.19 = f16[400,128]{1,0:T(8,128)(2,1)S(1)} collective-permute-done((f16[400,128]{1,0:T(8,128)(2,1)S(1)}, f16[400,128]{1,0:T(8,128)(2,1)S(1)}, u32[]{:S(2)}, u32[]{:S(2)}) %collective-permute-start.19) | collective-permute-done | bytes 102432 | tf_op jit(solution)/shard_map/ppermute | solution.py:65
  45.6 1.3 %collective-permute-start.20 = (bf16[208,128]{1,0:T(8,128)(2,1)S(1)}, bf16[208,128]{1,0:T(8,128)(2,1)S(1)}, u32[]{:S(2)}, u32[]{:S(2)}) collective-permute-start(bf16[208,128]{1,0:T(8,128)(2,1)S(1)} %shard_map.99.refs_13_), channel_id=1, source_target_pairs={{0,1},{1,0},{2,3},{3,2},{4,5},{5,4},{6,7},{7,6},{8,9},{9,8},{10,11... | collective-permute-start | bytes 159752 | tf_op jit(solution)/shard_map/ppermute | solution.py:65
  46.9 1.5 %collective-permute-start.23 = (bf16[208,128]{1,0:T(8,128)(2,1)S(1)}, bf16[208,128]{1,0:T(8,128)(2,1)S(1)}, u32[]{:S(2)}, u32[]{:S(2)}) collective-permute-start(bf16[208,128]{1,0:T(8,128)(2,1)S(1)} %shard_map.99.refs_13_), channel_id=1, source_target_pairs={{0,16},{1,17},{2,18},{3,19},{4,20},{5,21},{6,22},{7,23},{8,24},{9,... | collective-permute-start | bytes 159752 | tf_op jit(solution)/shard_map/ppermute | solution.py:65
  48.4 0.7 collective-permute-start.24
  49.1 0.6 collective-permute-done.20.refs_14_
  49.8 1.3 %collective-permute-done.23.refs_17_ = bf16[208,128]{1,0:T(8,128)(2,1)S(1)} collective-permute-done((bf16[208,128]{1,0:T(8,128)(2,1)S(1)}, bf16[208,128]{1,0:T(8,128)(2,1)S(1)}, u32[]{:S(2)}, u32[]{:S(2)}) %collective-permute-start.23) | collective-permute-done | bytes 53280 | tf_op jit(solution)/shard_map/ppermute | solution.py:65
  51.0 2.4 %collective-permute-done.24.refs_18_ = bf16[208,128]{1,0:T(8,128)(2,1)S(1)} collective-permute-done((bf16[208,128]{1,0:T(8,128)(2,1)S(1)}, bf16[208,128]{1,0:T(8,128)(2,1)S(1)}, u32[]{:S(2)}, u32[]{:S(2)}) %collective-permute-start.24) | collective-permute-done | bytes 53280 | tf_op jit(solution)/shard_map/ppermute | solution.py:65
  53.4 1.4 %shard_map.100 = (f32[64,512]{1,0:T(8,128)S(1)}, f32[64,1024]{1,0:T(8,128)S(1)}) custom-call(bf16[384,128]{1,0:T(8,128)(2,1)S(1)} %get-tuple-element.56.refs_0_, bf16[384,128]{1,0:T(8,128)(2,1)S(1)} %collective-permute-done.3.refs_1_, bf16[384,128]{1,0:T(8,128)(2,1)S(1)} %collective-permute-done.4.refs_2_, ...), custom_call_target="tpu_custom_call" | custom-call | flops 268435456 | bytes 2031616 | tf_op jit(solution)/shard_map/pallas_call | solution.py:71
  54.8 2.7 %shard_map.101 = (f32[128,512]{1,0:T(8,128)S(1)}, f32[128,1024]{1,0:T(8,128)S(1)}) custom-call(bf16[384,128]{1,0:T(8,128)(2,1)S(1)} %get-tuple-element.56.refs_0_, bf16[384,128]{1,0:T(8,128)(2,1)S(1)} %collective-permute-done.3.refs_1_, bf16[384,128]{1,0:T(8,128)(2,1)S(1)} %collective-permute-done.4.refs_2_, ...), custom_call_target="tpu_custom_call" | custom-call | flops 536870912 | bytes 2424832 | tf_op jit(solution)/shard_map/pallas_call | solution.py:71
  57.6 3.5 %shard_map.102 = (bf16[128,384]{1,0:T(8,128)(2,1)S(1)}, bf16[128,384]{1,0:T(8,128)(2,1)S(1)}, bf16[128,384]{1,0:T(8,128)(2,1)S(1)}, bf16[128,384]{1,0:T(8,128)(2...) custom-call(bf16[384,128]{1,0:T(8,128)(2,1)S(1)} %get-tuple-element., ...), custom_call_target="tpu_custom_call" | custom-call | flops 1006632960 | bytes 10452992 | tf_op jit(solution)/shard_map/pallas_call | solution.py:71
  61.0 0.6 collective-permute-start.30
  61.7 0.4 collective-permute-start.32
  63.5 0.6 collective-permute-start.34
  64.1 2.5 %collective-permute-start.27 = (bf16[128,384]{1,0:T(8,128)(2,1)S(1)}, bf16[128,384]{1,0:T(8,128)(2,1)S(1)}, u32[]{:S(2)}, u32[]{:S(2)}) collective-permute-start(bf16[128,384]{1,0:T(8,128)(2,1)S(1)} %get-tuple-element.80), channel_id=1, source_target_pairs={{0,2},{1,3},{2,0},{3,1},{4,6},{5,7},{6,4},{7,5},{8,10},{9,11},{10,... | collective-permute-start | bytes 294920 | tf_op jit(solution)/shard_map/ppermute | solution.py:65
  66.6 2.4 %collective-permute-start.29 = (bf16[128,384]{1,0:T(8,128)(2,1)S(1)}, bf16[128,384]{1,0:T(8,128)(2,1)S(1)}, u32[]{:S(2)}, u32[]{:S(2)}) collective-permute-start(bf16[128,384]{1,0:T(8,128)(2,1)S(1)} %get-tuple-element.82), channel_id=1, source_target_pairs={{0,6},{1,7},{2,4},{3,5},{4,2},{5,3},{6,0},{7,1},{8,14},{9,15},{10,... | collective-permute-start | bytes 294920 | tf_op jit(solution)/shard_map/ppermute | solution.py:65
  69.0 0.8 collective-permute-start.35
  69.8 2.3 %collective-permute-start.36 = (f16[208,128]{1,0:T(8,128)(2,1)S(1)}, f16[208,128]{1,0:T(8,128)(2,1)S(1)}, u32[]{:S(2)}, u32[]{:S(2)}) collective-permute-start(f16[208,128]{1,0:T(8,128)(2,1)S(1)} %convert_element_type.46), channel_id=1, source_target_pairs={{0,17},{1,16},{2,19},{3,18},{4,21},{5,20},{6,23},{7,22},{8,25},{9,... | collective-permute-start | bytes 159752 | tf_op jit(solution)/shard_map/ppermute | solution.py:65
  72.1 1.3 %collective-permute-done.35 = f16[208,128]{1,0:T(8,128)(2,1)S(1)} collective-permute-done((f16[208,128]{1,0:T(8,128)(2,1)S(1)}, f16[208,128]{1,0:T(8,128)(2,1)S(1)}, u32[]{:S(2)}, u32[]{:S(2)}) %collective-permute-start.35) | collective-permute-done | bytes 53280 | tf_op jit(solution)/shard_map/ppermute | solution.py:65
  73.3 1.6 %collective-permute-done.36 = f16[208,128]{1,0:T(8,128)(2,1)S(1)} collective-permute-done((f16[208,128]{1,0:T(8,128)(2,1)S(1)}, f16[208,128]{1,0:T(8,128)(2,1)S(1)}, u32[]{:S(2)}, u32[]{:S(2)}) %collective-permute-start.36) | collective-permute-done | bytes 53280 | tf_op jit(solution)/shard_map/ppermute | solution.py:65
  75.1 1.2 %collective-permute-start.37 = (f32[48,128]{1,0:T(8,128)S(1)}, f32[48,128]{1,0:T(8,128)S(1)}, u32[]{:S(2)}, u32[]{:S(2)}) collective-permute-start(f32[48,128]{1,0:T(8,128)S(1)} %get-tuple-element.98), channel_id=1, source_target_pairs={{0,2},{1,3},{2,0},{3,1},{4,6},{5,7},{6,4},{7,5},{8,10},{9,11},{10,... | collective-permute-start | bytes 73736 | tf_op jit(solution)/shard_map/ppermute | solution.py:65
  76.3 0.9 %collective-permute-start.38 = (f32[48,128]{1,0:T(8,128)S(1)}, f32[48,128]{1,0:T(8,128)S(1)}, u32[]{:S(2)}, u32[]{:S(2)}) collective-permute-start(f32[48,128]{1,0:T(8,128)S(1)} %get-tuple-element.99), channel_id=1, source_target_pairs={{0,4},{1,5},{2,6},{3,7},{4,0},{5,1},{6,2},{7,3},{8,12},{9,13},{10,... | collective-permute-start | bytes 73736 | tf_op jit(solution)/shard_map/ppermute | solution.py:65
  77.2 2.4 %collective-permute-start.39 = (f32[48,128]{1,0:T(8,128)S(1)}, f32[48,128]{1,0:T(8,128)S(1)}, u32[]{:S(2)}, u32[]{:S(2)}) collective-permute-start(f32[48,128]{1,0:T(8,128)S(1)} %get-tuple-element.100), channel_id=1, source_target_pairs={{0,6},{1,7},{2,4},{3,5},{4,2},{5,3},{6,0},{7,1},{8,14},{9,15},{10,... | collective-permute-start | bytes 73736 | tf_op jit(solution)/shard_map/ppermute | solution.py:65
  79.5 1.0 %shard_map.103 = (bf16[128,768]{1,0:T(8,128)(2,1)}, bf16[128,768]{1,0:T(8,128)(2,1)}) custom-call(bf16[128,384]{1,0:T(8,128)(2,1)S(1)} %get-tuple-element.79.refs_0_, bf16[128,384]{1,0:T(8,128)(2,1)S(1)} %collective-permute-done.27.refs_1_, bf16[128,384]{1,0:T(8,128)(2,1)S(1)} %collective-permute-done.28.refs_2_, ...), custom_call_target="tpu_custom_call" | custom-call | bytes 786432 | tf_op jit(solution)/shard_map/pallas_call | solution.py:71
  80.5 0.5 collective-permute-done.38.refs_2_
  81.0 1.8 %collective-permute-done.39.refs_3_ = f32[48,128]{1,0:T(8,128)S(1)} collective-permute-done((f32[48,128]{1,0:T(8,128)S(1)}, f32[48,128]{1,0:T(8,128)S(1)}, u32[]{:S(2)}, u32[]{:S(2)}) %collective-permute-start.39) | collective-permute-done | bytes 24608 | tf_op jit(solution)/shard_map/ppermute | solution.py:65
  82.8 0.8 shard_map.106
  (57 shorter events, 3.7 us)
Async XLA Ops:
  2.3 5.7 %collective-permute-start = (bf16[48,384]{1,0:T(8,128)(2,1)S(1)}, bf16[48,384]{1,0:T(8,128)(2,1)S(1)}, u32[]{:S(2)}, u32[]{:S(2)}) collective-permute-start(bf16[48,384]{1,0:T(8,128)(2,1)S(1)} %get-tuple-element.53), channel_id=1, source_target_pairs={{0,2},{1,3},{2,0},{3,1},{4,6},{5,7},{6,4},{7,5},{8,10},{9,11},{10,... | collective-permute-start | bytes 110600 | tf_op jit(solution)/shard_map/ppermute | solution.py:65
  5.5 5.5 %collective-permute-start.1 = (bf16[48,384]{1,0:T(8,128)(2,1)S(1)}, bf16[48,384]{1,0:T(8,128)(2,1)S(1)}, u32[]{:S(2)}, u32[]{:S(2)}) collective-permute-start(bf16[48,384]{1,0:T(8,128)(2,1)S(1)} %get-tuple-element.54), channel_id=1, source_target_pairs={{0,4},{1,5},{2,6},{3,7},{4,0},{5,1},{6,2},{7,3},{8,12},{9,13},{10,... | collective-permute-start | bytes 110600 | tf_op jit(solution)/shard_map/ppermute | solution.py:65
  8.1 5.8 %collective-permute-start.2 = (bf16[48,384]{1,0:T(8,128)(2,1)S(1)}, bf16[48,384]{1,0:T(8,128)(2,1)S(1)}, u32[]{:S(2)}, u32[]{:S(2)}) collective-permute-start(bf16[48,384]{1,0:T(8,128)(2,1)S(1)} %get-tuple-element.55), channel_id=1, source_target_pairs={{0,6},{1,7},{2,4},{3,5},{4,2},{5,3},{6,0},{7,1},{8,14},{9,15},{10,... | collective-permute-start | bytes 110600 | tf_op jit(solution)/shard_map/ppermute | solution.py:65
  14.0 4.7 %collective-permute-start.3 = (bf16[384,128]{1,0:T(8,128)(2,1)S(1)}, bf16[384,128]{1,0:T(8,128)(2,1)S(1)}, u32[]{:S(2)}, u32[]{:S(2)}) collective-permute-start(bf16[384,128]{1,0:T(8,128)(2,1)S(1)} %get-tuple-element.56.refs_0_), channel_id=1, source_target_pairs={{0,1},{1,0},{2,3},{3,2},{4,5},{5,4},{6,7},{7,6},{8,9},{9,8},{10,11... | collective-permute-start | bytes 294920 | tf_op jit(solution)/shard_map/ppermute | solution.py:65
  15.6 3.1 %collective-permute-start.4 = (bf16[384,128]{1,0:T(8,128)(2,1)S(1)}, bf16[384,128]{1,0:T(8,128)(2,1)S(1)}, u32[]{:S(2)}, u32[]{:S(2)}) collective-permute-start(bf16[384,128]{1,0:T(8,128)(2,1)S(1)} %get-tuple-element.56.refs_0_), channel_id=1, source_target_pairs={{0,8},{1,9},{2,10},{3,11},{4,12},{5,13},{6,14},{7,15},{8,0},{9,1},... | collective-permute-start | bytes 294920 | tf_op jit(solution)/shard_map/ppermute | solution.py:65
  15.6 7.5 %collective-permute-start.10 = (bf16[192,384]{1,0:T(8,128)(2,1)S(1)}, bf16[192,384]{1,0:T(8,128)(2,1)S(1)}, u32[]{:S(2)}, u32[]{:S(2)}) collective-permute-start(bf16[192,384]{1,0:T(8,128)(2,1)S(1)} %get-tuple-element.58), channel_id=1, source_target_pairs={{0,2},{1,3},{2,0},{3,1},{4,6},{5,7},{6,4},{7,5},{8,10},{9,11},{10,... | collective-permute-start | bytes 442376 | tf_op jit(solution)/shard_map/ppermute | solution.py:65
  15.6 6.4 %collective-permute-start.6 = (bf16[384,128]{1,0:T(8,128)(2,1)S(1)}, bf16[384,128]{1,0:T(8,128)(2,1)S(1)}, u32[]{:S(2)}, u32[]{:S(2)}) collective-permute-start(bf16[384,128]{1,0:T(8,128)(2,1)S(1)} %get-tuple-element.56.refs_0_), channel_id=1, source_target_pairs={{0,16},{1,17},{2,18},{3,19},{4,20},{5,21},{6,22},{7,23},{8,24},{9,... | collective-permute-start | bytes 294920 | tf_op jit(solution)/shard_map/ppermute | solution.py:65
  17.1 5.8 %collective-permute-start.7 = (bf16[384,128]{1,0:T(8,128)(2,1)S(1)}, bf16[384,128]{1,0:T(8,128)(2,1)S(1)}, u32[]{:S(2)}, u32[]{:S(2)}) collective-permute-start(bf16[384,128]{1,0:T(8,128)(2,1)S(1)} %get-tuple-element.56.refs_0_), channel_id=1, source_target_pairs={{0,17},{1,16},{2,19},{3,18},{4,21},{5,20},{6,23},{7,22},{8,25},{9,... | collective-permute-start | bytes 294920 | tf_op jit(solution)/shard_map/ppermute | solution.py:65
  18.7 13.1 %collective-permute-start.11 = (bf16[192,384]{1,0:T(8,128)(2,1)S(1)}, bf16[192,384]{1,0:T(8,128)(2,1)S(1)}, u32[]{:S(2)}, u32[]{:S(2)}) collective-permute-start(bf16[192,384]{1,0:T(8,128)(2,1)S(1)} %get-tuple-element.59), channel_id=1, source_target_pairs={{0,4},{1,5},{2,6},{3,7},{4,0},{5,1},{6,2},{7,3},{8,12},{9,13},{10,... | collective-permute-start | bytes 442376 | tf_op jit(solution)/shard_map/ppermute | solution.py:65
  18.7 13.1 %collective-permute-start.12 = (bf16[192,384]{1,0:T(8,128)(2,1)S(1)}, bf16[192,384]{1,0:T(8,128)(2,1)S(1)}, u32[]{:S(2)}, u32[]{:S(2)}) collective-permute-start(bf16[192,384]{1,0:T(8,128)(2,1)S(1)} %get-tuple-element.60), channel_id=1, source_target_pairs={{0,6},{1,7},{2,4},{3,5},{4,2},{5,3},{6,0},{7,1},{8,14},{9,15},{10,... | collective-permute-start | bytes 442376 | tf_op jit(solution)/shard_map/ppermute | solution.py:65
  21.9 9.8 %collective-permute-start.5 = (bf16[384,128]{1,0:T(8,128)(2,1)S(1)}, bf16[384,128]{1,0:T(8,128)(2,1)S(1)}, u32[]{:S(2)}, u32[]{:S(2)}) collective-permute-start(bf16[384,128]{1,0:T(8,128)(2,1)S(1)} %collective-permute-done.3.refs_1_), channel_id=1, source_target_pairs={{0,8},{1,9},{2,10},{3,11},{4,12},{5,13},{6,14},{7,15},{8,0},{9,1},... | collective-permute-start | bytes 294920 | tf_op jit(solution)/shard_map/ppermute | solution.py:65
  22.9 8.9 %collective-permute-start.8 = (bf16[384,128]{1,0:T(8,128)(2,1)S(1)}, bf16[384,128]{1,0:T(8,128)(2,1)S(1)}, u32[]{:S(2)}, u32[]{:S(2)}) collective-permute-start(bf16[384,128]{1,0:T(8,128)(2,1)S(1)} %collective-permute-done.6.refs_4_), channel_id=1, source_target_pairs={{0,8},{1,9},{2,10},{3,11},{4,12},{5,13},{6,14},{7,15},{8,0},{9,1},... | collective-permute-start | bytes 294920 | tf_op jit(solution)/shard_map/ppermute | solution.py:65
  23.1 8.7 %collective-permute-start.9 = (bf16[384,128]{1,0:T(8,128)(2,1)S(1)}, bf16[384,128]{1,0:T(8,128)(2,1)S(1)}, u32[]{:S(2)}, u32[]{:S(2)}) collective-permute-start(bf16[384,128]{1,0:T(8,128)(2,1)S(1)} %collective-permute-done.7.refs_5_), channel_id=1, source_target_pairs={{0,8},{1,9},{2,10},{3,11},{4,12},{5,13},{6,14},{7,15},{8,0},{9,1},... | collective-permute-start | bytes 294920 | tf_op jit(solution)/shard_map/ppermute | solution.py:65
  34.2 1.5 %collective-permute-start.13 = (f32[384,128]{1,0:T(8,128)S(1)}, f32[384,128]{1,0:T(8,128)S(1)}, u32[]{:S(2)}, u32[]{:S(2)}) collective-permute-start(f32[384,128]{1,0:T(8,128)S(1)} %get-tuple-element.67), channel_id=1, source_target_pairs={{0,8},{1,9},{2,10},{3,11},{4,12},{5,13},{6,14},{7,15},{8,0},{9,1},... | collective-permute-start | bytes 589832 | tf_op jit(solution)/shard_map/ppermute | solution.py:65
  34.2 1.7 %collective-permute-start.14 = (f32[384,128]{1,0:T(8,128)S(1)}, f32[384,128]{1,0:T(8,128)S(1)}, u32[]{:S(2)}, u32[]{:S(2)}) collective-permute-start(f32[384,128]{1,0:T(8,128)S(1)} %get-tuple-element.68), channel_id=1, source_target_pairs={{0,8},{1,9},{2,10},{3,11},{4,12},{5,13},{6,14},{7,15},{8,0},{9,1},... | collective-permute-start | bytes 589832 | tf_op jit(solution)/shard_map/ppermute | solution.py:65
  34.7 1.5 %collective-permute-start.15 = (f32[384,128]{1,0:T(8,128)S(1)}, f32[384,128]{1,0:T(8,128)S(1)}, u32[]{:S(2)}, u32[]{:S(2)}) collective-permute-start(f32[384,128]{1,0:T(8,128)S(1)} %get-tuple-element.69), channel_id=1, source_target_pairs={{0,8},{1,9},{2,10},{3,11},{4,12},{5,13},{6,14},{7,15},{8,0},{9,1},... | collective-permute-start | bytes 589832 | tf_op jit(solution)/shard_map/ppermute | solution.py:65
  34.8 1.7 %collective-permute-start.16 = (f32[384,128]{1,0:T(8,128)S(1)}, f32[384,128]{1,0:T(8,128)S(1)}, u32[]{:S(2)}, u32[]{:S(2)}) collective-permute-start(f32[384,128]{1,0:T(8,128)S(1)} %get-tuple-element.70), channel_id=1, source_target_pairs={{0,8},{1,9},{2,10},{3,11},{4,12},{5,13},{6,14},{7,15},{8,0},{9,1},... | collective-permute-start | bytes 589832 | tf_op jit(solution)/shard_map/ppermute | solution.py:65
  36.7 5.1 %collective-permute-start.17 = (f16[400,128]{1,0:T(8,128)(2,1)S(1)}, f16[400,128]{1,0:T(8,128)(2,1)S(1)}, u32[]{:S(2)}, u32[]{:S(2)}) collective-permute-start(f16[400,128]{1,0:T(8,128)(2,1)S(1)} %convert_element_type.36), channel_id=1, source_target_pairs={{0,1},{1,0},{2,3},{3,2},{4,5},{5,4},{6,7},{7,6},{8,9},{9,8},{10,11... | collective-permute-start | bytes 307208 | tf_op jit(solution)/shard_map/ppermute | solution.py:65
  38.3 5.8 %collective-permute-start.18 = (f16[400,128]{1,0:T(8,128)(2,1)S(1)}, f16[400,128]{1,0:T(8,128)(2,1)S(1)}, u32[]{:S(2)}, u32[]{:S(2)}) collective-permute-start(f16[400,128]{1,0:T(8,128)(2,1)S(1)} %convert_element_type.38), channel_id=1, source_target_pairs={{0,16},{1,17},{2,18},{3,19},{4,20},{5,21},{6,22},{7,23},{8,24},{9,... | collective-permute-start | bytes 307208 | tf_op jit(solution)/shard_map/ppermute | solution.py:65
  39.8 5.6 %collective-permute-start.19 = (f16[400,128]{1,0:T(8,128)(2,1)S(1)}, f16[400,128]{1,0:T(8,128)(2,1)S(1)}, u32[]{:S(2)}, u32[]{:S(2)}) collective-permute-start(f16[400,128]{1,0:T(8,128)(2,1)S(1)} %convert_element_type.40), channel_id=1, source_target_pairs={{0,17},{1,16},{2,19},{3,18},{4,21},{5,20},{6,23},{7,22},{8,25},{9,... | collective-permute-start | bytes 307208 | tf_op jit(solution)/shard_map/ppermute | solution.py:65
  45.6 4.2 %collective-permute-start.20 = (bf16[208,128]{1,0:T(8,128)(2,1)S(1)}, bf16[208,128]{1,0:T(8,128)(2,1)S(1)}, u32[]{:S(2)}, u32[]{:S(2)}) collective-permute-start(bf16[208,128]{1,0:T(8,128)(2,1)S(1)} %shard_map.99.refs_13_), channel_id=1, source_target_pairs={{0,1},{1,0},{2,3},{3,2},{4,5},{5,4},{6,7},{7,6},{8,9},{9,8},{10,11... | collective-permute-start | bytes 159752 | tf_op jit(solution)/shard_map/ppermute | solution.py:65
  46.9 4.1 %collective-permute-start.23 = (bf16[208,128]{1,0:T(8,128)(2,1)S(1)}, bf16[208,128]{1,0:T(8,128)(2,1)S(1)}, u32[]{:S(2)}, u32[]{:S(2)}) collective-permute-start(bf16[208,128]{1,0:T(8,128)(2,1)S(1)} %shard_map.99.refs_13_), channel_id=1, source_target_pairs={{0,16},{1,17},{2,18},{3,19},{4,20},{5,21},{6,22},{7,23},{8,24},{9,... | collective-permute-start | bytes 159752 | tf_op jit(solution)/shard_map/ppermute | solution.py:65
  48.4 5.0 %collective-permute-start.24 = (bf16[208,128]{1,0:T(8,128)(2,1)S(1)}, bf16[208,128]{1,0:T(8,128)(2,1)S(1)}, u32[]{:S(2)}, u32[]{:S(2)}) collective-permute-start(bf16[208,128]{1,0:T(8,128)(2,1)S(1)} %shard_map.99.refs_13_), channel_id=1, source_target_pairs={{0,17},{1,16},{2,19},{3,18},{4,21},{5,20},{6,23},{7,22},{8,25},{9,... | collective-permute-start | bytes 159752 | tf_op jit(solution)/shard_map/ppermute | solution.py:65
  49.1 8.4 %collective-permute-start.21 = (bf16[208,128]{1,0:T(8,128)(2,1)S(1)}, bf16[208,128]{1,0:T(8,128)(2,1)S(1)}, u32[]{:S(2)}, u32[]{:S(2)}) collective-permute-start(bf16[208,128]{1,0:T(8,128)(2,1)S(1)} %shard_map.99.refs_13_), channel_id=1, source_target_pairs={{0,8},{1,9},{2,10},{3,11},{4,12},{5,13},{6,14},{7,15},{8,0},{9,1},... | collective-permute-start | bytes 159752 | tf_op jit(solution)/shard_map/ppermute | solution.py:65
  49.8 7.8 %collective-permute-start.22 = (bf16[208,128]{1,0:T(8,128)(2,1)S(1)}, bf16[208,128]{1,0:T(8,128)(2,1)S(1)}, u32[]{:S(2)}, u32[]{:S(2)}) collective-permute-start(bf16[208,128]{1,0:T(8,128)(2,1)S(1)} %collective-permute-done.20.refs_14_), channel_id=1, source_target_pairs={{0,8},{1,9},{2,10},{3,11},{4,12},{5,13},{6,14},{7,15},{8,0},{9,1},... | collective-permute-start | bytes 159752 | tf_op jit(solution)/shard_map/ppermute | solution.py:65
  51.0 6.5 %collective-permute-start.25 = (bf16[208,128]{1,0:T(8,128)(2,1)S(1)}, bf16[208,128]{1,0:T(8,128)(2,1)S(1)}, u32[]{:S(2)}, u32[]{:S(2)}) collective-permute-start(bf16[208,128]{1,0:T(8,128)(2,1)S(1)} %collective-permute-done.23.refs_17_), channel_id=1, source_target_pairs={{0,8},{1,9},{2,10},{3,11},{4,12},{5,13},{6,14},{7,15},{8,0},{9,1},... | collective-permute-start | bytes 159752 | tf_op jit(solution)/shard_map/ppermute | solution.py:65
  53.4 4.1 %collective-permute-start.26 = (bf16[208,128]{1,0:T(8,128)(2,1)S(1)}, bf16[208,128]{1,0:T(8,128)(2,1)S(1)}, u32[]{:S(2)}, u32[]{:S(2)}) collective-permute-start(bf16[208,128]{1,0:T(8,128)(2,1)S(1)} %collective-permute-done.24.refs_18_), channel_id=1, source_target_pairs={{0,8},{1,9},{2,10},{3,11},{4,12},{5,13},{6,14},{7,15},{8,0},{9,1},... | collective-permute-start | bytes 159752 | tf_op jit(solution)/shard_map/ppermute | solution.py:65
  61.0 1.5 %collective-permute-start.30 = (f32[192,128]{1,0:T(8,128)S(1)}, f32[192,128]{1,0:T(8,128)S(1)}, u32[]{:S(2)}, u32[]{:S(2)}) collective-permute-start(f32[192,128]{1,0:T(8,128)S(1)} %get-tuple-element.89), channel_id=1, source_target_pairs={{0,8},{1,9},{2,10},{3,11},{4,12},{5,13},{6,14},{7,15},{8,0},{9,1},... | collective-permute-start | bytes 294920 | tf_op jit(solution)/shard_map/ppermute | solution.py:65
  61.6 1.3 %collective-permute-start.31 = (f32[192,128]{1,0:T(8,128)S(1)}, f32[192,128]{1,0:T(8,128)S(1)}, u32[]{:S(2)}, u32[]{:S(2)}) collective-permute-start(f32[192,128]{1,0:T(8,128)S(1)} %get-tuple-element.90), channel_id=1, source_target_pairs={{0,8},{1,9},{2,10},{3,11},{4,12},{5,13},{6,14},{7,15},{8,0},{9,1},... | collective-permute-start | bytes 294920 | tf_op jit(solution)/shard_map/ppermute | solution.py:65
  61.7 1.4 %collective-permute-start.32 = (f32[192,128]{1,0:T(8,128)S(1)}, f32[192,128]{1,0:T(8,128)S(1)}, u32[]{:S(2)}, u32[]{:S(2)}) collective-permute-start(f32[192,128]{1,0:T(8,128)S(1)} %get-tuple-element.91), channel_id=1, source_target_pairs={{0,8},{1,9},{2,10},{3,11},{4,12},{5,13},{6,14},{7,15},{8,0},{9,1},... | collective-permute-start | bytes 294920 | tf_op jit(solution)/shard_map/ppermute | solution.py:65
  62.1 1.3 %collective-permute-start.33 = (f32[192,128]{1,0:T(8,128)S(1)}, f32[192,128]{1,0:T(8,128)S(1)}, u32[]{:S(2)}, u32[]{:S(2)}) collective-permute-start(f32[192,128]{1,0:T(8,128)S(1)} %get-tuple-element.92), channel_id=1, source_target_pairs={{0,8},{1,9},{2,10},{3,11},{4,12},{5,13},{6,14},{7,15},{8,0},{9,1},... | collective-permute-start | bytes 294920 | tf_op jit(solution)/shard_map/ppermute | solution.py:65
  63.5 6.3 %collective-permute-start.34 = (f16[208,128]{1,0:T(8,128)(2,1)S(1)}, f16[208,128]{1,0:T(8,128)(2,1)S(1)}, u32[]{:S(2)}, u32[]{:S(2)}) collective-permute-start(f16[208,128]{1,0:T(8,128)(2,1)S(1)} %convert_element_type.42), channel_id=1, source_target_pairs={{0,1},{1,0},{2,3},{3,2},{4,5},{5,4},{6,7},{7,6},{8,9},{9,8},{10,11... | collective-permute-start | bytes 159752 | tf_op jit(solution)/shard_map/ppermute | solution.py:65
  64.1 13.1 %collective-permute-start.27 = (bf16[128,384]{1,0:T(8,128)(2,1)S(1)}, bf16[128,384]{1,0:T(8,128)(2,1)S(1)}, u32[]{:S(2)}, u32[]{:S(2)}) collective-permute-start(bf16[128,384]{1,0:T(8,128)(2,1)S(1)} %get-tuple-element.80), channel_id=1, source_target_pairs={{0,2},{1,3},{2,0},{3,1},{4,6},{5,7},{6,4},{7,5},{8,10},{9,11},{10,... | collective-permute-start | bytes 294920 | tf_op jit(solution)/shard_map/ppermute | solution.py:65
  66.6 13.0 %collective-permute-start.28 = (bf16[128,384]{1,0:T(8,128)(2,1)S(1)}, bf16[128,384]{1,0:T(8,128)(2,1)S(1)}, u32[]{:S(2)}, u32[]{:S(2)}) collective-permute-start(bf16[128,384]{1,0:T(8,128)(2,1)S(1)} %get-tuple-element.81), channel_id=1, source_target_pairs={{0,4},{1,5},{2,6},{3,7},{4,0},{5,1},{6,2},{7,3},{8,12},{9,13},{10,... | collective-permute-start | bytes 294920 | tf_op jit(solution)/shard_map/ppermute | solution.py:65
  66.6 13.0 %collective-permute-start.29 = (bf16[128,384]{1,0:T(8,128)(2,1)S(1)}, bf16[128,384]{1,0:T(8,128)(2,1)S(1)}, u32[]{:S(2)}, u32[]{:S(2)}) collective-permute-start(bf16[128,384]{1,0:T(8,128)(2,1)S(1)} %get-tuple-element.82), channel_id=1, source_target_pairs={{0,6},{1,7},{2,4},{3,5},{4,2},{5,3},{6,0},{7,1},{8,14},{9,15},{10,... | collective-permute-start | bytes 294920 | tf_op jit(solution)/shard_map/ppermute | solution.py:65
  69.0 4.4 %collective-permute-start.35 = (f16[208,128]{1,0:T(8,128)(2,1)S(1)}, f16[208,128]{1,0:T(8,128)(2,1)S(1)}, u32[]{:S(2)}, u32[]{:S(2)}) collective-permute-start(f16[208,128]{1,0:T(8,128)(2,1)S(1)} %convert_element_type.44), channel_id=1, source_target_pairs={{0,16},{1,17},{2,18},{3,19},{4,20},{5,21},{6,22},{7,23},{8,24},{9,... | collective-permute-start | bytes 159752 | tf_op jit(solution)/shard_map/ppermute | solution.py:65
  69.8 5.1 %collective-permute-start.36 = (f16[208,128]{1,0:T(8,128)(2,1)S(1)}, f16[208,128]{1,0:T(8,128)(2,1)S(1)}, u32[]{:S(2)}, u32[]{:S(2)}) collective-permute-start(f16[208,128]{1,0:T(8,128)(2,1)S(1)} %convert_element_type.46), channel_id=1, source_target_pairs={{0,17},{1,16},{2,19},{3,18},{4,21},{5,20},{6,23},{7,22},{8,25},{9,... | collective-permute-start | bytes 159752 | tf_op jit(solution)/shard_map/ppermute | solution.py:65
  75.1 5.4 %collective-permute-start.37 = (f32[48,128]{1,0:T(8,128)S(1)}, f32[48,128]{1,0:T(8,128)S(1)}, u32[]{:S(2)}, u32[]{:S(2)}) collective-permute-start(f32[48,128]{1,0:T(8,128)S(1)} %get-tuple-element.98), channel_id=1, source_target_pairs={{0,2},{1,3},{2,0},{3,1},{4,6},{5,7},{6,4},{7,5},{8,10},{9,11},{10,... | collective-permute-start | bytes 73736 | tf_op jit(solution)/shard_map/ppermute | solution.py:65
  76.3 4.7 %collective-permute-start.38 = (f32[48,128]{1,0:T(8,128)S(1)}, f32[48,128]{1,0:T(8,128)S(1)}, u32[]{:S(2)}, u32[]{:S(2)}) collective-permute-start(f32[48,128]{1,0:T(8,128)S(1)} %get-tuple-element.99), channel_id=1, source_target_pairs={{0,4},{1,5},{2,6},{3,7},{4,0},{5,1},{6,2},{7,3},{8,12},{9,13},{10,... | collective-permute-start | bytes 73736 | tf_op jit(solution)/shard_map/ppermute | solution.py:65
  77.2 5.6 %collective-permute-start.39 = (f32[48,128]{1,0:T(8,128)S(1)}, f32[48,128]{1,0:T(8,128)S(1)}, u32[]{:S(2)}, u32[]{:S(2)}) collective-permute-start(f32[48,128]{1,0:T(8,128)S(1)} %get-tuple-element.100), channel_id=1, source_target_pairs={{0,6},{1,7},{2,4},{3,5},{4,2},{5,3},{6,0},{7,1},{8,14},{9,15},{10,... | collective-permute-start | bytes 73736 | tf_op jit(solution)/shard_map/ppermute | solution.py:65

commit v6 on v5

--- a/solution.py
+++ b/solution.py
@@ -224,12 +224,19 @@
         outs[at // plan.block][rows, :] = value[:, at - lanes.start : at - lanes.start + plan.block]
 
 
-def first_pass(plan, lats, pts, dec_norm, enc_norm):
-    n_lat = len(lats)
+def load_blocks(plan, refs, rows, lanes):
+    blocks = range(lanes.start // plan.block, lanes.stop // plan.block)
+    return jnp.concatenate([refs[k][rows, :] for k in blocks], axis=1)
+
+
+def first_pass(plan, lats, pts, at, dec_norm, enc_norm, before=()):
+    n_lat, n_pts = len(lats), len(pts)
     c, m = plan.cols, plan.latents
-
-    def kernel(*refs):
-        lat_refs, pts_refs, (dec_ref, enc_ref) = refs[:n_lat], refs[n_lat:-6 - n_lat], refs[-6 - n_lat : -4 - n_lat]
+    points = n_pts * plan.rows
+
+    def kernel(*refs):
+        lat_refs, pts_refs, rest = refs[:n_lat], refs[n_lat : n_lat + n_pts], refs[n_lat + n_pts :]
+        (dec_ref, enc_ref), earlier = rest[:2], rest[2 : 2 + len(before)]
         outs, kept = refs[-4 - n_lat : -4], refs[-4]
         query, sides, keys = refs[-3:]
         for k, ref in enumerate(lat_refs):
@@ -245,24 +252,28 @@
             mine = slice(h * HEAD_DIM, (h + 1) * HEAD_DIM)
             below = slice(c + h * HEAD_DIM, c + (h + 1) * HEAD_DIM)
             key = keys[:, mine]
-            row_norm = dec_ref[:, h : h + 1] * LOG2E
+            row_norm = dec_ref[at * plan.rows : at * plan.rows + points, h : h + 1] * LOG2E
             for lanes in lane_tiles(plan):
                 scores = nn(key, query[mine, lanes]) * (HEAD_DIM**-0.5 * LOG2E)
                 dec = jnp.exp2(scores - row_norm).astype(jnp.bfloat16)
                 enc = jnp.exp2(scores - enc_ref[h : h + 1, lanes] * LOG2E)
                 kept[h, :, lanes] = enc
-                store_blocks(plan, outs, mine, lanes, nn(sides[mine, :], dec))
-                store_blocks(plan, outs, below, lanes, nn(sides[below, :], enc.astype(jnp.bfloat16)))
+                for rows, half in ((mine, dec), (below, enc.astype(jnp.bfloat16))):
+                    total = nn(sides[rows, :], half)
+                    if earlier:
+                        total = total + load_blocks(plan, earlier, rows, lanes)
+                    store_blocks(plan, outs, rows, lanes, total)
 
     outs = [shaped((2 * c, plan.block), jnp.float32)] * plan.plane
-    outs += [shaped((plan.heads, plan.points, m), jnp.float32)]
+    outs += [shaped((plan.heads, points, m), jnp.float32)]
     scratch = [
         pltpu.VMEM((c, m), jnp.bfloat16),
-        pltpu.VMEM((2 * c, plan.points), jnp.bfloat16),
-        pltpu.VMEM((plan.points, c), jnp.bfloat16),
+        pltpu.VMEM((2 * c, points), jnp.bfloat16),
+        pltpu.VMEM((points, c), jnp.bfloat16),
     ]
-    flops = 6 * plan.points * m * c
-    *sums, kept = call(kernel, outs, (*lats, *pts, dec_norm, enc_norm), scratch, flops)
+    flops = 6 * points * m * c
+    args = (*lats, *pts, dec_norm, enc_norm, *before)
+    *sums, kept = call(kernel, outs, args, scratch, flops)
     return sums, kept
 
 
@@ -374,7 +385,7 @@
             return got
 
         lat_refs, pts_refs = take(n_lat), take(n_pts)
-        (kept_ref,) = take(1)
+        kept_refs = take(len(kept))
         mix_refs = take(n_mix)
         parts_in = [take(2) for _ in before]
         pts_outs, lat_outs = take(n_pts), take(n_lat)
@@ -395,7 +406,7 @@
 
         def weigh(h, t, slot):
             mine, lanes = slice(h * HEAD_DIM, (h + 1) * HEAD_DIM), tiles[t]
-            enc = kept_ref[h, :, lanes]
+            enc = jnp.concatenate([ref[h, :, lanes] for ref in kept_refs], axis=0)
             grad = nn(values[:, mine], mix[mine, lanes])
             encs[slot] = enc.astype(jnp.bfloat16)
             ds[slot] = (enc * (grad - columns[h : h + 1, lanes])).astype(jnp.bfloat16)
@@ -439,7 +450,7 @@
         pltpu.VMEM((SLOTS, plan.points, 2 * plan.block), jnp.bfloat16),
     ]
     flops = 10 * plan.points * m * c
-    args = (*lats, *pts, kept, *mixes, *(a for _, part in before for a in part))
+    args = (*lats, *pts, *kept, *mixes, *(a for _, part in before for a in part))
     got = call(kernel, outs, args, scratch, flops)
     return got[:n_pts], got[n_pts:]
 
@@ -525,7 +536,10 @@
     norm = order_norm(plan, encoder_norm)
     block, dec_norm = turn_latents(plan, lat_slots)
     lats = to_plane(block)
-    sums, kept = first_pass(plan, lats, pts, dec_norm, norm)
+    half = GROUPS // 2
+    sums, kept = first_pass(plan, lats, pts[:half], 0, dec_norm, norm)
+    sums, more = first_pass(plan, lats, pts[half:], half, dec_norm, norm, sums)
+    kept = (kept, more)
     cores = sum_cores(sums)
     early, late = tuple(range(plan.heads))[:1], tuple(range(plan.heads))[1:]
     before = [(early, decoder_pass(plan, lats, pts, dec_norm, early))]

time: 83.8 us -> 82.4 us (0.983)
  waiting for transfers between devices: 32 us -> 30.6 us
    ppermute x40, waiting for transfers between devices: 32 us -> 30.6 us  [exchange(): return lax.ppermute(value, AXES, pairs)]
    pallas_call x13 -> x14, Pallas kernels: 15.3 us -> 15.6 us  [call(): pl.pallas_call(kernel, out_shape=tuple(outs), in_specs=[pl.BlockSpec(memo...]
  transfers between devices with their start and end apart: 40 -> 40, of which waited for: 24 -> 24; matrix products, arithmetic and copies ran while one was open for 0% -> 0% of each run, Pallas kernels for 8% -> 10%
where the time goes in v6:
time: 82.4 us; the launch traced here: 82.2 us
  starting transfers between devices  35.1 us (43%)
  waiting for transfers between devices  30.6 us (37%)
  Pallas kernels  15.6 us (19%)
  between operations  0.84 us (1%)
    ppermute x40, starting transfers between devices, exchange(): return lax.ppermute(value, AXES, pairs)  35.1 us
    ppermute x40, waiting for transfers between devices, exchange(): return lax.ppermute(value, AXES, pairs)  30.6 us
    pallas_call x14, Pallas kernels, call(): pl.pallas_call(kernel, out_shape=tuple(outs), in_specs=[pl.BlockSpec(memo...  15.6 us
  transfers between devices with their start and end apart: 40, of which 24 were waited for; matrix products, arithmetic and copies ran while one was open for 0% of the time, Pallas kernels for 10%

profile of v6, /device:TPU:0, one launch (start us, length us, event | category | flops | bytes accessed | tf_op | source)
XLA Modules:
  0.0 82.2 jit_solution(2010063098584515239)
XLA Ops:
  0.6 1.7 %shard_map.94 = (bf16[48,384]{1,0:T(8,128)(2,1)S(1)}, bf16[48,384]{1,0:T(8,128)(2,1)S(1)}, bf16[48,384]{1,0:T(8,128)(2,1)S(1)}, bf16[48,384]{1,0:T(8,128)(2,1)S(...) custom-call(bf16[32,768]{1,0:T(8,128)(2,1)} %refs_0_.2, ...), custom_call_target="tpu_custom_call" | custom-call | bytes 1431552 | tf_op jit(solution)/shard_map/pallas_call | solution.py:71
  2.3 3.1 %collective-permute-start = (bf16[48,384]{1,0:T(8,128)(2,1)S(1)}, bf16[48,384]{1,0:T(8,128)(2,1)S(1)}, u32[]{:S(2)}, u32[]{:S(2)}) collective-permute-start(bf16[48,384]{1,0:T(8,128)(2,1)S(1)} %get-tuple-element.62), channel_id=1, source_target_pairs={{0,2},{1,3},{2,0},{3,1},{4,6},{5,7},{6,4},{7,5},{8,10},{9,11},{10,... | collective-permute-start | bytes 110600 | tf_op jit(solution)/shard_map/ppermute | solution.py:65
  5.5 2.6 %collective-permute-start.1 = (bf16[48,384]{1,0:T(8,128)(2,1)S(1)}, bf16[48,384]{1,0:T(8,128)(2,1)S(1)}, u32[]{:S(2)}, u32[]{:S(2)}) collective-permute-start(bf16[48,384]{1,0:T(8,128)(2,1)S(1)} %get-tuple-element.63), channel_id=1, source_target_pairs={{0,4},{1,5},{2,6},{3,7},{4,0},{5,1},{6,2},{7,3},{8,12},{9,13},{10,... | collective-permute-start | bytes 110600 | tf_op jit(solution)/shard_map/ppermute | solution.py:65
  8.1 0.9 %collective-permute-start.10 = (bf16[192,384]{1,0:T(8,128)(2,1)S(1)}, bf16[192,384]{1,0:T(8,128)(2,1)S(1)}, u32[]{:S(2)}, u32[]{:S(2)}) collective-permute-start(bf16[192,384]{1,0:T(8,128)(2,1)S(1)} %get-tuple-element.67), channel_id=1, source_target_pairs={{0,2},{1,3},{2,0},{3,1},{4,6},{5,7},{6,4},{7,5},{8,10},{9,11},{10,... | collective-permute-start | bytes 442376 | tf_op jit(solution)/shard_map/ppermute | solution.py:65
  9.0 2.1 %collective-permute-done.1.refs_2_ = bf16[48,384]{1,0:T(8,128)(2,1)S(1)} collective-permute-done((bf16[48,384]{1,0:T(8,128)(2,1)S(1)}, bf16[48,384]{1,0:T(8,128)(2,1)S(1)}, u32[]{:S(2)}, u32[]{:S(2)}) %collective-permute-start.1) | collective-permute-done | bytes 36896 | tf_op jit(solution)/shard_map/ppermute | solution.py:65
  11.1 3.1 %collective-permute-done.2.refs_3_ = bf16[48,384]{1,0:T(8,128)(2,1)S(1)} collective-permute-done((bf16[48,384]{1,0:T(8,128)(2,1)S(1)}, bf16[48,384]{1,0:T(8,128)(2,1)S(1)}, u32[]{:S(2)}, u32[]{:S(2)}) %collective-permute-start.2) | collective-permute-done | bytes 36896 | tf_op jit(solution)/shard_map/ppermute | solution.py:65
  14.4 1.6 %collective-permute-start.3 = (bf16[384,128]{1,0:T(8,128)(2,1)S(1)}, bf16[384,128]{1,0:T(8,128)(2,1)S(1)}, u32[]{:S(2)}, u32[]{:S(2)}) collective-permute-start(bf16[384,128]{1,0:T(8,128)(2,1)S(1)} %get-tuple-element.65.refs_0_), channel_id=1, source_target_pairs={{0,1},{1,0},{2,3},{3,2},{4,5},{5,4},{6,7},{7,6},{8,9},{9,8},{10,11... | collective-permute-start | bytes 294920 | tf_op jit(solution)/shard_map/ppermute | solution.py:65
  16.0 1.5 %collective-permute-start.6 = (bf16[384,128]{1,0:T(8,128)(2,1)S(1)}, bf16[384,128]{1,0:T(8,128)(2,1)S(1)}, u32[]{:S(2)}, u32[]{:S(2)}) collective-permute-start(bf16[384,128]{1,0:T(8,128)(2,1)S(1)} %get-tuple-element.65.refs_0_), channel_id=1, source_target_pairs={{0,16},{1,17},{2,18},{3,19},{4,20},{5,21},{6,22},{7,23},{8,24},{9,... | collective-permute-start | bytes 294920 | tf_op jit(solution)/shard_map/ppermute | solution.py:65
  17.9 1.1 %collective-permute-done.3.refs_1_ = bf16[384,128]{1,0:T(8,128)(2,1)S(1)} collective-permute-done((bf16[384,128]{1,0:T(8,128)(2,1)S(1)}, bf16[384,128]{1,0:T(8,128)(2,1)S(1)}, u32[]{:S(2)}, u32[]{:S(2)}) %collective-permute-start.3) | collective-permute-done | bytes 98336 | tf_op jit(solution)/shard_map/ppermute | solution.py:65
  19.1 1.0 %collective-permute-start.12 = (bf16[192,384]{1,0:T(8,128)(2,1)S(1)}, bf16[192,384]{1,0:T(8,128)(2,1)S(1)}, u32[]{:S(2)}, u32[]{:S(2)}) collective-permute-start(bf16[192,384]{1,0:T(8,128)(2,1)S(1)} %get-tuple-element.69), channel_id=1, source_target_pairs={{0,6},{1,7},{2,4},{3,5},{4,2},{5,3},{6,0},{7,1},{8,14},{9,15},{10,... | collective-permute-start | bytes 442376 | tf_op jit(solution)/shard_map/ppermute | solution.py:65
  20.1 1.5 %collective-permute-done.6.refs_4_ = bf16[384,128]{1,0:T(8,128)(2,1)S(1)} collective-permute-done((bf16[384,128]{1,0:T(8,128)(2,1)S(1)}, bf16[384,128]{1,0:T(8,128)(2,1)S(1)}, u32[]{:S(2)}, u32[]{:S(2)}) %collective-permute-start.6) | collective-permute-done | bytes 98336 | tf_op jit(solution)/shard_map/ppermute | solution.py:65
  21.6 1.6 %collective-permute-done.7.refs_5_ = bf16[384,128]{1,0:T(8,128)(2,1)S(1)} collective-permute-done((bf16[384,128]{1,0:T(8,128)(2,1)S(1)}, bf16[384,128]{1,0:T(8,128)(2,1)S(1)}, u32[]{:S(2)}, u32[]{:S(2)}) %collective-permute-start.7) | collective-permute-done | bytes 98336 | tf_op jit(solution)/shard_map/ppermute | solution.py:65
  23.3 0.5 collective-permute-start.9
  23.8 1.3 %shard_map.96.refs_11_ = f32[3,1024]{1,0:T(4,128)S(1)} custom-call(f32[12,1024]{1,0:T(8,128)} %refs_0_.3), custom_call_target="tpu_custom_call" | custom-call | bytes 61440 | tf_op jit(solution)/shard_map/pallas_call | solution.py:71
  25.1 1.3 %shard_map.97 = (f32[384,128]{1,0:T(8,128)S(1)}, f32[384,128]{1,0:T(8,128)S(1)}, f32[384,128]{1,0:T(8,128)S(1)}, f32[384,128]{1,0:T(8,128)S(1)}, f32[384,128]{1,...) custom-call(bf16[384,128]{1,0:T(8,128)(2,1)S(1)} %get-tuple-element., ...), custom_call_target="tpu_custom_call" | custom-call | flops 301989888 | bytes 6074368 | tf_op jit(solution)/shard_map/pallas_call | solution.py:71
  26.4 3.2 %collective-permute-done.11.refs_8_.refs_10_ = bf16[192,384]{1,0:T(8,128)(2,1)S(1)} collective-permute-done((bf16[192,384]{1,0:T(8,128)(2,1)S(1)}, bf16[192,384]{1,0:T(8,128)(2,1)S(1)}, u32[]{:S(2)}, u32[]{:S(2)}) %collective-permute-start.11) | collective-permute-done | bytes 147488 | tf_op jit(solution)/shard_map/ppermute | solution.py:65
  29.6 1.3 %shard_map.98 = (f32[384,128]{1,0:T(8,128)S(1)}, f32[384,128]{1,0:T(8,128)S(1)}, f32[384,128]{1,0:T(8,128)S(1)}, f32[384,128]{1,0:T(8,128)S(1)}, f32[384,128]{1,...) custom-call(bf16[384,128]{1,0:T(8,128)(2,1)S(1)} %get-tuple-element., ...), custom_call_target="tpu_custom_call" | custom-call | flops 301989888 | bytes 7647232 | tf_op jit(solution)/shard_map/pallas_call | solution.py:71
  31.0 0.5 collective-permute-start.14
  33.5 1.6 %collective-permute-start.17 = (f16[400,128]{1,0:T(8,128)(2,1)S(1)}, f16[400,128]{1,0:T(8,128)(2,1)S(1)}, u32[]{:S(2)}, u32[]{:S(2)}) collective-permute-start(f16[400,128]{1,0:T(8,128)(2,1)S(1)} %convert_element_type.36), channel_id=1, source_target_pairs={{0,1},{1,0},{2,3},{3,2},{4,5},{5,4},{6,7},{7,6},{8,9},{9,8},{10,11... | collective-permute-start | bytes 307208 | tf_op jit(solution)/shard_map/ppermute | solution.py:65
  35.1 1.6 %collective-permute-start.18 = (f16[400,128]{1,0:T(8,128)(2,1)S(1)}, f16[400,128]{1,0:T(8,128)(2,1)S(1)}, u32[]{:S(2)}, u32[]{:S(2)}) collective-permute-start(f16[400,128]{1,0:T(8,128)(2,1)S(1)} %convert_element_type.38), channel_id=1, source_target_pairs={{0,16},{1,17},{2,18},{3,19},{4,20},{5,21},{6,22},{7,23},{8,24},{9,... | collective-permute-start | bytes 307208 | tf_op jit(solution)/shard_map/ppermute | solution.py:65
  36.6 0.5 collective-permute-start.19
  37.2 1.4 %collective-permute-done.17 = f16[400,128]{1,0:T(8,128)(2,1)S(1)} collective-permute-done((f16[400,128]{1,0:T(8,128)(2,1)S(1)}, f16[400,128]{1,0:T(8,128)(2,1)S(1)}, u32[]{:S(2)}, u32[]{:S(2)}) %collective-permute-start.17) | collective-permute-done | bytes 102432 | tf_op jit(solution)/shard_map/ppermute | solution.py:65
  38.6 2.3 %collective-permute-done.18 = f16[400,128]{1,0:T(8,128)(2,1)S(1)} collective-permute-done((f16[400,128]{1,0:T(8,128)(2,1)S(1)}, f16[400,128]{1,0:T(8,128)(2,1)S(1)}, u32[]{:S(2)}, u32[]{:S(2)}) %collective-permute-start.18) | collective-permute-done | bytes 102432 | tf_op jit(solution)/shard_map/ppermute | solution.py:65
  40.8 1.4 %collective-permute-done.19 = f16[400,128]{1,0:T(8,128)(2,1)S(1)} collective-permute-done((f16[400,128]{1,0:T(8,128)(2,1)S(1)}, f16[400,128]{1,0:T(8,128)(2,1)S(1)}, u32[]{:S(2)}, u32[]{:S(2)}) %collective-permute-start.19) | collective-permute-done | bytes 102432 | tf_op jit(solution)/shard_map/ppermute | solution.py:65
  42.4 1.3 %collective-permute-start.20 = (bf16[208,128]{1,0:T(8,128)(2,1)S(1)}, bf16[208,128]{1,0:T(8,128)(2,1)S(1)}, u32[]{:S(2)}, u32[]{:S(2)}) collective-permute-start(bf16[208,128]{1,0:T(8,128)(2,1)S(1)} %shard_map.100.refs_14_), channel_id=1, source_target_pairs={{0,1},{1,0},{2,3},{3,2},{4,5},{5,4},{6,7},{7,6},{8,9},{9,8},{10,11... | collective-permute-start | bytes 159752 | tf_op jit(solution)/shard_map/ppermute | solution.py:65
  43.7 1.5 %collective-permute-start.23 = (bf16[208,128]{1,0:T(8,128)(2,1)S(1)}, bf16[208,128]{1,0:T(8,128)(2,1)S(1)}, u32[]{:S(2)}, u32[]{:S(2)}) collective-permute-start(bf16[208,128]{1,0:T(8,128)(2,1)S(1)} %shard_map.100.refs_14_), channel_id=1, source_target_pairs={{0,16},{1,17},{2,18},{3,19},{4,20},{5,21},{6,22},{7,23},{8,24},{9,... | collective-permute-start | bytes 159752 | tf_op jit(solution)/shard_map/ppermute | solution.py:65
  45.2 0.7 collective-permute-start.24
  45.9 0.6 collective-permute-done.20.refs_15_
  46.6 1.3 %collective-permute-done.23.refs_18_ = bf16[208,128]{1,0:T(8,128)(2,1)S(1)} collective-permute-done((bf16[208,128]{1,0:T(8,128)(2,1)S(1)}, bf16[208,128]{1,0:T(8,128)(2,1)S(1)}, u32[]{:S(2)}, u32[]{:S(2)}) %collective-permute-start.23) | collective-permute-done | bytes 53280 | tf_op jit(solution)/shard_map/ppermute | solution.py:65
  47.8 2.4 %collective-permute-done.24.refs_19_ = bf16[208,128]{1,0:T(8,128)(2,1)S(1)} collective-permute-done((bf16[208,128]{1,0:T(8,128)(2,1)S(1)}, bf16[208,128]{1,0:T(8,128)(2,1)S(1)}, u32[]{:S(2)}, u32[]{:S(2)}) %collective-permute-start.24) | collective-permute-done | bytes 53280 | tf_op jit(solution)/shard_map/ppermute | solution.py:65
  50.2 1.4 %shard_map.101 = (f32[64,512]{1,0:T(8,128)S(1)}, f32[64,1024]{1,0:T(8,128)S(1)}) custom-call(bf16[384,128]{1,0:T(8,128)(2,1)S(1)} %get-tuple-element.65.refs_0_, bf16[384,128]{1,0:T(8,128)(2,1)S(1)} %collective-permute-done.3.refs_1_, bf16[384,128]{1,0:T(8,128)(2,1)S(1)} %collective-permute-done.4.refs_2_, ...), custom_call_target="tpu_custom_call" | custom-call | flops 268435456 | bytes 2031616 | tf_op jit(solution)/shard_map/pallas_call | solution.py:71
  51.6 2.7 %shard_map.102 = (f32[128,512]{1,0:T(8,128)S(1)}, f32[128,1024]{1,0:T(8,128)S(1)}) custom-call(bf16[384,128]{1,0:T(8,128)(2,1)S(1)} %get-tuple-element.65.refs_0_, bf16[384,128]{1,0:T(8,128)(2,1)S(1)} %collective-permute-done.3.refs_1_, bf16[384,128]{1,0:T(8,128)(2,1)S(1)} %collective-permute-done.4.refs_2_, ...), custom_call_target="tpu_custom_call" | custom-call | flops 536870912 | bytes 2424832 | tf_op jit(solution)/shard_map/pallas_call | solution.py:71
  54.3 3.5 %shard_map.103 = (bf16[128,384]{1,0:T(8,128)(2,1)S(1)}, bf16[128,384]{1,0:T(8,128)(2,1)S(1)}, bf16[128,384]{1,0:T(8,128)(2,1)S(1)}, bf16[128,384]{1,0:T(8,128)(2...) custom-call(bf16[384,128]{1,0:T(8,128)(2,1)S(1)} %get-tuple-element., ...), custom_call_target="tpu_custom_call" | custom-call | flops 1006632960 | bytes 10452992 | tf_op jit(solution)/shard_map/pallas_call | solution.py:71
  57.8 0.6 collective-permute-start.30
  60.3 0.6 collective-permute-start.34
  60.9 3.4 %collective-permute-start.27 = (bf16[128,384]{1,0:T(8,128)(2,1)S(1)}, bf16[128,384]{1,0:T(8,128)(2,1)S(1)}, u32[]{:S(2)}, u32[]{:S(2)}) collective-permute-start(bf16[128,384]{1,0:T(8,128)(2,1)S(1)} %get-tuple-element.98), channel_id=1, source_target_pairs={{0,2},{1,3},{2,0},{3,1},{4,6},{5,7},{6,4},{7,5},{8,10},{9,11},{10,... | collective-permute-start | bytes 294920 | tf_op jit(solution)/shard_map/ppermute | solution.py:65
  64.2 0.9 %collective-permute-start.28 = (bf16[128,384]{1,0:T(8,128)(2,1)S(1)}, bf16[128,384]{1,0:T(8,128)(2,1)S(1)}, u32[]{:S(2)}, u32[]{:S(2)}) collective-permute-start(bf16[128,384]{1,0:T(8,128)(2,1)S(1)} %get-tuple-element.99), channel_id=1, source_target_pairs={{0,4},{1,5},{2,6},{3,7},{4,0},{5,1},{6,2},{7,3},{8,12},{9,13},{10,... | collective-permute-start | bytes 294920 | tf_op jit(solution)/shard_map/ppermute | solution.py:65
  65.2 1.5 %collective-permute-start.29 = (bf16[128,384]{1,0:T(8,128)(2,1)S(1)}, bf16[128,384]{1,0:T(8,128)(2,1)S(1)}, u32[]{:S(2)}, u32[]{:S(2)}) collective-permute-start(bf16[128,384]{1,0:T(8,128)(2,1)S(1)} %get-tuple-element.100), channel_id=1, source_target_pairs={{0,6},{1,7},{2,4},{3,5},{4,2},{5,3},{6,0},{7,1},{8,14},{9,15},{10,... | collective-permute-start | bytes 294920 | tf_op jit(solution)/shard_map/ppermute | solution.py:65
  66.6 0.9 %collective-permute-start.35 = (f16[208,128]{1,0:T(8,128)(2,1)S(1)}, f16[208,128]{1,0:T(8,128)(2,1)S(1)}, u32[]{:S(2)}, u32[]{:S(2)}) collective-permute-start(f16[208,128]{1,0:T(8,128)(2,1)S(1)} %convert_element_type.44), channel_id=1, source_target_pairs={{0,16},{1,17},{2,18},{3,19},{4,20},{5,21},{6,22},{7,23},{8,24},{9,... | collective-permute-start | bytes 159752 | tf_op jit(solution)/shard_map/ppermute | solution.py:65
  67.5 2.3 %collective-permute-start.36 = (f16[208,128]{1,0:T(8,128)(2,1)S(1)}, f16[208,128]{1,0:T(8,128)(2,1)S(1)}, u32[]{:S(2)}, u32[]{:S(2)}) collective-permute-start(f16[208,128]{1,0:T(8,128)(2,1)S(1)} %convert_element_type.46), channel_id=1, source_target_pairs={{0,17},{1,16},{2,19},{3,18},{4,21},{5,20},{6,23},{7,22},{8,25},{9,... | collective-permute-start | bytes 159752 | tf_op jit(solution)/shard_map/ppermute | solution.py:65
  69.8 1.3 %collective-permute-done.35 = f16[208,128]{1,0:T(8,128)(2,1)S(1)} collective-permute-done((f16[208,128]{1,0:T(8,128)(2,1)S(1)}, f16[208,128]{1,0:T(8,128)(2,1)S(1)}, u32[]{:S(2)}, u32[]{:S(2)}) %collective-permute-start.35) | collective-permute-done | bytes 53280 | tf_op jit(solution)/shard_map/ppermute | solution.py:65
  71.1 1.6 %collective-permute-done.36 = f16[208,128]{1,0:T(8,128)(2,1)S(1)} collective-permute-done((f16[208,128]{1,0:T(8,128)(2,1)S(1)}, f16[208,128]{1,0:T(8,128)(2,1)S(1)}, u32[]{:S(2)}, u32[]{:S(2)}) %collective-permute-start.36) | collective-permute-done | bytes 53280 | tf_op jit(solution)/shard_map/ppermute | solution.py:65
  72.8 1.2 %collective-permute-start.37 = (f32[48,128]{1,0:T(8,128)S(1)}, f32[48,128]{1,0:T(8,128)S(1)}, u32[]{:S(2)}, u32[]{:S(2)}) collective-permute-start(f32[48,128]{1,0:T(8,128)S(1)} %get-tuple-element.116), channel_id=1, source_target_pairs={{0,2},{1,3},{2,0},{3,1},{4,6},{5,7},{6,4},{7,5},{8,10},{9,11},{10,... | collective-permute-start | bytes 73736 | tf_op jit(solution)/shard_map/ppermute | solution.py:65
  74.0 1.8 %collective-permute-start.38 = (f32[48,128]{1,0:T(8,128)S(1)}, f32[48,128]{1,0:T(8,128)S(1)}, u32[]{:S(2)}, u32[]{:S(2)}) collective-permute-start(f32[48,128]{1,0:T(8,128)S(1)} %get-tuple-element.117), channel_id=1, source_target_pairs={{0,4},{1,5},{2,6},{3,7},{4,0},{5,1},{6,2},{7,3},{8,12},{9,13},{10,... | collective-permute-start | bytes 73736 | tf_op jit(solution)/shard_map/ppermute | solution.py:65
  75.8 1.5 %collective-permute-start.39 = (f32[48,128]{1,0:T(8,128)S(1)}, f32[48,128]{1,0:T(8,128)S(1)}, u32[]{:S(2)}, u32[]{:S(2)}) collective-permute-start(f32[48,128]{1,0:T(8,128)S(1)} %get-tuple-element.118), channel_id=1, source_target_pairs={{0,6},{1,7},{2,4},{3,5},{4,2},{5,3},{6,0},{7,1},{8,14},{9,15},{10,... | collective-permute-start | bytes 73736 | tf_op jit(solution)/shard_map/ppermute | solution.py:65
  77.3 1.0 %shard_map.104 = (bf16[128,768]{1,0:T(8,128)(2,1)}, bf16[128,768]{1,0:T(8,128)(2,1)}) custom-call(bf16[128,384]{1,0:T(8,128)(2,1)S(1)} %get-tuple-element.97.refs_0_, bf16[128,384]{1,0:T(8,128)(2,1)S(1)} %collective-permute-done.27.refs_1_, bf16[128,384]{1,0:T(8,128)(2,1)S(1)} %collective-permute-done.28.refs_2_, ...), custom_call_target="tpu_custom_call" | custom-call | bytes 786432 | tf_op jit(solution)/shard_map/pallas_call | solution.py:71
  78.7 2.7 %collective-permute-done.39.refs_3_ = f32[48,128]{1,0:T(8,128)S(1)} collective-permute-done((f32[48,128]{1,0:T(8,128)S(1)}, f32[48,128]{1,0:T(8,128)S(1)}, u32[]{:S(2)}, u32[]{:S(2)}) %collective-permute-start.39) | collective-permute-done | bytes 24608 | tf_op jit(solution)/shard_map/ppermute | solution.py:65
  81.4 0.8 shard_map.107
  (58 shorter events, 5.5 us)
Async XLA Ops:
  2.3 6.6 %collective-permute-start = (bf16[48,384]{1,0:T(8,128)(2,1)S(1)}, bf16[48,384]{1,0:T(8,128)(2,1)S(1)}, u32[]{:S(2)}, u32[]{:S(2)}) collective-permute-start(bf16[48,384]{1,0:T(8,128)(2,1)S(1)} %get-tuple-element.62), channel_id=1, source_target_pairs={{0,2},{1,3},{2,0},{3,1},{4,6},{5,7},{6,4},{7,5},{8,10},{9,11},{10,... | collective-permute-start | bytes 110600 | tf_op jit(solution)/shard_map/ppermute | solution.py:65
  5.5 5.6 %collective-permute-start.1 = (bf16[48,384]{1,0:T(8,128)(2,1)S(1)}, bf16[48,384]{1,0:T(8,128)(2,1)S(1)}, u32[]{:S(2)}, u32[]{:S(2)}) collective-permute-start(bf16[48,384]{1,0:T(8,128)(2,1)S(1)} %get-tuple-element.63), channel_id=1, source_target_pairs={{0,4},{1,5},{2,6},{3,7},{4,0},{5,1},{6,2},{7,3},{8,12},{9,13},{10,... | collective-permute-start | bytes 110600 | tf_op jit(solution)/shard_map/ppermute | solution.py:65
  8.1 6.1 %collective-permute-start.2 = (bf16[48,384]{1,0:T(8,128)(2,1)S(1)}, bf16[48,384]{1,0:T(8,128)(2,1)S(1)}, u32[]{:S(2)}, u32[]{:S(2)}) collective-permute-start(bf16[48,384]{1,0:T(8,128)(2,1)S(1)} %get-tuple-element.64), channel_id=1, source_target_pairs={{0,6},{1,7},{2,4},{3,5},{4,2},{5,3},{6,0},{7,1},{8,14},{9,15},{10,... | collective-permute-start | bytes 110600 | tf_op jit(solution)/shard_map/ppermute | solution.py:65
  8.1 15.2 %collective-permute-start.10 = (bf16[192,384]{1,0:T(8,128)(2,1)S(1)}, bf16[192,384]{1,0:T(8,128)(2,1)S(1)}, u32[]{:S(2)}, u32[]{:S(2)}) collective-permute-start(bf16[192,384]{1,0:T(8,128)(2,1)S(1)} %get-tuple-element.67), channel_id=1, source_target_pairs={{0,2},{1,3},{2,0},{3,1},{4,6},{5,7},{6,4},{7,5},{8,10},{9,11},{10,... | collective-permute-start | bytes 442376 | tf_op jit(solution)/shard_map/ppermute | solution.py:65
  14.4 4.7 %collective-permute-start.3 = (bf16[384,128]{1,0:T(8,128)(2,1)S(1)}, bf16[384,128]{1,0:T(8,128)(2,1)S(1)}, u32[]{:S(2)}, u32[]{:S(2)}) collective-permute-start(bf16[384,128]{1,0:T(8,128)(2,1)S(1)} %get-tuple-element.65.refs_0_), channel_id=1, source_target_pairs={{0,1},{1,0},{2,3},{3,2},{4,5},{5,4},{6,7},{7,6},{8,9},{9,8},{10,11... | collective-permute-start | bytes 294920 | tf_op jit(solution)/shard_map/ppermute | solution.py:65
  16.0 3.1 %collective-permute-start.4 = (bf16[384,128]{1,0:T(8,128)(2,1)S(1)}, bf16[384,128]{1,0:T(8,128)(2,1)S(1)}, u32[]{:S(2)}, u32[]{:S(2)}) collective-permute-start(bf16[384,128]{1,0:T(8,128)(2,1)S(1)} %get-tuple-element.65.refs_0_), channel_id=1, source_target_pairs={{0,8},{1,9},{2,10},{3,11},{4,12},{5,13},{6,14},{7,15},{8,0},{9,1},... | collective-permute-start | bytes 294920 | tf_op jit(solution)/shard_map/ppermute | solution.py:65
  16.0 5.7 %collective-permute-start.6 = (bf16[384,128]{1,0:T(8,128)(2,1)S(1)}, bf16[384,128]{1,0:T(8,128)(2,1)S(1)}, u32[]{:S(2)}, u32[]{:S(2)}) collective-permute-start(bf16[384,128]{1,0:T(8,128)(2,1)S(1)} %get-tuple-element.65.refs_0_), channel_id=1, source_target_pairs={{0,16},{1,17},{2,18},{3,19},{4,20},{5,21},{6,22},{7,23},{8,24},{9,... | collective-permute-start | bytes 294920 | tf_op jit(solution)/shard_map/ppermute | solution.py:65
  17.5 5.8 %collective-permute-start.7 = (bf16[384,128]{1,0:T(8,128)(2,1)S(1)}, bf16[384,128]{1,0:T(8,128)(2,1)S(1)}, u32[]{:S(2)}, u32[]{:S(2)}) collective-permute-start(bf16[384,128]{1,0:T(8,128)(2,1)S(1)} %get-tuple-element.65.refs_0_), channel_id=1, source_target_pairs={{0,17},{1,16},{2,19},{3,18},{4,21},{5,20},{6,23},{7,22},{8,25},{9,... | collective-permute-start | bytes 294920 | tf_op jit(solution)/shard_map/ppermute | solution.py:65
  19.1 10.6 %collective-permute-start.11 = (bf16[192,384]{1,0:T(8,128)(2,1)S(1)}, bf16[192,384]{1,0:T(8,128)(2,1)S(1)}, u32[]{:S(2)}, u32[]{:S(2)}) collective-permute-start(bf16[192,384]{1,0:T(8,128)(2,1)S(1)} %get-tuple-element.68), channel_id=1, source_target_pairs={{0,4},{1,5},{2,6},{3,7},{4,0},{5,1},{6,2},{7,3},{8,12},{9,13},{10,... | collective-permute-start | bytes 442376 | tf_op jit(solution)/shard_map/ppermute | solution.py:65
  19.1 10.6 %collective-permute-start.12 = (bf16[192,384]{1,0:T(8,128)(2,1)S(1)}, bf16[192,384]{1,0:T(8,128)(2,1)S(1)}, u32[]{:S(2)}, u32[]{:S(2)}) collective-permute-start(bf16[192,384]{1,0:T(8,128)(2,1)S(1)} %get-tuple-element.69), channel_id=1, source_target_pairs={{0,6},{1,7},{2,4},{3,5},{4,2},{5,3},{6,0},{7,1},{8,14},{9,15},{10,... | collective-permute-start | bytes 442376 | tf_op jit(solution)/shard_map/ppermute | solution.py:65
  21.6 3.5 %collective-permute-start.5 = (bf16[384,128]{1,0:T(8,128)(2,1)S(1)}, bf16[384,128]{1,0:T(8,128)(2,1)S(1)}, u32[]{:S(2)}, u32[]{:S(2)}) collective-permute-start(bf16[384,128]{1,0:T(8,128)(2,1)S(1)} %collective-permute-done.3.refs_1_), channel_id=1, source_target_pairs={{0,8},{1,9},{2,10},{3,11},{4,12},{5,13},{6,14},{7,15},{8,0},{9,1},... | collective-permute-start | bytes 294920 | tf_op jit(solution)/shard_map/ppermute | solution.py:65
  23.3 1.8 %collective-permute-start.8 = (bf16[384,128]{1,0:T(8,128)(2,1)S(1)}, bf16[384,128]{1,0:T(8,128)(2,1)S(1)}, u32[]{:S(2)}, u32[]{:S(2)}) collective-permute-start(bf16[384,128]{1,0:T(8,128)(2,1)S(1)} %collective-permute-done.6.refs_4_), channel_id=1, source_target_pairs={{0,8},{1,9},{2,10},{3,11},{4,12},{5,13},{6,14},{7,15},{8,0},{9,1},... | collective-permute-start | bytes 294920 | tf_op jit(solution)/shard_map/ppermute | solution.py:65
  23.3 1.8 %collective-permute-start.9 = (bf16[384,128]{1,0:T(8,128)(2,1)S(1)}, bf16[384,128]{1,0:T(8,128)(2,1)S(1)}, u32[]{:S(2)}, u32[]{:S(2)}) collective-permute-start(bf16[384,128]{1,0:T(8,128)(2,1)S(1)} %collective-permute-done.7.refs_5_), channel_id=1, source_target_pairs={{0,8},{1,9},{2,10},{3,11},{4,12},{5,13},{6,14},{7,15},{8,0},{9,1},... | collective-permute-start | bytes 294920 | tf_op jit(solution)/shard_map/ppermute | solution.py:65
  30.9 1.5 %collective-permute-start.13 = (f32[384,128]{1,0:T(8,128)S(1)}, f32[384,128]{1,0:T(8,128)S(1)}, u32[]{:S(2)}, u32[]{:S(2)}) collective-permute-start(f32[384,128]{1,0:T(8,128)S(1)} %get-tuple-element.85), channel_id=1, source_target_pairs={{0,8},{1,9},{2,10},{3,11},{4,12},{5,13},{6,14},{7,15},{8,0},{9,1},... | collective-permute-start | bytes 589832 | tf_op jit(solution)/shard_map/ppermute | solution.py:65
  31.0 1.7 %collective-permute-start.14 = (f32[384,128]{1,0:T(8,128)S(1)}, f32[384,128]{1,0:T(8,128)S(1)}, u32[]{:S(2)}, u32[]{:S(2)}) collective-permute-start(f32[384,128]{1,0:T(8,128)S(1)} %get-tuple-element.86), channel_id=1, source_target_pairs={{0,8},{1,9},{2,10},{3,11},{4,12},{5,13},{6,14},{7,15},{8,0},{9,1},... | collective-permute-start | bytes 589832 | tf_op jit(solution)/shard_map/ppermute | solution.py:65
  31.5 1.5 %collective-permute-start.15 = (f32[384,128]{1,0:T(8,128)S(1)}, f32[384,128]{1,0:T(8,128)S(1)}, u32[]{:S(2)}, u32[]{:S(2)}) collective-permute-start(f32[384,128]{1,0:T(8,128)S(1)} %get-tuple-element.87), channel_id=1, source_target_pairs={{0,8},{1,9},{2,10},{3,11},{4,12},{5,13},{6,14},{7,15},{8,0},{9,1},... | collective-permute-start | bytes 589832 | tf_op jit(solution)/shard_map/ppermute | solution.py:65
  31.6 1.7 %collective-permute-start.16 = (f32[384,128]{1,0:T(8,128)S(1)}, f32[384,128]{1,0:T(8,128)S(1)}, u32[]{:S(2)}, u32[]{:S(2)}) collective-permute-start(f32[384,128]{1,0:T(8,128)S(1)} %get-tuple-element.88), channel_id=1, source_target_pairs={{0,8},{1,9},{2,10},{3,11},{4,12},{5,13},{6,14},{7,15},{8,0},{9,1},... | collective-permute-start | bytes 589832 | tf_op jit(solution)/shard_map/ppermute | solution.py:65
  33.5 5.1 %collective-permute-start.17 = (f16[400,128]{1,0:T(8,128)(2,1)S(1)}, f16[400,128]{1,0:T(8,128)(2,1)S(1)}, u32[]{:S(2)}, u32[]{:S(2)}) collective-permute-start(f16[400,128]{1,0:T(8,128)(2,1)S(1)} %convert_element_type.36), channel_id=1, source_target_pairs={{0,1},{1,0},{2,3},{3,2},{4,5},{5,4},{6,7},{7,6},{8,9},{9,8},{10,11... | collective-permute-start | bytes 307208 | tf_op jit(solution)/shard_map/ppermute | solution.py:65
  35.1 5.8 %collective-permute-start.18 = (f16[400,128]{1,0:T(8,128)(2,1)S(1)}, f16[400,128]{1,0:T(8,128)(2,1)S(1)}, u32[]{:S(2)}, u32[]{:S(2)}) collective-permute-start(f16[400,128]{1,0:T(8,128)(2,1)S(1)} %convert_element_type.38), channel_id=1, source_target_pairs={{0,16},{1,17},{2,18},{3,19},{4,20},{5,21},{6,22},{7,23},{8,24},{9,... | collective-permute-start | bytes 307208 | tf_op jit(solution)/shard_map/ppermute | solution.py:65
  36.6 5.6 %collective-permute-start.19 = (f16[400,128]{1,0:T(8,128)(2,1)S(1)}, f16[400,128]{1,0:T(8,128)(2,1)S(1)}, u32[]{:S(2)}, u32[]{:S(2)}) collective-permute-start(f16[400,128]{1,0:T(8,128)(2,1)S(1)} %convert_element_type.40), channel_id=1, source_target_pairs={{0,17},{1,16},{2,19},{3,18},{4,21},{5,20},{6,23},{7,22},{8,25},{9,... | collective-permute-start | bytes 307208 | tf_op jit(solution)/shard_map/ppermute | solution.py:65
  42.4 4.2 %collective-permute-start.20 = (bf16[208,128]{1,0:T(8,128)(2,1)S(1)}, bf16[208,128]{1,0:T(8,128)(2,1)S(1)}, u32[]{:S(2)}, u32[]{:S(2)}) collective-permute-start(bf16[208,128]{1,0:T(8,128)(2,1)S(1)} %shard_map.100.refs_14_), channel_id=1, source_target_pairs={{0,1},{1,0},{2,3},{3,2},{4,5},{5,4},{6,7},{7,6},{8,9},{9,8},{10,11... | collective-permute-start | bytes 159752 | tf_op jit(solution)/shard_map/ppermute | solution.py:65
  43.7 4.1 %collective-permute-start.23 = (bf16[208,128]{1,0:T(8,128)(2,1)S(1)}, bf16[208,128]{1,0:T(8,128)(2,1)S(1)}, u32[]{:S(2)}, u32[]{:S(2)}) collective-permute-start(bf16[208,128]{1,0:T(8,128)(2,1)S(1)} %shard_map.100.refs_14_), channel_id=1, source_target_pairs={{0,16},{1,17},{2,18},{3,19},{4,20},{5,21},{6,22},{7,23},{8,24},{9,... | collective-permute-start | bytes 159752 | tf_op jit(solution)/shard_map/ppermute | solution.py:65
  45.2 5.0 %collective-permute-start.24 = (bf16[208,128]{1,0:T(8,128)(2,1)S(1)}, bf16[208,128]{1,0:T(8,128)(2,1)S(1)}, u32[]{:S(2)}, u32[]{:S(2)}) collective-permute-start(bf16[208,128]{1,0:T(8,128)(2,1)S(1)} %shard_map.100.refs_14_), channel_id=1, source_target_pairs={{0,17},{1,16},{2,19},{3,18},{4,21},{5,20},{6,23},{7,22},{8,25},{9,... | collective-permute-start | bytes 159752 | tf_op jit(solution)/shard_map/ppermute | solution.py:65
  45.9 8.4 %collective-permute-start.21 = (bf16[208,128]{1,0:T(8,128)(2,1)S(1)}, bf16[208,128]{1,0:T(8,128)(2,1)S(1)}, u32[]{:S(2)}, u32[]{:S(2)}) collective-permute-start(bf16[208,128]{1,0:T(8,128)(2,1)S(1)} %shard_map.100.refs_14_), channel_id=1, source_target_pairs={{0,8},{1,9},{2,10},{3,11},{4,12},{5,13},{6,14},{7,15},{8,0},{9,1},... | collective-permute-start | bytes 159752 | tf_op jit(solution)/shard_map/ppermute | solution.py:65
  46.6 7.7 %collective-permute-start.22 = (bf16[208,128]{1,0:T(8,128)(2,1)S(1)}, bf16[208,128]{1,0:T(8,128)(2,1)S(1)}, u32[]{:S(2)}, u32[]{:S(2)}) collective-permute-start(bf16[208,128]{1,0:T(8,128)(2,1)S(1)} %collective-permute-done.20.refs_15_), channel_id=1, source_target_pairs={{0,8},{1,9},{2,10},{3,11},{4,12},{5,13},{6,14},{7,15},{8,0},{9,1},... | collective-permute-start | bytes 159752 | tf_op jit(solution)/shard_map/ppermute | solution.py:65
  47.8 6.5 %collective-permute-start.25 = (bf16[208,128]{1,0:T(8,128)(2,1)S(1)}, bf16[208,128]{1,0:T(8,128)(2,1)S(1)}, u32[]{:S(2)}, u32[]{:S(2)}) collective-permute-start(bf16[208,128]{1,0:T(8,128)(2,1)S(1)} %collective-permute-done.23.refs_18_), channel_id=1, source_target_pairs={{0,8},{1,9},{2,10},{3,11},{4,12},{5,13},{6,14},{7,15},{8,0},{9,1},... | collective-permute-start | bytes 159752 | tf_op jit(solution)/shard_map/ppermute | solution.py:65
  50.2 4.1 %collective-permute-start.26 = (bf16[208,128]{1,0:T(8,128)(2,1)S(1)}, bf16[208,128]{1,0:T(8,128)(2,1)S(1)}, u32[]{:S(2)}, u32[]{:S(2)}) collective-permute-start(bf16[208,128]{1,0:T(8,128)(2,1)S(1)} %collective-permute-done.24.refs_19_), channel_id=1, source_target_pairs={{0,8},{1,9},{2,10},{3,11},{4,12},{5,13},{6,14},{7,15},{8,0},{9,1},... | collective-permute-start | bytes 159752 | tf_op jit(solution)/shard_map/ppermute | solution.py:65
  57.8 1.5 %collective-permute-start.30 = (f32[192,128]{1,0:T(8,128)S(1)}, f32[192,128]{1,0:T(8,128)S(1)}, u32[]{:S(2)}, u32[]{:S(2)}) collective-permute-start(f32[192,128]{1,0:T(8,128)S(1)} %get-tuple-element.107), channel_id=1, source_target_pairs={{0,8},{1,9},{2,10},{3,11},{4,12},{5,13},{6,14},{7,15},{8,0},{9,1},... | collective-permute-start | bytes 294920 | tf_op jit(solution)/shard_map/ppermute | solution.py:65
  58.4 1.3 %collective-permute-start.31 = (f32[192,128]{1,0:T(8,128)S(1)}, f32[192,128]{1,0:T(8,128)S(1)}, u32[]{:S(2)}, u32[]{:S(2)}) collective-permute-start(f32[192,128]{1,0:T(8,128)S(1)} %get-tuple-element.108), channel_id=1, source_target_pairs={{0,8},{1,9},{2,10},{3,11},{4,12},{5,13},{6,14},{7,15},{8,0},{9,1},... | collective-permute-start | bytes 294920 | tf_op jit(solution)/shard_map/ppermute | solution.py:65
  58.5 1.4 %collective-permute-start.32 = (f32[192,128]{1,0:T(8,128)S(1)}, f32[192,128]{1,0:T(8,128)S(1)}, u32[]{:S(2)}, u32[]{:S(2)}) collective-permute-start(f32[192,128]{1,0:T(8,128)S(1)} %get-tuple-element.109), channel_id=1, source_target_pairs={{0,8},{1,9},{2,10},{3,11},{4,12},{5,13},{6,14},{7,15},{8,0},{9,1},... | collective-permute-start | bytes 294920 | tf_op jit(solution)/shard_map/ppermute | solution.py:65
  58.9 1.3 %collective-permute-start.33 = (f32[192,128]{1,0:T(8,128)S(1)}, f32[192,128]{1,0:T(8,128)S(1)}, u32[]{:S(2)}, u32[]{:S(2)}) collective-permute-start(f32[192,128]{1,0:T(8,128)S(1)} %get-tuple-element.110), channel_id=1, source_target_pairs={{0,8},{1,9},{2,10},{3,11},{4,12},{5,13},{6,14},{7,15},{8,0},{9,1},... | collective-permute-start | bytes 294920 | tf_op jit(solution)/shard_map/ppermute | solution.py:65
  60.3 7.2 %collective-permute-start.34 = (f16[208,128]{1,0:T(8,128)(2,1)S(1)}, f16[208,128]{1,0:T(8,128)(2,1)S(1)}, u32[]{:S(2)}, u32[]{:S(2)}) collective-permute-start(f16[208,128]{1,0:T(8,128)(2,1)S(1)} %convert_element_type.42), channel_id=1, source_target_pairs={{0,1},{1,0},{2,3},{3,2},{4,5},{5,4},{6,7},{7,6},{8,9},{9,8},{10,11... | collective-permute-start | bytes 159752 | tf_op jit(solution)/shard_map/ppermute | solution.py:65
  60.9 14.9 %collective-permute-start.27 = (bf16[128,384]{1,0:T(8,128)(2,1)S(1)}, bf16[128,384]{1,0:T(8,128)(2,1)S(1)}, u32[]{:S(2)}, u32[]{:S(2)}) collective-permute-start(bf16[128,384]{1,0:T(8,128)(2,1)S(1)} %get-tuple-element.98), channel_id=1, source_target_pairs={{0,2},{1,3},{2,0},{3,1},{4,6},{5,7},{6,4},{7,5},{8,10},{9,11},{10,... | collective-permute-start | bytes 294920 | tf_op jit(solution)/shard_map/ppermute | solution.py:65
  64.2 13.0 %collective-permute-start.28 = (bf16[128,384]{1,0:T(8,128)(2,1)S(1)}, bf16[128,384]{1,0:T(8,128)(2,1)S(1)}, u32[]{:S(2)}, u32[]{:S(2)}) collective-permute-start(bf16[128,384]{1,0:T(8,128)(2,1)S(1)} %get-tuple-element.99), channel_id=1, source_target_pairs={{0,4},{1,5},{2,6},{3,7},{4,0},{5,1},{6,2},{7,3},{8,12},{9,13},{10,... | collective-permute-start | bytes 294920 | tf_op jit(solution)/shard_map/ppermute | solution.py:65
  65.2 12.1 %collective-permute-start.29 = (bf16[128,384]{1,0:T(8,128)(2,1)S(1)}, bf16[128,384]{1,0:T(8,128)(2,1)S(1)}, u32[]{:S(2)}, u32[]{:S(2)}) collective-permute-start(bf16[128,384]{1,0:T(8,128)(2,1)S(1)} %get-tuple-element.100), channel_id=1, source_target_pairs={{0,6},{1,7},{2,4},{3,5},{4,2},{5,3},{6,0},{7,1},{8,14},{9,15},{10,... | collective-permute-start | bytes 294920 | tf_op jit(solution)/shard_map/ppermute | solution.py:65
  66.6 4.4 %collective-permute-start.35 = (f16[208,128]{1,0:T(8,128)(2,1)S(1)}, f16[208,128]{1,0:T(8,128)(2,1)S(1)}, u32[]{:S(2)}, u32[]{:S(2)}) collective-permute-start(f16[208,128]{1,0:T(8,128)(2,1)S(1)} %convert_element_type.44), channel_id=1, source_target_pairs={{0,16},{1,17},{2,18},{3,19},{4,20},{5,21},{6,22},{7,23},{8,24},{9,... | collective-permute-start | bytes 159752 | tf_op jit(solution)/shard_map/ppermute | solution.py:65
  67.5 5.1 %collective-permute-start.36 = (f16[208,128]{1,0:T(8,128)(2,1)S(1)}, f16[208,128]{1,0:T(8,128)(2,1)S(1)}, u32[]{:S(2)}, u32[]{:S(2)}) collective-permute-start(f16[208,128]{1,0:T(8,128)(2,1)S(1)} %convert_element_type.46), channel_id=1, source_target_pairs={{0,17},{1,16},{2,19},{3,18},{4,21},{5,20},{6,23},{7,22},{8,25},{9,... | collective-permute-start | bytes 159752 | tf_op jit(solution)/shard_map/ppermute | solution.py:65
  72.8 5.4 %collective-permute-start.37 = (f32[48,128]{1,0:T(8,128)S(1)}, f32[48,128]{1,0:T(8,128)S(1)}, u32[]{:S(2)}, u32[]{:S(2)}) collective-permute-start(f32[48,128]{1,0:T(8,128)S(1)} %get-tuple-element.116), channel_id=1, source_target_pairs={{0,2},{1,3},{2,0},{3,1},{4,6},{5,7},{6,4},{7,5},{8,10},{9,11},{10,... | collective-permute-start | bytes 73736 | tf_op jit(solution)/shard_map/ppermute | solution.py:65
  74.0 4.7 %collective-permute-start.38 = (f32[48,128]{1,0:T(8,128)S(1)}, f32[48,128]{1,0:T(8,128)S(1)}, u32[]{:S(2)}, u32[]{:S(2)}) collective-permute-start(f32[48,128]{1,0:T(8,128)S(1)} %get-tuple-element.117), channel_id=1, source_target_pairs={{0,4},{1,5},{2,6},{3,7},{4,0},{5,1},{6,2},{7,3},{8,12},{9,13},{10,... | collective-permute-start | bytes 73736 | tf_op jit(solution)/shard_map/ppermute | solution.py:65
  75.8 5.6 %collective-permute-start.39 = (f32[48,128]{1,0:T(8,128)S(1)}, f32[48,128]{1,0:T(8,128)S(1)}, u32[]{:S(2)}, u32[]{:S(2)}) collective-permute-start(f32[48,128]{1,0:T(8,128)S(1)} %get-tuple-element.118), channel_id=1, source_target_pairs={{0,6},{1,7},{2,4},{3,5},{4,2},{5,3},{6,0},{7,1},{8,14},{9,15},{10,... | collective-permute-start | bytes 73736 | tf_op jit(solution)/shard_map/ppermute | solution.py:65

commit v7 on v6

--- a/solution.py
+++ b/solution.py
@@ -51,6 +51,16 @@
             and width == HEADS * HEAD_DIM
             and 2 * width // GROUPS == 3 * LANES
         )
+
+    def chip_steps(self):
+        return [k for k in range(self.plane) if not k & self.fast]
+
+    def views(self, mine, away, tall):
+        at = {k: slice(i * tall, (i + 1) * tall) for i, k in enumerate(self.chip_steps())}
+        return [(away if k & self.fast else mine).at[at[k & ~self.fast]] for k in range(self.plane)]
+
+    def stack(self, tall):
+        return shaped((len(self.chip_steps()) * tall, self.block), jnp.float32)
 
     def exchange(self, value, over_group, step):
         pairs = []
@@ -236,8 +246,9 @@
 
     def kernel(*refs):
         lat_refs, pts_refs, rest = refs[:n_lat], refs[n_lat : n_lat + n_pts], refs[n_lat + n_pts :]
-        (dec_ref, enc_ref), earlier = rest[:2], rest[2 : 2 + len(before)]
-        outs, kept = refs[-4 - n_lat : -4], refs[-4]
+        dec_ref, enc_ref = rest[:2]
+        earlier = plan.views(*rest[2:4], 2 * c) if before else ()
+        outs, kept = plan.views(*refs[-6:-4], 2 * c), refs[-4]
         query, sides, keys = refs[-3:]
         for k, ref in enumerate(lat_refs):
             query[:, k * plan.block : (k + 1) * plan.block] = ref[:c, :]
@@ -264,8 +275,7 @@
                         total = total + load_blocks(plan, earlier, rows, lanes)
                     store_blocks(plan, outs, rows, lanes, total)
 
-    outs = [shaped((2 * c, plan.block), jnp.float32)] * plan.plane
-    outs += [shaped((plan.heads, points, m), jnp.float32)]
+    outs = [plan.stack(2 * c)] * 2 + [shaped((plan.heads, points, m), jnp.float32)]
     scratch = [
         pltpu.VMEM((c, m), jnp.bfloat16),
         pltpu.VMEM((2 * c, points), jnp.bfloat16),
@@ -316,12 +326,13 @@
 
 
 def add_and_scale(plan, mine, theirs):
-    tall = mine[0].shape[0]
-
-    def kernel(*refs):
-        n = len(mine)
-        for k, (a, b, out) in enumerate(zip(refs[:n], refs[n : 2 * n], refs[2 * n :], strict=True)):
-            total = a[...] + b[...]
+    n = len(plan.chip_steps())
+    tall = mine.shape[0] // n
+
+    def kernel(mine_ref, theirs_ref, *outs):
+        for k, out in enumerate(outs):
+            rows = slice(k * tall, (k + 1) * tall)
+            total = mine_ref[rows, :] + theirs_ref[rows, :]
             if k == 0:
                 out[...] = total
                 continue
@@ -335,8 +346,8 @@
             fill = jnp.zeros((16 - len(sizes), plan.block), jnp.float32)
             out[tall:, :] = jnp.concatenate([*sizes, fill], axis=0)
 
-    outs = [shaped((tall + 16 * (k > 0), plan.block), jnp.float32) for k in range(len(mine))]
-    return call(kernel, outs, (*mine, *theirs))
+    outs = [shaped((tall + 16 * (k > 0), plan.block), jnp.float32) for k in range(n)]
+    return call(kernel, outs, (mine, theirs))
 
 
 def scaled_sum(own, *scaled):
@@ -388,7 +399,7 @@
         kept_refs = take(len(kept))
         mix_refs = take(n_mix)
         parts_in = [take(2) for _ in before]
-        pts_outs, lat_outs = take(n_pts), take(n_lat)
+        pts_outs, lat_outs = take(n_pts), plan.views(*take(2), c)
         query, mix, keys_t, values, ds, encs = refs
         for k, ref in enumerate(lat_refs):
             query[:, k * plan.block : (k + 1) * plan.block] = ref[:c, :]
@@ -440,7 +451,7 @@
             gather(*work[n], n % SLOTS)
 
     outs = [shaped((plan.rows, 2 * c), jnp.bfloat16)] * n_pts
-    outs += [shaped((c, plan.block), jnp.float32)] * n_lat
+    outs += [plan.stack(c)] * 2
     scratch = [
         pltpu.VMEM((c, m), jnp.bfloat16),
         pltpu.VMEM((plan.ct_rows, m), jnp.bfloat16),
@@ -504,27 +515,23 @@
             got.append(plan.exchange(slots[j], True, j))
         return got
 
-    def chip_steps():
-        return [k for k in range(plan.plane) if not k & plan.fast]
-
     def from_chips(blocks):
         got = []
-        for k, block in zip(chip_steps(), blocks, strict=True):
+        for k, block in zip(plan.chip_steps(), blocks, strict=True):
             got.append(plan.exchange(block, False, k) if k else block)
         return got
 
-    def sum_cores(blocks):
-        near = chip_steps()
-        theirs = [plan.exchange(blocks[k | plan.fast], False, plan.fast) for k in near]
-        return add_and_scale(plan, [blocks[k] for k in near], theirs)
+    def sum_cores(mine, away):
+        theirs = plan.exchange(away, False, plan.fast)
+        return add_and_scale(plan, mine, theirs)
 
     def sum_chips(blocks):
         halves = [blocks[0], *(block.astype(jnp.float16) for block in blocks[1:])]
         return [block.astype(jnp.float32) for block in from_chips(halves)]
 
     def to_plane(block):
-        got = dict(zip(chip_steps(), from_chips([block] * len(chip_steps())), strict=True))
-        for k in chip_steps():
+        got = dict(zip(plan.chip_steps(), from_chips([block] * len(plan.chip_steps())), strict=True))
+        for k in plan.chip_steps():
             got[k | plan.fast] = plan.exchange(got[k], False, plan.fast)
         return tuple(got[k] for k in range(plan.plane))
 
@@ -540,14 +547,13 @@
     sums, kept = first_pass(plan, lats, pts[:half], 0, dec_norm, norm)
     sums, more = first_pass(plan, lats, pts[half:], half, dec_norm, norm, sums)
     kept = (kept, more)
-    cores = sum_cores(sums)
-    early, late = tuple(range(plan.heads))[:1], tuple(range(plan.heads))[1:]
-    before = [(early, decoder_pass(plan, lats, pts, dec_norm, early))]
+    cores = sum_cores(*sums)
     sums = sum_chips(cores)
-    before.append((late, decoder_pass(plan, lats, pts, dec_norm, late)))
+    every = tuple(range(plan.heads))
+    before = [(every, decoder_pass(plan, lats, pts, dec_norm, every))]
     mixes = to_plane(reduce_mix(plan, sums))
     pts_out, lat_out = encoder_pass(plan, lats, pts, kept, mixes, before)
-    lat_out = sum_chips(sum_cores(lat_out))
+    lat_out = sum_chips(sum_cores(*lat_out))
     pts_out = over_group(pts_out)
     lat_rows = over_group(reduce_latents(plan, lat_out))
     keys_grad, values_grad = place_points(plan, pts_out)

time: 82.4 us -> 81.8 us (level)
  starting transfers between devices: 35.1 us -> 33.5 us
  waiting for transfers between devices: 30.6 us -> 31.8 us
    ppermute x40 -> x34, starting transfers between devices: 35.1 us -> 33.5 us  [exchange(): return lax.ppermute(value, AXES, pairs)]
    ppermute x40 -> x34, waiting for transfers between devices: 30.6 us -> 31.8 us  [exchange(): return lax.ppermute(value, AXES, pairs)]
    pallas_call x14 -> x13, Pallas kernels: 15.6 us -> 15.4 us  [call(): pl.pallas_call(kernel, out_shape=tuple(outs), in_specs=[pl.BlockSpec(memo...]
  transfers between devices with their start and end apart: 40 -> 34, of which waited for: 24 -> 18; matrix products, arithmetic and copies ran while one was open for 0% -> 0% of each run, Pallas kernels for 10% -> 10%
where the time goes in v7:
time: 81.8 us; the launch traced here: 81.6 us
  starting transfers between devices  33.5 us (41%)
  waiting for transfers between devices  31.8 us (39%)
  Pallas kernels  15.4 us (19%)
  between operations  0.84 us (1%)
    ppermute x34, starting transfers between devices, exchange(): return lax.ppermute(value, AXES, pairs)  33.5 us
    ppermute x34, waiting for transfers between devices, exchange(): return lax.ppermute(value, AXES, pairs)  31.8 us
    pallas_call x13, Pallas kernels, call(): pl.pallas_call(kernel, out_shape=tuple(outs), in_specs=[pl.BlockSpec(memo...  15.4 us
  transfers between devices with their start and end apart: 34, of which 18 were waited for; matrix products, arithmetic and copies ran while one was open for 0% of the time, Pallas kernels for 10%

profile of v7, /device:TPU:0, one launch (start us, length us, event | category | flops | bytes accessed | tf_op | source)
XLA Modules:
  0.0 81.6 jit_solution(18336758871729748705)
XLA Ops:
  0.6 1.7 %shard_map.94 = (bf16[48,384]{1,0:T(8,128)(2,1)S(1)}, bf16[48,384]{1,0:T(8,128)(2,1)S(1)}, bf16[48,384]{1,0:T(8,128)(2,1)S(1)}, bf16[48,384]{1,0:T(8,128)(2,1)S(...) custom-call(bf16[32,768]{1,0:T(8,128)(2,1)} %refs_0_.2, ...), custom_call_target="tpu_custom_call" | custom-call | bytes 1431552 | tf_op jit(solution)/shard_map/pallas_call | solution.py:81
  2.3 3.1 %collective-permute-start = (bf16[48,384]{1,0:T(8,128)(2,1)S(1)}, bf16[48,384]{1,0:T(8,128)(2,1)S(1)}, u32[]{:S(2)}, u32[]{:S(2)}) collective-permute-start(bf16[48,384]{1,0:T(8,128)(2,1)S(1)} %get-tuple-element.42), channel_id=1, source_target_pairs={{0,2},{1,3},{2,0},{3,1},{4,6},{5,7},{6,4},{7,5},{8,10},{9,11},{10,... | collective-permute-start | bytes 110600 | tf_op jit(solution)/shard_map/ppermute | solution.py:75
  5.5 2.6 %collective-permute-start.1 = (bf16[48,384]{1,0:T(8,128)(2,1)S(1)}, bf16[48,384]{1,0:T(8,128)(2,1)S(1)}, u32[]{:S(2)}, u32[]{:S(2)}) collective-permute-start(bf16[48,384]{1,0:T(8,128)(2,1)S(1)} %get-tuple-element.43), channel_id=1, source_target_pairs={{0,4},{1,5},{2,6},{3,7},{4,0},{5,1},{6,2},{7,3},{8,12},{9,13},{10,... | collective-permute-start | bytes 110600 | tf_op jit(solution)/shard_map/ppermute | solution.py:75
  8.1 0.9 %collective-permute-start.10 = (bf16[192,384]{1,0:T(8,128)(2,1)S(1)}, bf16[192,384]{1,0:T(8,128)(2,1)S(1)}, u32[]{:S(2)}, u32[]{:S(2)}) collective-permute-start(bf16[192,384]{1,0:T(8,128)(2,1)S(1)} %get-tuple-element.47), channel_id=1, source_target_pairs={{0,2},{1,3},{2,0},{3,1},{4,6},{5,7},{6,4},{7,5},{8,10},{9,11},{10,... | collective-permute-start | bytes 442376 | tf_op jit(solution)/shard_map/ppermute | solution.py:75
  9.0 2.1 %collective-permute-done.1.refs_2_ = bf16[48,384]{1,0:T(8,128)(2,1)S(1)} collective-permute-done((bf16[48,384]{1,0:T(8,128)(2,1)S(1)}, bf16[48,384]{1,0:T(8,128)(2,1)S(1)}, u32[]{:S(2)}, u32[]{:S(2)}) %collective-permute-start.1) | collective-permute-done | bytes 36896 | tf_op jit(solution)/shard_map/ppermute | solution.py:75
  11.1 3.1 %collective-permute-done.2.refs_3_ = bf16[48,384]{1,0:T(8,128)(2,1)S(1)} collective-permute-done((bf16[48,384]{1,0:T(8,128)(2,1)S(1)}, bf16[48,384]{1,0:T(8,128)(2,1)S(1)}, u32[]{:S(2)}, u32[]{:S(2)}) %collective-permute-start.2) | collective-permute-done | bytes 36896 | tf_op jit(solution)/shard_map/ppermute | solution.py:75
  14.4 1.6 %collective-permute-start.3 = (bf16[384,128]{1,0:T(8,128)(2,1)S(1)}, bf16[384,128]{1,0:T(8,128)(2,1)S(1)}, u32[]{:S(2)}, u32[]{:S(2)}) collective-permute-start(bf16[384,128]{1,0:T(8,128)(2,1)S(1)} %get-tuple-element.45.refs_0_), channel_id=1, source_target_pairs={{0,1},{1,0},{2,3},{3,2},{4,5},{5,4},{6,7},{7,6},{8,9},{9,8},{10,11... | collective-permute-start | bytes 294920 | tf_op jit(solution)/shard_map/ppermute | solution.py:75
  16.0 1.5 %collective-permute-start.6 = (bf16[384,128]{1,0:T(8,128)(2,1)S(1)}, bf16[384,128]{1,0:T(8,128)(2,1)S(1)}, u32[]{:S(2)}, u32[]{:S(2)}) collective-permute-start(bf16[384,128]{1,0:T(8,128)(2,1)S(1)} %get-tuple-element.45.refs_0_), channel_id=1, source_target_pairs={{0,16},{1,17},{2,18},{3,19},{4,20},{5,21},{6,22},{7,23},{8,24},{9,... | collective-permute-start | bytes 294920 | tf_op jit(solution)/shard_map/ppermute | solution.py:75
  17.9 1.1 %collective-permute-done.3.refs_1_ = bf16[384,128]{1,0:T(8,128)(2,1)S(1)} collective-permute-done((bf16[384,128]{1,0:T(8,128)(2,1)S(1)}, bf16[384,128]{1,0:T(8,128)(2,1)S(1)}, u32[]{:S(2)}, u32[]{:S(2)}) %collective-permute-start.3) | collective-permute-done | bytes 98336 | tf_op jit(solution)/shard_map/ppermute | solution.py:75
  19.1 1.0 %collective-permute-start.12 = (bf16[192,384]{1,0:T(8,128)(2,1)S(1)}, bf16[192,384]{1,0:T(8,128)(2,1)S(1)}, u32[]{:S(2)}, u32[]{:S(2)}) collective-permute-start(bf16[192,384]{1,0:T(8,128)(2,1)S(1)} %get-tuple-element.49), channel_id=1, source_target_pairs={{0,6},{1,7},{2,4},{3,5},{4,2},{5,3},{6,0},{7,1},{8,14},{9,15},{10,... | collective-permute-start | bytes 442376 | tf_op jit(solution)/shard_map/ppermute | solution.py:75
  20.1 1.5 %collective-permute-done.6.refs_4_ = bf16[384,128]{1,0:T(8,128)(2,1)S(1)} collective-permute-done((bf16[384,128]{1,0:T(8,128)(2,1)S(1)}, bf16[384,128]{1,0:T(8,128)(2,1)S(1)}, u32[]{:S(2)}, u32[]{:S(2)}) %collective-permute-start.6) | collective-permute-done | bytes 98336 | tf_op jit(solution)/shard_map/ppermute | solution.py:75
  21.6 1.6 %collective-permute-done.7.refs_5_ = bf16[384,128]{1,0:T(8,128)(2,1)S(1)} collective-permute-done((bf16[384,128]{1,0:T(8,128)(2,1)S(1)}, bf16[384,128]{1,0:T(8,128)(2,1)S(1)}, u32[]{:S(2)}, u32[]{:S(2)}) %collective-permute-start.7) | collective-permute-done | bytes 98336 | tf_op jit(solution)/shard_map/ppermute | solution.py:75
  23.3 0.5 collective-permute-start.9
  23.8 1.3 %shard_map.96.refs_11_ = f32[3,1024]{1,0:T(4,128)S(1)} custom-call(f32[12,1024]{1,0:T(8,128)} %refs_0_.3), custom_call_target="tpu_custom_call" | custom-call | bytes 61440 | tf_op jit(solution)/shard_map/pallas_call | solution.py:81
  25.1 1.3 %shard_map.97 = (f32[1536,128]{1,0:T(8,128)S(1)}, f32[1536,128]{1,0:T(8,128)S(1)}, f32[3,256,1024]{2,1,0:T(8,128)S(1)}) custom-call(bf16[384,128]{1,0:T(8,128)(2,1)S(1)} %get-tuple-element.45.refs_0_, bf16[384,128]{1,0:T(8,128)(2,1)S(1)} %collective-permute-done.3.refs_1_, bf16[384,128]{1,0:T(8,128)(2,1)S(1)} %collective-permute-done.4.refs_2_, ...), custom_call_target="tpu_custom_call" | custom-call | flops 301989888 | bytes 6074368 | tf_op jit(solution)/shard_map/pallas_call | solution.py:81
  26.4 3.2 %collective-permute-done.11.refs_8_.refs_10_ = bf16[192,384]{1,0:T(8,128)(2,1)S(1)} collective-permute-done((bf16[192,384]{1,0:T(8,128)(2,1)S(1)}, bf16[192,384]{1,0:T(8,128)(2,1)S(1)}, u32[]{:S(2)}, u32[]{:S(2)}) %collective-permute-start.11) | collective-permute-done | bytes 147488 | tf_op jit(solution)/shard_map/ppermute | solution.py:75
  29.6 1.3 %shard_map.98 = (f32[1536,128]{1,0:T(8,128)S(1)}, f32[1536,128]{1,0:T(8,128)S(1)}, f32[3,256,1024]{2,1,0:T(8,128)S(1)}) custom-call(bf16[384,128]{1,0:T(8,128)(2,1)S(1)} %get-tuple-element.45.refs_0_, bf16[384,128]{1,0:T(8,128)(2,1)S(1)} %collective-permute-done.3.refs_1_, bf16[384,128]{1,0:T(8,128)(2,1)S(1)} %collective-permute-done.4.refs_2_, ...), custom_call_target="tpu_custom_call" | custom-call | flops 301989888 | bytes 7647232 | tf_op jit(solution)/shard_map/pallas_call | solution.py:81
  31.0 2.3 %collective-permute-done.13.theirs_ref = f32[1536,128]{1,0:T(8,128)S(1)} collective-permute-done((f32[1536,128]{1,0:T(8,128)S(1)}, f32[1536,128]{1,0:T(8,128)S(1)}, u32[]{:S(2)}, u32[]{:S(2)}) %collective-permute-start.13) | collective-permute-done | bytes 786464 | tf_op jit(solution)/shard_map/ppermute | solution.py:75
  33.4 1.6 %collective-permute-start.14 = (f16[400,128]{1,0:T(8,128)(2,1)S(1)}, f16[400,128]{1,0:T(8,128)(2,1)S(1)}, u32[]{:S(2)}, u32[]{:S(2)}) collective-permute-start(f16[400,128]{1,0:T(8,128)(2,1)S(1)} %convert_element_type.36), channel_id=1, source_target_pairs={{0,1},{1,0},{2,3},{3,2},{4,5},{5,4},{6,7},{7,6},{8,9},{9,8},{10,11... | collective-permute-start | bytes 307208 | tf_op jit(solution)/shard_map/ppermute | solution.py:75
  35.1 1.6 %collective-permute-start.15 = (f16[400,128]{1,0:T(8,128)(2,1)S(1)}, f16[400,128]{1,0:T(8,128)(2,1)S(1)}, u32[]{:S(2)}, u32[]{:S(2)}) collective-permute-start(f16[400,128]{1,0:T(8,128)(2,1)S(1)} %convert_element_type.38), channel_id=1, source_target_pairs={{0,16},{1,17},{2,18},{3,19},{4,20},{5,21},{6,22},{7,23},{8,24},{9,... | collective-permute-start | bytes 307208 | tf_op jit(solution)/shard_map/ppermute | solution.py:75
  36.6 0.5 collective-permute-start.16
  37.2 1.3 %collective-permute-done.14 = f16[400,128]{1,0:T(8,128)(2,1)S(1)} collective-permute-done((f16[400,128]{1,0:T(8,128)(2,1)S(1)}, f16[400,128]{1,0:T(8,128)(2,1)S(1)}, u32[]{:S(2)}, u32[]{:S(2)}) %collective-permute-start.14) | collective-permute-done | bytes 102432 | tf_op jit(solution)/shard_map/ppermute | solution.py:75
  38.5 2.3 %collective-permute-done.15 = f16[400,128]{1,0:T(8,128)(2,1)S(1)} collective-permute-done((f16[400,128]{1,0:T(8,128)(2,1)S(1)}, f16[400,128]{1,0:T(8,128)(2,1)S(1)}, u32[]{:S(2)}, u32[]{:S(2)}) %collective-permute-start.15) | collective-permute-done | bytes 102432 | tf_op jit(solution)/shard_map/ppermute | solution.py:75
  40.8 1.5 %collective-permute-done.16 = f16[400,128]{1,0:T(8,128)(2,1)S(1)} collective-permute-done((f16[400,128]{1,0:T(8,128)(2,1)S(1)}, f16[400,128]{1,0:T(8,128)(2,1)S(1)}, u32[]{:S(2)}, u32[]{:S(2)}) %collective-permute-start.16) | collective-permute-done | bytes 102432 | tf_op jit(solution)/shard_map/ppermute | solution.py:75
  42.4 1.2 %collective-permute-start.17 = (bf16[208,128]{1,0:T(8,128)(2,1)S(1)}, bf16[208,128]{1,0:T(8,128)(2,1)S(1)}, u32[]{:S(2)}, u32[]{:S(2)}) collective-permute-start(bf16[208,128]{1,0:T(8,128)(2,1)S(1)} %shard_map.100.refs_14_), channel_id=1, source_target_pairs={{0,1},{1,0},{2,3},{3,2},{4,5},{5,4},{6,7},{7,6},{8,9},{9,8},{10,11... | collective-permute-start | bytes 159752 | tf_op jit(solution)/shard_map/ppermute | solution.py:75
  43.6 1.5 %collective-permute-start.20 = (bf16[208,128]{1,0:T(8,128)(2,1)S(1)}, bf16[208,128]{1,0:T(8,128)(2,1)S(1)}, u32[]{:S(2)}, u32[]{:S(2)}) collective-permute-start(bf16[208,128]{1,0:T(8,128)(2,1)S(1)} %shard_map.100.refs_14_), channel_id=1, source_target_pairs={{0,16},{1,17},{2,18},{3,19},{4,20},{5,21},{6,22},{7,23},{8,24},{9,... | collective-permute-start | bytes 159752 | tf_op jit(solution)/shard_map/ppermute | solution.py:75
  45.1 0.8 %collective-permute-start.21 = (bf16[208,128]{1,0:T(8,128)(2,1)S(1)}, bf16[208,128]{1,0:T(8,128)(2,1)S(1)}, u32[]{:S(2)}, u32[]{:S(2)}) collective-permute-start(bf16[208,128]{1,0:T(8,128)(2,1)S(1)} %shard_map.100.refs_14_), channel_id=1, source_target_pairs={{0,17},{1,16},{2,19},{3,18},{4,21},{5,20},{6,23},{7,22},{8,25},{9,... | collective-permute-start | bytes 159752 | tf_op jit(solution)/shard_map/ppermute | solution.py:75
  45.9 0.6 collective-permute-done.17.refs_15_
  46.6 1.2 %collective-permute-done.20.refs_18_ = bf16[208,128]{1,0:T(8,128)(2,1)S(1)} collective-permute-done((bf16[208,128]{1,0:T(8,128)(2,1)S(1)}, bf16[208,128]{1,0:T(8,128)(2,1)S(1)}, u32[]{:S(2)}, u32[]{:S(2)}) %collective-permute-start.20) | collective-permute-done | bytes 53280 | tf_op jit(solution)/shard_map/ppermute | solution.py:75
  47.7 2.4 %collective-permute-done.21.refs_19_ = bf16[208,128]{1,0:T(8,128)(2,1)S(1)} collective-permute-done((bf16[208,128]{1,0:T(8,128)(2,1)S(1)}, bf16[208,128]{1,0:T(8,128)(2,1)S(1)}, u32[]{:S(2)}, u32[]{:S(2)}) %collective-permute-start.21) | collective-permute-done | bytes 53280 | tf_op jit(solution)/shard_map/ppermute | solution.py:75
  50.1 3.9 %shard_map.101 = (f32[192,512]{1,0:T(8,128)S(1)}, f32[192,1024]{1,0:T(8,128)S(1)}) custom-call(bf16[384,128]{1,0:T(8,128)(2,1)S(1)} %get-tuple-element.45.refs_0_, bf16[384,128]{1,0:T(8,128)(2,1)S(1)} %collective-permute-done.3.refs_1_, bf16[384,128]{1,0:T(8,128)(2,1)S(1)} %collective-permute-done.4.refs_2_, ...), custom_call_target="tpu_custom_call" | custom-call | flops 805306368 | bytes 2818048 | tf_op jit(solution)/shard_map/pallas_call | solution.py:81
  54.1 3.5 %shard_map.102 = (bf16[128,384]{1,0:T(8,128)(2,1)S(1)}, bf16[128,384]{1,0:T(8,128)(2,1)S(1)}, bf16[128,384]{1,0:T(8,128)(2,1)S(1)}, bf16[128,384]{1,0:T(8,128)(2...) custom-call(bf16[384,128]{1,0:T(8,128)(2,1)S(1)} %get-tuple-element.45.refs_0_, ...), custom_call_target="tpu_custom_call" | custom-call | flops 1006632960 | bytes 10452992 | tf_op jit(solution)/shard_map/pallas_call | solution.py:81
  57.5 0.6 collective-permute-start.27
  58.1 1.3 %collective-permute-done.27.theirs_ref = f32[768,128]{1,0:T(8,128)S(1)} collective-permute-done((f32[768,128]{1,0:T(8,128)S(1)}, f32[768,128]{1,0:T(8,128)S(1)}, u32[]{:S(2)}, u32[]{:S(2)}) %collective-permute-start.27) | collective-permute-done | bytes 393248 | tf_op jit(solution)/shard_map/ppermute | solution.py:75
  59.6 0.6 collective-permute-start.28
  60.2 3.4 %collective-permute-start.24 = (bf16[128,384]{1,0:T(8,128)(2,1)S(1)}, bf16[128,384]{1,0:T(8,128)(2,1)S(1)}, u32[]{:S(2)}, u32[]{:S(2)}) collective-permute-start(bf16[128,384]{1,0:T(8,128)(2,1)S(1)} %get-tuple-element.64), channel_id=1, source_target_pairs={{0,2},{1,3},{2,0},{3,1},{4,6},{5,7},{6,4},{7,5},{8,10},{9,11},{10,... | collective-permute-start | bytes 294920 | tf_op jit(solution)/shard_map/ppermute | solution.py:75
  63.5 0.9 %collective-permute-start.25 = (bf16[128,384]{1,0:T(8,128)(2,1)S(1)}, bf16[128,384]{1,0:T(8,128)(2,1)S(1)}, u32[]{:S(2)}, u32[]{:S(2)}) collective-permute-start(bf16[128,384]{1,0:T(8,128)(2,1)S(1)} %get-tuple-element.65), channel_id=1, source_target_pairs={{0,4},{1,5},{2,6},{3,7},{4,0},{5,1},{6,2},{7,3},{8,12},{9,13},{10,... | collective-permute-start | bytes 294920 | tf_op jit(solution)/shard_map/ppermute | solution.py:75
  64.5 1.5 %collective-permute-start.26 = (bf16[128,384]{1,0:T(8,128)(2,1)S(1)}, bf16[128,384]{1,0:T(8,128)(2,1)S(1)}, u32[]{:S(2)}, u32[]{:S(2)}) collective-permute-start(bf16[128,384]{1,0:T(8,128)(2,1)S(1)} %get-tuple-element.66), channel_id=1, source_target_pairs={{0,6},{1,7},{2,4},{3,5},{4,2},{5,3},{6,0},{7,1},{8,14},{9,15},{10,... | collective-permute-start | bytes 294920 | tf_op jit(solution)/shard_map/ppermute | solution.py:75
  65.9 0.9 %collective-permute-start.29 = (f16[208,128]{1,0:T(8,128)(2,1)S(1)}, f16[208,128]{1,0:T(8,128)(2,1)S(1)}, u32[]{:S(2)}, u32[]{:S(2)}) collective-permute-start(f16[208,128]{1,0:T(8,128)(2,1)S(1)} %convert_element_type.44), channel_id=1, source_target_pairs={{0,16},{1,17},{2,18},{3,19},{4,20},{5,21},{6,22},{7,23},{8,24},{9,... | collective-permute-start | bytes 159752 | tf_op jit(solution)/shard_map/ppermute | solution.py:75
  66.9 2.2 %collective-permute-start.30 = (f16[208,128]{1,0:T(8,128)(2,1)S(1)}, f16[208,128]{1,0:T(8,128)(2,1)S(1)}, u32[]{:S(2)}, u32[]{:S(2)}) collective-permute-start(f16[208,128]{1,0:T(8,128)(2,1)S(1)} %convert_element_type.46), channel_id=1, source_target_pairs={{0,17},{1,16},{2,19},{3,18},{4,21},{5,20},{6,23},{7,22},{8,25},{9,... | collective-permute-start | bytes 159752 | tf_op jit(solution)/shard_map/ppermute | solution.py:75
  69.1 1.5 %collective-permute-done.29 = f16[208,128]{1,0:T(8,128)(2,1)S(1)} collective-permute-done((f16[208,128]{1,0:T(8,128)(2,1)S(1)}, f16[208,128]{1,0:T(8,128)(2,1)S(1)}, u32[]{:S(2)}, u32[]{:S(2)}) %collective-permute-start.29) | collective-permute-done | bytes 53280 | tf_op jit(solution)/shard_map/ppermute | solution.py:75
  70.6 1.4 %collective-permute-done.30 = f16[208,128]{1,0:T(8,128)(2,1)S(1)} collective-permute-done((f16[208,128]{1,0:T(8,128)(2,1)S(1)}, f16[208,128]{1,0:T(8,128)(2,1)S(1)}, u32[]{:S(2)}, u32[]{:S(2)}) %collective-permute-start.30) | collective-permute-done | bytes 53280 | tf_op jit(solution)/shard_map/ppermute | solution.py:75
  72.2 1.2 %collective-permute-start.31 = (f32[48,128]{1,0:T(8,128)S(1)}, f32[48,128]{1,0:T(8,128)S(1)}, u32[]{:S(2)}, u32[]{:S(2)}) collective-permute-start(f32[48,128]{1,0:T(8,128)S(1)} %get-tuple-element.76), channel_id=1, source_target_pairs={{0,2},{1,3},{2,0},{3,1},{4,6},{5,7},{6,4},{7,5},{8,10},{9,11},{10,... | collective-permute-start | bytes 73736 | tf_op jit(solution)/shard_map/ppermute | solution.py:75
  73.3 1.8 %collective-permute-start.32 = (f32[48,128]{1,0:T(8,128)S(1)}, f32[48,128]{1,0:T(8,128)S(1)}, u32[]{:S(2)}, u32[]{:S(2)}) collective-permute-start(f32[48,128]{1,0:T(8,128)S(1)} %get-tuple-element.77), channel_id=1, source_target_pairs={{0,4},{1,5},{2,6},{3,7},{4,0},{5,1},{6,2},{7,3},{8,12},{9,13},{10,... | collective-permute-start | bytes 73736 | tf_op jit(solution)/shard_map/ppermute | solution.py:75
  75.2 1.5 %collective-permute-start.33 = (f32[48,128]{1,0:T(8,128)S(1)}, f32[48,128]{1,0:T(8,128)S(1)}, u32[]{:S(2)}, u32[]{:S(2)}) collective-permute-start(f32[48,128]{1,0:T(8,128)S(1)} %get-tuple-element.78), channel_id=1, source_target_pairs={{0,6},{1,7},{2,4},{3,5},{4,2},{5,3},{6,0},{7,1},{8,14},{9,15},{10,... | collective-permute-start | bytes 73736 | tf_op jit(solution)/shard_map/ppermute | solution.py:75
  76.6 0.9 %shard_map.103 = (bf16[128,768]{1,0:T(8,128)(2,1)}, bf16[128,768]{1,0:T(8,128)(2,1)}) custom-call(bf16[128,384]{1,0:T(8,128)(2,1)S(1)} %get-tuple-element.63.refs_0_, bf16[128,384]{1,0:T(8,128)(2,1)S(1)} %collective-permute-done.24.refs_1_, bf16[128,384]{1,0:T(8,128)(2,1)S(1)} %collective-permute-done.25.refs_2_, ...), custom_call_target="tpu_custom_call" | custom-call | bytes 786432 | tf_op jit(solution)/shard_map/pallas_call | solution.py:81
  78.1 2.7 %collective-permute-done.33.refs_3_ = f32[48,128]{1,0:T(8,128)S(1)} collective-permute-done((f32[48,128]{1,0:T(8,128)S(1)}, f32[48,128]{1,0:T(8,128)S(1)}, u32[]{:S(2)}, u32[]{:S(2)}) %collective-permute-start.33) | collective-permute-done | bytes 24608 | tf_op jit(solution)/shard_map/ppermute | solution.py:75
  80.8 0.8 shard_map.106
  (45 shorter events, 1.9 us)
Async XLA Ops:
  2.3 6.6 %collective-permute-start = (bf16[48,384]{1,0:T(8,128)(2,1)S(1)}, bf16[48,384]{1,0:T(8,128)(2,1)S(1)}, u32[]{:S(2)}, u32[]{:S(2)}) collective-permute-start(bf16[48,384]{1,0:T(8,128)(2,1)S(1)} %get-tuple-element.42), channel_id=1, source_target_pairs={{0,2},{1,3},{2,0},{3,1},{4,6},{5,7},{6,4},{7,5},{8,10},{9,11},{10,... | collective-permute-start | bytes 110600 | tf_op jit(solution)/shard_map/ppermute | solution.py:75
  5.5 5.6 %collective-permute-start.1 = (bf16[48,384]{1,0:T(8,128)(2,1)S(1)}, bf16[48,384]{1,0:T(8,128)(2,1)S(1)}, u32[]{:S(2)}, u32[]{:S(2)}) collective-permute-start(bf16[48,384]{1,0:T(8,128)(2,1)S(1)} %get-tuple-element.43), channel_id=1, source_target_pairs={{0,4},{1,5},{2,6},{3,7},{4,0},{5,1},{6,2},{7,3},{8,12},{9,13},{10,... | collective-permute-start | bytes 110600 | tf_op jit(solution)/shard_map/ppermute | solution.py:75
  8.1 6.1 %collective-permute-start.2 = (bf16[48,384]{1,0:T(8,128)(2,1)S(1)}, bf16[48,384]{1,0:T(8,128)(2,1)S(1)}, u32[]{:S(2)}, u32[]{:S(2)}) collective-permute-start(bf16[48,384]{1,0:T(8,128)(2,1)S(1)} %get-tuple-element.44), channel_id=1, source_target_pairs={{0,6},{1,7},{2,4},{3,5},{4,2},{5,3},{6,0},{7,1},{8,14},{9,15},{10,... | collective-permute-start | bytes 110600 | tf_op jit(solution)/shard_map/ppermute | solution.py:75
  8.1 15.2 %collective-permute-start.10 = (bf16[192,384]{1,0:T(8,128)(2,1)S(1)}, bf16[192,384]{1,0:T(8,128)(2,1)S(1)}, u32[]{:S(2)}, u32[]{:S(2)}) collective-permute-start(bf16[192,384]{1,0:T(8,128)(2,1)S(1)} %get-tuple-element.47), channel_id=1, source_target_pairs={{0,2},{1,3},{2,0},{3,1},{4,6},{5,7},{6,4},{7,5},{8,10},{9,11},{10,... | collective-permute-start | bytes 442376 | tf_op jit(solution)/shard_map/ppermute | solution.py:75
  14.4 4.7 %collective-permute-start.3 = (bf16[384,128]{1,0:T(8,128)(2,1)S(1)}, bf16[384,128]{1,0:T(8,128)(2,1)S(1)}, u32[]{:S(2)}, u32[]{:S(2)}) collective-permute-start(bf16[384,128]{1,0:T(8,128)(2,1)S(1)} %get-tuple-element.45.refs_0_), channel_id=1, source_target_pairs={{0,1},{1,0},{2,3},{3,2},{4,5},{5,4},{6,7},{7,6},{8,9},{9,8},{10,11... | collective-permute-start | bytes 294920 | tf_op jit(solution)/shard_map/ppermute | solution.py:75
  16.0 3.1 %collective-permute-start.4 = (bf16[384,128]{1,0:T(8,128)(2,1)S(1)}, bf16[384,128]{1,0:T(8,128)(2,1)S(1)}, u32[]{:S(2)}, u32[]{:S(2)}) collective-permute-start(bf16[384,128]{1,0:T(8,128)(2,1)S(1)} %get-tuple-element.45.refs_0_), channel_id=1, source_target_pairs={{0,8},{1,9},{2,10},{3,11},{4,12},{5,13},{6,14},{7,15},{8,0},{9,1},... | collective-permute-start | bytes 294920 | tf_op jit(solution)/shard_map/ppermute | solution.py:75
  16.0 5.7 %collective-permute-start.6 = (bf16[384,128]{1,0:T(8,128)(2,1)S(1)}, bf16[384,128]{1,0:T(8,128)(2,1)S(1)}, u32[]{:S(2)}, u32[]{:S(2)}) collective-permute-start(bf16[384,128]{1,0:T(8,128)(2,1)S(1)} %get-tuple-element.45.refs_0_), channel_id=1, source_target_pairs={{0,16},{1,17},{2,18},{3,19},{4,20},{5,21},{6,22},{7,23},{8,24},{9,... | collective-permute-start | bytes 294920 | tf_op jit(solution)/shard_map/ppermute | solution.py:75
  17.5 5.8 %collective-permute-start.7 = (bf16[384,128]{1,0:T(8,128)(2,1)S(1)}, bf16[384,128]{1,0:T(8,128)(2,1)S(1)}, u32[]{:S(2)}, u32[]{:S(2)}) collective-permute-start(bf16[384,128]{1,0:T(8,128)(2,1)S(1)} %get-tuple-element.45.refs_0_), channel_id=1, source_target_pairs={{0,17},{1,16},{2,19},{3,18},{4,21},{5,20},{6,23},{7,22},{8,25},{9,... | collective-permute-start | bytes 294920 | tf_op jit(solution)/shard_map/ppermute | solution.py:75
  19.1 10.6 %collective-permute-start.11 = (bf16[192,384]{1,0:T(8,128)(2,1)S(1)}, bf16[192,384]{1,0:T(8,128)(2,1)S(1)}, u32[]{:S(2)}, u32[]{:S(2)}) collective-permute-start(bf16[192,384]{1,0:T(8,128)(2,1)S(1)} %get-tuple-element.48), channel_id=1, source_target_pairs={{0,4},{1,5},{2,6},{3,7},{4,0},{5,1},{6,2},{7,3},{8,12},{9,13},{10,... | collective-permute-start | bytes 442376 | tf_op jit(solution)/shard_map/ppermute | solution.py:75
  19.1 10.6 %collective-permute-start.12 = (bf16[192,384]{1,0:T(8,128)(2,1)S(1)}, bf16[192,384]{1,0:T(8,128)(2,1)S(1)}, u32[]{:S(2)}, u32[]{:S(2)}) collective-permute-start(bf16[192,384]{1,0:T(8,128)(2,1)S(1)} %get-tuple-element.49), channel_id=1, source_target_pairs={{0,6},{1,7},{2,4},{3,5},{4,2},{5,3},{6,0},{7,1},{8,14},{9,15},{10,... | collective-permute-start | bytes 442376 | tf_op jit(solution)/shard_map/ppermute | solution.py:75
  21.6 3.5 %collective-permute-start.5 = (bf16[384,128]{1,0:T(8,128)(2,1)S(1)}, bf16[384,128]{1,0:T(8,128)(2,1)S(1)}, u32[]{:S(2)}, u32[]{:S(2)}) collective-permute-start(bf16[384,128]{1,0:T(8,128)(2,1)S(1)} %collective-permute-done.3.refs_1_), channel_id=1, source_target_pairs={{0,8},{1,9},{2,10},{3,11},{4,12},{5,13},{6,14},{7,15},{8,0},{9,1},... | collective-permute-start | bytes 294920 | tf_op jit(solution)/shard_map/ppermute | solution.py:75
  23.3 1.8 %collective-permute-start.8 = (bf16[384,128]{1,0:T(8,128)(2,1)S(1)}, bf16[384,128]{1,0:T(8,128)(2,1)S(1)}, u32[]{:S(2)}, u32[]{:S(2)}) collective-permute-start(bf16[384,128]{1,0:T(8,128)(2,1)S(1)} %collective-permute-done.6.refs_4_), channel_id=1, source_target_pairs={{0,8},{1,9},{2,10},{3,11},{4,12},{5,13},{6,14},{7,15},{8,0},{9,1},... | collective-permute-start | bytes 294920 | tf_op jit(solution)/shard_map/ppermute | solution.py:75
  23.3 1.8 %collective-permute-start.9 = (bf16[384,128]{1,0:T(8,128)(2,1)S(1)}, bf16[384,128]{1,0:T(8,128)(2,1)S(1)}, u32[]{:S(2)}, u32[]{:S(2)}) collective-permute-start(bf16[384,128]{1,0:T(8,128)(2,1)S(1)} %collective-permute-done.7.refs_5_), channel_id=1, source_target_pairs={{0,8},{1,9},{2,10},{3,11},{4,12},{5,13},{6,14},{7,15},{8,0},{9,1},... | collective-permute-start | bytes 294920 | tf_op jit(solution)/shard_map/ppermute | solution.py:75
  30.9 2.4 %collective-permute-start.13 = (f32[1536,128]{1,0:T(8,128)S(1)}, f32[1536,128]{1,0:T(8,128)S(1)}, u32[]{:S(2)}, u32[]{:S(2)}) collective-permute-start(f32[1536,128]{1,0:T(8,128)S(1)} %get-tuple-element.56), channel_id=1, source_target_pairs={{0,8},{1,9},{2,10},{3,11},{4,12},{5,13},{6,14},{7,15},{8,0},{9,1},... | collective-permute-start | bytes 2359304 | tf_op jit(solution)/shard_map/ppermute | solution.py:75
  33.4 5.0 %collective-permute-start.14 = (f16[400,128]{1,0:T(8,128)(2,1)S(1)}, f16[400,128]{1,0:T(8,128)(2,1)S(1)}, u32[]{:S(2)}, u32[]{:S(2)}) collective-permute-start(f16[400,128]{1,0:T(8,128)(2,1)S(1)} %convert_element_type.36), channel_id=1, source_target_pairs={{0,1},{1,0},{2,3},{3,2},{4,5},{5,4},{6,7},{7,6},{8,9},{9,8},{10,11... | collective-permute-start | bytes 307208 | tf_op jit(solution)/shard_map/ppermute | solution.py:75
  35.1 5.7 %collective-permute-start.15 = (f16[400,128]{1,0:T(8,128)(2,1)S(1)}, f16[400,128]{1,0:T(8,128)(2,1)S(1)}, u32[]{:S(2)}, u32[]{:S(2)}) collective-permute-start(f16[400,128]{1,0:T(8,128)(2,1)S(1)} %convert_element_type.38), channel_id=1, source_target_pairs={{0,16},{1,17},{2,18},{3,19},{4,20},{5,21},{6,22},{7,23},{8,24},{9,... | collective-permute-start | bytes 307208 | tf_op jit(solution)/shard_map/ppermute | solution.py:75
  36.6 5.6 %collective-permute-start.16 = (f16[400,128]{1,0:T(8,128)(2,1)S(1)}, f16[400,128]{1,0:T(8,128)(2,1)S(1)}, u32[]{:S(2)}, u32[]{:S(2)}) collective-permute-start(f16[400,128]{1,0:T(8,128)(2,1)S(1)} %convert_element_type.40), channel_id=1, source_target_pairs={{0,17},{1,16},{2,19},{3,18},{4,21},{5,20},{6,23},{7,22},{8,25},{9,... | collective-permute-start | bytes 307208 | tf_op jit(solution)/shard_map/ppermute | solution.py:75
  42.4 4.2 %collective-permute-start.17 = (bf16[208,128]{1,0:T(8,128)(2,1)S(1)}, bf16[208,128]{1,0:T(8,128)(2,1)S(1)}, u32[]{:S(2)}, u32[]{:S(2)}) collective-permute-start(bf16[208,128]{1,0:T(8,128)(2,1)S(1)} %shard_map.100.refs_14_), channel_id=1, source_target_pairs={{0,1},{1,0},{2,3},{3,2},{4,5},{5,4},{6,7},{7,6},{8,9},{9,8},{10,11... | collective-permute-start | bytes 159752 | tf_op jit(solution)/shard_map/ppermute | solution.py:75
  43.6 4.1 %collective-permute-start.20 = (bf16[208,128]{1,0:T(8,128)(2,1)S(1)}, bf16[208,128]{1,0:T(8,128)(2,1)S(1)}, u32[]{:S(2)}, u32[]{:S(2)}) collective-permute-start(bf16[208,128]{1,0:T(8,128)(2,1)S(1)} %shard_map.100.refs_14_), channel_id=1, source_target_pairs={{0,16},{1,17},{2,18},{3,19},{4,20},{5,21},{6,22},{7,23},{8,24},{9,... | collective-permute-start | bytes 159752 | tf_op jit(solution)/shard_map/ppermute | solution.py:75
  45.1 5.0 %collective-permute-start.21 = (bf16[208,128]{1,0:T(8,128)(2,1)S(1)}, bf16[208,128]{1,0:T(8,128)(2,1)S(1)}, u32[]{:S(2)}, u32[]{:S(2)}) collective-permute-start(bf16[208,128]{1,0:T(8,128)(2,1)S(1)} %shard_map.100.refs_14_), channel_id=1, source_target_pairs={{0,17},{1,16},{2,19},{3,18},{4,21},{5,20},{6,23},{7,22},{8,25},{9,... | collective-permute-start | bytes 159752 | tf_op jit(solution)/shard_map/ppermute | solution.py:75
  45.9 8.1 %collective-permute-start.18 = (bf16[208,128]{1,0:T(8,128)(2,1)S(1)}, bf16[208,128]{1,0:T(8,128)(2,1)S(1)}, u32[]{:S(2)}, u32[]{:S(2)}) collective-permute-start(bf16[208,128]{1,0:T(8,128)(2,1)S(1)} %shard_map.100.refs_14_), channel_id=1, source_target_pairs={{0,8},{1,9},{2,10},{3,11},{4,12},{5,13},{6,14},{7,15},{8,0},{9,1},... | collective-permute-start | bytes 159752 | tf_op jit(solution)/shard_map/ppermute | solution.py:75
  46.6 7.5 %collective-permute-start.19 = (bf16[208,128]{1,0:T(8,128)(2,1)S(1)}, bf16[208,128]{1,0:T(8,128)(2,1)S(1)}, u32[]{:S(2)}, u32[]{:S(2)}) collective-permute-start(bf16[208,128]{1,0:T(8,128)(2,1)S(1)} %collective-permute-done.17.refs_15_), channel_id=1, source_target_pairs={{0,8},{1,9},{2,10},{3,11},{4,12},{5,13},{6,14},{7,15},{8,0},{9,1},... | collective-permute-start | bytes 159752 | tf_op jit(solution)/shard_map/ppermute | solution.py:75
  47.7 6.3 %collective-permute-start.22 = (bf16[208,128]{1,0:T(8,128)(2,1)S(1)}, bf16[208,128]{1,0:T(8,128)(2,1)S(1)}, u32[]{:S(2)}, u32[]{:S(2)}) collective-permute-start(bf16[208,128]{1,0:T(8,128)(2,1)S(1)} %collective-permute-done.20.refs_18_), channel_id=1, source_target_pairs={{0,8},{1,9},{2,10},{3,11},{4,12},{5,13},{6,14},{7,15},{8,0},{9,1},... | collective-permute-start | bytes 159752 | tf_op jit(solution)/shard_map/ppermute | solution.py:75
  50.1 3.9 %collective-permute-start.23 = (bf16[208,128]{1,0:T(8,128)(2,1)S(1)}, bf16[208,128]{1,0:T(8,128)(2,1)S(1)}, u32[]{:S(2)}, u32[]{:S(2)}) collective-permute-start(bf16[208,128]{1,0:T(8,128)(2,1)S(1)} %collective-permute-done.21.refs_19_), channel_id=1, source_target_pairs={{0,8},{1,9},{2,10},{3,11},{4,12},{5,13},{6,14},{7,15},{8,0},{9,1},... | collective-permute-start | bytes 159752 | tf_op jit(solution)/shard_map/ppermute | solution.py:75
  57.5 1.9 %collective-permute-start.27 = (f32[768,128]{1,0:T(8,128)S(1)}, f32[768,128]{1,0:T(8,128)S(1)}, u32[]{:S(2)}, u32[]{:S(2)}) collective-permute-start(f32[768,128]{1,0:T(8,128)S(1)} %get-tuple-element.70), channel_id=1, source_target_pairs={{0,8},{1,9},{2,10},{3,11},{4,12},{5,13},{6,14},{7,15},{8,0},{9,1},... | collective-permute-start | bytes 1179656 | tf_op jit(solution)/shard_map/ppermute | solution.py:75
  59.6 7.3 %collective-permute-start.28 = (f16[208,128]{1,0:T(8,128)(2,1)S(1)}, f16[208,128]{1,0:T(8,128)(2,1)S(1)}, u32[]{:S(2)}, u32[]{:S(2)}) collective-permute-start(f16[208,128]{1,0:T(8,128)(2,1)S(1)} %convert_element_type.42), channel_id=1, source_target_pairs={{0,1},{1,0},{2,3},{3,2},{4,5},{5,4},{6,7},{7,6},{8,9},{9,8},{10,11... | collective-permute-start | bytes 159752 | tf_op jit(solution)/shard_map/ppermute | solution.py:75
  60.2 15.0 %collective-permute-start.24 = (bf16[128,384]{1,0:T(8,128)(2,1)S(1)}, bf16[128,384]{1,0:T(8,128)(2,1)S(1)}, u32[]{:S(2)}, u32[]{:S(2)}) collective-permute-start(bf16[128,384]{1,0:T(8,128)(2,1)S(1)} %get-tuple-element.64), channel_id=1, source_target_pairs={{0,2},{1,3},{2,0},{3,1},{4,6},{5,7},{6,4},{7,5},{8,10},{9,11},{10,... | collective-permute-start | bytes 294920 | tf_op jit(solution)/shard_map/ppermute | solution.py:75
  63.5 13.1 %collective-permute-start.25 = (bf16[128,384]{1,0:T(8,128)(2,1)S(1)}, bf16[128,384]{1,0:T(8,128)(2,1)S(1)}, u32[]{:S(2)}, u32[]{:S(2)}) collective-permute-start(bf16[128,384]{1,0:T(8,128)(2,1)S(1)} %get-tuple-element.65), channel_id=1, source_target_pairs={{0,4},{1,5},{2,6},{3,7},{4,0},{5,1},{6,2},{7,3},{8,12},{9,13},{10,... | collective-permute-start | bytes 294920 | tf_op jit(solution)/shard_map/ppermute | solution.py:75
  64.5 12.2 %collective-permute-start.26 = (bf16[128,384]{1,0:T(8,128)(2,1)S(1)}, bf16[128,384]{1,0:T(8,128)(2,1)S(1)}, u32[]{:S(2)}, u32[]{:S(2)}) collective-permute-start(bf16[128,384]{1,0:T(8,128)(2,1)S(1)} %get-tuple-element.66), channel_id=1, source_target_pairs={{0,6},{1,7},{2,4},{3,5},{4,2},{5,3},{6,0},{7,1},{8,14},{9,15},{10,... | collective-permute-start | bytes 294920 | tf_op jit(solution)/shard_map/ppermute | solution.py:75
  65.9 4.6 %collective-permute-start.29 = (f16[208,128]{1,0:T(8,128)(2,1)S(1)}, f16[208,128]{1,0:T(8,128)(2,1)S(1)}, u32[]{:S(2)}, u32[]{:S(2)}) collective-permute-start(f16[208,128]{1,0:T(8,128)(2,1)S(1)} %convert_element_type.44), channel_id=1, source_target_pairs={{0,16},{1,17},{2,18},{3,19},{4,20},{5,21},{6,22},{7,23},{8,24},{9,... | collective-permute-start | bytes 159752 | tf_op jit(solution)/shard_map/ppermute | solution.py:75
  66.9 5.1 %collective-permute-start.30 = (f16[208,128]{1,0:T(8,128)(2,1)S(1)}, f16[208,128]{1,0:T(8,128)(2,1)S(1)}, u32[]{:S(2)}, u32[]{:S(2)}) collective-permute-start(f16[208,128]{1,0:T(8,128)(2,1)S(1)} %convert_element_type.46), channel_id=1, source_target_pairs={{0,17},{1,16},{2,19},{3,18},{4,21},{5,20},{6,23},{7,22},{8,25},{9,... | collective-permute-start | bytes 159752 | tf_op jit(solution)/shard_map/ppermute | solution.py:75
  72.2 5.4 %collective-permute-start.31 = (f32[48,128]{1,0:T(8,128)S(1)}, f32[48,128]{1,0:T(8,128)S(1)}, u32[]{:S(2)}, u32[]{:S(2)}) collective-permute-start(f32[48,128]{1,0:T(8,128)S(1)} %get-tuple-element.76), channel_id=1, source_target_pairs={{0,2},{1,3},{2,0},{3,1},{4,6},{5,7},{6,4},{7,5},{8,10},{9,11},{10,... | collective-permute-start | bytes 73736 | tf_op jit(solution)/shard_map/ppermute | solution.py:75
  73.3 4.7 %collective-permute-start.32 = (f32[48,128]{1,0:T(8,128)S(1)}, f32[48,128]{1,0:T(8,128)S(1)}, u32[]{:S(2)}, u32[]{:S(2)}) collective-permute-start(f32[48,128]{1,0:T(8,128)S(1)} %get-tuple-element.77), channel_id=1, source_target_pairs={{0,4},{1,5},{2,6},{3,7},{4,0},{5,1},{6,2},{7,3},{8,12},{9,13},{10,... | collective-permute-start | bytes 73736 | tf_op jit(solution)/shard_map/ppermute | solution.py:75
  75.2 5.6 %collective-permute-start.33 = (f32[48,128]{1,0:T(8,128)S(1)}, f32[48,128]{1,0:T(8,128)S(1)}, u32[]{:S(2)}, u32[]{:S(2)}) collective-permute-start(f32[48,128]{1,0:T(8,128)S(1)} %get-tuple-element.78), channel_id=1, source_target_pairs={{0,6},{1,7},{2,4},{3,5},{4,2},{5,3},{6,0},{7,1},{8,14},{9,15},{10,... | collective-permute-start | bytes 73736 | tf_op jit(solution)/shard_map/ppermute | solution.py:75

commit v8 on v7

--- a/solution.py
+++ b/solution.py
@@ -42,7 +42,7 @@
         return (
             power(npa)
             and power(npb)
-            and npb % GROUPS == 0
+            and npb % (2 * GROUPS) == 0
             and npa * npb // GROUPS <= MOST_IN_PLANE
             and lat_rows * GROUPS == LANES
             and rows == LANES
@@ -382,10 +382,14 @@
     return call(kernel, outs, parts)[0]
 
 
-def encoder_pass(plan, lats, pts, kept, mixes, before):
+def encoder_pass(plan, lats, pts, kept, mixes, before, carried=None):
     places = [(part, at) for part, (heads, _) in enumerate(before) for at in range(len(heads))]
     n_lat, n_pts, n_mix = len(lats), len(pts), len(mixes)
     c, m, hs = plan.cols, plan.latents, plan.heads
+
+    held = [k for k in range(plan.plane) if bool(k & plan.fast) == bool(carried)]
+    mixes = [mixes[k] for k in held]
+    n_mix = len(mixes)
 
     def kernel(*refs):
         refs = list(refs)
@@ -399,28 +403,32 @@
         kept_refs = take(len(kept))
         mix_refs = take(n_mix)
         parts_in = [take(2) for _ in before]
-        pts_outs, lat_outs = take(n_pts), plan.views(*take(2), c)
+        so_far = take(2) if carried else None
+        pts_outs = take(n_pts if carried else 2)
+        (stack,) = take(1)
+        lat_outs = plan.views(stack, stack, c)
         query, mix, keys_t, values, ds, encs = refs
         for k, ref in enumerate(lat_refs):
             query[:, k * plan.block : (k + 1) * plan.block] = ref[:c, :]
-        for k, ref in enumerate(mix_refs):
+        for k, ref in zip(held, mix_refs, strict=True):
             mix[:, k * plan.block : (k + 1) * plan.block] = ref[...]
         for j, ref in enumerate(pts_refs):
             rows = slice(j * plan.rows, (j + 1) * plan.rows)
             keys_t[:, rows] = turned(ref[: plan.rows, :c])
             across = [ref[plan.rows :, h * plan.rows : (h + 1) * plan.rows] for h in range(hs)]
             values[rows, :] = turned(jnp.concatenate(across, axis=0))
-        tail = mix[c:, :].astype(jnp.float32)
-        columns = (tail[:hs] + tail[hs : 2 * hs]) + tail[2 * hs : 3 * hs]
         tiles = lane_tiles(plan)
         sums = {}
+        chosen = [t for t, s in enumerate(tiles) if bool(s.start // plan.block & plan.fast) == bool(carried)]
 
         def weigh(h, t, slot):
             mine, lanes = slice(h * HEAD_DIM, (h + 1) * HEAD_DIM), tiles[t]
             enc = jnp.concatenate([ref[h, :, lanes] for ref in kept_refs], axis=0)
             grad = nn(values[:, mine], mix[mine, lanes])
+            tail = [mix[c : c + 16, lanes].astype(jnp.float32)[n * hs + h : n * hs + h + 1] for n in range(3)]
+            column = (tail[0] + tail[1]) + tail[2]
             encs[slot] = enc.astype(jnp.bfloat16)
-            ds[slot] = (enc * (grad - columns[h : h + 1, lanes])).astype(jnp.bfloat16)
+            ds[slot] = (enc * (grad - column)).astype(jnp.bfloat16)
 
         def gather(h, t, slot):
             mine, lanes = slice(h * HEAD_DIM, (h + 1) * HEAD_DIM), tiles[t]
@@ -430,11 +438,20 @@
             lat = (lat_in[put, lanes] + nn(keys_t[mine, :], ds[slot])) * HEAD_DIM**-0.5
             store_blocks(plan, lat_outs, mine, lanes, lat)
             key, value = nt(query[mine, lanes], ds[slot]), nt(mix[mine, lanes], encs[slot])
-            key = key + (sums[h][0] if t else key_in[put, :])
-            sums[h] = (key, value + sums[h][1] if t else value)
-            if t < len(tiles) - 1:
+            if t != chosen[0]:
+                key, value = key + sums[h][0], value + sums[h][1]
+            elif carried:
+                key, value = key + so_far[0][mine, :], value + so_far[1][mine, :]
+            else:
+                key = key + key_in[put, :]
+            sums[h] = key, value
+            if t != chosen[-1]:
                 return
             key, value = sums.pop(h)
+            if not carried:
+                pts_outs[0][mine, :] = key
+                pts_outs[1][mine, :] = value
+                return
             key = (key * HEAD_DIM**-0.5).T.astype(jnp.bfloat16)
             value = value.T.astype(jnp.bfloat16)
             for j, out in enumerate(pts_outs):
@@ -442,7 +459,7 @@
                 out[:, mine] = key[rows]
                 out[:, c + h * HEAD_DIM : c + (h + 1) * HEAD_DIM] = value[rows]
 
-        work = [(h, t) for h in range(hs) for t in range(len(tiles))]
+        work = [(h, t) for h in range(hs) for t in chosen]
         for n, place in enumerate(work):
             weigh(*place, n % SLOTS)
             if n >= LAG:
@@ -450,8 +467,10 @@
         for n in range(len(work) - LAG, len(work)):
             gather(*work[n], n % SLOTS)
 
-    outs = [shaped((plan.rows, 2 * c), jnp.bfloat16)] * n_pts
-    outs += [plan.stack(c)] * 2
+    outs = [shaped((c, plan.points), jnp.float32)] * 2
+    if carried:
+        outs = [shaped((plan.rows, 2 * c), jnp.bfloat16)] * n_pts
+    outs += [plan.stack(c)]
     scratch = [
         pltpu.VMEM((c, m), jnp.bfloat16),
         pltpu.VMEM((plan.ct_rows, m), jnp.bfloat16),
@@ -460,10 +479,10 @@
         pltpu.VMEM((SLOTS, plan.points, 2 * plan.block), jnp.bfloat16),
         pltpu.VMEM((SLOTS, plan.points, 2 * plan.block), jnp.bfloat16),
     ]
-    flops = 10 * plan.points * m * c
-    args = (*lats, *pts, *kept, *mixes, *(a for _, part in before for a in part))
+    flops = 5 * plan.points * m * c
+    args = (*lats, *pts, *kept, *mixes, *(a for _, part in before for a in part), *(carried or ()))
     got = call(kernel, outs, args, scratch, flops)
-    return got[:n_pts], got[n_pts:]
+    return got[:-1], got[-1]
 
 
 def reduce_latents(plan, parts):
@@ -552,8 +571,9 @@
     every = tuple(range(plan.heads))
     before = [(every, decoder_pass(plan, lats, pts, dec_norm, every))]
     mixes = to_plane(reduce_mix(plan, sums))
-    pts_out, lat_out = encoder_pass(plan, lats, pts, kept, mixes, before)
-    lat_out = sum_chips(sum_cores(*lat_out))
+    carried, lat_mine = encoder_pass(plan, lats, pts, kept, mixes, before)
+    pts_out, lat_away = encoder_pass(plan, lats, pts, kept, mixes, before, carried)
+    lat_out = sum_chips(sum_cores(lat_mine, lat_away))
     pts_out = over_group(pts_out)
     lat_rows = over_group(reduce_latents(plan, lat_out))
     keys_grad, values_grad = place_points(plan, pts_out)

time: 81.8 us -> 82.2 us (level)
    pallas_call x13 -> x14, Pallas kernels: 15.4 us -> 15.8 us  [call(): pl.pallas_call(kernel, out_shape=tuple(outs), in_specs=[pl.BlockSpec(memo...]
  transfers between devices with their start and end apart: 34 -> 34, of which waited for: 18 -> 18; matrix products, arithmetic and copies ran while one was open for 0% -> 0% of each run, Pallas kernels for 10% -> 12%
where the time goes in v8:
time: 82.2 us; the launch traced here: 82 us
  starting transfers between devices  33.5 us (41%)
  waiting for transfers between devices  31.7 us (39%)
  Pallas kernels  15.8 us (19%)
  between operations  0.84 us (1%)
    ppermute x34, starting transfers between devices, exchange(): return lax.ppermute(value, AXES, pairs)  33.5 us
    ppermute x34, waiting for transfers between devices, exchange(): return lax.ppermute(value, AXES, pairs)  31.7 us
    pallas_call x14, Pallas kernels, call(): pl.pallas_call(kernel, out_shape=tuple(outs), in_specs=[pl.BlockSpec(memo...  15.8 us
  transfers between devices with their start and end apart: 34, of which 18 were waited for; matrix products, arithmetic and copies ran while one was open for 0% of the time, Pallas kernels for 12%

profile of v8, /device:TPU:0, one launch (start us, length us, event | category | flops | bytes accessed | tf_op | source)
XLA Modules:
  0.0 82.0 jit_solution(14132580611882104816)
XLA Ops:
  0.6 1.7 %shard_map.94 = (bf16[48,384]{1,0:T(8,128)(2,1)S(1)}, bf16[48,384]{1,0:T(8,128)(2,1)S(1)}, bf16[48,384]{1,0:T(8,128)(2,1)S(1)}, bf16[48,384]{1,0:T(8,128)(2,1)S(...) custom-call(bf16[32,768]{1,0:T(8,128)(2,1)} %refs_0_.2, ...), custom_call_target="tpu_custom_call" | custom-call | bytes 1431552 | tf_op jit(solution)/shard_map/pallas_call | solution.py:81
  2.3 3.1 %collective-permute-start = (bf16[48,384]{1,0:T(8,128)(2,1)S(1)}, bf16[48,384]{1,0:T(8,128)(2,1)S(1)}, u32[]{:S(2)}, u32[]{:S(2)}) collective-permute-start(bf16[48,384]{1,0:T(8,128)(2,1)S(1)} %get-tuple-element.44), channel_id=1, source_target_pairs={{0,2},{1,3},{2,0},{3,1},{4,6},{5,7},{6,4},{7,5},{8,10},{9,11},{10,... | collective-permute-start | bytes 110600 | tf_op jit(solution)/shard_map/ppermute | solution.py:75
  5.5 2.6 %collective-permute-start.1 = (bf16[48,384]{1,0:T(8,128)(2,1)S(1)}, bf16[48,384]{1,0:T(8,128)(2,1)S(1)}, u32[]{:S(2)}, u32[]{:S(2)}) collective-permute-start(bf16[48,384]{1,0:T(8,128)(2,1)S(1)} %get-tuple-element.45), channel_id=1, source_target_pairs={{0,4},{1,5},{2,6},{3,7},{4,0},{5,1},{6,2},{7,3},{8,12},{9,13},{10,... | collective-permute-start | bytes 110600 | tf_op jit(solution)/shard_map/ppermute | solution.py:75
  8.1 0.9 %collective-permute-start.10 = (bf16[192,384]{1,0:T(8,128)(2,1)S(1)}, bf16[192,384]{1,0:T(8,128)(2,1)S(1)}, u32[]{:S(2)}, u32[]{:S(2)}) collective-permute-start(bf16[192,384]{1,0:T(8,128)(2,1)S(1)} %get-tuple-element.49), channel_id=1, source_target_pairs={{0,2},{1,3},{2,0},{3,1},{4,6},{5,7},{6,4},{7,5},{8,10},{9,11},{10,... | collective-permute-start | bytes 442376 | tf_op jit(solution)/shard_map/ppermute | solution.py:75
  9.0 2.1 %collective-permute-done.1.refs_2_ = bf16[48,384]{1,0:T(8,128)(2,1)S(1)} collective-permute-done((bf16[48,384]{1,0:T(8,128)(2,1)S(1)}, bf16[48,384]{1,0:T(8,128)(2,1)S(1)}, u32[]{:S(2)}, u32[]{:S(2)}) %collective-permute-start.1) | collective-permute-done | bytes 36896 | tf_op jit(solution)/shard_map/ppermute | solution.py:75
  11.1 3.1 %collective-permute-done.2.refs_3_ = bf16[48,384]{1,0:T(8,128)(2,1)S(1)} collective-permute-done((bf16[48,384]{1,0:T(8,128)(2,1)S(1)}, bf16[48,384]{1,0:T(8,128)(2,1)S(1)}, u32[]{:S(2)}, u32[]{:S(2)}) %collective-permute-start.2) | collective-permute-done | bytes 36896 | tf_op jit(solution)/shard_map/ppermute | solution.py:75
  14.4 1.6 %collective-permute-start.3 = (bf16[384,128]{1,0:T(8,128)(2,1)S(1)}, bf16[384,128]{1,0:T(8,128)(2,1)S(1)}, u32[]{:S(2)}, u32[]{:S(2)}) collective-permute-start(bf16[384,128]{1,0:T(8,128)(2,1)S(1)} %get-tuple-element.47.refs_0_), channel_id=1, source_target_pairs={{0,1},{1,0},{2,3},{3,2},{4,5},{5,4},{6,7},{7,6},{8,9},{9,8},{10,11... | collective-permute-start | bytes 294920 | tf_op jit(solution)/shard_map/ppermute | solution.py:75
  16.0 1.5 %collective-permute-start.6 = (bf16[384,128]{1,0:T(8,128)(2,1)S(1)}, bf16[384,128]{1,0:T(8,128)(2,1)S(1)}, u32[]{:S(2)}, u32[]{:S(2)}) collective-permute-start(bf16[384,128]{1,0:T(8,128)(2,1)S(1)} %get-tuple-element.47.refs_0_), channel_id=1, source_target_pairs={{0,16},{1,17},{2,18},{3,19},{4,20},{5,21},{6,22},{7,23},{8,24},{9,... | collective-permute-start | bytes 294920 | tf_op jit(solution)/shard_map/ppermute | solution.py:75
  17.9 1.1 %collective-permute-done.3.refs_1_ = bf16[384,128]{1,0:T(8,128)(2,1)S(1)} collective-permute-done((bf16[384,128]{1,0:T(8,128)(2,1)S(1)}, bf16[384,128]{1,0:T(8,128)(2,1)S(1)}, u32[]{:S(2)}, u32[]{:S(2)}) %collective-permute-start.3) | collective-permute-done | bytes 98336 | tf_op jit(solution)/shard_map/ppermute | solution.py:75
  19.1 1.0 %collective-permute-start.12 = (bf16[192,384]{1,0:T(8,128)(2,1)S(1)}, bf16[192,384]{1,0:T(8,128)(2,1)S(1)}, u32[]{:S(2)}, u32[]{:S(2)}) collective-permute-start(bf16[192,384]{1,0:T(8,128)(2,1)S(1)} %get-tuple-element.51), channel_id=1, source_target_pairs={{0,6},{1,7},{2,4},{3,5},{4,2},{5,3},{6,0},{7,1},{8,14},{9,15},{10,... | collective-permute-start | bytes 442376 | tf_op jit(solution)/shard_map/ppermute | solution.py:75
  20.1 1.5 %collective-permute-done.6.refs_4_ = bf16[384,128]{1,0:T(8,128)(2,1)S(1)} collective-permute-done((bf16[384,128]{1,0:T(8,128)(2,1)S(1)}, bf16[384,128]{1,0:T(8,128)(2,1)S(1)}, u32[]{:S(2)}, u32[]{:S(2)}) %collective-permute-start.6) | collective-permute-done | bytes 98336 | tf_op jit(solution)/shard_map/ppermute | solution.py:75
  21.6 1.6 %collective-permute-done.7.refs_5_ = bf16[384,128]{1,0:T(8,128)(2,1)S(1)} collective-permute-done((bf16[384,128]{1,0:T(8,128)(2,1)S(1)}, bf16[384,128]{1,0:T(8,128)(2,1)S(1)}, u32[]{:S(2)}, u32[]{:S(2)}) %collective-permute-start.7) | collective-permute-done | bytes 98336 | tf_op jit(solution)/shard_map/ppermute | solution.py:75
  23.8 1.3 %shard_map.96.refs_11_ = f32[3,1024]{1,0:T(4,128)S(1)} custom-call(f32[12,1024]{1,0:T(8,128)} %refs_0_.3), custom_call_target="tpu_custom_call" | custom-call | bytes 61440 | tf_op jit(solution)/shard_map/pallas_call | solution.py:81
  25.1 1.3 %shard_map.97 = (f32[1536,128]{1,0:T(8,128)S(1)}, f32[1536,128]{1,0:T(8,128)S(1)}, f32[3,256,1024]{2,1,0:T(8,128)S(1)}) custom-call(bf16[384,128]{1,0:T(8,128)(2,1)S(1)} %get-tuple-element.47.refs_0_, bf16[384,128]{1,0:T(8,128)(2,1)S(1)} %collective-permute-done.3.refs_1_, bf16[384,128]{1,0:T(8,128)(2,1)S(1)} %collective-permute-done.4.refs_2_, ...), custom_call_target="tpu_custom_call" | custom-call | flops 301989888 | bytes 6074368 | tf_op jit(solution)/shard_map/pallas_call | solution.py:81
  26.4 3.2 %collective-permute-done.11.refs_8_.refs_10_ = bf16[192,384]{1,0:T(8,128)(2,1)S(1)} collective-permute-done((bf16[192,384]{1,0:T(8,128)(2,1)S(1)}, bf16[192,384]{1,0:T(8,128)(2,1)S(1)}, u32[]{:S(2)}, u32[]{:S(2)}) %collective-permute-start.11) | collective-permute-done | bytes 147488 | tf_op jit(solution)/shard_map/ppermute | solution.py:75
  29.6 1.3 %shard_map.98 = (f32[1536,128]{1,0:T(8,128)S(1)}, f32[1536,128]{1,0:T(8,128)S(1)}, f32[3,256,1024]{2,1,0:T(8,128)S(1)}) custom-call(bf16[384,128]{1,0:T(8,128)(2,1)S(1)} %get-tuple-element.47.refs_0_, bf16[384,128]{1,0:T(8,128)(2,1)S(1)} %collective-permute-done.3.refs_1_, bf16[384,128]{1,0:T(8,128)(2,1)S(1)} %collective-permute-done.4.refs_2_, ...), custom_call_target="tpu_custom_call" | custom-call | flops 301989888 | bytes 7647232 | tf_op jit(solution)/shard_map/pallas_call | solution.py:81
  31.0 2.3 %collective-permute-done.13.theirs_ref = f32[1536,128]{1,0:T(8,128)S(1)} collective-permute-done((f32[1536,128]{1,0:T(8,128)S(1)}, f32[1536,128]{1,0:T(8,128)S(1)}, u32[]{:S(2)}, u32[]{:S(2)}) %collective-permute-start.13) | collective-permute-done | bytes 786464 | tf_op jit(solution)/shard_map/ppermute | solution.py:75
  33.5 1.6 %collective-permute-start.14 = (f16[400,128]{1,0:T(8,128)(2,1)S(1)}, f16[400,128]{1,0:T(8,128)(2,1)S(1)}, u32[]{:S(2)}, u32[]{:S(2)}) collective-permute-start(f16[400,128]{1,0:T(8,128)(2,1)S(1)} %convert_element_type.36), channel_id=1, source_target_pairs={{0,1},{1,0},{2,3},{3,2},{4,5},{5,4},{6,7},{7,6},{8,9},{9,8},{10,11... | collective-permute-start | bytes 307208 | tf_op jit(solution)/shard_map/ppermute | solution.py:75
  35.1 1.6 %collective-permute-start.15 = (f16[400,128]{1,0:T(8,128)(2,1)S(1)}, f16[400,128]{1,0:T(8,128)(2,1)S(1)}, u32[]{:S(2)}, u32[]{:S(2)}) collective-permute-start(f16[400,128]{1,0:T(8,128)(2,1)S(1)} %convert_element_type.38), channel_id=1, source_target_pairs={{0,16},{1,17},{2,18},{3,19},{4,20},{5,21},{6,22},{7,23},{8,24},{9,... | collective-permute-start | bytes 307208 | tf_op jit(solution)/shard_map/ppermute | solution.py:75
  36.7 0.5 collective-permute-start.16
  37.2 1.3 %collective-permute-done.14 = f16[400,128]{1,0:T(8,128)(2,1)S(1)} collective-permute-done((f16[400,128]{1,0:T(8,128)(2,1)S(1)}, f16[400,128]{1,0:T(8,128)(2,1)S(1)}, u32[]{:S(2)}, u32[]{:S(2)}) %collective-permute-start.14) | collective-permute-done | bytes 102432 | tf_op jit(solution)/shard_map/ppermute | solution.py:75
  38.5 2.3 %collective-permute-done.15 = f16[400,128]{1,0:T(8,128)(2,1)S(1)} collective-permute-done((f16[400,128]{1,0:T(8,128)(2,1)S(1)}, f16[400,128]{1,0:T(8,128)(2,1)S(1)}, u32[]{:S(2)}, u32[]{:S(2)}) %collective-permute-start.15) | collective-permute-done | bytes 102432 | tf_op jit(solution)/shard_map/ppermute | solution.py:75
  40.8 1.5 %collective-permute-done.16 = f16[400,128]{1,0:T(8,128)(2,1)S(1)} collective-permute-done((f16[400,128]{1,0:T(8,128)(2,1)S(1)}, f16[400,128]{1,0:T(8,128)(2,1)S(1)}, u32[]{:S(2)}, u32[]{:S(2)}) %collective-permute-start.16) | collective-permute-done | bytes 102432 | tf_op jit(solution)/shard_map/ppermute | solution.py:75
  42.4 1.2 %collective-permute-start.18 = (bf16[208,128]{1,0:T(8,128)(2,1)S(1)}, bf16[208,128]{1,0:T(8,128)(2,1)S(1)}, u32[]{:S(2)}, u32[]{:S(2)}) collective-permute-start(bf16[208,128]{1,0:T(8,128)(2,1)S(1)} %shard_map.100.refs_14_), channel_id=1, source_target_pairs={{0,1},{1,0},{2,3},{3,2},{4,5},{5,4},{6,7},{7,6},{8,9},{9,8},{10,11... | collective-permute-start | bytes 159752 | tf_op jit(solution)/shard_map/ppermute | solution.py:75
  43.6 1.5 %collective-permute-start.20 = (bf16[208,128]{1,0:T(8,128)(2,1)S(1)}, bf16[208,128]{1,0:T(8,128)(2,1)S(1)}, u32[]{:S(2)}, u32[]{:S(2)}) collective-permute-start(bf16[208,128]{1,0:T(8,128)(2,1)S(1)} %shard_map.100.refs_14_), channel_id=1, source_target_pairs={{0,16},{1,17},{2,18},{3,19},{4,20},{5,21},{6,22},{7,23},{8,24},{9,... | collective-permute-start | bytes 159752 | tf_op jit(solution)/shard_map/ppermute | solution.py:75
  45.1 0.8 %collective-permute-start.22 = (bf16[208,128]{1,0:T(8,128)(2,1)S(1)}, bf16[208,128]{1,0:T(8,128)(2,1)S(1)}, u32[]{:S(2)}, u32[]{:S(2)}) collective-permute-start(bf16[208,128]{1,0:T(8,128)(2,1)S(1)} %shard_map.100.refs_14_), channel_id=1, source_target_pairs={{0,17},{1,16},{2,19},{3,18},{4,21},{5,20},{6,23},{7,22},{8,25},{9,... | collective-permute-start | bytes 159752 | tf_op jit(solution)/shard_map/ppermute | solution.py:75
  45.9 0.6 collective-permute-done.18.refs_15_
  46.6 1.2 %collective-permute-done.20.refs_16_ = bf16[208,128]{1,0:T(8,128)(2,1)S(1)} collective-permute-done((bf16[208,128]{1,0:T(8,128)(2,1)S(1)}, bf16[208,128]{1,0:T(8,128)(2,1)S(1)}, u32[]{:S(2)}, u32[]{:S(2)}) %collective-permute-start.20) | collective-permute-done | bytes 53280 | tf_op jit(solution)/shard_map/ppermute | solution.py:75
  47.8 2.4 %collective-permute-done.22.refs_17_ = bf16[208,128]{1,0:T(8,128)(2,1)S(1)} collective-permute-done((bf16[208,128]{1,0:T(8,128)(2,1)S(1)}, bf16[208,128]{1,0:T(8,128)(2,1)S(1)}, u32[]{:S(2)}, u32[]{:S(2)}) %collective-permute-start.22) | collective-permute-done | bytes 53280 | tf_op jit(solution)/shard_map/ppermute | solution.py:75
  50.1 3.9 %shard_map.101 = (f32[192,512]{1,0:T(8,128)S(1)}, f32[192,1024]{1,0:T(8,128)S(1)}) custom-call(bf16[384,128]{1,0:T(8,128)(2,1)S(1)} %get-tuple-element.47.refs_0_, bf16[384,128]{1,0:T(8,128)(2,1)S(1)} %collective-permute-done.3.refs_1_, bf16[384,128]{1,0:T(8,128)(2,1)S(1)} %collective-permute-done.4.refs_2_, ...), custom_call_target="tpu_custom_call" | custom-call | flops 805306368 | bytes 2818048 | tf_op jit(solution)/shard_map/pallas_call | solution.py:81
  54.1 1.8 %shard_map.102 = (f32[192,512]{1,0:T(8,128)S(1)}, f32[192,512]{1,0:T(8,128)S(1)}, f32[768,128]{1,0:T(8,128)S(1)}) custom-call(bf16[384,128]{1,0:T(8,128)(2,1)S(1)} %get-tuple-element.47.refs_0_, bf16[384,128]{1,0:T(8,128)(2,1)S(1)} %collective-permute-done.3.refs_1_, bf16[384,128]{1,0:T(8,128)(2,1)S(1)} %collective-permute-done.4.refs_2_, ...), custom_call_target="tpu_custom_call" | custom-call | flops 503316480 | bytes 10240000 | tf_op jit(solution)/shard_map/pallas_call | solution.py:81
  55.9 2.1 %shard_map.103 = (bf16[128,384]{1,0:T(8,128)(2,1)S(1)}, bf16[128,384]{1,0:T(8,128)(2,1)S(1)}, bf16[128,384]{1,0:T(8,128)(2,1)S(1)}, bf16[128,384]{1,0:T(8,128)(2,1)S(1)}, f32[768,128]{1,0:T(8,128)S(1)}) custom-call(bf16[384,128]{1,0:T(8,128)(2,1)S(1)} %get-tuple-element.47.refs_0_, bf16[384,128]{1,0:T(8,128)(2,1)S(1)} %collective-permute-done.3.refs_1_, ...), custom_call_target="tpu_custom_call" | custom-call | flops 503316480 | bytes 10633216 | tf_op jit(solution)/shard_map/pallas_call | solution.py:81
  57.9 0.6 collective-permute-start.27
  58.5 1.3 %collective-permute-done.27.theirs_ref = f32[768,128]{1,0:T(8,128)S(1)} collective-permute-done((f32[768,128]{1,0:T(8,128)S(1)}, f32[768,128]{1,0:T(8,128)S(1)}, u32[]{:S(2)}, u32[]{:S(2)}) %collective-permute-start.27) | collective-permute-done | bytes 393248 | tf_op jit(solution)/shard_map/ppermute | solution.py:75
  60.0 0.6 collective-permute-start.28
  60.6 3.4 %collective-permute-start.24 = (bf16[128,384]{1,0:T(8,128)(2,1)S(1)}, bf16[128,384]{1,0:T(8,128)(2,1)S(1)}, u32[]{:S(2)}, u32[]{:S(2)}) collective-permute-start(bf16[128,384]{1,0:T(8,128)(2,1)S(1)} %get-tuple-element.68), channel_id=1, source_target_pairs={{0,2},{1,3},{2,0},{3,1},{4,6},{5,7},{6,4},{7,5},{8,10},{9,11},{10,... | collective-permute-start | bytes 294920 | tf_op jit(solution)/shard_map/ppermute | solution.py:75
  63.9 0.9 %collective-permute-start.25 = (bf16[128,384]{1,0:T(8,128)(2,1)S(1)}, bf16[128,384]{1,0:T(8,128)(2,1)S(1)}, u32[]{:S(2)}, u32[]{:S(2)}) collective-permute-start(bf16[128,384]{1,0:T(8,128)(2,1)S(1)} %get-tuple-element.69), channel_id=1, source_target_pairs={{0,4},{1,5},{2,6},{3,7},{4,0},{5,1},{6,2},{7,3},{8,12},{9,13},{10,... | collective-permute-start | bytes 294920 | tf_op jit(solution)/shard_map/ppermute | solution.py:75
  64.9 1.5 %collective-permute-start.26 = (bf16[128,384]{1,0:T(8,128)(2,1)S(1)}, bf16[128,384]{1,0:T(8,128)(2,1)S(1)}, u32[]{:S(2)}, u32[]{:S(2)}) collective-permute-start(bf16[128,384]{1,0:T(8,128)(2,1)S(1)} %get-tuple-element.70), channel_id=1, source_target_pairs={{0,6},{1,7},{2,4},{3,5},{4,2},{5,3},{6,0},{7,1},{8,14},{9,15},{10,... | collective-permute-start | bytes 294920 | tf_op jit(solution)/shard_map/ppermute | solution.py:75
  66.3 0.9 %collective-permute-start.29 = (f16[208,128]{1,0:T(8,128)(2,1)S(1)}, f16[208,128]{1,0:T(8,128)(2,1)S(1)}, u32[]{:S(2)}, u32[]{:S(2)}) collective-permute-start(f16[208,128]{1,0:T(8,128)(2,1)S(1)} %convert_element_type.44), channel_id=1, source_target_pairs={{0,16},{1,17},{2,18},{3,19},{4,20},{5,21},{6,22},{7,23},{8,24},{9,... | collective-permute-start | bytes 159752 | tf_op jit(solution)/shard_map/ppermute | solution.py:75
  67.3 2.2 %collective-permute-start.30 = (f16[208,128]{1,0:T(8,128)(2,1)S(1)}, f16[208,128]{1,0:T(8,128)(2,1)S(1)}, u32[]{:S(2)}, u32[]{:S(2)}) collective-permute-start(f16[208,128]{1,0:T(8,128)(2,1)S(1)} %convert_element_type.46), channel_id=1, source_target_pairs={{0,17},{1,16},{2,19},{3,18},{4,21},{5,20},{6,23},{7,22},{8,25},{9,... | collective-permute-start | bytes 159752 | tf_op jit(solution)/shard_map/ppermute | solution.py:75
  69.5 1.5 %collective-permute-done.29 = f16[208,128]{1,0:T(8,128)(2,1)S(1)} collective-permute-done((f16[208,128]{1,0:T(8,128)(2,1)S(1)}, f16[208,128]{1,0:T(8,128)(2,1)S(1)}, u32[]{:S(2)}, u32[]{:S(2)}) %collective-permute-start.29) | collective-permute-done | bytes 53280 | tf_op jit(solution)/shard_map/ppermute | solution.py:75
  71.0 1.4 %collective-permute-done.30 = f16[208,128]{1,0:T(8,128)(2,1)S(1)} collective-permute-done((f16[208,128]{1,0:T(8,128)(2,1)S(1)}, f16[208,128]{1,0:T(8,128)(2,1)S(1)}, u32[]{:S(2)}, u32[]{:S(2)}) %collective-permute-start.30) | collective-permute-done | bytes 53280 | tf_op jit(solution)/shard_map/ppermute | solution.py:75
  72.6 1.2 %collective-permute-start.31 = (f32[48,128]{1,0:T(8,128)S(1)}, f32[48,128]{1,0:T(8,128)S(1)}, u32[]{:S(2)}, u32[]{:S(2)}) collective-permute-start(f32[48,128]{1,0:T(8,128)S(1)} %get-tuple-element.80), channel_id=1, source_target_pairs={{0,2},{1,3},{2,0},{3,1},{4,6},{5,7},{6,4},{7,5},{8,10},{9,11},{10,... | collective-permute-start | bytes 73736 | tf_op jit(solution)/shard_map/ppermute | solution.py:75
  73.8 1.8 %collective-permute-start.32 = (f32[48,128]{1,0:T(8,128)S(1)}, f32[48,128]{1,0:T(8,128)S(1)}, u32[]{:S(2)}, u32[]{:S(2)}) collective-permute-start(f32[48,128]{1,0:T(8,128)S(1)} %get-tuple-element.81), channel_id=1, source_target_pairs={{0,4},{1,5},{2,6},{3,7},{4,0},{5,1},{6,2},{7,3},{8,12},{9,13},{10,... | collective-permute-start | bytes 73736 | tf_op jit(solution)/shard_map/ppermute | solution.py:75
  75.6 1.5 %collective-permute-start.33 = (f32[48,128]{1,0:T(8,128)S(1)}, f32[48,128]{1,0:T(8,128)S(1)}, u32[]{:S(2)}, u32[]{:S(2)}) collective-permute-start(f32[48,128]{1,0:T(8,128)S(1)} %get-tuple-element.82), channel_id=1, source_target_pairs={{0,6},{1,7},{2,4},{3,5},{4,2},{5,3},{6,0},{7,1},{8,14},{9,15},{10,... | collective-permute-start | bytes 73736 | tf_op jit(solution)/shard_map/ppermute | solution.py:75
  77.0 1.0 %shard_map.104 = (bf16[128,768]{1,0:T(8,128)(2,1)}, bf16[128,768]{1,0:T(8,128)(2,1)}) custom-call(bf16[128,384]{1,0:T(8,128)(2,1)S(1)} %get-tuple-element.67.refs_0_, bf16[128,384]{1,0:T(8,128)(2,1)S(1)} %collective-permute-done.24.refs_1_, bf16[128,384]{1,0:T(8,128)(2,1)S(1)} %collective-permute-done.25.refs_2_, ...), custom_call_target="tpu_custom_call" | custom-call | bytes 786432 | tf_op jit(solution)/shard_map/pallas_call | solution.py:81
  78.5 2.7 %collective-permute-done.33.refs_3_ = f32[48,128]{1,0:T(8,128)S(1)} collective-permute-done((f32[48,128]{1,0:T(8,128)S(1)}, f32[48,128]{1,0:T(8,128)S(1)}, u32[]{:S(2)}, u32[]{:S(2)}) %collective-permute-start.33) | collective-permute-done | bytes 24608 | tf_op jit(solution)/shard_map/ppermute | solution.py:75
  81.2 0.8 shard_map.107
  (46 shorter events, 2.4 us)
Async XLA Ops:
  2.3 6.6 %collective-permute-start = (bf16[48,384]{1,0:T(8,128)(2,1)S(1)}, bf16[48,384]{1,0:T(8,128)(2,1)S(1)}, u32[]{:S(2)}, u32[]{:S(2)}) collective-permute-start(bf16[48,384]{1,0:T(8,128)(2,1)S(1)} %get-tuple-element.44), channel_id=1, source_target_pairs={{0,2},{1,3},{2,0},{3,1},{4,6},{5,7},{6,4},{7,5},{8,10},{9,11},{10,... | collective-permute-start | bytes 110600 | tf_op jit(solution)/shard_map/ppermute | solution.py:75
  5.5 5.6 %collective-permute-start.1 = (bf16[48,384]{1,0:T(8,128)(2,1)S(1)}, bf16[48,384]{1,0:T(8,128)(2,1)S(1)}, u32[]{:S(2)}, u32[]{:S(2)}) collective-permute-start(bf16[48,384]{1,0:T(8,128)(2,1)S(1)} %get-tuple-element.45), channel_id=1, source_target_pairs={{0,4},{1,5},{2,6},{3,7},{4,0},{5,1},{6,2},{7,3},{8,12},{9,13},{10,... | collective-permute-start | bytes 110600 | tf_op jit(solution)/shard_map/ppermute | solution.py:75
  8.1 6.1 %collective-permute-start.2 = (bf16[48,384]{1,0:T(8,128)(2,1)S(1)}, bf16[48,384]{1,0:T(8,128)(2,1)S(1)}, u32[]{:S(2)}, u32[]{:S(2)}) collective-permute-start(bf16[48,384]{1,0:T(8,128)(2,1)S(1)} %get-tuple-element.46), channel_id=1, source_target_pairs={{0,6},{1,7},{2,4},{3,5},{4,2},{5,3},{6,0},{7,1},{8,14},{9,15},{10,... | collective-permute-start | bytes 110600 | tf_op jit(solution)/shard_map/ppermute | solution.py:75
  8.1 15.2 %collective-permute-start.10 = (bf16[192,384]{1,0:T(8,128)(2,1)S(1)}, bf16[192,384]{1,0:T(8,128)(2,1)S(1)}, u32[]{:S(2)}, u32[]{:S(2)}) collective-permute-start(bf16[192,384]{1,0:T(8,128)(2,1)S(1)} %get-tuple-element.49), channel_id=1, source_target_pairs={{0,2},{1,3},{2,0},{3,1},{4,6},{5,7},{6,4},{7,5},{8,10},{9,11},{10,... | collective-permute-start | bytes 442376 | tf_op jit(solution)/shard_map/ppermute | solution.py:75
  14.4 4.7 %collective-permute-start.3 = (bf16[384,128]{1,0:T(8,128)(2,1)S(1)}, bf16[384,128]{1,0:T(8,128)(2,1)S(1)}, u32[]{:S(2)}, u32[]{:S(2)}) collective-permute-start(bf16[384,128]{1,0:T(8,128)(2,1)S(1)} %get-tuple-element.47.refs_0_), channel_id=1, source_target_pairs={{0,1},{1,0},{2,3},{3,2},{4,5},{5,4},{6,7},{7,6},{8,9},{9,8},{10,11... | collective-permute-start | bytes 294920 | tf_op jit(solution)/shard_map/ppermute | solution.py:75
  16.0 3.1 %collective-permute-start.4 = (bf16[384,128]{1,0:T(8,128)(2,1)S(1)}, bf16[384,128]{1,0:T(8,128)(2,1)S(1)}, u32[]{:S(2)}, u32[]{:S(2)}) collective-permute-start(bf16[384,128]{1,0:T(8,128)(2,1)S(1)} %get-tuple-element.47.refs_0_), channel_id=1, source_target_pairs={{0,8},{1,9},{2,10},{3,11},{4,12},{5,13},{6,14},{7,15},{8,0},{9,1},... | collective-permute-start | bytes 294920 | tf_op jit(solution)/shard_map/ppermute | solution.py:75
  16.0 5.7 %collective-permute-start.6 = (bf16[384,128]{1,0:T(8,128)(2,1)S(1)}, bf16[384,128]{1,0:T(8,128)(2,1)S(1)}, u32[]{:S(2)}, u32[]{:S(2)}) collective-permute-start(bf16[384,128]{1,0:T(8,128)(2,1)S(1)} %get-tuple-element.47.refs_0_), channel_id=1, source_target_pairs={{0,16},{1,17},{2,18},{3,19},{4,20},{5,21},{6,22},{7,23},{8,24},{9,... | collective-permute-start | bytes 294920 | tf_op jit(solution)/shard_map/ppermute | solution.py:75
  17.5 5.8 %collective-permute-start.7 = (bf16[384,128]{1,0:T(8,128)(2,1)S(1)}, bf16[384,128]{1,0:T(8,128)(2,1)S(1)}, u32[]{:S(2)}, u32[]{:S(2)}) collective-permute-start(bf16[384,128]{1,0:T(8,128)(2,1)S(1)} %get-tuple-element.47.refs_0_), channel_id=1, source_target_pairs={{0,17},{1,16},{2,19},{3,18},{4,21},{5,20},{6,23},{7,22},{8,25},{9,... | collective-permute-start | bytes 294920 | tf_op jit(solution)/shard_map/ppermute | solution.py:75
  19.1 10.6 %collective-permute-start.11 = (bf16[192,384]{1,0:T(8,128)(2,1)S(1)}, bf16[192,384]{1,0:T(8,128)(2,1)S(1)}, u32[]{:S(2)}, u32[]{:S(2)}) collective-permute-start(bf16[192,384]{1,0:T(8,128)(2,1)S(1)} %get-tuple-element.50), channel_id=1, source_target_pairs={{0,4},{1,5},{2,6},{3,7},{4,0},{5,1},{6,2},{7,3},{8,12},{9,13},{10,... | collective-permute-start | bytes 442376 | tf_op jit(solution)/shard_map/ppermute | solution.py:75
  19.1 10.6 %collective-permute-start.12 = (bf16[192,384]{1,0:T(8,128)(2,1)S(1)}, bf16[192,384]{1,0:T(8,128)(2,1)S(1)}, u32[]{:S(2)}, u32[]{:S(2)}) collective-permute-start(bf16[192,384]{1,0:T(8,128)(2,1)S(1)} %get-tuple-element.51), channel_id=1, source_target_pairs={{0,6},{1,7},{2,4},{3,5},{4,2},{5,3},{6,0},{7,1},{8,14},{9,15},{10,... | collective-permute-start | bytes 442376 | tf_op jit(solution)/shard_map/ppermute | solution.py:75
  21.6 3.5 %collective-permute-start.5 = (bf16[384,128]{1,0:T(8,128)(2,1)S(1)}, bf16[384,128]{1,0:T(8,128)(2,1)S(1)}, u32[]{:S(2)}, u32[]{:S(2)}) collective-permute-start(bf16[384,128]{1,0:T(8,128)(2,1)S(1)} %collective-permute-done.3.refs_1_), channel_id=1, source_target_pairs={{0,8},{1,9},{2,10},{3,11},{4,12},{5,13},{6,14},{7,15},{8,0},{9,1},... | collective-permute-start | bytes 294920 | tf_op jit(solution)/shard_map/ppermute | solution.py:75
  23.3 1.8 %collective-permute-start.8 = (bf16[384,128]{1,0:T(8,128)(2,1)S(1)}, bf16[384,128]{1,0:T(8,128)(2,1)S(1)}, u32[]{:S(2)}, u32[]{:S(2)}) collective-permute-start(bf16[384,128]{1,0:T(8,128)(2,1)S(1)} %collective-permute-done.6.refs_4_), channel_id=1, source_target_pairs={{0,8},{1,9},{2,10},{3,11},{4,12},{5,13},{6,14},{7,15},{8,0},{9,1},... | collective-permute-start | bytes 294920 | tf_op jit(solution)/shard_map/ppermute | solution.py:75
  23.3 1.8 %collective-permute-start.9 = (bf16[384,128]{1,0:T(8,128)(2,1)S(1)}, bf16[384,128]{1,0:T(8,128)(2,1)S(1)}, u32[]{:S(2)}, u32[]{:S(2)}) collective-permute-start(bf16[384,128]{1,0:T(8,128)(2,1)S(1)} %collective-permute-done.7.refs_5_), channel_id=1, source_target_pairs={{0,8},{1,9},{2,10},{3,11},{4,12},{5,13},{6,14},{7,15},{8,0},{9,1},... | collective-permute-start | bytes 294920 | tf_op jit(solution)/shard_map/ppermute | solution.py:75
  31.0 2.4 %collective-permute-start.13 = (f32[1536,128]{1,0:T(8,128)S(1)}, f32[1536,128]{1,0:T(8,128)S(1)}, u32[]{:S(2)}, u32[]{:S(2)}) collective-permute-start(f32[1536,128]{1,0:T(8,128)S(1)} %get-tuple-element.58), channel_id=1, source_target_pairs={{0,8},{1,9},{2,10},{3,11},{4,12},{5,13},{6,14},{7,15},{8,0},{9,1},... | collective-permute-start | bytes 2359304 | tf_op jit(solution)/shard_map/ppermute | solution.py:75
  33.5 5.0 %collective-permute-start.14 = (f16[400,128]{1,0:T(8,128)(2,1)S(1)}, f16[400,128]{1,0:T(8,128)(2,1)S(1)}, u32[]{:S(2)}, u32[]{:S(2)}) collective-permute-start(f16[400,128]{1,0:T(8,128)(2,1)S(1)} %convert_element_type.36), channel_id=1, source_target_pairs={{0,1},{1,0},{2,3},{3,2},{4,5},{5,4},{6,7},{7,6},{8,9},{9,8},{10,11... | collective-permute-start | bytes 307208 | tf_op jit(solution)/shard_map/ppermute | solution.py:75
  35.1 5.7 %collective-permute-start.15 = (f16[400,128]{1,0:T(8,128)(2,1)S(1)}, f16[400,128]{1,0:T(8,128)(2,1)S(1)}, u32[]{:S(2)}, u32[]{:S(2)}) collective-permute-start(f16[400,128]{1,0:T(8,128)(2,1)S(1)} %convert_element_type.38), channel_id=1, source_target_pairs={{0,16},{1,17},{2,18},{3,19},{4,20},{5,21},{6,22},{7,23},{8,24},{9,... | collective-permute-start | bytes 307208 | tf_op jit(solution)/shard_map/ppermute | solution.py:75
  36.7 5.6 %collective-permute-start.16 = (f16[400,128]{1,0:T(8,128)(2,1)S(1)}, f16[400,128]{1,0:T(8,128)(2,1)S(1)}, u32[]{:S(2)}, u32[]{:S(2)}) collective-permute-start(f16[400,128]{1,0:T(8,128)(2,1)S(1)} %convert_element_type.40), channel_id=1, source_target_pairs={{0,17},{1,16},{2,19},{3,18},{4,21},{5,20},{6,23},{7,22},{8,25},{9,... | collective-permute-start | bytes 307208 | tf_op jit(solution)/shard_map/ppermute | solution.py:75
  42.4 4.2 %collective-permute-start.18 = (bf16[208,128]{1,0:T(8,128)(2,1)S(1)}, bf16[208,128]{1,0:T(8,128)(2,1)S(1)}, u32[]{:S(2)}, u32[]{:S(2)}) collective-permute-start(bf16[208,128]{1,0:T(8,128)(2,1)S(1)} %shard_map.100.refs_14_), channel_id=1, source_target_pairs={{0,1},{1,0},{2,3},{3,2},{4,5},{5,4},{6,7},{7,6},{8,9},{9,8},{10,11... | collective-permute-start | bytes 159752 | tf_op jit(solution)/shard_map/ppermute | solution.py:75
  43.6 4.1 %collective-permute-start.20 = (bf16[208,128]{1,0:T(8,128)(2,1)S(1)}, bf16[208,128]{1,0:T(8,128)(2,1)S(1)}, u32[]{:S(2)}, u32[]{:S(2)}) collective-permute-start(bf16[208,128]{1,0:T(8,128)(2,1)S(1)} %shard_map.100.refs_14_), channel_id=1, source_target_pairs={{0,16},{1,17},{2,18},{3,19},{4,20},{5,21},{6,22},{7,23},{8,24},{9,... | collective-permute-start | bytes 159752 | tf_op jit(solution)/shard_map/ppermute | solution.py:75
  45.1 5.0 %collective-permute-start.22 = (bf16[208,128]{1,0:T(8,128)(2,1)S(1)}, bf16[208,128]{1,0:T(8,128)(2,1)S(1)}, u32[]{:S(2)}, u32[]{:S(2)}) collective-permute-start(bf16[208,128]{1,0:T(8,128)(2,1)S(1)} %shard_map.100.refs_14_), channel_id=1, source_target_pairs={{0,17},{1,16},{2,19},{3,18},{4,21},{5,20},{6,23},{7,22},{8,25},{9,... | collective-permute-start | bytes 159752 | tf_op jit(solution)/shard_map/ppermute | solution.py:75
  45.9 9.9 %collective-permute-start.17 = (bf16[208,128]{1,0:T(8,128)(2,1)S(1)}, bf16[208,128]{1,0:T(8,128)(2,1)S(1)}, u32[]{:S(2)}, u32[]{:S(2)}) collective-permute-start(bf16[208,128]{1,0:T(8,128)(2,1)S(1)} %shard_map.100.refs_14_), channel_id=1, source_target_pairs={{0,8},{1,9},{2,10},{3,11},{4,12},{5,13},{6,14},{7,15},{8,0},{9,1},... | collective-permute-start | bytes 159752 | tf_op jit(solution)/shard_map/ppermute | solution.py:75
  46.6 9.3 %collective-permute-start.19 = (bf16[208,128]{1,0:T(8,128)(2,1)S(1)}, bf16[208,128]{1,0:T(8,128)(2,1)S(1)}, u32[]{:S(2)}, u32[]{:S(2)}) collective-permute-start(bf16[208,128]{1,0:T(8,128)(2,1)S(1)} %collective-permute-done.18.refs_15_), channel_id=1, source_target_pairs={{0,8},{1,9},{2,10},{3,11},{4,12},{5,13},{6,14},{7,15},{8,0},{9,1},... | collective-permute-start | bytes 159752 | tf_op jit(solution)/shard_map/ppermute | solution.py:75
  47.8 8.1 %collective-permute-start.21 = (bf16[208,128]{1,0:T(8,128)(2,1)S(1)}, bf16[208,128]{1,0:T(8,128)(2,1)S(1)}, u32[]{:S(2)}, u32[]{:S(2)}) collective-permute-start(bf16[208,128]{1,0:T(8,128)(2,1)S(1)} %collective-permute-done.20.refs_16_), channel_id=1, source_target_pairs={{0,8},{1,9},{2,10},{3,11},{4,12},{5,13},{6,14},{7,15},{8,0},{9,1},... | collective-permute-start | bytes 159752 | tf_op jit(solution)/shard_map/ppermute | solution.py:75
  50.1 5.7 %collective-permute-start.23 = (bf16[208,128]{1,0:T(8,128)(2,1)S(1)}, bf16[208,128]{1,0:T(8,128)(2,1)S(1)}, u32[]{:S(2)}, u32[]{:S(2)}) collective-permute-start(bf16[208,128]{1,0:T(8,128)(2,1)S(1)} %collective-permute-done.22.refs_17_), channel_id=1, source_target_pairs={{0,8},{1,9},{2,10},{3,11},{4,12},{5,13},{6,14},{7,15},{8,0},{9,1},... | collective-permute-start | bytes 159752 | tf_op jit(solution)/shard_map/ppermute | solution.py:75
  57.9 1.9 %collective-permute-start.27 = (f32[768,128]{1,0:T(8,128)S(1)}, f32[768,128]{1,0:T(8,128)S(1)}, u32[]{:S(2)}, u32[]{:S(2)}) collective-permute-start(f32[768,128]{1,0:T(8,128)S(1)} %get-tuple-element.74), channel_id=1, source_target_pairs={{0,8},{1,9},{2,10},{3,11},{4,12},{5,13},{6,14},{7,15},{8,0},{9,1},... | collective-permute-start | bytes 1179656 | tf_op jit(solution)/shard_map/ppermute | solution.py:75
  60.0 7.3 %collective-permute-start.28 = (f16[208,128]{1,0:T(8,128)(2,1)S(1)}, f16[208,128]{1,0:T(8,128)(2,1)S(1)}, u32[]{:S(2)}, u32[]{:S(2)}) collective-permute-start(f16[208,128]{1,0:T(8,128)(2,1)S(1)} %convert_element_type.42), channel_id=1, source_target_pairs={{0,1},{1,0},{2,3},{3,2},{4,5},{5,4},{6,7},{7,6},{8,9},{9,8},{10,11... | collective-permute-start | bytes 159752 | tf_op jit(solution)/shard_map/ppermute | solution.py:75
  60.6 15.0 %collective-permute-start.24 = (bf16[128,384]{1,0:T(8,128)(2,1)S(1)}, bf16[128,384]{1,0:T(8,128)(2,1)S(1)}, u32[]{:S(2)}, u32[]{:S(2)}) collective-permute-start(bf16[128,384]{1,0:T(8,128)(2,1)S(1)} %get-tuple-element.68), channel_id=1, source_target_pairs={{0,2},{1,3},{2,0},{3,1},{4,6},{5,7},{6,4},{7,5},{8,10},{9,11},{10,... | collective-permute-start | bytes 294920 | tf_op jit(solution)/shard_map/ppermute | solution.py:75
  63.9 13.1 %collective-permute-start.25 = (bf16[128,384]{1,0:T(8,128)(2,1)S(1)}, bf16[128,384]{1,0:T(8,128)(2,1)S(1)}, u32[]{:S(2)}, u32[]{:S(2)}) collective-permute-start(bf16[128,384]{1,0:T(8,128)(2,1)S(1)} %get-tuple-element.69), channel_id=1, source_target_pairs={{0,4},{1,5},{2,6},{3,7},{4,0},{5,1},{6,2},{7,3},{8,12},{9,13},{10,... | collective-permute-start | bytes 294920 | tf_op jit(solution)/shard_map/ppermute | solution.py:75
  64.9 12.2 %collective-permute-start.26 = (bf16[128,384]{1,0:T(8,128)(2,1)S(1)}, bf16[128,384]{1,0:T(8,128)(2,1)S(1)}, u32[]{:S(2)}, u32[]{:S(2)}) collective-permute-start(bf16[128,384]{1,0:T(8,128)(2,1)S(1)} %get-tuple-element.70), channel_id=1, source_target_pairs={{0,6},{1,7},{2,4},{3,5},{4,2},{5,3},{6,0},{7,1},{8,14},{9,15},{10,... | collective-permute-start | bytes 294920 | tf_op jit(solution)/shard_map/ppermute | solution.py:75
  66.3 4.6 %collective-permute-start.29 = (f16[208,128]{1,0:T(8,128)(2,1)S(1)}, f16[208,128]{1,0:T(8,128)(2,1)S(1)}, u32[]{:S(2)}, u32[]{:S(2)}) collective-permute-start(f16[208,128]{1,0:T(8,128)(2,1)S(1)} %convert_element_type.44), channel_id=1, source_target_pairs={{0,16},{1,17},{2,18},{3,19},{4,20},{5,21},{6,22},{7,23},{8,24},{9,... | collective-permute-start | bytes 159752 | tf_op jit(solution)/shard_map/ppermute | solution.py:75
  67.3 5.1 %collective-permute-start.30 = (f16[208,128]{1,0:T(8,128)(2,1)S(1)}, f16[208,128]{1,0:T(8,128)(2,1)S(1)}, u32[]{:S(2)}, u32[]{:S(2)}) collective-permute-start(f16[208,128]{1,0:T(8,128)(2,1)S(1)} %convert_element_type.46), channel_id=1, source_target_pairs={{0,17},{1,16},{2,19},{3,18},{4,21},{5,20},{6,23},{7,22},{8,25},{9,... | collective-permute-start | bytes 159752 | tf_op jit(solution)/shard_map/ppermute | solution.py:75
  72.6 5.4 %collective-permute-start.31 = (f32[48,128]{1,0:T(8,128)S(1)}, f32[48,128]{1,0:T(8,128)S(1)}, u32[]{:S(2)}, u32[]{:S(2)}) collective-permute-start(f32[48,128]{1,0:T(8,128)S(1)} %get-tuple-element.80), channel_id=1, source_target_pairs={{0,2},{1,3},{2,0},{3,1},{4,6},{5,7},{6,4},{7,5},{8,10},{9,11},{10,... | collective-permute-start | bytes 73736 | tf_op jit(solution)/shard_map/ppermute | solution.py:75
  73.8 4.7 %collective-permute-start.32 = (f32[48,128]{1,0:T(8,128)S(1)}, f32[48,128]{1,0:T(8,128)S(1)}, u32[]{:S(2)}, u32[]{:S(2)}) collective-permute-start(f32[48,128]{1,0:T(8,128)S(1)} %get-tuple-element.81), channel_id=1, source_target_pairs={{0,4},{1,5},{2,6},{3,7},{4,0},{5,1},{6,2},{7,3},{8,12},{9,13},{10,... | collective-permute-start | bytes 73736 | tf_op jit(solution)/shard_map/ppermute | solution.py:75
  75.6 5.6 %collective-permute-start.33 = (f32[48,128]{1,0:T(8,128)S(1)}, f32[48,128]{1,0:T(8,128)S(1)}, u32[]{:S(2)}, u32[]{:S(2)}) collective-permute-start(f32[48,128]{1,0:T(8,128)S(1)} %get-tuple-element.82), channel_id=1, source_target_pairs={{0,6},{1,7},{2,4},{3,5},{4,2},{5,3},{6,0},{7,1},{8,14},{9,15},{10,... | collective-permute-start | bytes 73736 | tf_op jit(solution)/shard_map/ppermute | solution.py:75
